TPU v7x, 256 devices: a whole 4x4x8 slice. The times are simulated.
256 devices in a mesh: tile: 16 (over z, core), state: 16 (over x, y).
Axes of the slice: x: 4, y: 4, z: 8, core: 2. Of those that a mesh axis runs over, the one named last changes fastest.
Arguments:
- states: float32 [2, 128, 512, 128], P(None, 'tile', 'state'), parts along dimension 2, may hold values from -6 to 6
- onsite: float32 [2, 128, 128], P(None, 'tile'), may hold values from -0.5 to 0.5
- hop_row: float32 [2, 128, 128], P(None, 'tile'), may hold values from -3.2 to -2.2
- hop_up: float32 [2, 128, 128], P(None, 'tile'), may hold values from -3.2 to -2.2
- partner: int32 [128, 16], P('tile'), may hold values from -1 to 127, as said below
- coupling: bfloat16 [128, 16, 128, 128], P('tile'), may hold values from -0.125 to 0.125
- coefs: float32 [7], replicated, may hold values from 0.3 to 1
Outputs:
- filtered: float32 [2, 128, 512, 128], P(None, 'tile', 'state'), parts along dimension 2
There are 16 independent parts, one for each index of `state`. A program takes and returns all parts, laid end to end along the dimension named above; an argument that names none is the same for every part. Nothing has to cross between parts.
Inputs may be any that keep to these rules, and one draw needn't show every extreme that they name: `partner`: A layer-one row r names only layer-two rows within 8 rows of r, cyclically; every row has at least 8 filled slots, filled slots come first.
All inputs are finite; a program needn't handle non-finite values.
Results may differ from a plain program's by a relative error of at most 0.00087.
Values may be sent and summed in bfloat16 or wider, within the bound.
No kernel may reach another device: no remote copies, remote signals or barrier semaphores. Data moves between devices by JAX's collectives and lax.ppermute only.
A program may use at most 64 MiB of HBM per device.

v0:
```python
import jax
import jax.numpy as jnp
from jax import lax
from jax.sharding import PartitionSpec as P

REACH = 8


def passed_along(x, axis, by):
    size = lax.axis_size(axis)
    return lax.ppermute(x, axis, [(i, (i + by) % size) for i in range(size)])


def with_halo(cells, sides, width):
    for axis, dim in sides:
        count = lax.axis_size(axis)
        head = lax.slice_in_dim(cells, 0, width, axis=dim)
        tail = lax.slice_in_dim(cells, cells.shape[dim] - width, cells.shape[dim], axis=dim)
        cells = jnp.concatenate(
            [
                lax.ppermute(tail, axis, [(i, (i + 1) % count) for i in range(count)]),
                cells,
                lax.ppermute(head, axis, [((i + 1) % count, i) for i in range(count)]),
            ],
            axis=dim,
        )
    return cells


def body(states, onsite, hop_row, hop_up, partner, coupling, coefs):
    rows = states.shape[1]
    tile_index = lax.axis_index("tile")
    total = rows * lax.axis_size("tile")
    global_row = tile_index * rows + jnp.arange(rows, dtype=jnp.int32)
    column = jnp.arange(states.shape[3], dtype=jnp.int32)
    parity = (global_row[:, None] + column[None, :]) % 2 == 0
    bond_up = jnp.where(parity[None], hop_up, jnp.float32(0.0))
    bond_last = passed_along(bond_up[:, rows - 1 :], "tile", 1)
    bond_below = jnp.concatenate([bond_last, bond_up[:, : rows - 1]], axis=1)
    row_left = jnp.roll(hop_row, 1, 2)
    valid = partner >= 0
    mask_low = valid.astype(jnp.bfloat16)[:, :, None, None]
    mask_high = valid.astype(jnp.float32)[:, :, None, None]
    target = jnp.where(valid, partner, 0)
    near_index = (target - (tile_index * rows - REACH)) % total
    slot_count = partner.shape[0] * partner.shape[1]

    def hamiltonian(field):
        rounded = field.astype(jnp.bfloat16)
        first = rounded[0]
        rim_rows = with_halo(field, (("tile", 1),), 1)
        above = rim_rows[:, 2:]
        below = rim_rows[:, :-2]
        nearby = with_halo(rounded[1], (("tile", 0),), REACH)
        intra = onsite[:, :, None, :] * field
        intra = intra + hop_row[:, :, None, :] * jnp.roll(field, -1, 3)
        intra = intra + row_left[:, :, None, :] * jnp.roll(field, 1, 3)
        intra = intra + bond_up[:, :, None, :] * above
        intra = intra + bond_below[:, :, None, :] * below
        picked = nearby[near_index] * mask_low
        upper = jnp.einsum("bksj,bkij->bsi", picked, coupling, preferred_element_type=jnp.float32)
        terms = (
            jnp.einsum("bsi,bkij->bksj", first, coupling, preferred_element_type=jnp.float32)
            * mask_high
        )
        flat_terms = terms.reshape((slot_count,) + terms.shape[2:])
        gathered = (
            jnp.zeros((rows + 2 * REACH,) + first.shape[1:], jnp.float32)
            .at[near_index.reshape(slot_count)]
            .add(flat_terms)
        )
        lower = gathered[REACH : REACH + rows]
        next_terms = passed_along(gathered[:REACH], "tile", -1)
        prev_terms = passed_along(gathered[REACH + rows :], "tile", 1)
        lower = lower.at[rows - REACH :].add(next_terms)
        lower = lower.at[:REACH].add(prev_terms)
        return (intra + jnp.stack([upper, lower])) * (1.0 / 12.0)

    previous = states
    current = hamiltonian(states)
    filtered = coefs[0] * previous + coefs[1] * current
    for order in range(2, coefs.shape[0]):
        following = 2.0 * hamiltonian(current) - previous
        filtered = filtered + coefs[order] * following
        previous, current = (current, following)
    return filtered


def solution(mesh):
    placed = (
        P(None, "tile", "state", None),
        P(None, "tile", None),
        P(None, "tile", None),
        P(None, "tile", None),
        P("tile", None),
        P("tile", None, None, None),
        P(),
    )
    return jax.shard_map(
        body, mesh=mesh, in_specs=placed, out_specs=P(None, "tile", "state", None), check_vma=False
    )
```

profile of v0, /device:TPU:1, one launch (start us, length us, event | category | flops | bytes accessed | tf_op | source)
XLA Modules:
  0.0 163.1 jit_solution(4188410201737491138)
XLA Ops:
  0.0 1.0 convert_element_type.24
  1.0 3.0 %collective-permute-start.3 = (bf16[8,32,128]{2,1,0:T(8,128)(2,1)S(1)}, bf16[8,32,128]{2,1,0:T(8,128)(2,1)S(1)}, u32[]{:S(2)}, u32[]{:S(2)}) collective-permute-start(bf16[8,32,128]{2,1,0:T(8,128)(2,1)S(1)} %slice_bitcast_fusion.17), channel_id=1, source_target_pairs={{0,16},{16,32},{32,48},{48,64},{64,80},{80,96},{96,112},{112,128},... | collective-permute-start | bytes 196616 | tf_op jit(solution)/shard_map/ppermute | solution.py:21
  5.8 2.9 %convolution_multiply_fusion = f32[8,16,128,32]{2,3,1,0:T(8,128)S(1)} fusion(bf16[8,16,128,128]{3,2,1,0:T(8,128)(2,1)} %param.60, f32[8,16]{1,0:T(8,128)S(1)} %get-tuple-element.306, bf16[2,8,32,128]{3,2,1,0:T(8,128)(2,1)S(1)} %convert_element_type.24), kind=kOutput, calls=%fused_computation.12 | convolution fusion | flops 134742016 | bytes 6361088 | tf_op jit(solution)/shard_map/bsi,bkij->bksj/dot_general | solution.py:63
  8.7 5.8 %scatter_fusion = f32[24,32,128]{2,1,0:T(8,128)S(1)} fusion(f32[24,32,128]{2,1,0:T(8,128)S(1)} %broadcast.524.clone.1, s32[128]{0:T(128)S(1)} %fusion.84, f32[128,32,128]{2,1,0:T(8,128)S(1)} %bitcast.136), kind=kCustom, calls=%fused_computation.6 | custom fusion | flops 524288 | bytes 6291968 | tf_op jit(solution)/shard_map/scatter-add | solution.py:70
  15.2 3.6 %collective-permute-start.5 = (f32[8,32,128]{2,1,0:T(8,128)}, f32[8,32,128]{2,1,0:T(8,128)S(1)}, u32[]{:S(2)}, u32[]{:S(2)}) collective-permute-start(f32[8,32,128]{2,1,0:T(8,128)} %get-tuple-element.267), channel_id=1, source_target_pairs={{0,240},{16,0},{32,16},{48,32},{64,48},{80,64},{96,80},{112,96},{1... | collective-permute-start | bytes 393224 | tf_op jit(solution)/shard_map/ppermute | solution.py:11
  22.0 3.2 %collective-permute-start = (f32[2,1,32,128]{3,2,1,0:T(8,128)}, f32[2,1,32,128]{3,2,1,0:T(8,128)S(1)}, u32[]{:S(2)}, u32[]{:S(2)}) collective-permute-start(f32[2,1,32,128]{3,2,1,0:T(8,128)} %get-tuple-element.303), channel_id=1, source_target_pairs={{16,0},{32,16},{48,32},{64,48},{80,64},{96,80},{112,96},{128,112},... | collective-permute-start | bytes 98312 | tf_op jit(solution)/shard_map/ppermute | solution.py:23
  26.1 3.8 %convolution_bitcast_fusion.5 = f32[1,8,32,128]{3,2,1,0:T(8,128)S(1)} fusion(bf16[8,16,128,128]{3,2,1,0:T(8,128)(2,1)} %param.60, bf16[8,16,32,128]{3,2,1,0:T(8,128)(2,1)S(1)} %bitcast.138, bf16[8,16]{1,0:T(8,128)(2,1)S(1)} %get-tuple-element.305), kind=kOutput, calls=%fused_computation.23 | convolution fusion | flops 134742016 | bytes 5374208 | tf_op jit(solution)/shard_map/bksj,bkij->bsi/dot_general | solution.py:61
  30.0 0.9 fusion.77
  31.5 1.0 fusion.87
  33.1 1.3 collective-permute-start.9
  36.9 5.8 %scatter_fusion.1 = f32[24,32,128]{2,1,0:T(8,128)S(1)} fusion(f32[24,32,128]{2,1,0:T(8,128)S(1)} %broadcast.524.clone, s32[128]{0:T(128)S(1)} %copy-done.56, f32[128,32,128]{2,1,0:T(8,128)S(1)} %bitcast.132), kind=kCustom, calls=%fused_computation.7 | custom fusion | flops 524288 | bytes 6291968 | tf_op jit(solution)/shard_map/scatter-add | solution.py:70
  44.0 1.6 %collective-permute-start.11 = (f32[8,32,128]{2,1,0:T(8,128)}, f32[8,32,128]{2,1,0:T(8,128)}, u32[]{:S(2)}, u32[]{:S(2)}) collective-permute-start(f32[8,32,128]{2,1,0:T(8,128)} %get-tuple-element.265), channel_id=1, source_target_pairs={{0,240},{16,0},{32,16},{48,32},{64,48},{80,64},{96,80},{112,96},{1... | collective-permute-start | bytes 393224 | tf_op jit(solution)/shard_map/ppermute | solution.py:11
  45.8 2.9 %collective-permute-start.7 = (f32[2,1,32,128]{3,2,1,0:T(8,128)}, f32[2,1,32,128]{3,2,1,0:T(8,128)}, u32[]{:S(2)}, u32[]{:S(2)}) collective-permute-start(f32[2,1,32,128]{3,2,1,0:T(8,128)} %get-tuple-element.297), channel_id=1, source_target_pairs={{16,0},{32,16},{48,32},{64,48},{80,64},{96,80},{112,96},{128,112},... | collective-permute-start | bytes 98312 | tf_op jit(solution)/shard_map/ppermute | solution.py:23
  49.3 0.9 pad_maximum_fusion.13
  50.2 0.9 gather_fusion.1
  51.1 3.8 %convolution_bitcast_fusion.4 = f32[1,8,32,128]{3,2,1,0:T(8,128)S(1)} fusion(bf16[8,16,128,128]{3,2,1,0:T(8,128)(2,1)} %param.60, bf16[8,16,32,128]{3,2,1,0:T(8,128)(2,1)S(1)} %bitcast.139, bf16[8,16]{1,0:T(8,128)(2,1)} %copy-done.47), kind=kOutput, calls=%fused_computation.22 | convolution fusion | flops 134742016 | bytes 5374208 | tf_op jit(solution)/shard_map/bksj,bkij->bsi/dot_general | solution.py:61
  55.0 1.0 fusion.75
  56.1 1.1 fusion.94
  57.8 2.9 %collective-permute-start.16 = (bf16[8,32,128]{2,1,0:T(8,128)(2,1)}, bf16[8,32,128]{2,1,0:T(8,128)(2,1)}, u32[]{:S(2)}, u32[]{:S(2)}) collective-permute-start(bf16[8,32,128]{2,1,0:T(8,128)(2,1)} %slice_bitcast_fusion.11), channel_id=1, source_target_pairs={{16,0},{32,16},{48,32},{64,48},{80,64},{96,80},{112,96},{128,112},... | collective-permute-start | bytes 196616 | tf_op jit(solution)/shard_map/ppermute | solution.py:23
  63.1 5.9 %scatter_fusion.2 = f32[24,32,128]{2,1,0:T(8,128)S(1)} fusion(f32[24,32,128]{2,1,0:T(8,128)S(1)} %broadcast.524.clone.3, s32[128]{0:T(128)} %copy-done.55, f32[128,32,128]{2,1,0:T(8,128)S(1)} %bitcast.133), kind=kCustom, calls=%fused_computation.8 | custom fusion | flops 524288 | bytes 6291968 | tf_op jit(solution)/shard_map/scatter-add | solution.py:70
  70.4 3.0 %collective-permute-start.17 = (f32[8,32,128]{2,1,0:T(8,128)}, f32[8,32,128]{2,1,0:T(8,128)}, u32[]{:S(2)}, u32[]{:S(2)}) collective-permute-start(f32[8,32,128]{2,1,0:T(8,128)} %get-tuple-element.263), channel_id=1, source_target_pairs={{0,240},{16,0},{32,16},{48,32},{64,48},{80,64},{96,80},{112,96},{1... | collective-permute-start | bytes 393224 | tf_op jit(solution)/shard_map/ppermute | solution.py:11
  73.9 1.2 collective-permute-start.14
  75.1 0.9 pad_maximum_fusion.14
  77.0 3.8 %convolution_bitcast_fusion.3 = f32[1,8,32,128]{3,2,1,0:T(8,128)S(1)} fusion(bf16[8,16,128,128]{3,2,1,0:T(8,128)(2,1)} %param.60, bf16[8,16,32,128]{3,2,1,0:T(8,128)(2,1)S(1)} %bitcast.140, bf16[8,16]{1,0:T(8,128)(2,1)S(1)} %copy-done.48), kind=kOutput, calls=%fused_computation.21 | convolution fusion | flops 134742016 | bytes 5374208 | tf_op jit(solution)/shard_map/bksj,bkij->bsi/dot_general | solution.py:61
  80.9 1.0 fusion.73
  82.0 1.1 fusion.92
  83.7 1.2 collective-permute-start.22
  87.3 6.1 %scatter_fusion.3 = f32[24,32,128]{2,1,0:T(8,128)S(1)} fusion(f32[24,32,128]{2,1,0:T(8,128)S(1)} %broadcast.524.clone.2, s32[128]{0:T(128)} %copy-done.55, f32[128,32,128]{2,1,0:T(8,128)S(1)} %bitcast.134), kind=kCustom, calls=%fused_computation.9 | custom fusion | flops 524288 | bytes 6291968 | tf_op jit(solution)/shard_map/scatter-add | solution.py:70
  94.8 3.0 %collective-permute-start.23 = (f32[8,32,128]{2,1,0:T(8,128)}, f32[8,32,128]{2,1,0:T(8,128)}, u32[]{:S(2)}, u32[]{:S(2)}) collective-permute-start(f32[8,32,128]{2,1,0:T(8,128)} %get-tuple-element.261), channel_id=1, source_target_pairs={{0,240},{16,0},{32,16},{48,32},{64,48},{80,64},{96,80},{112,96},{1... | collective-permute-start | bytes 393224 | tf_op jit(solution)/shard_map/ppermute | solution.py:11
  98.3 1.2 collective-permute-start.20
  99.5 0.9 pad_maximum_fusion.15
  101.4 3.8 %convolution_bitcast_fusion.2 = f32[1,8,32,128]{3,2,1,0:T(8,128)S(1)} fusion(bf16[8,16,128,128]{3,2,1,0:T(8,128)(2,1)} %param.60, bf16[8,16,32,128]{3,2,1,0:T(8,128)(2,1)S(1)} %bitcast.141, bf16[8,16]{1,0:T(8,128)(2,1)S(1)} %copy-done.49), kind=kOutput, calls=%fused_computation.20 | convolution fusion | flops 134742016 | bytes 5374208 | tf_op jit(solution)/shard_map/bksj,bkij->bsi/dot_general | solution.py:61
  105.3 1.0 fusion.71
  106.4 1.0 fusion.90
  108.0 1.7 %collective-permute-start.28 = (bf16[8,32,128]{2,1,0:T(8,128)(2,1)}, bf16[8,32,128]{2,1,0:T(8,128)(2,1)}, u32[]{:S(2)}, u32[]{:S(2)}) collective-permute-start(bf16[8,32,128]{2,1,0:T(8,128)(2,1)} %slice_bitcast_fusion.5), channel_id=1, source_target_pairs={{16,0},{32,16},{48,32},{64,48},{80,64},{96,80},{112,96},{128,112},... | collective-permute-start | bytes 196616 | tf_op jit(solution)/shard_map/ppermute | solution.py:23
  112.2 5.9 %scatter_fusion.4 = f32[24,32,128]{2,1,0:T(8,128)S(1)} fusion(f32[24,32,128]{2,1,0:T(8,128)S(1)} %broadcast.524.clone.4, s32[128]{0:T(128)} %copy-done.55, f32[128,32,128]{2,1,0:T(8,128)S(1)} %bitcast.135), kind=kCustom, calls=%fused_computation.10 | custom fusion | flops 524288 | bytes 6291968 | tf_op jit(solution)/shard_map/scatter-add | solution.py:70
  118.2 3.0 %collective-permute-start.29 = (f32[8,32,128]{2,1,0:T(8,128)S(1)}, f32[8,32,128]{2,1,0:T(8,128)S(1)}, u32[]{:S(2)}, u32[]{:S(2)}) collective-permute-start(f32[8,32,128]{2,1,0:T(8,128)S(1)} %get-tuple-element.259), channel_id=1, source_target_pairs={{0,240},{16,0},{32,16},{48,32},{64,48},{80,64},{96,80},{112,96},{1... | collective-permute-start | bytes 393224 | tf_op jit(solution)/shard_map/ppermute | solution.py:11
  121.7 1.2 collective-permute-start.26
  122.9 0.9 pad_maximum_fusion.16
  124.9 3.8 %convolution_bitcast_fusion.1 = f32[1,8,32,128]{3,2,1,0:T(8,128)S(1)} fusion(bf16[8,16,128,128]{3,2,1,0:T(8,128)(2,1)} %param.60, bf16[8,16,32,128]{3,2,1,0:T(8,128)(2,1)S(1)} %bitcast.142, bf16[8,16]{1,0:T(8,128)(2,1)S(1)} %copy-done.50), kind=kOutput, calls=%fused_computation.19 | convolution fusion | flops 134742016 | bytes 5374208 | tf_op jit(solution)/shard_map/bksj,bkij->bsi/dot_general | solution.py:61
  129.2 1.7 %collective-permute-start.34 = (bf16[8,32,128]{2,1,0:T(8,128)(2,1)S(1)}, bf16[8,32,128]{2,1,0:T(8,128)(2,1)S(1)}, u32[]{:S(2)}, u32[]{:S(2)}) collective-permute-start(bf16[8,32,128]{2,1,0:T(8,128)(2,1)S(1)} %slice_bitcast_fusion.2), channel_id=1, source_target_pairs={{16,0},{32,16},{48,32},{64,48},{80,64},{96,80},{112,96},{128,112},... | collective-permute-start | bytes 196616 | tf_op jit(solution)/shard_map/ppermute | solution.py:23
  130.9 2.0 %convolution_multiply_fusion.1 = f32[8,32,16,128]{3,1,2,0:T(8,128)} fusion(bf16[8,16,128,128]{3,2,1,0:T(8,128)(2,1)S(1)} %copy-done.4, f32[8,16]{1,0:T(8,128)S(1)} %copy-done.46, bf16[2,8,32,128]{3,2,1,0:T(8,128)(2,1)S(1)} %get-tuple-element.245), kind=kOutput, calls=%fused_computation.13 | convolution fusion | flops 134742016 | bytes 6361088 | tf_op jit(solution)/shard_map/bsi,bkij->bksj/dot_general | solution.py:63
  134.0 11.8 %scatter_fusion.5 = f32[24,32,128]{2,1,0:T(8,128)S(1)} fusion(f32[24,32,128]{2,1,0:T(8,128)S(1)} %broadcast.524, s32[128]{0:T(128)S(1)} %copy-done.57, f32[128,32,128]{2,1,0:T(8,128)} %bitcast.131), kind=kCustom, calls=%fused_computation.11 | custom fusion | flops 524288 | bytes 6291968 | tf_op jit(solution)/shard_map/scatter-add | solution.py:70
  147.1 3.0 %collective-permute-start.35 = (f32[8,32,128]{2,1,0:T(8,128)}, f32[8,32,128]{2,1,0:T(8,128)}, u32[]{:S(2)}, u32[]{:S(2)}) collective-permute-start(f32[8,32,128]{2,1,0:T(8,128)} %get-tuple-element.257), channel_id=1, source_target_pairs={{0,240},{16,0},{32,16},{48,32},{64,48},{80,64},{96,80},{112,96},{1... | collective-permute-start | bytes 393224 | tf_op jit(solution)/shard_map/ppermute | solution.py:11
  150.6 1.2 collective-permute-start.32
  152.7 3.7 %convolution_bitcast_fusion = f32[1,8,32,128]{3,2,1,0:T(8,128)S(1)} fusion(bf16[8,16,128,128]{3,2,1,0:T(8,128)(2,1)} %param.60, bf16[8,16,32,128]{3,2,1,0:T(8,128)(2,1)S(1)} %bitcast.137, bf16[8,16]{1,0:T(8,128)(2,1)S(1)} %copy-done.50), kind=kOutput, calls=%fused_computation.18 | convolution fusion | flops 134742016 | bytes 5374208 | tf_op jit(solution)/shard_map/bksj,bkij->bsi/dot_general | solution.py:61
  156.4 1.0 fusion.67
  157.5 5.7 %fusion.18 = f32[2,8,32,128]{3,2,1,0:T(8,128)} fusion(f32[2,8,32,128]{3,2,1,0:T(8,128)S(1)} %get-tuple-element.248, f32[2,8,32,128]{3,2,1,0:T(8,128)S(1)} %get-tuple-element.246, f32[2,1,32,128]{3,2,1,0:T(8,128)} %collective-permute-done.32, f32[2,1,32,128]{3,2,1,0:T(8,128)S(1)} %collective-permute-done.31, f32[2,8,32,1]{3,2,1,0:T(8,128)S(1)} %get-tuple-element.270, ...), kind=kLoop, calls=%fused_computation.43 | loop fusion | flops 1966080 | bytes 2727964 | tf_op jit(solution)/shard_map/add | solution.py:84
  (239 shorter events, 31.8 us)
Async XLA Ops:
  1.0 24.2 %collective-permute-start.3 = (bf16[8,32,128]{2,1,0:T(8,128)(2,1)S(1)}, bf16[8,32,128]{2,1,0:T(8,128)(2,1)S(1)}, u32[]{:S(2)}, u32[]{:S(2)}) collective-permute-start(bf16[8,32,128]{2,1,0:T(8,128)(2,1)S(1)} %slice_bitcast_fusion.17), channel_id=1, source_target_pairs={{0,16},{16,32},{32,48},{48,64},{64,80},{80,96},{96,112},{112,128},... | collective-permute-start | bytes 196616 | tf_op jit(solution)/shard_map/ppermute | solution.py:21
  4.0 21.2 %collective-permute-start.4 = (bf16[8,32,128]{2,1,0:T(8,128)(2,1)S(1)}, bf16[8,32,128]{2,1,0:T(8,128)(2,1)S(1)}, u32[]{:S(2)}, u32[]{:S(2)}) collective-permute-start(bf16[8,32,128]{2,1,0:T(8,128)(2,1)S(1)} %slice_bitcast_fusion.17), channel_id=1, source_target_pairs={{16,0},{32,16},{48,32},{64,48},{80,64},{96,80},{112,96},{128,112},... | collective-permute-start | bytes 196616 | tf_op jit(solution)/shard_map/ppermute | solution.py:23
  5.0 21.1 %copy-start.47 = (bf16[8,16]{1,0:T(8,128)(2,1)}, bf16[8,16]{1,0:T(8,128)(2,1)S(1)}, u32[]{:S(2)}) copy-start(bf16[8,16]{1,0:T(8,128)(2,1)S(1)} %get-tuple-element.305) | copy-start | bytes 772
  8.7 10.2 %copy-start.58 = (f32[2,8,128]{2,1,0:T(8,128)S(1)}, f32[2,8,128]{2,1,0:T(8,128)}, u32[]{:S(2)}) copy-start(f32[2,8,128]{2,1,0:T(8,128)} %param.58) | copy-start | bytes 24580
  8.7 10.3 %copy-start.5 = (f32[2,8,32,128]{3,2,1,0:T(8,128)S(1)}, f32[2,8,32,128]{3,2,1,0:T(8,128)}, u32[]{:S(2)}) copy-start(f32[2,8,32,128]{3,2,1,0:T(8,128)} %param.55) | copy-start | bytes 786436
  15.2 14.7 %collective-permute-start.5 = (f32[8,32,128]{2,1,0:T(8,128)}, f32[8,32,128]{2,1,0:T(8,128)S(1)}, u32[]{:S(2)}, u32[]{:S(2)}) collective-permute-start(f32[8,32,128]{2,1,0:T(8,128)} %get-tuple-element.267), channel_id=1, source_target_pairs={{0,240},{16,0},{32,16},{48,32},{64,48},{80,64},{96,80},{112,96},{1... | collective-permute-start | bytes 393224 | tf_op jit(solution)/shard_map/ppermute | solution.py:11
  18.8 11.1 %collective-permute-start.6 = (f32[8,32,128]{2,1,0:T(8,128)S(1)}, f32[8,32,128]{2,1,0:T(8,128)}, u32[]{:S(2)}, u32[]{:S(2)}) collective-permute-start(f32[8,32,128]{2,1,0:T(8,128)S(1)} %get-tuple-element.268), channel_id=1, source_target_pairs={{0,16},{16,32},{32,48},{48,64},{64,80},{80,96},{96,112},{112,128},... | collective-permute-start | bytes 393224 | tf_op jit(solution)/shard_map/ppermute | solution.py:11
  18.9 3.1 %collective-permute-start.1 = (f32[2,1,128]{2,1,0:T(1,128)S(1)}, f32[2,1,128]{2,1,0:T(1,128)S(1)}, u32[]{:S(2)}, u32[]{:S(2)}) collective-permute-start(f32[2,1,128]{2,1,0:T(1,128)S(1)} %slice.614), channel_id=1, source_target_pairs={{0,16},{16,32},{32,48},{48,64},{64,80},{80,96},{96,112},{112,128},... | collective-permute-start | bytes 3080 | tf_op jit(solution)/shard_map/ppermute | solution.py:11
  21.4 10.1 %copy-start.25 = (f32[2,8,128]{2,1,0:T(8,128)}, f32[2,8,128]{2,1,0:T(8,128)S(1)}, u32[]{:S(2)}) copy-start(f32[2,8,128]{2,1,0:T(8,128)S(1)} %pad_maximum_fusion.18) | copy-start | bytes 24580
  21.4 8.5 %copy-start.39 = (s32[1024]{0:T(1024)}, s32[1024]{0:T(1024)S(1)}, u32[]{:S(2)}) copy-start(s32[1024]{0:T(1024)S(1)} %pad_clamp_fusion) | copy-start | bytes 12292
  22.0 8.9 %collective-permute-start = (f32[2,1,32,128]{3,2,1,0:T(8,128)}, f32[2,1,32,128]{3,2,1,0:T(8,128)S(1)}, u32[]{:S(2)}, u32[]{:S(2)}) collective-permute-start(f32[2,1,32,128]{3,2,1,0:T(8,128)} %get-tuple-element.303), channel_id=1, source_target_pairs={{16,0},{32,16},{48,32},{64,48},{80,64},{96,80},{112,96},{128,112},... | collective-permute-start | bytes 98312 | tf_op jit(solution)/shard_map/ppermute | solution.py:23
  25.2 5.7 %collective-permute-start.2 = (f32[2,1,32,128]{3,2,1,0:T(8,128)}, f32[2,1,32,128]{3,2,1,0:T(8,128)}, u32[]{:S(2)}, u32[]{:S(2)}) collective-permute-start(f32[2,1,32,128]{3,2,1,0:T(8,128)} %get-tuple-element.304), channel_id=1, source_target_pairs={{0,16},{16,32},{32,48},{48,64},{64,80},{80,96},{96,112},{112,128},... | collective-permute-start | bytes 98312 | tf_op jit(solution)/shard_map/ppermute | solution.py:21
  26.1 8.3 %copy-start = (bf16[8,16,128,128]{3,2,1,0:T(8,128)(2,1)S(1)}, bf16[8,16,128,128]{3,2,1,0:T(8,128)(2,1)}, u32[]{:S(2)}) copy-start(bf16[8,16,128,128]{3,2,1,0:T(8,128)(2,1)} %param.60) | copy-start | bytes 12582916
  32.6 49.4 %copy-start.6 = (f32[2,8,32,128]{3,2,1,0:T(8,128)}, f32[2,8,32,128]{3,2,1,0:T(8,128)S(1)}, u32[]{:S(2)}) copy-start(f32[2,8,32,128]{3,2,1,0:T(8,128)S(1)} %get-tuple-element.254) | copy-start | bytes 786436
  32.6 16.0 %collective-permute-start.10 = (bf16[8,32,128]{2,1,0:T(8,128)(2,1)S(1)}, bf16[8,32,128]{2,1,0:T(8,128)(2,1)S(1)}, u32[]{:S(2)}, u32[]{:S(2)}) collective-permute-start(bf16[8,32,128]{2,1,0:T(8,128)(2,1)S(1)} %slice_bitcast_fusion.14), channel_id=1, source_target_pairs={{16,0},{32,16},{48,32},{64,48},{80,64},{96,80},{112,96},{128,112},... | collective-permute-start | bytes 196616 | tf_op jit(solution)/shard_map/ppermute | solution.py:23
  33.1 16.2 %collective-permute-start.9 = (bf16[8,32,128]{2,1,0:T(8,128)(2,1)S(1)}, bf16[8,32,128]{2,1,0:T(8,128)(2,1)}, u32[]{:S(2)}, u32[]{:S(2)}) collective-permute-start(bf16[8,32,128]{2,1,0:T(8,128)(2,1)S(1)} %slice_bitcast_fusion.14), channel_id=1, source_target_pairs={{0,16},{16,32},{32,48},{48,64},{64,80},{80,96},{96,112},{112,128},... | collective-permute-start | bytes 196616 | tf_op jit(solution)/shard_map/ppermute | solution.py:21
  44.0 10.9 %collective-permute-start.11 = (f32[8,32,128]{2,1,0:T(8,128)}, f32[8,32,128]{2,1,0:T(8,128)}, u32[]{:S(2)}, u32[]{:S(2)}) collective-permute-start(f32[8,32,128]{2,1,0:T(8,128)} %get-tuple-element.265), channel_id=1, source_target_pairs={{0,240},{16,0},{32,16},{48,32},{64,48},{80,64},{96,80},{112,96},{1... | collective-permute-start | bytes 393224 | tf_op jit(solution)/shard_map/ppermute | solution.py:11
  45.7 9.3 %collective-permute-start.12 = (f32[8,32,128]{2,1,0:T(8,128)}, f32[8,32,128]{2,1,0:T(8,128)}, u32[]{:S(2)}, u32[]{:S(2)}) collective-permute-start(f32[8,32,128]{2,1,0:T(8,128)} %get-tuple-element.266), channel_id=1, source_target_pairs={{0,16},{16,32},{32,48},{48,64},{64,80},{80,96},{96,112},{112,128},... | collective-permute-start | bytes 393224 | tf_op jit(solution)/shard_map/ppermute | solution.py:11
  45.8 10.2 %collective-permute-start.7 = (f32[2,1,32,128]{3,2,1,0:T(8,128)}, f32[2,1,32,128]{3,2,1,0:T(8,128)}, u32[]{:S(2)}, u32[]{:S(2)}) collective-permute-start(f32[2,1,32,128]{3,2,1,0:T(8,128)} %get-tuple-element.297), channel_id=1, source_target_pairs={{16,0},{32,16},{48,32},{64,48},{80,64},{96,80},{112,96},{128,112},... | collective-permute-start | bytes 98312 | tf_op jit(solution)/shard_map/ppermute | solution.py:23
  48.6 7.4 %collective-permute-start.8 = (f32[2,1,32,128]{3,2,1,0:T(8,128)}, f32[2,1,32,128]{3,2,1,0:T(8,128)}, u32[]{:S(2)}, u32[]{:S(2)}) collective-permute-start(f32[2,1,32,128]{3,2,1,0:T(8,128)} %get-tuple-element.298), channel_id=1, source_target_pairs={{0,16},{16,32},{32,48},{48,64},{64,80},{80,96},{96,112},{112,128},... | collective-permute-start | bytes 98312 | tf_op jit(solution)/shard_map/ppermute | solution.py:21
  51.1 9.6 %copy-start.1 = (bf16[8,16,128,128]{3,2,1,0:T(8,128)(2,1)S(1)}, bf16[8,16,128,128]{3,2,1,0:T(8,128)(2,1)}, u32[]{:S(2)}) copy-start(bf16[8,16,128,128]{3,2,1,0:T(8,128)(2,1)} %param.60) | copy-start | bytes 12582916
  57.8 16.1 %collective-permute-start.15 = (bf16[8,32,128]{2,1,0:T(8,128)(2,1)}, bf16[8,32,128]{2,1,0:T(8,128)(2,1)}, u32[]{:S(2)}, u32[]{:S(2)}) collective-permute-start(bf16[8,32,128]{2,1,0:T(8,128)(2,1)} %slice_bitcast_fusion.11), channel_id=1, source_target_pairs={{0,16},{16,32},{32,48},{48,64},{64,80},{80,96},{96,112},{112,128},... | collective-permute-start | bytes 196616 | tf_op jit(solution)/shard_map/ppermute | solution.py:21
  57.8 17.4 %collective-permute-start.16 = (bf16[8,32,128]{2,1,0:T(8,128)(2,1)}, bf16[8,32,128]{2,1,0:T(8,128)(2,1)}, u32[]{:S(2)}, u32[]{:S(2)}) collective-permute-start(bf16[8,32,128]{2,1,0:T(8,128)(2,1)} %slice_bitcast_fusion.11), channel_id=1, source_target_pairs={{16,0},{32,16},{48,32},{64,48},{80,64},{96,80},{112,96},{128,112},... | collective-permute-start | bytes 196616 | tf_op jit(solution)/shard_map/ppermute | solution.py:23
  69.0 7.9 %copy-start.48 = (bf16[8,16]{1,0:T(8,128)(2,1)S(1)}, bf16[8,16]{1,0:T(8,128)(2,1)}, u32[]{:S(2)}) copy-start(bf16[8,16]{1,0:T(8,128)(2,1)} %copy-done.47) | copy-start | bytes 772
  70.4 10.5 %collective-permute-start.17 = (f32[8,32,128]{2,1,0:T(8,128)}, f32[8,32,128]{2,1,0:T(8,128)}, u32[]{:S(2)}, u32[]{:S(2)}) collective-permute-start(f32[8,32,128]{2,1,0:T(8,128)} %get-tuple-element.263), channel_id=1, source_target_pairs={{0,240},{16,0},{32,16},{48,32},{64,48},{80,64},{96,80},{112,96},{1... | collective-permute-start | bytes 393224 | tf_op jit(solution)/shard_map/ppermute | solution.py:11
  73.4 7.5 %collective-permute-start.18 = (f32[8,32,128]{2,1,0:T(8,128)}, f32[8,32,128]{2,1,0:T(8,128)}, u32[]{:S(2)}, u32[]{:S(2)}) collective-permute-start(f32[8,32,128]{2,1,0:T(8,128)} %get-tuple-element.264), channel_id=1, source_target_pairs={{0,16},{16,32},{32,48},{48,64},{64,80},{80,96},{96,112},{112,128},... | collective-permute-start | bytes 393224 | tf_op jit(solution)/shard_map/ppermute | solution.py:11
  73.4 8.5 %collective-permute-start.13 = (f32[2,1,32,128]{3,2,1,0:T(8,128)}, f32[2,1,32,128]{3,2,1,0:T(8,128)S(1)}, u32[]{:S(2)}, u32[]{:S(2)}) collective-permute-start(f32[2,1,32,128]{3,2,1,0:T(8,128)} %get-tuple-element.291), channel_id=1, source_target_pairs={{16,0},{32,16},{48,32},{64,48},{80,64},{96,80},{112,96},{128,112},... | collective-permute-start | bytes 98312 | tf_op jit(solution)/shard_map/ppermute | solution.py:23
  73.9 8.0 %collective-permute-start.14 = (f32[2,1,32,128]{3,2,1,0:T(8,128)}, f32[2,1,32,128]{3,2,1,0:T(8,128)}, u32[]{:S(2)}, u32[]{:S(2)}) collective-permute-start(f32[2,1,32,128]{3,2,1,0:T(8,128)} %get-tuple-element.292), channel_id=1, source_target_pairs={{0,16},{16,32},{32,48},{48,64},{64,80},{80,96},{96,112},{112,128},... | collective-permute-start | bytes 98312 | tf_op jit(solution)/shard_map/ppermute | solution.py:21
  83.7 14.6 %collective-permute-start.21 = (bf16[8,32,128]{2,1,0:T(8,128)(2,1)}, bf16[8,32,128]{2,1,0:T(8,128)(2,1)}, u32[]{:S(2)}, u32[]{:S(2)}) collective-permute-start(bf16[8,32,128]{2,1,0:T(8,128)(2,1)} %slice_bitcast_fusion.8), channel_id=1, source_target_pairs={{0,16},{16,32},{32,48},{48,64},{64,80},{80,96},{96,112},{112,128},... | collective-permute-start | bytes 196616 | tf_op jit(solution)/shard_map/ppermute | solution.py:21
  83.7 15.8 %collective-permute-start.22 = (bf16[8,32,128]{2,1,0:T(8,128)(2,1)}, bf16[8,32,128]{2,1,0:T(8,128)(2,1)}, u32[]{:S(2)}, u32[]{:S(2)}) collective-permute-start(bf16[8,32,128]{2,1,0:T(8,128)(2,1)} %slice_bitcast_fusion.8), channel_id=1, source_target_pairs={{16,0},{32,16},{48,32},{64,48},{80,64},{96,80},{112,96},{128,112},... | collective-permute-start | bytes 196616 | tf_op jit(solution)/shard_map/ppermute | solution.py:23
  94.8 10.5 %collective-permute-start.23 = (f32[8,32,128]{2,1,0:T(8,128)}, f32[8,32,128]{2,1,0:T(8,128)}, u32[]{:S(2)}, u32[]{:S(2)}) collective-permute-start(f32[8,32,128]{2,1,0:T(8,128)} %get-tuple-element.261), channel_id=1, source_target_pairs={{0,240},{16,0},{32,16},{48,32},{64,48},{80,64},{96,80},{112,96},{1... | collective-permute-start | bytes 393224 | tf_op jit(solution)/shard_map/ppermute | solution.py:11
  97.8 7.5 %collective-permute-start.24 = (f32[8,32,128]{2,1,0:T(8,128)}, f32[8,32,128]{2,1,0:T(8,128)}, u32[]{:S(2)}, u32[]{:S(2)}) collective-permute-start(f32[8,32,128]{2,1,0:T(8,128)} %get-tuple-element.262), channel_id=1, source_target_pairs={{0,16},{16,32},{32,48},{48,64},{64,80},{80,96},{96,112},{112,128},... | collective-permute-start | bytes 393224 | tf_op jit(solution)/shard_map/ppermute | solution.py:11
  97.8 8.5 %collective-permute-start.19 = (f32[2,1,32,128]{3,2,1,0:T(8,128)}, f32[2,1,32,128]{3,2,1,0:T(8,128)S(1)}, u32[]{:S(2)}, u32[]{:S(2)}) collective-permute-start(f32[2,1,32,128]{3,2,1,0:T(8,128)} %get-tuple-element.285), channel_id=1, source_target_pairs={{16,0},{32,16},{48,32},{64,48},{80,64},{96,80},{112,96},{128,112},... | collective-permute-start | bytes 98312 | tf_op jit(solution)/shard_map/ppermute | solution.py:23
  98.3 8.0 %collective-permute-start.20 = (f32[2,1,32,128]{3,2,1,0:T(8,128)}, f32[2,1,32,128]{3,2,1,0:T(8,128)}, u32[]{:S(2)}, u32[]{:S(2)}) collective-permute-start(f32[2,1,32,128]{3,2,1,0:T(8,128)} %get-tuple-element.286), channel_id=1, source_target_pairs={{0,16},{16,32},{32,48},{48,64},{64,80},{80,96},{96,112},{112,128},... | collective-permute-start | bytes 98312 | tf_op jit(solution)/shard_map/ppermute | solution.py:21
  101.4 8.3 %copy-start.3 = (bf16[8,16,128,128]{3,2,1,0:T(8,128)(2,1)S(1)}, bf16[8,16,128,128]{3,2,1,0:T(8,128)(2,1)}, u32[]{:S(2)}) copy-start(bf16[8,16,128,128]{3,2,1,0:T(8,128)(2,1)} %param.60) | copy-start | bytes 12582916
  108.0 13.7 %collective-permute-start.27 = (bf16[8,32,128]{2,1,0:T(8,128)(2,1)}, bf16[8,32,128]{2,1,0:T(8,128)(2,1)}, u32[]{:S(2)}, u32[]{:S(2)}) collective-permute-start(bf16[8,32,128]{2,1,0:T(8,128)(2,1)} %slice_bitcast_fusion.5), channel_id=1, source_target_pairs={{0,16},{16,32},{32,48},{48,64},{64,80},{80,96},{96,112},{112,128},... | collective-permute-start | bytes 196616 | tf_op jit(solution)/shard_map/ppermute | solution.py:21
  108.0 14.9 %collective-permute-start.28 = (bf16[8,32,128]{2,1,0:T(8,128)(2,1)}, bf16[8,32,128]{2,1,0:T(8,128)(2,1)}, u32[]{:S(2)}, u32[]{:S(2)}) collective-permute-start(bf16[8,32,128]{2,1,0:T(8,128)(2,1)} %slice_bitcast_fusion.5), channel_id=1, source_target_pairs={{16,0},{32,16},{48,32},{64,48},{80,64},{96,80},{112,96},{128,112},... | collective-permute-start | bytes 196616 | tf_op jit(solution)/shard_map/ppermute | solution.py:23
  118.2 10.5 %collective-permute-start.29 = (f32[8,32,128]{2,1,0:T(8,128)S(1)}, f32[8,32,128]{2,1,0:T(8,128)S(1)}, u32[]{:S(2)}, u32[]{:S(2)}) collective-permute-start(f32[8,32,128]{2,1,0:T(8,128)S(1)} %get-tuple-element.259), channel_id=1, source_target_pairs={{0,240},{16,0},{32,16},{48,32},{64,48},{80,64},{96,80},{112,96},{1... | collective-permute-start | bytes 393224 | tf_op jit(solution)/shard_map/ppermute | solution.py:11
  121.2 7.5 %collective-permute-start.30 = (f32[8,32,128]{2,1,0:T(8,128)S(1)}, f32[8,32,128]{2,1,0:T(8,128)S(1)}, u32[]{:S(2)}, u32[]{:S(2)}) collective-permute-start(f32[8,32,128]{2,1,0:T(8,128)S(1)} %get-tuple-element.260), channel_id=1, source_target_pairs={{0,16},{16,32},{32,48},{48,64},{64,80},{80,96},{96,112},{112,128},... | collective-permute-start | bytes 393224 | tf_op jit(solution)/shard_map/ppermute | solution.py:11
  121.2 7.6 %collective-permute-start.25 = (f32[2,1,32,128]{3,2,1,0:T(8,128)S(1)}, f32[2,1,32,128]{3,2,1,0:T(8,128)S(1)}, u32[]{:S(2)}, u32[]{:S(2)}) collective-permute-start(f32[2,1,32,128]{3,2,1,0:T(8,128)S(1)} %get-tuple-element.279), channel_id=1, source_target_pairs={{16,0},{32,16},{48,32},{64,48},{80,64},{96,80},{112,96},{128,112},... | collective-permute-start | bytes 98312 | tf_op jit(solution)/shard_map/ppermute | solution.py:23
  121.7 7.1 %collective-permute-start.26 = (f32[2,1,32,128]{3,2,1,0:T(8,128)S(1)}, f32[2,1,32,128]{3,2,1,0:T(8,128)S(1)}, u32[]{:S(2)}, u32[]{:S(2)}) collective-permute-start(f32[2,1,32,128]{3,2,1,0:T(8,128)S(1)} %get-tuple-element.280), channel_id=1, source_target_pairs={{0,16},{16,32},{32,48},{48,64},{64,80},{80,96},{96,112},{112,128},... | collective-permute-start | bytes 98312 | tf_op jit(solution)/shard_map/ppermute | solution.py:21
  129.1 21.4 %collective-permute-start.33 = (bf16[8,32,128]{2,1,0:T(8,128)(2,1)S(1)}, bf16[8,32,128]{2,1,0:T(8,128)(2,1)S(1)}, u32[]{:S(2)}, u32[]{:S(2)}) collective-permute-start(bf16[8,32,128]{2,1,0:T(8,128)(2,1)S(1)} %slice_bitcast_fusion.2), channel_id=1, source_target_pairs={{0,16},{16,32},{32,48},{48,64},{64,80},{80,96},{96,112},{112,128},... | collective-permute-start | bytes 196616 | tf_op jit(solution)/shard_map/ppermute | solution.py:21
  129.2 22.7 %collective-permute-start.34 = (bf16[8,32,128]{2,1,0:T(8,128)(2,1)S(1)}, bf16[8,32,128]{2,1,0:T(8,128)(2,1)S(1)}, u32[]{:S(2)}, u32[]{:S(2)}) collective-permute-start(bf16[8,32,128]{2,1,0:T(8,128)(2,1)S(1)} %slice_bitcast_fusion.2), channel_id=1, source_target_pairs={{16,0},{32,16},{48,32},{64,48},{80,64},{96,80},{112,96},{128,112},... | collective-permute-start | bytes 196616 | tf_op jit(solution)/shard_map/ppermute | solution.py:23
  134.0 17.9 %copy-start.40 = (s32[1024]{0:T(1024)S(1)}, s32[1024]{0:T(1024)}, u32[]{:S(2)}) copy-start(s32[1024]{0:T(1024)} %copy-done.39) | copy-start | bytes 12292
  147.1 9.3 %collective-permute-start.35 = (f32[8,32,128]{2,1,0:T(8,128)}, f32[8,32,128]{2,1,0:T(8,128)}, u32[]{:S(2)}, u32[]{:S(2)}) collective-permute-start(f32[8,32,128]{2,1,0:T(8,128)} %get-tuple-element.257), channel_id=1, source_target_pairs={{0,240},{16,0},{32,16},{48,32},{64,48},{80,64},{96,80},{112,96},{1... | collective-permute-start | bytes 393224 | tf_op jit(solution)/shard_map/ppermute | solution.py:11
  150.1 6.4 %collective-permute-start.36 = (f32[8,32,128]{2,1,0:T(8,128)}, f32[8,32,128]{2,1,0:T(8,128)}, u32[]{:S(2)}, u32[]{:S(2)}) collective-permute-start(f32[8,32,128]{2,1,0:T(8,128)} %get-tuple-element.258), channel_id=1, source_target_pairs={{0,16},{16,32},{32,48},{48,64},{64,80},{80,96},{96,112},{112,128},... | collective-permute-start | bytes 393224 | tf_op jit(solution)/shard_map/ppermute | solution.py:11
  150.1 7.4 %collective-permute-start.31 = (f32[2,1,32,128]{3,2,1,0:T(8,128)}, f32[2,1,32,128]{3,2,1,0:T(8,128)S(1)}, u32[]{:S(2)}, u32[]{:S(2)}) collective-permute-start(f32[2,1,32,128]{3,2,1,0:T(8,128)} %get-tuple-element.273), channel_id=1, source_target_pairs={{16,0},{32,16},{48,32},{64,48},{80,64},{96,80},{112,96},{128,112},... | collective-permute-start | bytes 98312 | tf_op jit(solution)/shard_map/ppermute | solution.py:23
  150.6 6.9 %collective-permute-start.32 = (f32[2,1,32,128]{3,2,1,0:T(8,128)}, f32[2,1,32,128]{3,2,1,0:T(8,128)}, u32[]{:S(2)}, u32[]{:S(2)}) collective-permute-start(f32[2,1,32,128]{3,2,1,0:T(8,128)} %get-tuple-element.274), channel_id=1, source_target_pairs={{0,16},{16,32},{32,48},{48,64},{64,80},{80,96},{96,112},{112,128},... | collective-permute-start | bytes 98312 | tf_op jit(solution)/shard_map/ppermute | solution.py:21
  (48 other events, 220.6 us)
where the time goes:
time: 165 us; the launch traced here: 163 us
  other arithmetic  63.3 us (38%)
  starting transfers between devices  43 us (26%)
  matrix products  30.4 us (18%)
  local copies, waits for them, and re-layouts  24.4 us (15%)
  between operations  1.91 us (1%)
    scatter-add x6, other arithmetic, hamiltonian(): gathered = jnp.zeros((rows + 2 * REACH,) + first.shape[1:], jnp.float32)....  41.3 us
    dot_general x6, matrix products, hamiltonian(): jnp.einsum('bksj,bkij->bsi', picked, coupling, preferred_element_type=jnp...  22.8 us
    ppermute x13, starting transfers between devices, passed_along(): return lax.ppermute(x, axis, [(i, (i + by) % size) for i in range(size)])  17.3 us
    ppermute x12, starting transfers between devices, with_halo(): lax.ppermute(head, axis, [((i + 1) % count, i) for i in range(count)])  16.4 us
    ppermute x12, starting transfers between devices, with_halo(): lax.ppermute(tail, axis, [(i, (i + 1) % count) for i in range(count)])  9.32 us
    dot_general x6, matrix products, hamiltonian(): jnp.einsum('bsi,bkij->bksj', first, coupling, preferred_element_type=jnp....  7.59 us
    slice x10, local copies, waits for them, and re-layouts, hamiltonian(): intra = intra + hop_row[:, :, None, :] * jnp.roll(field, -1, 3)  7.05 us
    add x1, other arithmetic, body(): filtered = filtered + coefs[order] * following  5.65 us
  transfers between devices with their start and end apart: 37, of which 0 were waited for; matrix products, arithmetic and copies ran while one was open for 63% of the time, Pallas kernels for 0%

commit v1 on v0

v1 whole, which is shorter than its diff:
```python
import functools

import jax
import jax.numpy as jnp
from jax import lax
from jax.experimental import pallas as pl
from jax.experimental.pallas import tpu as pltpu
from jax.sharding import PartitionSpec as P

REACH = 8
LOCAL, MATE, FAR = 0, 1, 2
IN_VMEM = pl.BlockSpec(memory_space=pltpu.VMEM)
IN_SMEM = pl.BlockSpec(memory_space=pltpu.SMEM)
ANYWHERE = pl.BlockSpec(memory_space=pl.ANY)


def near(x):
    return pltpu.with_memory_space_constraint(x, pltpu.VMEM)


def held(shape, dtype):
    return pltpu.VMEM(shape, dtype)


def times(x, w):
    return lax.dot_general(x, w, (((1,), (0,)), ((), ())), preferred_element_type=jnp.float32)


def times_back(x, w):
    return lax.dot_general(x, w, (((1,), (1,)), ((), ())), preferred_element_type=jnp.float32)


def core():
    return lax.rem(lax.axis_index("tile"), 2)


def lanes(row, cols):
    return pl.ds(pl.multiple_of(row * cols, cols), cols)


def write_payloads(x_ref, w_ref, rim_ref, far_ref, mate_ref):
    wide = x_ref.shape[2]
    cols = rim_ref.shape[2]
    rows = wide // cols
    second = x_ref[1].astype(jnp.bfloat16)
    first = x_ref[0].astype(jnp.bfloat16)
    far_row = (rows - 1) * core()
    for side, (ref, row, w) in enumerate(
        ((far_ref, far_row, FAR), (mate_ref, rows - 1 - far_row, MATE))
    ):
        ref[:, 0:wide] = second
        ref[:, wide : 2 * wide] = times(first, w_ref[w]).astype(jnp.bfloat16)
        for layer in range(2):
            edge = x_ref[layer, :, lanes(row, cols)] * rim_ref[layer, side : side + 1, :]
            high = edge.astype(jnp.bfloat16)
            low = (edge - high.astype(jnp.float32)).astype(jnp.bfloat16)
            at = 2 * wide + 2 * layer * cols
            ref[:, at : at + cols] = high
            ref[:, at + cols : at + 2 * cols] = low


def add_received(scale, got_ref, side, w, row, w_ref, rim_ref, sum_ref):
    wide = sum_ref.shape[2]
    cols = rim_ref.shape[2]
    sum_ref[0] += scale * times_back(got_ref[:, 0:wide], w_ref[w])
    sum_ref[1] += scale * got_ref[:, wide : 2 * wide].astype(jnp.float32)
    for layer in range(2):
        at = 2 * wide + 2 * layer * cols
        edge = got_ref[:, at : at + cols].astype(jnp.float32) + got_ref[
            :, at + cols : at + 2 * cols
        ].astype(jnp.float32)
        sum_ref[layer, :, lanes(row, cols)] += scale * (edge * rim_ref[layer, side : side + 1, :])


def prepare(
    partner_ref, states_ref, onsite_ref, hop_row_ref, hop_up_ref, coupling_ref,
    x_ref, w_ref, coef_ref, rim_ref, far_ref, mate_ref, blocks, total, sems,
):
    rows, slots = partner_ref.shape
    cols = onsite_ref.shape[2]
    tile = lax.axis_index("tile")
    all_rows = rows * lax.axis_size("tile")
    here = core()

    def fetch(r):
        return pltpu.make_async_copy(coupling_ref.at[r], blocks.at[r], sems.at[r])

    for r in range(rows):
        fetch(r).start()
    for layer in range(2):
        for r in range(rows):
            x_ref[layer, :, r * cols : (r + 1) * cols] = states_ref[layer, r]
        hop_row = hop_row_ref[layer]
        row = lax.broadcasted_iota(jnp.int32, (rows, cols), 0) + tile * rows
        column = lax.broadcasted_iota(jnp.int32, (rows, cols), 1)
        bond = jnp.where((row + column) % 2 == 0, hop_up_ref[layer], 0.0)
        coef_ref[layer, 0] = onsite_ref[layer]
        coef_ref[layer, 1] = hop_row
        coef_ref[layer, 2] = pltpu.roll(hop_row, 1, axis=1)
        coef_ref[layer, 3] = bond
        coef_ref[layer, 4] = pltpu.roll(bond, 1, axis=0)
        last = bond[rows - 1 :]
        ones = jnp.ones_like(last)
        rim_ref[layer, 0:1] = jnp.where(here == 0, ones, last)
        rim_ref[layer, 1:2] = jnp.where(here == 0, last, ones)

    def one_row(r, carry):
        fetch(r).wait()
        total[...] = jnp.zeros_like(total)
        for k in range(slots):
            slot = partner_ref[r, k]

            @pl.when(slot >= 0)
            def _():
                away = lax.rem(slot - tile * rows + REACH + all_rows, all_rows)
                part = lax.div(away, rows)
                is_far = part == 2 * here
                place = jnp.where(part == 1, LOCAL, jnp.where(is_far, FAR, MATE))
                at = place * rows + lax.rem(away, rows)
                total[at] += blocks[r, k].astype(jnp.float32)

        for w in range(3):
            for g in range(rows):
                w_ref[w, pl.ds(pl.multiple_of(r * cols, cols), cols), g * cols : (g + 1) * cols] = total[
                    w * rows + g
                ].astype(jnp.bfloat16)
        return carry

    lax.fori_loop(0, rows, one_row, 0)
    write_payloads(x_ref, w_ref, rim_ref, far_ref, mate_ref)


def inner(order, coefs_ref, *refs):
    if order == 0:
        x_ref, w_ref, coef_ref, rim_ref, got_ref, sum_ref, filt_out = refs
        scale = 1.0 / 12.0
    else:
        x_ref, prev_ref, filt_ref, w_ref, coef_ref, rim_ref, got_ref, sum_ref, filt_out = refs
        scale = 2.0 / 12.0
    wide = x_ref.shape[2]
    cols = rim_ref.shape[2]
    rows = wide // cols
    first = x_ref[0].astype(jnp.bfloat16)
    second = x_ref[1].astype(jnp.bfloat16)
    sum_ref[0] = scale * times_back(second, w_ref[LOCAL])
    sum_ref[1] = scale * times(first, w_ref[LOCAL])
    for layer in range(2):
        for r in range(rows):
            here = slice(r * cols, (r + 1) * cols)
            x = x_ref[layer, :, here]

            def factor(i):
                return coef_ref[layer, i, r : r + 1, :]

            hop = factor(0) * x
            hop += factor(1) * pltpu.roll(x, cols - 1, axis=1)
            hop += factor(2) * pltpu.roll(x, 1, axis=1)
            if r < rows - 1:
                hop += factor(3) * x_ref[layer, :, (r + 1) * cols : (r + 2) * cols]
            if r > 0:
                hop += factor(4) * x_ref[layer, :, (r - 1) * cols : r * cols]
            term = sum_ref[layer, :, here] + scale * hop
            if order == 0:
                filt_out[layer, :, here] = coefs_ref[0] * x
            else:
                term -= prev_ref[layer, :, here]
                filt_out[layer, :, here] = filt_ref[layer, :, here] + coefs_ref[order] * x
            sum_ref[layer, :, here] = term
    mate_row = (rows - 1) * (1 - core())
    add_received(scale, got_ref, 1, MATE, mate_row, w_ref, rim_ref, sum_ref)


def outer(order, degree, coefs_ref, *refs):
    scale = 1.0 / 12.0 if order == 0 else 2.0 / 12.0
    last = order == degree - 1
    if last:
        sum_ref, filt_ref, w_ref, rim_ref, got_ref, out_ref, x_ref = refs
    else:
        sum_ref, w_ref, rim_ref, got_ref, x_ref, far_ref, mate_ref = refs
    wide = x_ref.shape[2]
    cols = rim_ref.shape[2]
    rows = wide // cols
    x_ref[...] = sum_ref[...]
    add_received(scale, got_ref, 0, FAR, (rows - 1) * core(), w_ref, rim_ref, x_ref)
    if last:
        for layer in range(2):
            for r in range(rows):
                here = slice(r * cols, (r + 1) * cols)
                out_ref[layer, r] = filt_ref[layer, :, here] + coefs_ref[degree] * x_ref[layer, :, here]
    else:
        write_payloads(x_ref, w_ref, rim_ref, far_ref, mate_ref)


def call(kernel, outs, args, scratch=(), specs=None, out_specs=None, limit=12):
    return pl.pallas_call(
        kernel,
        out_shape=outs,
        in_specs=specs or [IN_SMEM] + [IN_VMEM] * (len(args) - 1),
        out_specs=out_specs or [IN_VMEM] * len(outs),
        scratch_shapes=list(scratch),
        compiler_params=pltpu.CompilerParams(vmem_limit_bytes=limit << 20),
    )(*args)


def body(states, onsite, hop_row, hop_up, partner, coupling, coefs):
    rows, count, cols = states.shape[1:]
    slots = partner.shape[1]
    wide = rows * cols
    degree = coefs.shape[0] - 1
    size = lax.axis_size("tile")
    far_pairs = [(i, (i + 1) % size if i % 2 else (i - 1) % size) for i in range(size)]
    mate_pairs = [(i, i ^ 1) for i in range(size)]

    field = held((2, count, wide), jnp.float32)
    payload = held((count, 2 * wide + 4 * cols), jnp.bfloat16)
    x, w, coef, rim, far, mate = call(
        prepare,
        [field, held((3, wide, wide), jnp.bfloat16), held((2, 5, rows, cols), jnp.float32),
         held((2, 2, cols), jnp.float32), payload, payload],
        [partner, states, onsite, hop_row, hop_up, coupling],
        scratch=[
            pltpu.VMEM((rows, slots, cols, cols), jnp.bfloat16),
            pltpu.VMEM((3 * rows, cols, cols), jnp.float32),
            pltpu.SemaphoreType.DMA((rows,)),
        ],
        specs=[IN_SMEM] + [IN_VMEM] * 4 + [ANYWHERE],
        limit=24,
    )
    w, coef, rim = near(w), near(coef), near(rim)
    prev = filt = None
    for order in range(degree):
        got_far = lax.ppermute(far, "tile", far_pairs)
        got_mate = lax.ppermute(mate, "tile", mate_pairs)
        x = near(x)
        past = [] if order == 0 else [near(prev), near(filt)]
        partial, filt = call(
            functools.partial(inner, order),
            [field, field],
            [coefs, x, *past, w, coef, rim, near(got_mate)],
        )
        prev = x
        partial = near(partial)
        if order < degree - 1:
            x, far, mate = call(
                functools.partial(outer, order, degree),
                [field, payload, payload],
                [coefs, partial, w, rim, near(got_far)],
            )
        else:
            (out,) = call(
                functools.partial(outer, order, degree),
                [jax.ShapeDtypeStruct(states.shape, jnp.float32)],
                [coefs, partial, near(filt), w, rim, near(got_far)],
                scratch=[pltpu.VMEM((2, count, wide), jnp.float32)],
            )
    return out


def solution(mesh):
    placed = (
        P(None, "tile", "state", None),
        P(None, "tile", None),
        P(None, "tile", None),
        P(None, "tile", None),
        P("tile", None),
        P("tile", None, None, None),
        P(),
    )
    return jax.shard_map(
        body, mesh=mesh, in_specs=placed, out_specs=P(None, "tile", "state", None), check_vma=False
    )
```

time: 165 us -> 65.4 us (0.40)
  other arithmetic: 63.3 us -> 0 us
  Pallas kernels: 0 us -> 32.5 us
  starting transfers between devices: 43 us -> 10.6 us
  matrix products: 30.4 us -> 0 us
  local copies, waits for them, and re-layouts: 24.4 us -> 6.57 us
  waiting for transfers between devices: 0.11 us -> 15.3 us
  between operations: 1.91 us -> 0.08 us
    scatter-add x6 -> x0, other arithmetic: 41.3 us -> none  [hamiltonian(): gathered = jnp.zeros((rows + 2 * REACH,) + first.shape[1:], jnp.float32)....]
    pallas_call x0 -> x13, Pallas kernels: none -> 32.5 us  [call(): pl.pallas_call(kernel, out_shape=outs, in_specs=specs or [IN_SMEM] + [IN_...]
    ppermute x37 -> x12, starting transfers between devices: 43 us -> 10.6 us  [the longest x6 10.4 us: body(): got_mate = lax.ppermute(mate, 'tile', mate_pairs)]
    dot_general x12 -> x0, matrix products: 30.4 us -> none  [the longest x6 22.8 us: hamiltonian(): jnp.einsum('bksj,bkij->bsi', picked, coupling, preferred_element_type=jnp...]
    slice x27 -> x0, local copies, waits for them, and re-layouts: 15.5 us -> none  [the longest x10 7.05 us: hamiltonian(): intra = intra + hop_row[:, :, None, :] * jnp.roll(field, -1, 3)]
    ppermute x37 -> x12, waiting for transfers between devices: 0.11 us -> 15.3 us  [the longest x6 9.3 us: body(): got_far = lax.ppermute(far, 'tile', far_pairs)]
    convert_element_type x7 -> x0, other arithmetic: 6.13 us -> none  [the longest x6 5.44 us: hamiltonian(): rounded = field.astype(jnp.bfloat16)]
    add x2 -> x0, other arithmetic: 5.66 us -> none  [the longest x1 5.65 us: body(): filtered = filtered + coefs[order] * following]
  transfers between devices with their start and end apart: 37 -> 12, of which waited for: 0 -> 12; matrix products, arithmetic and copies ran while one was open for 63% -> 0% of each run, Pallas kernels for 0% -> 21%
where the time goes in v1:
time: 65.4 us; the launch traced here: 65.1 us
  Pallas kernels  32.5 us (50%)
  waiting for transfers between devices  15.3 us (23%)
  starting transfers between devices  10.6 us (16%)
  local copies, waits for them, and re-layouts  6.57 us (10%)
    pallas_call x13, Pallas kernels, call(): pl.pallas_call(kernel, out_shape=outs, in_specs=specs or [IN_SMEM] + [IN_...  32.5 us
    ppermute x6, starting transfers between devices, body(): got_mate = lax.ppermute(mate, 'tile', mate_pairs)  10.4 us
    ppermute x6, waiting for transfers between devices, body(): got_far = lax.ppermute(far, 'tile', far_pairs)  9.3 us
    unnamed x16, local copies, waits for them, and re-layouts  6.57 us
    ppermute x6, waiting for transfers between devices, body(): got_mate = lax.ppermute(mate, 'tile', mate_pairs)  6.04 us
  transfers between devices with their start and end apart: 12, of which 12 were waited for; matrix products, arithmetic and copies ran while one was open for 0% of the time, Pallas kernels for 21%

profile of v1, /device:TPU:1, one launch (start us, length us, event | category | flops | bytes accessed | tf_op | source)
XLA Modules:
  0.0 65.1 jit_solution(16127990404636971742)
XLA Ops:
  0.0 0.0 copy-start
  0.0 2.2 %copy-done = bf16[8,16,128,128]{3,2,1,0:T(8,128)(2,1)S(1)} copy-done((bf16[8,16,128,128]{3,2,1,0:T(8,128)(2,1)S(1)}, bf16[8,16,128,128]{3,2,1,0:T(8,128)(2,1)}, u32[]{:S(2)}) %copy-start) | copy-done | bytes 4194328
  2.2 0.9 %copy-done.1 = f32[2,8,32,128]{3,2,1,0:T(8,128)S(1)} copy-done((f32[2,8,32,128]{3,2,1,0:T(8,128)S(1)}, f32[2,8,32,128]{3,2,1,0:T(8,128)}, u32[]{:S(2)}) %copy-start.1) | copy-done | bytes 262168
  3.1 0.0 copy-start.4
  3.1 0.7 %copy-done.4 = f32[2,8,128]{2,1,0:T(8,128)S(1)} copy-done((f32[2,8,128]{2,1,0:T(8,128)S(1)}, f32[2,8,128]{2,1,0:T(8,128)}, u32[]{:S(2)}) %copy-start.4) | copy-done | bytes 8216
  3.8 0.0 copy-start.5
  3.8 0.7 %copy-done.5 = f32[2,8,128]{2,1,0:T(8,128)S(1)} copy-done((f32[2,8,128]{2,1,0:T(8,128)S(1)}, f32[2,8,128]{2,1,0:T(8,128)}, u32[]{:S(2)}) %copy-start.5) | copy-done | bytes 8216
  4.5 0.7 %copy-done.6 = f32[2,8,128]{2,1,0:T(8,128)S(1)} copy-done((f32[2,8,128]{2,1,0:T(8,128)S(1)}, f32[2,8,128]{2,1,0:T(8,128)}, u32[]{:S(2)}) %copy-start.6) | copy-done | bytes 8216
  5.2 0.7 %copy-done.7 = s32[8,16]{1,0:T(8,128)S(1)} copy-done((s32[8,16]{1,0:T(8,128)S(1)}, s32[8,16]{1,0:T(8,128)}, u32[]{:S(2)}) %copy-start.7) | copy-done | bytes 536
  5.9 6.2 %shard_map.73 = (f32[2,32,1024]{2,1,0:T(8,128)S(1)}, bf16[3,1024,1024]{2,1,0:T(8,128)(2,1)S(1)}, f32[2,5,8,128]{3,2,1,0:T(8,128)S(1)}, f32[2,2,128]{2,1,0:T(2,12...) custom-call(s32[8,16]{1,0:T(8,128)S(1)} %copy-done.7, f32[2,8,32,128]{3,2,1,0:T(8,128)S(1)} %copy-done.1, ...), custom_call_target="tpu_custom_call" | custom-call | tf_op jit(solution)/shard_map/pallas_call | solution.py:195
  12.1 3.4 %collective-permute-start = (bf16[32,2560]{1,0:T(8,128)(2,1)S(1)}, bf16[32,2560]{1,0:T(8,128)(2,1)S(1)}, u32[]{:S(2)}, u32[]{:S(2)}) collective-permute-start(bf16[32,2560]{1,0:T(8,128)(2,1)S(1)} %get-tuple-element.42), channel_id=1, source_target_pairs={{0,16},{16,0},{32,48},{48,32},{64,80},{80,64},{96,112},{112,96},{1... | collective-permute-start | bytes 491528 | tf_op jit(solution)/shard_map/ppermute | solution.py:233
  15.5 0.1 collective-permute-start.1
  15.6 0.9 %collective-permute-done.refs_4_ = bf16[32,2560]{1,0:T(8,128)(2,1)S(1)} collective-permute-done((bf16[32,2560]{1,0:T(8,128)(2,1)S(1)}, bf16[32,2560]{1,0:T(8,128)(2,1)S(1)}, u32[]{:S(2)}, u32[]{:S(2)}) %collective-permute-start) | collective-permute-done | bytes 163872 | tf_op jit(solution)/shard_map/ppermute | solution.py:233
  16.5 0.7 %copy-done.2 = f32[7]{0:T(128)S(1)} copy-done((f32[7]{0:T(128)S(1)}, f32[7]{0:T(128)}, u32[]{:S(2)}) %copy-start.2) | copy-done | bytes 52
  17.2 2.3 %shard_map.74 = (f32[2,32,1024]{2,1,0:T(8,128)S(1)}, f32[2,32,1024]{2,1,0:T(8,128)S(1)}) custom-call(f32[7]{0:T(128)S(1)} %copy-done.2, f32[2,32,1024]{2,1,0:T(8,128)S(1)} %get-tuple-element.38.refs_0_.refs_1_, bf16[3,1024,1024]{2,1,0:T(8,128)(2,1)S(1)} %get-tuple-element.39.refs_1_.refs_3_.refs_2_, f32[2,5,8,128]{3,2,1,0:T(8,128)S(1)} %get-tuple-element.40.refs_2_.refs_4_, ...), custom_call_target="tpu_custom_call" | custom-call | tf_op jit(solution)/shard_map/pallas_call | solution.py:195
  19.5 0.8 %collective-permute-done.1.refs_3_ = bf16[32,2560]{1,0:T(8,128)(2,1)S(1)} collective-permute-done((bf16[32,2560]{1,0:T(8,128)(2,1)S(1)}, bf16[32,2560]{1,0:T(8,128)(2,1)S(1)}, u32[]{:S(2)}, u32[]{:S(2)}) %collective-permute-start.1) | collective-permute-done | bytes 163872 | tf_op jit(solution)/shard_map/ppermute | solution.py:232
  20.2 2.1 %shard_map.75 = (f32[2,32,1024]{2,1,0:T(8,128)S(1)}, bf16[32,2560]{1,0:T(8,128)(2,1)S(1)}, bf16[32,2560]{1,0:T(8,128)(2,1)S(1)}) custom-call(f32[7]{0:T(128)S(1)} %copy-done.2, f32[2,32,1024]{2,1,0:T(8,128)S(1)} %get-tuple-element.43.refs_0_, bf16[3,1024,1024]{2,1,0:T(8,128)(2,1)S(1)} %get-tuple-element.39.refs_1_.refs_3_.refs_2_, ...), custom_call_target="tpu_custom_call" | custom-call | tf_op jit(solution)/shard_map/pallas_call | solution.py:195
  22.4 2.6 %collective-permute-start.2 = (bf16[32,2560]{1,0:T(8,128)(2,1)S(1)}, bf16[32,2560]{1,0:T(8,128)(2,1)S(1)}, u32[]{:S(2)}, u32[]{:S(2)}) collective-permute-start(bf16[32,2560]{1,0:T(8,128)(2,1)S(1)} %get-tuple-element.47), channel_id=1, source_target_pairs={{0,16},{16,0},{32,48},{48,32},{64,80},{80,64},{96,112},{112,96},{1... | collective-permute-start | bytes 491528 | tf_op jit(solution)/shard_map/ppermute | solution.py:233
  24.9 0.0 collective-permute-start.3
  24.9 1.0 %collective-permute-done.2.refs_6_ = bf16[32,2560]{1,0:T(8,128)(2,1)S(1)} collective-permute-done((bf16[32,2560]{1,0:T(8,128)(2,1)S(1)}, bf16[32,2560]{1,0:T(8,128)(2,1)S(1)}, u32[]{:S(2)}, u32[]{:S(2)}) %collective-permute-start.2) | collective-permute-done | bytes 163872 | tf_op jit(solution)/shard_map/ppermute | solution.py:233
  26.0 2.3 %shard_map.76 = (f32[2,32,1024]{2,1,0:T(8,128)S(1)}, f32[2,32,1024]{2,1,0:T(8,128)S(1)}) custom-call(f32[7]{0:T(128)S(1)} %copy-done.2, f32[2,32,1024]{2,1,0:T(8,128)S(1)} %get-tuple-element.45.refs_0_.refs_1_, f32[2,32,1024]{2,1,0:T(8,128)S(1)} %get-tuple-element.38.refs_0_.refs_1_, f32[2,32,1024]{2,1,0:T(8,128)S(1)} %get-tuple-element.46.refs_2_, ...), custom_call_target="tpu_custom_call" | custom-call | tf_op jit(solution)/shard_map/pallas_call | solution.py:195
  28.3 1.7 %collective-permute-done.3.refs_3_ = bf16[32,2560]{1,0:T(8,128)(2,1)S(1)} collective-permute-done((bf16[32,2560]{1,0:T(8,128)(2,1)S(1)}, bf16[32,2560]{1,0:T(8,128)(2,1)S(1)}, u32[]{:S(2)}, u32[]{:S(2)}) %collective-permute-start.3) | collective-permute-done | bytes 163872 | tf_op jit(solution)/shard_map/ppermute | solution.py:232
  30.0 2.1 %shard_map.77 = (f32[2,32,1024]{2,1,0:T(8,128)S(1)}, bf16[32,2560]{1,0:T(8,128)(2,1)S(1)}, bf16[32,2560]{1,0:T(8,128)(2,1)S(1)}) custom-call(f32[7]{0:T(128)S(1)} %copy-done.2, f32[2,32,1024]{2,1,0:T(8,128)S(1)} %get-tuple-element.48.refs_0_, bf16[3,1024,1024]{2,1,0:T(8,128)(2,1)S(1)} %get-tuple-element.39.refs_1_.refs_3_.refs_2_, ...), custom_call_target="tpu_custom_call" | custom-call | tf_op jit(solution)/shard_map/pallas_call | solution.py:195
  32.1 1.1 %collective-permute-start.4 = (bf16[32,2560]{1,0:T(8,128)(2,1)S(1)}, bf16[32,2560]{1,0:T(8,128)(2,1)S(1)}, u32[]{:S(2)}, u32[]{:S(2)}) collective-permute-start(bf16[32,2560]{1,0:T(8,128)(2,1)S(1)} %get-tuple-element.52), channel_id=1, source_target_pairs={{0,16},{16,0},{32,48},{48,32},{64,80},{80,64},{96,112},{112,96},{1... | collective-permute-start | bytes 491528 | tf_op jit(solution)/shard_map/ppermute | solution.py:233
  33.2 0.0 collective-permute-start.5
  33.2 1.0 %collective-permute-done.4.refs_6_ = bf16[32,2560]{1,0:T(8,128)(2,1)S(1)} collective-permute-done((bf16[32,2560]{1,0:T(8,128)(2,1)S(1)}, bf16[32,2560]{1,0:T(8,128)(2,1)S(1)}, u32[]{:S(2)}, u32[]{:S(2)}) %collective-permute-start.4) | collective-permute-done | bytes 163872 | tf_op jit(solution)/shard_map/ppermute | solution.py:233
  34.2 0.0 copy-done.3
  34.2 2.3 %shard_map.78 = (f32[2,32,1024]{2,1,0:T(8,128)S(1)}, f32[2,32,1024]{2,1,0:T(8,128)S(1)}) custom-call(f32[7]{0:T(128)S(1)} %copy-done.3, f32[2,32,1024]{2,1,0:T(8,128)S(1)} %get-tuple-element.50.refs_0_.refs_1_, f32[2,32,1024]{2,1,0:T(8,128)S(1)} %get-tuple-element.45.refs_0_.refs_1_, f32[2,32,1024]{2,1,0:T(8,128)S(1)} %get-tuple-element.51.refs_2_, ...), custom_call_target="tpu_custom_call" | custom-call | tf_op jit(solution)/shard_map/pallas_call | solution.py:195
  36.5 1.7 %collective-permute-done.5.refs_3_ = bf16[32,2560]{1,0:T(8,128)(2,1)S(1)} collective-permute-done((bf16[32,2560]{1,0:T(8,128)(2,1)S(1)}, bf16[32,2560]{1,0:T(8,128)(2,1)S(1)}, u32[]{:S(2)}, u32[]{:S(2)}) %collective-permute-start.5) | collective-permute-done | bytes 163872 | tf_op jit(solution)/shard_map/ppermute | solution.py:232
  38.2 2.1 %shard_map.79 = (f32[2,32,1024]{2,1,0:T(8,128)S(1)}, bf16[32,2560]{1,0:T(8,128)(2,1)S(1)}, bf16[32,2560]{1,0:T(8,128)(2,1)S(1)}) custom-call(f32[7]{0:T(128)S(1)} %copy-done.3, f32[2,32,1024]{2,1,0:T(8,128)S(1)} %get-tuple-element.53.refs_0_, bf16[3,1024,1024]{2,1,0:T(8,128)(2,1)S(1)} %get-tuple-element.39.refs_1_.refs_3_.refs_2_, ...), custom_call_target="tpu_custom_call" | custom-call | tf_op jit(solution)/shard_map/pallas_call | solution.py:195
  40.3 1.1 %collective-permute-start.6 = (bf16[32,2560]{1,0:T(8,128)(2,1)S(1)}, bf16[32,2560]{1,0:T(8,128)(2,1)S(1)}, u32[]{:S(2)}, u32[]{:S(2)}) collective-permute-start(bf16[32,2560]{1,0:T(8,128)(2,1)S(1)} %get-tuple-element.57), channel_id=1, source_target_pairs={{0,16},{16,0},{32,48},{48,32},{64,80},{80,64},{96,112},{112,96},{1... | collective-permute-start | bytes 491528 | tf_op jit(solution)/shard_map/ppermute | solution.py:233
  41.4 0.0 collective-permute-start.7
  41.4 1.0 %collective-permute-done.6.refs_6_ = bf16[32,2560]{1,0:T(8,128)(2,1)S(1)} collective-permute-done((bf16[32,2560]{1,0:T(8,128)(2,1)S(1)}, bf16[32,2560]{1,0:T(8,128)(2,1)S(1)}, u32[]{:S(2)}, u32[]{:S(2)}) %collective-permute-start.6) | collective-permute-done | bytes 163872 | tf_op jit(solution)/shard_map/ppermute | solution.py:233
  42.4 2.3 %shard_map.80 = (f32[2,32,1024]{2,1,0:T(8,128)S(1)}, f32[2,32,1024]{2,1,0:T(8,128)S(1)}) custom-call(f32[7]{0:T(128)S(1)} %copy-done.3, f32[2,32,1024]{2,1,0:T(8,128)S(1)} %get-tuple-element.55.refs_0_.refs_1_, f32[2,32,1024]{2,1,0:T(8,128)S(1)} %get-tuple-element.50.refs_0_.refs_1_, f32[2,32,1024]{2,1,0:T(8,128)S(1)} %get-tuple-element.56.refs_2_, ...), custom_call_target="tpu_custom_call" | custom-call | tf_op jit(solution)/shard_map/pallas_call | solution.py:195
  44.7 1.7 %collective-permute-done.7.refs_3_ = bf16[32,2560]{1,0:T(8,128)(2,1)S(1)} collective-permute-done((bf16[32,2560]{1,0:T(8,128)(2,1)S(1)}, bf16[32,2560]{1,0:T(8,128)(2,1)S(1)}, u32[]{:S(2)}, u32[]{:S(2)}) %collective-permute-start.7) | collective-permute-done | bytes 163872 | tf_op jit(solution)/shard_map/ppermute | solution.py:232
  46.4 2.1 %shard_map.81 = (f32[2,32,1024]{2,1,0:T(8,128)S(1)}, bf16[32,2560]{1,0:T(8,128)(2,1)S(1)}, bf16[32,2560]{1,0:T(8,128)(2,1)S(1)}) custom-call(f32[7]{0:T(128)S(1)} %copy-done.3, f32[2,32,1024]{2,1,0:T(8,128)S(1)} %get-tuple-element.58.refs_0_, bf16[3,1024,1024]{2,1,0:T(8,128)(2,1)S(1)} %get-tuple-element.39.refs_1_.refs_3_.refs_2_, ...), custom_call_target="tpu_custom_call" | custom-call | tf_op jit(solution)/shard_map/pallas_call | solution.py:195
  48.5 1.3 %collective-permute-start.8 = (bf16[32,2560]{1,0:T(8,128)(2,1)S(1)}, bf16[32,2560]{1,0:T(8,128)(2,1)S(1)}, u32[]{:S(2)}, u32[]{:S(2)}) collective-permute-start(bf16[32,2560]{1,0:T(8,128)(2,1)S(1)} %get-tuple-element.62), channel_id=1, source_target_pairs={{0,16},{16,0},{32,48},{48,32},{64,80},{80,64},{96,112},{112,96},{1... | collective-permute-start | bytes 491528 | tf_op jit(solution)/shard_map/ppermute | solution.py:233
  49.8 0.0 collective-permute-start.9
  49.8 1.0 %collective-permute-done.8.refs_6_ = bf16[32,2560]{1,0:T(8,128)(2,1)S(1)} collective-permute-done((bf16[32,2560]{1,0:T(8,128)(2,1)S(1)}, bf16[32,2560]{1,0:T(8,128)(2,1)S(1)}, u32[]{:S(2)}, u32[]{:S(2)}) %collective-permute-start.8) | collective-permute-done | bytes 163872 | tf_op jit(solution)/shard_map/ppermute | solution.py:233
  50.8 2.3 %shard_map.82 = (f32[2,32,1024]{2,1,0:T(8,128)S(1)}, f32[2,32,1024]{2,1,0:T(8,128)S(1)}) custom-call(f32[7]{0:T(128)S(1)} %copy-done.3, f32[2,32,1024]{2,1,0:T(8,128)S(1)} %get-tuple-element.60.refs_0_.refs_1_, f32[2,32,1024]{2,1,0:T(8,128)S(1)} %get-tuple-element.55.refs_0_.refs_1_, f32[2,32,1024]{2,1,0:T(8,128)S(1)} %get-tuple-element.61.refs_2_, ...), custom_call_target="tpu_custom_call" | custom-call | tf_op jit(solution)/shard_map/pallas_call | solution.py:195
  53.1 1.7 %collective-permute-done.9.refs_3_ = bf16[32,2560]{1,0:T(8,128)(2,1)S(1)} collective-permute-done((bf16[32,2560]{1,0:T(8,128)(2,1)S(1)}, bf16[32,2560]{1,0:T(8,128)(2,1)S(1)}, u32[]{:S(2)}, u32[]{:S(2)}) %collective-permute-start.9) | collective-permute-done | bytes 163872 | tf_op jit(solution)/shard_map/ppermute | solution.py:232
  54.8 2.1 %shard_map.83 = (f32[2,32,1024]{2,1,0:T(8,128)S(1)}, bf16[32,2560]{1,0:T(8,128)(2,1)S(1)}, bf16[32,2560]{1,0:T(8,128)(2,1)S(1)}) custom-call(f32[7]{0:T(128)S(1)} %copy-done.3, f32[2,32,1024]{2,1,0:T(8,128)S(1)} %get-tuple-element.63.refs_0_, bf16[3,1024,1024]{2,1,0:T(8,128)(2,1)S(1)} %get-tuple-element.39.refs_1_.refs_3_.refs_2_, ...), custom_call_target="tpu_custom_call" | custom-call | tf_op jit(solution)/shard_map/pallas_call | solution.py:195
  56.9 1.1 %collective-permute-start.10 = (bf16[32,2560]{1,0:T(8,128)(2,1)S(1)}, bf16[32,2560]{1,0:T(8,128)(2,1)S(1)}, u32[]{:S(2)}, u32[]{:S(2)}) collective-permute-start(bf16[32,2560]{1,0:T(8,128)(2,1)S(1)} %get-tuple-element.67), channel_id=1, source_target_pairs={{0,16},{16,0},{32,48},{48,32},{64,80},{80,64},{96,112},{112,96},{1... | collective-permute-start | bytes 491528 | tf_op jit(solution)/shard_map/ppermute | solution.py:233
  58.0 0.0 collective-permute-start.11
  58.0 1.0 %collective-permute-done.10.refs_6_ = bf16[32,2560]{1,0:T(8,128)(2,1)S(1)} collective-permute-done((bf16[32,2560]{1,0:T(8,128)(2,1)S(1)}, bf16[32,2560]{1,0:T(8,128)(2,1)S(1)}, u32[]{:S(2)}, u32[]{:S(2)}) %collective-permute-start.10) | collective-permute-done | bytes 163872 | tf_op jit(solution)/shard_map/ppermute | solution.py:233
  59.0 2.3 %shard_map.84 = (f32[2,32,1024]{2,1,0:T(8,128)S(1)}, f32[2,32,1024]{2,1,0:T(8,128)S(1)}) custom-call(f32[7]{0:T(128)S(1)} %copy-done.3, f32[2,32,1024]{2,1,0:T(8,128)S(1)} %get-tuple-element.65.refs_0_, f32[2,32,1024]{2,1,0:T(8,128)S(1)} %get-tuple-element.60.refs_0_.refs_1_, f32[2,32,1024]{2,1,0:T(8,128)S(1)} %get-tuple-element.66.refs_2_, ...), custom_call_target="tpu_custom_call" | custom-call | tf_op jit(solution)/shard_map/pallas_call | solution.py:195
  61.3 1.7 %collective-permute-done.11.refs_4_ = bf16[32,2560]{1,0:T(8,128)(2,1)S(1)} collective-permute-done((bf16[32,2560]{1,0:T(8,128)(2,1)S(1)}, bf16[32,2560]{1,0:T(8,128)(2,1)S(1)}, u32[]{:S(2)}, u32[]{:S(2)}) %collective-permute-start.11) | collective-permute-done | bytes 163872 | tf_op jit(solution)/shard_map/ppermute | solution.py:232
  63.1 2.0 %shard_map.85 = f32[2,8,32,128]{3,2,1,0:T(8,128)} custom-call(f32[7]{0:T(128)S(1)} %copy-done.3, f32[2,32,1024]{2,1,0:T(8,128)S(1)} %get-tuple-element.68.refs_0_, f32[2,32,1024]{2,1,0:T(8,128)S(1)} %get-tuple-element.69.refs_1_, bf16[3,1024,1024]{2,1,0:T(8,128)(2,1)S(1)} %get-tuple-element.39.refs_1_.refs_3_.refs_2_, ...), custom_call_target="tpu_custom_call" | custom-call | tf_op jit(solution)/shard_map/pallas_call | solution.py:195
  (5 shorter events, 0.0 us)
Async XLA Ops:
  0.0 2.2 %copy-start = (bf16[8,16,128,128]{3,2,1,0:T(8,128)(2,1)S(1)}, bf16[8,16,128,128]{3,2,1,0:T(8,128)(2,1)}, u32[]{:S(2)}) copy-start(bf16[8,16,128,128]{3,2,1,0:T(8,128)(2,1)} %coupling_ref.1) | copy-start | bytes 12582916
  2.2 0.9 %copy-start.1 = (f32[2,8,32,128]{3,2,1,0:T(8,128)S(1)}, f32[2,8,32,128]{3,2,1,0:T(8,128)}, u32[]{:S(2)}) copy-start(f32[2,8,32,128]{3,2,1,0:T(8,128)} %states_ref.1) | copy-start | bytes 786436
  3.1 0.7 %copy-start.4 = (f32[2,8,128]{2,1,0:T(8,128)S(1)}, f32[2,8,128]{2,1,0:T(8,128)}, u32[]{:S(2)}) copy-start(f32[2,8,128]{2,1,0:T(8,128)} %onsite_ref.1) | copy-start | bytes 24580
  3.8 0.7 %copy-start.5 = (f32[2,8,128]{2,1,0:T(8,128)S(1)}, f32[2,8,128]{2,1,0:T(8,128)}, u32[]{:S(2)}) copy-start(f32[2,8,128]{2,1,0:T(8,128)} %hop_row_ref.1) | copy-start | bytes 24580
  4.5 0.7 %copy-start.6 = (f32[2,8,128]{2,1,0:T(8,128)S(1)}, f32[2,8,128]{2,1,0:T(8,128)}, u32[]{:S(2)}) copy-start(f32[2,8,128]{2,1,0:T(8,128)} %hop_up_ref.1) | copy-start | bytes 24580
  5.2 0.7 %copy-start.7 = (s32[8,16]{1,0:T(8,128)S(1)}, s32[8,16]{1,0:T(8,128)}, u32[]{:S(2)}) copy-start(s32[8,16]{1,0:T(8,128)} %partner_ref.1) | copy-start | bytes 1540
  12.1 4.4 %collective-permute-start = (bf16[32,2560]{1,0:T(8,128)(2,1)S(1)}, bf16[32,2560]{1,0:T(8,128)(2,1)S(1)}, u32[]{:S(2)}, u32[]{:S(2)}) collective-permute-start(bf16[32,2560]{1,0:T(8,128)(2,1)S(1)} %get-tuple-element.42), channel_id=1, source_target_pairs={{0,16},{16,0},{32,48},{48,32},{64,80},{80,64},{96,112},{112,96},{1... | collective-permute-start | bytes 491528 | tf_op jit(solution)/shard_map/ppermute | solution.py:233
  15.5 4.7 %collective-permute-start.1 = (bf16[32,2560]{1,0:T(8,128)(2,1)S(1)}, bf16[32,2560]{1,0:T(8,128)(2,1)S(1)}, u32[]{:S(2)}, u32[]{:S(2)}) collective-permute-start(bf16[32,2560]{1,0:T(8,128)(2,1)S(1)} %get-tuple-element.44), channel_id=1, source_target_pairs={{0,240},{16,32},{32,16},{48,64},{64,48},{80,96},{96,80},{112,128},... | collective-permute-start | bytes 491528 | tf_op jit(solution)/shard_map/ppermute | solution.py:232
  16.5 0.7 %copy-start.2 = (f32[7]{0:T(128)S(1)}, f32[7]{0:T(128)}, u32[]{:S(2)}) copy-start(f32[7]{0:T(128)} %coefs_ref.23) | copy-start | bytes 88
  22.4 3.6 %collective-permute-start.2 = (bf16[32,2560]{1,0:T(8,128)(2,1)S(1)}, bf16[32,2560]{1,0:T(8,128)(2,1)S(1)}, u32[]{:S(2)}, u32[]{:S(2)}) collective-permute-start(bf16[32,2560]{1,0:T(8,128)(2,1)S(1)} %get-tuple-element.47), channel_id=1, source_target_pairs={{0,16},{16,0},{32,48},{48,32},{64,80},{80,64},{96,112},{112,96},{1... | collective-permute-start | bytes 491528 | tf_op jit(solution)/shard_map/ppermute | solution.py:233
  24.9 5.0 %collective-permute-start.3 = (bf16[32,2560]{1,0:T(8,128)(2,1)S(1)}, bf16[32,2560]{1,0:T(8,128)(2,1)S(1)}, u32[]{:S(2)}, u32[]{:S(2)}) collective-permute-start(bf16[32,2560]{1,0:T(8,128)(2,1)S(1)} %get-tuple-element.49), channel_id=1, source_target_pairs={{0,240},{16,32},{32,16},{48,64},{64,48},{80,96},{96,80},{112,128},... | collective-permute-start | bytes 491528 | tf_op jit(solution)/shard_map/ppermute | solution.py:232
  26.0 8.2 %copy-start.3 = (f32[7]{0:T(128)S(1)}, f32[7]{0:T(128)}, u32[]{:S(2)}) copy-start(f32[7]{0:T(128)} %coefs_ref.23) | copy-start | bytes 88
  32.1 2.1 %collective-permute-start.4 = (bf16[32,2560]{1,0:T(8,128)(2,1)S(1)}, bf16[32,2560]{1,0:T(8,128)(2,1)S(1)}, u32[]{:S(2)}, u32[]{:S(2)}) collective-permute-start(bf16[32,2560]{1,0:T(8,128)(2,1)S(1)} %get-tuple-element.52), channel_id=1, source_target_pairs={{0,16},{16,0},{32,48},{48,32},{64,80},{80,64},{96,112},{112,96},{1... | collective-permute-start | bytes 491528 | tf_op jit(solution)/shard_map/ppermute | solution.py:233
  33.2 5.0 %collective-permute-start.5 = (bf16[32,2560]{1,0:T(8,128)(2,1)S(1)}, bf16[32,2560]{1,0:T(8,128)(2,1)S(1)}, u32[]{:S(2)}, u32[]{:S(2)}) collective-permute-start(bf16[32,2560]{1,0:T(8,128)(2,1)S(1)} %get-tuple-element.54), channel_id=1, source_target_pairs={{0,240},{16,32},{32,16},{48,64},{64,48},{80,96},{96,80},{112,128},... | collective-permute-start | bytes 491528 | tf_op jit(solution)/shard_map/ppermute | solution.py:232
  40.3 2.1 %collective-permute-start.6 = (bf16[32,2560]{1,0:T(8,128)(2,1)S(1)}, bf16[32,2560]{1,0:T(8,128)(2,1)S(1)}, u32[]{:S(2)}, u32[]{:S(2)}) collective-permute-start(bf16[32,2560]{1,0:T(8,128)(2,1)S(1)} %get-tuple-element.57), channel_id=1, source_target_pairs={{0,16},{16,0},{32,48},{48,32},{64,80},{80,64},{96,112},{112,96},{1... | collective-permute-start | bytes 491528 | tf_op jit(solution)/shard_map/ppermute | solution.py:233
  41.4 5.0 %collective-permute-start.7 = (bf16[32,2560]{1,0:T(8,128)(2,1)S(1)}, bf16[32,2560]{1,0:T(8,128)(2,1)S(1)}, u32[]{:S(2)}, u32[]{:S(2)}) collective-permute-start(bf16[32,2560]{1,0:T(8,128)(2,1)S(1)} %get-tuple-element.59), channel_id=1, source_target_pairs={{0,240},{16,32},{32,16},{48,64},{64,48},{80,96},{96,80},{112,128},... | collective-permute-start | bytes 491528 | tf_op jit(solution)/shard_map/ppermute | solution.py:232
  48.5 2.3 %collective-permute-start.8 = (bf16[32,2560]{1,0:T(8,128)(2,1)S(1)}, bf16[32,2560]{1,0:T(8,128)(2,1)S(1)}, u32[]{:S(2)}, u32[]{:S(2)}) collective-permute-start(bf16[32,2560]{1,0:T(8,128)(2,1)S(1)} %get-tuple-element.62), channel_id=1, source_target_pairs={{0,16},{16,0},{32,48},{48,32},{64,80},{80,64},{96,112},{112,96},{1... | collective-permute-start | bytes 491528 | tf_op jit(solution)/shard_map/ppermute | solution.py:233
  49.8 5.0 %collective-permute-start.9 = (bf16[32,2560]{1,0:T(8,128)(2,1)S(1)}, bf16[32,2560]{1,0:T(8,128)(2,1)S(1)}, u32[]{:S(2)}, u32[]{:S(2)}) collective-permute-start(bf16[32,2560]{1,0:T(8,128)(2,1)S(1)} %get-tuple-element.64), channel_id=1, source_target_pairs={{0,240},{16,32},{32,16},{48,64},{64,48},{80,96},{96,80},{112,128},... | collective-permute-start | bytes 491528 | tf_op jit(solution)/shard_map/ppermute | solution.py:232
  56.9 2.1 %collective-permute-start.10 = (bf16[32,2560]{1,0:T(8,128)(2,1)S(1)}, bf16[32,2560]{1,0:T(8,128)(2,1)S(1)}, u32[]{:S(2)}, u32[]{:S(2)}) collective-permute-start(bf16[32,2560]{1,0:T(8,128)(2,1)S(1)} %get-tuple-element.67), channel_id=1, source_target_pairs={{0,16},{16,0},{32,48},{48,32},{64,80},{80,64},{96,112},{112,96},{1... | collective-permute-start | bytes 491528 | tf_op jit(solution)/shard_map/ppermute | solution.py:233
  58.0 5.0 %collective-permute-start.11 = (bf16[32,2560]{1,0:T(8,128)(2,1)S(1)}, bf16[32,2560]{1,0:T(8,128)(2,1)S(1)}, u32[]{:S(2)}, u32[]{:S(2)}) collective-permute-start(bf16[32,2560]{1,0:T(8,128)(2,1)S(1)} %get-tuple-element.70), channel_id=1, source_target_pairs={{0,240},{16,32},{32,16},{48,64},{64,48},{80,96},{96,80},{112,128},... | collective-permute-start | bytes 491528 | tf_op jit(solution)/shard_map/ppermute | solution.py:232

commit v2 on v1

v2 whole, which is shorter than its diff:
```python
import functools

import jax
import jax.numpy as jnp
from jax import lax
from jax.experimental import pallas as pl
from jax.experimental.pallas import tpu as pltpu
from jax.sharding import PartitionSpec as P

REACH = 8
LOCAL, MATE, FAR = 0, 1, 2
IN_VMEM = pl.BlockSpec(memory_space=pltpu.VMEM)
ANYWHERE = pl.BlockSpec(memory_space=pl.ANY)
PAIR = 2


def near(x):
    return pltpu.with_memory_space_constraint(x, pltpu.VMEM)


def outside(x):
    return pltpu.with_memory_space_constraint(x, pltpu.HBM)


def held(shape, dtype):
    return pltpu.VMEM(shape, dtype)


def dot(x, w, contract):
    return lax.dot_general(x, w, (((1,), (contract,)), ((), ())), preferred_element_type=jnp.float32)


def span(side, group, groups, step):
    if side == FAR:
        return slice(0, (groups - group) * step)
    if side == MATE:
        return slice((groups - 1 - group) * step, groups * step)
    return slice(0, groups * step)


def products(x, w_ref, side, contract, cols):
    step = PAIR * cols
    groups = w_ref.shape[1] // step
    for group in range(groups):
        outs = slice(group * step, (group + 1) * step)
        ins = span(side, group, groups, step)
        block = w_ref[side, ins, outs] if contract == 0 else w_ref[side, outs, ins]
        yield outs, dot(x[:, ins], block, contract)


def write_payload(x_ref, w_ref, rim_ref, side, out_ref):
    wide = x_ref.shape[2]
    cols = rim_ref.shape[2]
    edge = slice(0, cols) if side == FAR else slice(wide - cols, wide)
    which = side - 1
    out_ref[:, 0:wide] = x_ref[1].astype(jnp.bfloat16)
    rim = x_ref[0, :, edge] * rim_ref[which, 0:1, :]
    rim += pltpu.roll(x_ref[1, :, edge] * rim_ref[which, 1:2, :], cols - 1, axis=1)
    high = rim.astype(jnp.bfloat16)
    out_ref[:, 2 * wide : 2 * wide + cols] = high
    out_ref[:, 2 * wide + cols :] = (rim - high.astype(jnp.float32)).astype(jnp.bfloat16)
    first = x_ref[0].astype(jnp.bfloat16)
    for outs, term in products(first, w_ref, side, 0, cols):
        out_ref[:, wide + outs.start : wide + outs.stop] = term.astype(jnp.bfloat16)


def add_received(scale, got_ref, w_ref, rim_ref, side, from_ref, to_ref):
    wide = to_ref.shape[2]
    cols = rim_ref.shape[2]
    edge = slice(0, cols) if side == FAR else slice(wide - cols, wide)
    which = side - 1
    to_ref[1] = from_ref[1] + scale * got_ref[:, wide : 2 * wide].astype(jnp.float32)
    for outs, term in products(got_ref[:, 0:wide], w_ref, side, 1, cols):
        to_ref[0, :, outs] = from_ref[0, :, outs] + scale * term
    rim = got_ref[:, 2 * wide : 2 * wide + cols].astype(jnp.float32)
    rim += got_ref[:, 2 * wide + cols :].astype(jnp.float32)
    to_ref[0, :, edge] += scale * (rim * rim_ref[which, 0:1, :])
    to_ref[1, :, edge] += scale * (pltpu.roll(rim, 1, axis=1) * rim_ref[which, 1:2, :])


def prepare(
    partner_hbm, states_hbm, onsite_hbm, hop_row_hbm, hop_up_hbm, coefs_hbm, coupling_hbm,
    x_ref, w_ref, coef_ref, rim_ref, weight_ref, far_ref, mate_ref,
    partner_ref, states_ref, small_ref, coefs_ref, blocks, total, sems, row_sems,
):
    rows, slots = partner_hbm.shape
    cols = onsite_hbm.shape[2]
    tile = lax.axis_index("tile")
    all_rows = rows * lax.axis_size("tile")
    here = lax.rem(tile, 2)
    offsets = 2 * REACH + 1
    spare = offsets + 1

    def kept(place):
        return place + here * (rows - 1 - 2 * place)

    copies = [
        pltpu.make_async_copy(src, dst, sems.at[i])
        for i, (src, dst) in enumerate(
            (
                (partner_hbm, partner_ref),
                (hop_up_hbm, small_ref.at[0]),
                (onsite_hbm, small_ref.at[1]),
                (hop_row_hbm, small_ref.at[2]),
                (coefs_hbm, coefs_ref),
                (states_hbm, states_ref),
            )
        )
    ]

    def fetch(r):
        return pltpu.make_async_copy(coupling_hbm.at[r], blocks.at[r], row_sems.at[r])

    copies[0].start()
    for place in range(rows):
        fetch(kept(place)).start()
    for copy in copies[1:]:
        copy.start()

    total[...] = jnp.zeros_like(total)
    for side, place, sigma in (
        [(FAR, p, rows - p) for p in range(1, rows, PAIR)]
        + [(MATE, p, rows - PAIR - p) for p in range(0, rows, PAIR)]
    ):
        w_ref[side, place * cols : (place + 1) * cols, sigma * cols : (sigma + 1) * cols] = jnp.zeros(
            (cols, cols), jnp.bfloat16
        )

    for copy in copies:
        copy.wait()
    for n in range(coefs_ref.shape[0]):
        weight_ref[n : n + 1, :] = jnp.full((1, cols), coefs_ref[n], jnp.float32)
    column = lax.broadcasted_iota(jnp.int32, (rows, cols), 1)
    parity = lax.broadcasted_iota(jnp.int32, (rows, cols), 0) + column + tile * rows
    odd = lax.rem(column[0:1], 2) == 1
    for layer in range(2):
        bond = jnp.where(lax.rem(parity, 2) == 0, small_ref[0, layer], 0.0)
        hop_row = small_ref[2, layer]
        left = pltpu.roll(hop_row, 1, axis=1)
        for place in range(rows):
            back = rows - 1 - place
            at = slice(place, place + 1)

            def ours(value):
                return jnp.where(here == 0, value[at], value[back : back + 1])

            coef_ref[layer, 0, at] = ours(small_ref[1, layer])
            coef_ref[layer, 1, at] = ours(hop_row)
            coef_ref[layer, 2, at] = ours(left)
            if place < rows - 1:
                coef_ref[layer, 3, at] = jnp.where(here == 0, bond[at], bond[back - 1 : back])
            if place > 0:
                coef_ref[layer, 4, at] = jnp.where(here == 0, bond[place - 1 : place], bond[back : back + 1])
        last = bond[rows - 1 :]
        raw = jnp.where(odd, 1.0, 0.0)
        rim_ref[FAR - 1, layer : layer + 1] = jnp.where(here == 0, raw, last)
        rim_ref[MATE - 1, layer : layer + 1] = jnp.where(here == 0, last, raw)
        for place in range(rows):
            x_ref[layer, :, place * cols : (place + 1) * cols] = states_ref[layer, kept(place)]

    for place in range(rows):
        row = kept(place)
        fetch(row).wait()
        for k in range(slots):
            slot = partner_ref[row, k]
            away = slot - tile * rows - row
            away = jnp.where(away > all_rows // 2, away - all_rows, away)
            away = jnp.where(away < -(all_rows // 2), away + all_rows, away)
            at = jnp.where(slot >= 0, REACH + (1 - 2 * here) * away, offsets) + place * spare
            total[at] += blocks[row, k].astype(jnp.float32)
        for offset in range(offsets):
            reached = place + offset - REACH
            if reached < 0:
                side, sigma = FAR, -1 - reached
            elif reached < rows:
                side, sigma = LOCAL, reached
            else:
                side, sigma = MATE, 2 * rows - 1 - reached
            w_ref[side, place * cols : (place + 1) * cols, sigma * cols : (sigma + 1) * cols] = total[
                place * spare + offset
            ].astype(jnp.bfloat16)
    write_payload(x_ref, w_ref, rim_ref, FAR, far_ref)
    write_payload(x_ref, w_ref, rim_ref, MATE, mate_ref)


def inner(order, *refs):
    if order == 0:
        x_ref, w_ref, coef_ref, weight_ref, sum_ref, filt_out = refs
        scale = 1.0 / 12.0
    else:
        x_ref, prev_ref, filt_ref, w_ref, coef_ref, weight_ref, sum_ref, filt_out = refs
        scale = 2.0 / 12.0
    wide = x_ref.shape[2]
    cols = weight_ref.shape[1]
    rows = wide // cols
    first = x_ref[0].astype(jnp.bfloat16)
    second = x_ref[1].astype(jnp.bfloat16)
    for outs, term in products(second, w_ref, LOCAL, 1, cols):
        sum_ref[0, :, outs] = scale * term
    for outs, term in products(first, w_ref, LOCAL, 0, cols):
        sum_ref[1, :, outs] = scale * term
    for layer in range(2):
        for r in range(rows):
            here = slice(r * cols, (r + 1) * cols)
            x = x_ref[layer, :, here]

            def factor(i):
                return coef_ref[layer, i, r : r + 1, :]

            hop = factor(0) * x
            hop += factor(1) * pltpu.roll(x, cols - 1, axis=1)
            hop += factor(2) * pltpu.roll(x, 1, axis=1)
            if r < rows - 1:
                hop += factor(3) * x_ref[layer, :, (r + 1) * cols : (r + 2) * cols]
            if r > 0:
                hop += factor(4) * x_ref[layer, :, (r - 1) * cols : r * cols]
            term = sum_ref[layer, :, here] + scale * hop
            filt = weight_ref[order : order + 1, :] * x
            if order > 0:
                term -= prev_ref[layer, :, here]
                filt += filt_ref[layer, :, here]
            filt_out[layer, :, here] = filt
            sum_ref[layer, :, here] = term


def from_mate(scale, part_ref, w_ref, rim_ref, got_ref, sum_ref):
    add_received(scale, got_ref, w_ref, rim_ref, MATE, part_ref, sum_ref)


def outer(scale, sum_ref, w_ref, rim_ref, got_ref, x_ref, far_ref, mate_ref):
    add_received(scale, got_ref, w_ref, rim_ref, FAR, sum_ref, x_ref)
    write_payload(x_ref, w_ref, rim_ref, FAR, far_ref)
    write_payload(x_ref, w_ref, rim_ref, MATE, mate_ref)


def finish(scale, degree, sum_ref, filt_ref, w_ref, rim_ref, weight_ref, got_ref, out_ref, x_ref):
    cols = rim_ref.shape[2]
    rows = out_ref.shape[1]
    add_received(scale, got_ref, w_ref, rim_ref, FAR, sum_ref, x_ref)
    flip = lax.rem(lax.axis_index("tile"), 2)
    for layer in range(2):
        for place in range(rows):
            here = slice(place * cols, (place + 1) * cols)
            out_ref[layer, place + flip * (rows - 1 - 2 * place)] = (
                filt_ref[layer, :, here] + weight_ref[degree : degree + 1, :] * x_ref[layer, :, here]
            )


def call(kernel, outs, args, scratch=(), specs=None, limit=12):
    return pl.pallas_call(
        kernel,
        out_shape=outs,
        in_specs=specs or [IN_VMEM] * len(args),
        out_specs=[IN_VMEM] * len(outs),
        scratch_shapes=list(scratch),
        cost_estimate=pl.CostEstimate(flops=1 << 20, bytes_accessed=1 << 12, transcendentals=0),
        compiler_params=pltpu.CompilerParams(vmem_limit_bytes=limit << 20),
    )(*args)


def body(states, onsite, hop_row, hop_up, partner, coupling, coefs):
    rows, count, cols = states.shape[1:]
    slots = partner.shape[1]
    wide = rows * cols
    degree = coefs.shape[0] - 1
    size = lax.axis_size("tile")
    far_pairs = [(i, (i + 1) % size if i % 2 else (i - 1) % size) for i in range(size)]
    mate_pairs = [(i, i ^ 1) for i in range(size)]

    field = held((2, count, wide), jnp.float32)
    payload = held((count, 2 * wide + 2 * cols), jnp.bfloat16)
    x, w, coef, rim, weight, far, mate = call(
        prepare,
        [field, held((3, wide, wide), jnp.bfloat16), held((2, 5, rows, cols), jnp.float32),
         held((2, 2, cols), jnp.float32), held((degree + 1, cols), jnp.float32), payload, payload],
        [outside(v) for v in (partner, states, onsite, hop_row, hop_up, coefs, coupling)],
        scratch=[
            pltpu.SMEM((rows, slots), jnp.int32),
            pltpu.VMEM((2, rows, count, cols), jnp.float32),
            pltpu.VMEM((3, 2, rows, cols), jnp.float32),
            pltpu.SMEM((degree + 1,), jnp.float32),
            pltpu.VMEM((rows, slots, cols, cols), jnp.bfloat16),
            pltpu.VMEM((rows * (2 * REACH + 2), cols, cols), jnp.float32),
            pltpu.SemaphoreType.DMA((6,)),
            pltpu.SemaphoreType.DMA((rows,)),
        ],
        specs=[ANYWHERE] * 7,
        limit=24,
    )
    w, coef, rim, weight, x = near(w), near(coef), near(rim), near(weight), near(x)
    prev = filt = None
    for order in range(degree):
        scale = 1.0 / 12.0 if order == 0 else 2.0 / 12.0
        got_far = lax.ppermute(far, "tile", far_pairs)
        got_mate = lax.ppermute(mate, "tile", mate_pairs)
        past = [] if order == 0 else [near(prev), near(filt)]
        part, filt = call(
            functools.partial(inner, order), [field, field], [x, *past, w, coef, weight]
        )
        (part,) = call(
            functools.partial(from_mate, scale), [field], [near(part), w, rim, near(got_mate)]
        )
        prev = x
        if order < degree - 1:
            x, far, mate = call(
                functools.partial(outer, scale),
                [field, payload, payload],
                [near(part), w, rim, near(got_far)],
            )
            x = near(x)
        else:
            (out,) = call(
                functools.partial(finish, scale, degree),
                [jax.ShapeDtypeStruct(states.shape, jnp.float32)],
                [near(part), near(filt), w, rim, weight, near(got_far)],
                scratch=[pltpu.VMEM((2, count, wide), jnp.float32)],
            )
    return out


def solution(mesh):
    placed = (
        P(None, "tile", "state", None),
        P(None, "tile", None),
        P(None, "tile", None),
        P(None, "tile", None),
        P("tile", None),
        P("tile", None, None, None),
        P(),
    )
    return jax.shard_map(
        body, mesh=mesh, in_specs=placed, out_specs=P(None, "tile", "state", None), check_vma=False
    )
```

time: 65.4 us -> 50.5 us (0.77)
  Pallas kernels: 32.5 us -> 20.8 us
  local copies, waits for them, and re-layouts: 6.57 us -> 0 us
  waiting for transfers between devices: 15.3 us -> 19 us
    pallas_call x13 -> x19, Pallas kernels: 32.5 us -> 20.8 us  [call(): pl.pallas_call(kernel, out_shape=outs, in_specs=specs or [IN_VMEM] * len(...]
    ppermute x6, waiting for transfers between devices: 9.3 us -> 19 us  [body(): got_far = lax.ppermute(far, 'tile', far_pairs)]
    unnamed x16 -> x0, local copies, waits for them, and re-layouts: 6.57 us -> none
    ppermute x6, waiting for transfers between devices: 6.04 us -> 0.02 us  [body(): got_mate = lax.ppermute(mate, 'tile', mate_pairs)]
  transfers between devices with their start and end apart: 12 -> 12, of which waited for: 12 -> 6; matrix products, arithmetic and copies ran while one was open for 0% -> 0% of each run, Pallas kernels for 21% -> 19%
where the time goes in v2:
time: 50.5 us; the launch traced here: 50.4 us
  Pallas kernels  20.8 us (41%)
  waiting for transfers between devices  19 us (38%)
  starting transfers between devices  10.5 us (21%)
    pallas_call x19, Pallas kernels, call(): pl.pallas_call(kernel, out_shape=outs, in_specs=specs or [IN_VMEM] * len(...  20.8 us
    ppermute x6, waiting for transfers between devices, body(): got_far = lax.ppermute(far, 'tile', far_pairs)  19 us
    ppermute x6, starting transfers between devices, body(): got_mate = lax.ppermute(mate, 'tile', mate_pairs)  10.4 us
  transfers between devices with their start and end apart: 12, of which 6 were waited for; matrix products, arithmetic and copies ran while one was open for 0% of the time, Pallas kernels for 19%

profile of v2, /device:TPU:1, one launch (start us, length us, event | category | flops | bytes accessed | tf_op | source)
XLA Modules:
  0.0 50.4 jit_solution(3870919222272721787)
XLA Ops:
  0.0 4.9 %shard_map.73 = (f32[2,32,1024]{2,1,0:T(8,128)S(1)}, bf16[3,1024,1024]{2,1,0:T(8,128)(2,1)S(1)}, f32[2,5,8,128]{3,2,1,0:T(8,128)S(1)}, f32[2,2,128]{2,1,0:T(2,12...) custom-call(s32[8,16]{1,0:T(8,128)} %partner_hbm.1, ...), custom_call_target="tpu_custom_call" | custom-call | flops 1048576 | bytes 4096 | tf_op jit(solution)/shard_map/pallas_call | solution.py:250
  4.9 3.3 %collective-permute-start = (bf16[32,2304]{1,0:T(8,128)(2,1)S(1)}, bf16[32,2304]{1,0:T(8,128)(2,1)S(1)}, u32[]{:S(2)}, u32[]{:S(2)}) collective-permute-start(bf16[32,2304]{1,0:T(8,128)(2,1)S(1)} %get-tuple-element.45), channel_id=1, source_target_pairs={{0,16},{16,0},{32,48},{48,32},{64,80},{80,64},{96,112},{112,96},{1... | collective-permute-start | bytes 442376 | tf_op jit(solution)/shard_map/ppermute | solution.py:295
  8.3 0.0 collective-permute-start.1
  8.3 1.1 %shard_map.74 = (f32[2,32,1024]{2,1,0:T(8,128)S(1)}, f32[2,32,1024]{2,1,0:T(8,128)S(1)}) custom-call(f32[2,32,1024]{2,1,0:T(8,128)S(1)} %get-tuple-element.39.refs_0_.refs_1_, bf16[3,1024,1024]{2,1,0:T(8,128)(2,1)S(1)} %get-tuple-element.40.refs_1_.w_ref.refs_3_, f32[2,5,8,128]{3,2,1,0:T(8,128)S(1)} %get-tuple-element.41.refs_2_.refs_4_, ...), custom_call_target="tpu_custom_call" | custom-call | flops 1048576 | bytes 4096 | tf_op jit(solution)/shard_map/pallas_call | solution.py:250
  9.4 0.0 collective-permute-done.got_ref
  9.4 0.5 %shard_map.75.sum_ref = f32[2,32,1024]{2,1,0:T(8,128)S(1)} custom-call(f32[2,32,1024]{2,1,0:T(8,128)S(1)} %get-tuple-element.43.part_ref, bf16[3,1024,1024]{2,1,0:T(8,128)(2,1)S(1)} %get-tuple-element.40.refs_1_.w_ref.refs_3_, f32[2,2,128]{2,1,0:T(2,128)S(1)} %get-tuple-element.44.rim_ref, bf16[32,2304]{1,0:T(8,128)(2,1)S(1)} %collective-permute-done.got_ref), custom_call_target="tpu_custom_call" | custom-call | flops 1048576 | bytes 4096 | tf_op jit(solution)/shard_map/pallas_call | solution.py:250
  9.9 3.0 %collective-permute-done.1.got_ref = bf16[32,2304]{1,0:T(8,128)(2,1)S(1)} collective-permute-done((bf16[32,2304]{1,0:T(8,128)(2,1)S(1)}, bf16[32,2304]{1,0:T(8,128)(2,1)S(1)}, u32[]{:S(2)}, u32[]{:S(2)}) %collective-permute-start.1) | collective-permute-done | bytes 147488 | tf_op jit(solution)/shard_map/ppermute | solution.py:294
  12.8 1.0 %shard_map.76 = (f32[2,32,1024]{2,1,0:T(8,128)S(1)}, bf16[32,2304]{1,0:T(8,128)(2,1)S(1)}, bf16[32,2304]{1,0:T(8,128)(2,1)S(1)}) custom-call(f32[2,32,1024]{2,1,0:T(8,128)S(1)} %shard_map.75.sum_ref, bf16[3,1024,1024]{2,1,0:T(8,128)(2,1)S(1)} %get-tuple-element.40.refs_1_.w_ref.refs_3_, f32[2,2,128]{2,1,0:T(2,128)S(1)} %get-tuple-element.44.rim_ref, ...), custom_call_target="tpu_custom_call" | custom-call | flops 1048576 | bytes 4096 | tf_op jit(solution)/shard_map/pallas_call | solution.py:250
  13.8 2.6 %collective-permute-start.2 = (bf16[32,2304]{1,0:T(8,128)(2,1)S(1)}, bf16[32,2304]{1,0:T(8,128)(2,1)S(1)}, u32[]{:S(2)}, u32[]{:S(2)}) collective-permute-start(bf16[32,2304]{1,0:T(8,128)(2,1)S(1)} %get-tuple-element.50), channel_id=1, source_target_pairs={{0,16},{16,0},{32,48},{48,32},{64,80},{80,64},{96,112},{112,96},{1... | collective-permute-start | bytes 442376 | tf_op jit(solution)/shard_map/ppermute | solution.py:295
  16.4 0.0 collective-permute-start.3
  16.4 1.1 %shard_map.77 = (f32[2,32,1024]{2,1,0:T(8,128)S(1)}, f32[2,32,1024]{2,1,0:T(8,128)S(1)}) custom-call(f32[2,32,1024]{2,1,0:T(8,128)S(1)} %get-tuple-element.47.refs_0_.refs_1_, f32[2,32,1024]{2,1,0:T(8,128)S(1)} %get-tuple-element.39.refs_0_.refs_1_, f32[2,32,1024]{2,1,0:T(8,128)S(1)} %get-tuple-element.48.refs_2_, ...), custom_call_target="tpu_custom_call" | custom-call | flops 1048576 | bytes 4096 | tf_op jit(solution)/shard_map/pallas_call | solution.py:250
  17.5 0.0 collective-permute-done.2.got_ref
  17.5 0.5 shard_map.78.sum_ref
  18.0 3.2 %collective-permute-done.3.got_ref = bf16[32,2304]{1,0:T(8,128)(2,1)S(1)} collective-permute-done((bf16[32,2304]{1,0:T(8,128)(2,1)S(1)}, bf16[32,2304]{1,0:T(8,128)(2,1)S(1)}, u32[]{:S(2)}, u32[]{:S(2)}) %collective-permute-start.3) | collective-permute-done | bytes 147488 | tf_op jit(solution)/shard_map/ppermute | solution.py:294
  21.3 1.0 %shard_map.79 = (f32[2,32,1024]{2,1,0:T(8,128)S(1)}, bf16[32,2304]{1,0:T(8,128)(2,1)S(1)}, bf16[32,2304]{1,0:T(8,128)(2,1)S(1)}) custom-call(f32[2,32,1024]{2,1,0:T(8,128)S(1)} %shard_map.78.sum_ref, bf16[3,1024,1024]{2,1,0:T(8,128)(2,1)S(1)} %get-tuple-element.40.refs_1_.w_ref.refs_3_, f32[2,2,128]{2,1,0:T(2,128)S(1)} %get-tuple-element.44.rim_ref, ...), custom_call_target="tpu_custom_call" | custom-call | flops 1048576 | bytes 4096 | tf_op jit(solution)/shard_map/pallas_call | solution.py:250
  22.2 1.1 %collective-permute-start.4 = (bf16[32,2304]{1,0:T(8,128)(2,1)S(1)}, bf16[32,2304]{1,0:T(8,128)(2,1)S(1)}, u32[]{:S(2)}, u32[]{:S(2)}) collective-permute-start(bf16[32,2304]{1,0:T(8,128)(2,1)S(1)} %get-tuple-element.55), channel_id=1, source_target_pairs={{0,16},{16,0},{32,48},{48,32},{64,80},{80,64},{96,112},{112,96},{1... | collective-permute-start | bytes 442376 | tf_op jit(solution)/shard_map/ppermute | solution.py:295
  23.3 0.0 collective-permute-start.5
  23.3 1.1 %shard_map.80 = (f32[2,32,1024]{2,1,0:T(8,128)S(1)}, f32[2,32,1024]{2,1,0:T(8,128)S(1)}) custom-call(f32[2,32,1024]{2,1,0:T(8,128)S(1)} %get-tuple-element.52.refs_0_.refs_1_, f32[2,32,1024]{2,1,0:T(8,128)S(1)} %get-tuple-element.47.refs_0_.refs_1_, f32[2,32,1024]{2,1,0:T(8,128)S(1)} %get-tuple-element.53.refs_2_, ...), custom_call_target="tpu_custom_call" | custom-call | flops 1048576 | bytes 4096 | tf_op jit(solution)/shard_map/pallas_call | solution.py:250
  24.5 0.0 collective-permute-done.4.got_ref
  24.5 0.5 shard_map.81.sum_ref
  25.0 3.2 %collective-permute-done.5.got_ref = bf16[32,2304]{1,0:T(8,128)(2,1)S(1)} collective-permute-done((bf16[32,2304]{1,0:T(8,128)(2,1)S(1)}, bf16[32,2304]{1,0:T(8,128)(2,1)S(1)}, u32[]{:S(2)}, u32[]{:S(2)}) %collective-permute-start.5) | collective-permute-done | bytes 147488 | tf_op jit(solution)/shard_map/ppermute | solution.py:294
  28.2 1.0 %shard_map.82 = (f32[2,32,1024]{2,1,0:T(8,128)S(1)}, bf16[32,2304]{1,0:T(8,128)(2,1)S(1)}, bf16[32,2304]{1,0:T(8,128)(2,1)S(1)}) custom-call(f32[2,32,1024]{2,1,0:T(8,128)S(1)} %shard_map.81.sum_ref, bf16[3,1024,1024]{2,1,0:T(8,128)(2,1)S(1)} %get-tuple-element.40.refs_1_.w_ref.refs_3_, f32[2,2,128]{2,1,0:T(2,128)S(1)} %get-tuple-element.44.rim_ref, ...), custom_call_target="tpu_custom_call" | custom-call | flops 1048576 | bytes 4096 | tf_op jit(solution)/shard_map/pallas_call | solution.py:250
  29.2 1.1 %collective-permute-start.6 = (bf16[32,2304]{1,0:T(8,128)(2,1)S(1)}, bf16[32,2304]{1,0:T(8,128)(2,1)S(1)}, u32[]{:S(2)}, u32[]{:S(2)}) collective-permute-start(bf16[32,2304]{1,0:T(8,128)(2,1)S(1)} %get-tuple-element.60), channel_id=1, source_target_pairs={{0,16},{16,0},{32,48},{48,32},{64,80},{80,64},{96,112},{112,96},{1... | collective-permute-start | bytes 442376 | tf_op jit(solution)/shard_map/ppermute | solution.py:295
  30.3 0.0 collective-permute-start.7
  30.3 1.1 %shard_map.83 = (f32[2,32,1024]{2,1,0:T(8,128)S(1)}, f32[2,32,1024]{2,1,0:T(8,128)S(1)}) custom-call(f32[2,32,1024]{2,1,0:T(8,128)S(1)} %get-tuple-element.57.refs_0_.refs_1_, f32[2,32,1024]{2,1,0:T(8,128)S(1)} %get-tuple-element.52.refs_0_.refs_1_, f32[2,32,1024]{2,1,0:T(8,128)S(1)} %get-tuple-element.58.refs_2_, ...), custom_call_target="tpu_custom_call" | custom-call | flops 1048576 | bytes 4096 | tf_op jit(solution)/shard_map/pallas_call | solution.py:250
  31.4 0.0 collective-permute-done.6.got_ref
  31.4 0.5 shard_map.84.sum_ref
  31.9 3.2 %collective-permute-done.7.got_ref = bf16[32,2304]{1,0:T(8,128)(2,1)S(1)} collective-permute-done((bf16[32,2304]{1,0:T(8,128)(2,1)S(1)}, bf16[32,2304]{1,0:T(8,128)(2,1)S(1)}, u32[]{:S(2)}, u32[]{:S(2)}) %collective-permute-start.7) | collective-permute-done | bytes 147488 | tf_op jit(solution)/shard_map/ppermute | solution.py:294
  35.1 1.0 %shard_map.85 = (f32[2,32,1024]{2,1,0:T(8,128)S(1)}, bf16[32,2304]{1,0:T(8,128)(2,1)S(1)}, bf16[32,2304]{1,0:T(8,128)(2,1)S(1)}) custom-call(f32[2,32,1024]{2,1,0:T(8,128)S(1)} %shard_map.84.sum_ref, bf16[3,1024,1024]{2,1,0:T(8,128)(2,1)S(1)} %get-tuple-element.40.refs_1_.w_ref.refs_3_, f32[2,2,128]{2,1,0:T(2,128)S(1)} %get-tuple-element.44.rim_ref, ...), custom_call_target="tpu_custom_call" | custom-call | flops 1048576 | bytes 4096 | tf_op jit(solution)/shard_map/pallas_call | solution.py:250
  36.1 1.3 %collective-permute-start.8 = (bf16[32,2304]{1,0:T(8,128)(2,1)S(1)}, bf16[32,2304]{1,0:T(8,128)(2,1)S(1)}, u32[]{:S(2)}, u32[]{:S(2)}) collective-permute-start(bf16[32,2304]{1,0:T(8,128)(2,1)S(1)} %get-tuple-element.65), channel_id=1, source_target_pairs={{0,16},{16,0},{32,48},{48,32},{64,80},{80,64},{96,112},{112,96},{1... | collective-permute-start | bytes 442376 | tf_op jit(solution)/shard_map/ppermute | solution.py:295
  37.4 0.0 collective-permute-start.9
  37.4 1.1 %shard_map.86 = (f32[2,32,1024]{2,1,0:T(8,128)S(1)}, f32[2,32,1024]{2,1,0:T(8,128)S(1)}) custom-call(f32[2,32,1024]{2,1,0:T(8,128)S(1)} %get-tuple-element.62.refs_0_.refs_1_, f32[2,32,1024]{2,1,0:T(8,128)S(1)} %get-tuple-element.57.refs_0_.refs_1_, f32[2,32,1024]{2,1,0:T(8,128)S(1)} %get-tuple-element.63.refs_2_, ...), custom_call_target="tpu_custom_call" | custom-call | flops 1048576 | bytes 4096 | tf_op jit(solution)/shard_map/pallas_call | solution.py:250
  38.5 0.0 collective-permute-done.8.got_ref
  38.5 0.5 shard_map.87.sum_ref
  39.0 3.2 %collective-permute-done.9.got_ref = bf16[32,2304]{1,0:T(8,128)(2,1)S(1)} collective-permute-done((bf16[32,2304]{1,0:T(8,128)(2,1)S(1)}, bf16[32,2304]{1,0:T(8,128)(2,1)S(1)}, u32[]{:S(2)}, u32[]{:S(2)}) %collective-permute-start.9) | collective-permute-done | bytes 147488 | tf_op jit(solution)/shard_map/ppermute | solution.py:294
  42.2 1.0 %shard_map.88 = (f32[2,32,1024]{2,1,0:T(8,128)S(1)}, bf16[32,2304]{1,0:T(8,128)(2,1)S(1)}, bf16[32,2304]{1,0:T(8,128)(2,1)S(1)}) custom-call(f32[2,32,1024]{2,1,0:T(8,128)S(1)} %shard_map.87.sum_ref, bf16[3,1024,1024]{2,1,0:T(8,128)(2,1)S(1)} %get-tuple-element.40.refs_1_.w_ref.refs_3_, f32[2,2,128]{2,1,0:T(2,128)S(1)} %get-tuple-element.44.rim_ref, ...), custom_call_target="tpu_custom_call" | custom-call | flops 1048576 | bytes 4096 | tf_op jit(solution)/shard_map/pallas_call | solution.py:250
  43.2 1.1 %collective-permute-start.10 = (bf16[32,2304]{1,0:T(8,128)(2,1)S(1)}, bf16[32,2304]{1,0:T(8,128)(2,1)S(1)}, u32[]{:S(2)}, u32[]{:S(2)}) collective-permute-start(bf16[32,2304]{1,0:T(8,128)(2,1)S(1)} %get-tuple-element.70), channel_id=1, source_target_pairs={{0,16},{16,0},{32,48},{48,32},{64,80},{80,64},{96,112},{112,96},{1... | collective-permute-start | bytes 442376 | tf_op jit(solution)/shard_map/ppermute | solution.py:295
  44.3 0.0 collective-permute-start.11
  44.3 1.1 %shard_map.89 = (f32[2,32,1024]{2,1,0:T(8,128)S(1)}, f32[2,32,1024]{2,1,0:T(8,128)S(1)}) custom-call(f32[2,32,1024]{2,1,0:T(8,128)S(1)} %get-tuple-element.67.refs_0_, f32[2,32,1024]{2,1,0:T(8,128)S(1)} %get-tuple-element.62.refs_0_.refs_1_, f32[2,32,1024]{2,1,0:T(8,128)S(1)} %get-tuple-element.68.refs_2_, ...), custom_call_target="tpu_custom_call" | custom-call | flops 1048576 | bytes 4096 | tf_op jit(solution)/shard_map/pallas_call | solution.py:250
  45.4 0.0 collective-permute-done.10.got_ref
  45.4 0.5 %shard_map.90.sum_ref = f32[2,32,1024]{2,1,0:T(8,128)S(1)} custom-call(f32[2,32,1024]{2,1,0:T(8,128)S(1)} %get-tuple-element.69.part_ref, bf16[3,1024,1024]{2,1,0:T(8,128)(2,1)S(1)} %get-tuple-element.40.refs_1_.w_ref.refs_3_, f32[2,2,128]{2,1,0:T(2,128)S(1)} %get-tuple-element.44.rim_ref, bf16[32,2304]{1,0:T(8,128)(2,1)S(1)} %collective-permute-done.10.got_ref), custom_call_target="tpu_custom_call" | custom-call | flops 1048576 | bytes 4096 | tf_op jit(solution)/shard_map/pallas_call | solution.py:250
  46.0 3.2 %collective-permute-done.11.got_ref = bf16[32,2304]{1,0:T(8,128)(2,1)S(1)} collective-permute-done((bf16[32,2304]{1,0:T(8,128)(2,1)S(1)}, bf16[32,2304]{1,0:T(8,128)(2,1)S(1)}, u32[]{:S(2)}, u32[]{:S(2)}) %collective-permute-start.11) | collective-permute-done | bytes 147488 | tf_op jit(solution)/shard_map/ppermute | solution.py:294
  49.2 1.2 %shard_map.91 = f32[2,8,32,128]{3,2,1,0:T(8,128)} custom-call(f32[2,32,1024]{2,1,0:T(8,128)S(1)} %shard_map.90.sum_ref, f32[2,32,1024]{2,1,0:T(8,128)S(1)} %get-tuple-element.71.filt_ref, bf16[3,1024,1024]{2,1,0:T(8,128)(2,1)S(1)} %get-tuple-element.40.refs_1_.w_ref.refs_3_, f32[2,2,128]{2,1,0:T(2,128)S(1)} %get-tuple-element.44.rim_ref, ...), custom_call_target="tpu_custom_call" | custom-call | flops 1048576 | bytes 4096 | tf_op jit(solution)/shard_map/pallas_call | solution.py:250
Async XLA Ops:
  4.9 4.4 %collective-permute-start = (bf16[32,2304]{1,0:T(8,128)(2,1)S(1)}, bf16[32,2304]{1,0:T(8,128)(2,1)S(1)}, u32[]{:S(2)}, u32[]{:S(2)}) collective-permute-start(bf16[32,2304]{1,0:T(8,128)(2,1)S(1)} %get-tuple-element.45), channel_id=1, source_target_pairs={{0,16},{16,0},{32,48},{48,32},{64,80},{80,64},{96,112},{112,96},{1... | collective-permute-start | bytes 442376 | tf_op jit(solution)/shard_map/ppermute | solution.py:295
  8.3 4.6 %collective-permute-start.1 = (bf16[32,2304]{1,0:T(8,128)(2,1)S(1)}, bf16[32,2304]{1,0:T(8,128)(2,1)S(1)}, u32[]{:S(2)}, u32[]{:S(2)}) collective-permute-start(bf16[32,2304]{1,0:T(8,128)(2,1)S(1)} %get-tuple-element.46), channel_id=1, source_target_pairs={{0,240},{16,32},{32,16},{48,64},{64,48},{80,96},{96,80},{112,128},... | collective-permute-start | bytes 442376 | tf_op jit(solution)/shard_map/ppermute | solution.py:294
  13.8 3.7 %collective-permute-start.2 = (bf16[32,2304]{1,0:T(8,128)(2,1)S(1)}, bf16[32,2304]{1,0:T(8,128)(2,1)S(1)}, u32[]{:S(2)}, u32[]{:S(2)}) collective-permute-start(bf16[32,2304]{1,0:T(8,128)(2,1)S(1)} %get-tuple-element.50), channel_id=1, source_target_pairs={{0,16},{16,0},{32,48},{48,32},{64,80},{80,64},{96,112},{112,96},{1... | collective-permute-start | bytes 442376 | tf_op jit(solution)/shard_map/ppermute | solution.py:295
  16.4 4.9 %collective-permute-start.3 = (bf16[32,2304]{1,0:T(8,128)(2,1)S(1)}, bf16[32,2304]{1,0:T(8,128)(2,1)S(1)}, u32[]{:S(2)}, u32[]{:S(2)}) collective-permute-start(bf16[32,2304]{1,0:T(8,128)(2,1)S(1)} %get-tuple-element.51), channel_id=1, source_target_pairs={{0,240},{16,32},{32,16},{48,64},{64,48},{80,96},{96,80},{112,128},... | collective-permute-start | bytes 442376 | tf_op jit(solution)/shard_map/ppermute | solution.py:294
  22.2 2.2 %collective-permute-start.4 = (bf16[32,2304]{1,0:T(8,128)(2,1)S(1)}, bf16[32,2304]{1,0:T(8,128)(2,1)S(1)}, u32[]{:S(2)}, u32[]{:S(2)}) collective-permute-start(bf16[32,2304]{1,0:T(8,128)(2,1)S(1)} %get-tuple-element.55), channel_id=1, source_target_pairs={{0,16},{16,0},{32,48},{48,32},{64,80},{80,64},{96,112},{112,96},{1... | collective-permute-start | bytes 442376 | tf_op jit(solution)/shard_map/ppermute | solution.py:295
  23.3 4.9 %collective-permute-start.5 = (bf16[32,2304]{1,0:T(8,128)(2,1)S(1)}, bf16[32,2304]{1,0:T(8,128)(2,1)S(1)}, u32[]{:S(2)}, u32[]{:S(2)}) collective-permute-start(bf16[32,2304]{1,0:T(8,128)(2,1)S(1)} %get-tuple-element.56), channel_id=1, source_target_pairs={{0,240},{16,32},{32,16},{48,64},{64,48},{80,96},{96,80},{112,128},... | collective-permute-start | bytes 442376 | tf_op jit(solution)/shard_map/ppermute | solution.py:294
  29.2 2.2 %collective-permute-start.6 = (bf16[32,2304]{1,0:T(8,128)(2,1)S(1)}, bf16[32,2304]{1,0:T(8,128)(2,1)S(1)}, u32[]{:S(2)}, u32[]{:S(2)}) collective-permute-start(bf16[32,2304]{1,0:T(8,128)(2,1)S(1)} %get-tuple-element.60), channel_id=1, source_target_pairs={{0,16},{16,0},{32,48},{48,32},{64,80},{80,64},{96,112},{112,96},{1... | collective-permute-start | bytes 442376 | tf_op jit(solution)/shard_map/ppermute | solution.py:295
  30.3 4.9 %collective-permute-start.7 = (bf16[32,2304]{1,0:T(8,128)(2,1)S(1)}, bf16[32,2304]{1,0:T(8,128)(2,1)S(1)}, u32[]{:S(2)}, u32[]{:S(2)}) collective-permute-start(bf16[32,2304]{1,0:T(8,128)(2,1)S(1)} %get-tuple-element.61), channel_id=1, source_target_pairs={{0,240},{16,32},{32,16},{48,64},{64,48},{80,96},{96,80},{112,128},... | collective-permute-start | bytes 442376 | tf_op jit(solution)/shard_map/ppermute | solution.py:294
  36.1 2.4 %collective-permute-start.8 = (bf16[32,2304]{1,0:T(8,128)(2,1)S(1)}, bf16[32,2304]{1,0:T(8,128)(2,1)S(1)}, u32[]{:S(2)}, u32[]{:S(2)}) collective-permute-start(bf16[32,2304]{1,0:T(8,128)(2,1)S(1)} %get-tuple-element.65), channel_id=1, source_target_pairs={{0,16},{16,0},{32,48},{48,32},{64,80},{80,64},{96,112},{112,96},{1... | collective-permute-start | bytes 442376 | tf_op jit(solution)/shard_map/ppermute | solution.py:295
  37.4 4.9 %collective-permute-start.9 = (bf16[32,2304]{1,0:T(8,128)(2,1)S(1)}, bf16[32,2304]{1,0:T(8,128)(2,1)S(1)}, u32[]{:S(2)}, u32[]{:S(2)}) collective-permute-start(bf16[32,2304]{1,0:T(8,128)(2,1)S(1)} %get-tuple-element.66), channel_id=1, source_target_pairs={{0,240},{16,32},{32,16},{48,64},{64,48},{80,96},{96,80},{112,128},... | collective-permute-start | bytes 442376 | tf_op jit(solution)/shard_map/ppermute | solution.py:294
  43.2 2.2 %collective-permute-start.10 = (bf16[32,2304]{1,0:T(8,128)(2,1)S(1)}, bf16[32,2304]{1,0:T(8,128)(2,1)S(1)}, u32[]{:S(2)}, u32[]{:S(2)}) collective-permute-start(bf16[32,2304]{1,0:T(8,128)(2,1)S(1)} %get-tuple-element.70), channel_id=1, source_target_pairs={{0,16},{16,0},{32,48},{48,32},{64,80},{80,64},{96,112},{112,96},{1... | collective-permute-start | bytes 442376 | tf_op jit(solution)/shard_map/ppermute | solution.py:295
  44.3 4.9 %collective-permute-start.11 = (bf16[32,2304]{1,0:T(8,128)(2,1)S(1)}, bf16[32,2304]{1,0:T(8,128)(2,1)S(1)}, u32[]{:S(2)}, u32[]{:S(2)}) collective-permute-start(bf16[32,2304]{1,0:T(8,128)(2,1)S(1)} %get-tuple-element.72), channel_id=1, source_target_pairs={{0,240},{16,32},{32,16},{48,64},{64,48},{80,96},{96,80},{112,128},... | collective-permute-start | bytes 442376 | tf_op jit(solution)/shard_map/ppermute | solution.py:294

commit v3 on v2

--- a/solution.py
+++ b/solution.py
@@ -48,40 +48,55 @@
         yield outs, dot(x[:, ins], block, contract)
 
 
-def write_payload(x_ref, w_ref, rim_ref, side, out_ref):
+def edge_of(x_ref, rim_ref, side, layer):
     wide = x_ref.shape[2]
     cols = rim_ref.shape[2]
-    edge = slice(0, cols) if side == FAR else slice(wide - cols, wide)
-    which = side - 1
-    out_ref[:, 0:wide] = x_ref[1].astype(jnp.bfloat16)
-    rim = x_ref[0, :, edge] * rim_ref[which, 0:1, :]
-    rim += pltpu.roll(x_ref[1, :, edge] * rim_ref[which, 1:2, :], cols - 1, axis=1)
-    high = rim.astype(jnp.bfloat16)
-    out_ref[:, 2 * wide : 2 * wide + cols] = high
-    out_ref[:, 2 * wide + cols :] = (rim - high.astype(jnp.float32)).astype(jnp.bfloat16)
-    first = x_ref[0].astype(jnp.bfloat16)
+    at = slice(0, cols) if side == FAR else slice(wide - cols, wide)
+    value = x_ref[layer, :, at] * rim_ref[side - 1, layer : layer + 1, :]
+    high = value.astype(jnp.bfloat16).astype(jnp.float32)
+    return (high + pltpu.roll(value - high, cols - 1, axis=1)).astype(jnp.bfloat16)
+
+
+def write_terms(first, w_ref, side, cols, out_ref):
     for outs, term in products(first, w_ref, side, 0, cols):
-        out_ref[:, wide + outs.start : wide + outs.stop] = term.astype(jnp.bfloat16)
-
-
-def add_received(scale, got_ref, w_ref, rim_ref, side, from_ref, to_ref):
-    wide = to_ref.shape[2]
+        out_ref[:, outs] = term.astype(jnp.bfloat16)
+
+
+def write_payloads(x_ref, rim_ref, far_terms, mate_terms, rows_ref, terms_ref, mate_ref):
+    wide = x_ref.shape[2]
+    second = x_ref[1].astype(jnp.bfloat16)
+    rows_ref[:, 0:wide] = second
+    rows_ref[:, wide:] = edge_of(x_ref, rim_ref, FAR, 0)
+    terms_ref[:, 0:wide] = far_terms[...]
+    terms_ref[:, wide:] = edge_of(x_ref, rim_ref, FAR, 1)
+    half = mate_ref.shape[1] // 2
+    mate_ref[:, 0:wide] = second
+    mate_ref[:, wide:half] = edge_of(x_ref, rim_ref, MATE, 0)
+    mate_ref[:, half : half + wide] = mate_terms[...]
+    mate_ref[:, half + wide :] = edge_of(x_ref, rim_ref, MATE, 1)
+
+
+def edge_sum(edge, rim_ref, side, layer):
+    edge = edge.astype(jnp.float32)
+    return (edge + pltpu.roll(edge, 1, axis=1)) * rim_ref[side - 1, layer : layer + 1, :]
+
+
+def add_rows(scale, got, w_ref, rim_ref, side, base, to_ref):
+    for outs, term in products(got, w_ref, side, 1, rim_ref.shape[2]):
+        to_ref[:, outs] = base[:, outs] + scale * term
+
+
+def add_edge(scale, edge, rim_ref, side, layer, to_ref):
+    wide = to_ref.shape[1]
     cols = rim_ref.shape[2]
-    edge = slice(0, cols) if side == FAR else slice(wide - cols, wide)
-    which = side - 1
-    to_ref[1] = from_ref[1] + scale * got_ref[:, wide : 2 * wide].astype(jnp.float32)
-    for outs, term in products(got_ref[:, 0:wide], w_ref, side, 1, cols):
-        to_ref[0, :, outs] = from_ref[0, :, outs] + scale * term
-    rim = got_ref[:, 2 * wide : 2 * wide + cols].astype(jnp.float32)
-    rim += got_ref[:, 2 * wide + cols :].astype(jnp.float32)
-    to_ref[0, :, edge] += scale * (rim * rim_ref[which, 0:1, :])
-    to_ref[1, :, edge] += scale * (pltpu.roll(rim, 1, axis=1) * rim_ref[which, 1:2, :])
+    at = slice(0, cols) if side == FAR else slice(wide - cols, wide)
+    to_ref[:, at] += scale * edge_sum(edge, rim_ref, side, layer)
 
 
 def prepare(
     partner_hbm, states_hbm, onsite_hbm, hop_row_hbm, hop_up_hbm, coefs_hbm, coupling_hbm,
-    x_ref, w_ref, coef_ref, rim_ref, weight_ref, far_ref, mate_ref,
-    partner_ref, states_ref, small_ref, coefs_ref, blocks, total, sems, row_sems,
+    x_ref, w_ref, coef_ref, rim_ref, weight_ref, rows_ref, terms_ref, mate_ref,
+    partner_ref, states_ref, small_ref, coefs_ref, blocks, total, far_terms, mate_terms, sems, row_sems,
 ):
     rows, slots = partner_hbm.shape
     cols = onsite_hbm.shape[2]
@@ -179,8 +194,10 @@
             w_ref[side, place * cols : (place + 1) * cols, sigma * cols : (sigma + 1) * cols] = total[
                 place * spare + offset
             ].astype(jnp.bfloat16)
-    write_payload(x_ref, w_ref, rim_ref, FAR, far_ref)
-    write_payload(x_ref, w_ref, rim_ref, MATE, mate_ref)
+    first = x_ref[0].astype(jnp.bfloat16)
+    write_terms(first, w_ref, FAR, cols, far_terms)
+    write_terms(first, w_ref, MATE, cols, mate_terms)
+    write_payloads(x_ref, rim_ref, far_terms, mate_terms, rows_ref, terms_ref, mate_ref)
 
 
 def inner(order, *refs):
@@ -224,25 +241,49 @@
 
 
 def from_mate(scale, part_ref, w_ref, rim_ref, got_ref, sum_ref):
-    add_received(scale, got_ref, w_ref, rim_ref, MATE, part_ref, sum_ref)
-
-
-def outer(scale, sum_ref, w_ref, rim_ref, got_ref, x_ref, far_ref, mate_ref):
-    add_received(scale, got_ref, w_ref, rim_ref, FAR, sum_ref, x_ref)
-    write_payload(x_ref, w_ref, rim_ref, FAR, far_ref)
-    write_payload(x_ref, w_ref, rim_ref, MATE, mate_ref)
-
-
-def finish(scale, degree, sum_ref, filt_ref, w_ref, rim_ref, weight_ref, got_ref, out_ref, x_ref):
+    wide = sum_ref.shape[2]
+    half = got_ref.shape[1] // 2
+    add_rows(scale, got_ref[:, 0:wide], w_ref, rim_ref, MATE, part_ref[0], sum_ref.at[0])
+    add_edge(scale, got_ref[:, wide:half], rim_ref, MATE, 0, sum_ref.at[0])
+    sum_ref[1] = part_ref[1] + scale * got_ref[:, half : half + wide].astype(jnp.float32)
+    add_edge(scale, got_ref[:, half + wide :], rim_ref, MATE, 1, sum_ref.at[1])
+
+
+def outer_first(scale, last, sum_ref, w_ref, rim_ref, rows_ref, first_ref, *terms):
+    wide = sum_ref.shape[2]
+    cols = rim_ref.shape[2]
+    add_rows(scale, rows_ref[:, 0:wide], w_ref, rim_ref, FAR, sum_ref[0], first_ref)
+    add_edge(scale, rows_ref[:, wide:], rim_ref, FAR, 0, first_ref)
+    if not last:
+        first = first_ref[...].astype(jnp.bfloat16)
+        write_terms(first, w_ref, FAR, cols, terms[0])
+        write_terms(first, w_ref, MATE, cols, terms[1])
+
+
+def add_terms(scale, sum_ref, rim_ref, terms_ref, second_ref):
+    wide = sum_ref.shape[2]
+    second_ref[...] = sum_ref[1] + scale * terms_ref[:, 0:wide].astype(jnp.float32)
+    add_edge(scale, terms_ref[:, wide:], rim_ref, FAR, 1, second_ref)
+
+
+def outer_second(
+    scale, sum_ref, first_ref, far_ref, near_ref, rim_ref, got_ref, x_ref, rows_ref, terms_ref, mate_ref
+):
+    x_ref[0] = first_ref[...]
+    add_terms(scale, sum_ref, rim_ref, got_ref, x_ref.at[1])
+    write_payloads(x_ref, rim_ref, far_ref, near_ref, rows_ref, terms_ref, mate_ref)
+
+
+def finish(scale, degree, sum_ref, first_ref, filt_ref, rim_ref, weight_ref, got_ref, out_ref, second_ref):
     cols = rim_ref.shape[2]
     rows = out_ref.shape[1]
-    add_received(scale, got_ref, w_ref, rim_ref, FAR, sum_ref, x_ref)
+    add_terms(scale, sum_ref, rim_ref, got_ref, second_ref)
     flip = lax.rem(lax.axis_index("tile"), 2)
-    for layer in range(2):
+    for layer, x_ref in enumerate((first_ref, second_ref)):
         for place in range(rows):
             here = slice(place * cols, (place + 1) * cols)
             out_ref[layer, place + flip * (rows - 1 - 2 * place)] = (
-                filt_ref[layer, :, here] + weight_ref[degree : degree + 1, :] * x_ref[layer, :, here]
+                filt_ref[layer, :, here] + weight_ref[degree : degree + 1, :] * x_ref[:, here]
             )
 
 
@@ -268,11 +309,14 @@
     mate_pairs = [(i, i ^ 1) for i in range(size)]
 
     field = held((2, count, wide), jnp.float32)
-    payload = held((count, 2 * wide + 2 * cols), jnp.bfloat16)
-    x, w, coef, rim, weight, far, mate = call(
+    layer = held((count, wide), jnp.float32)
+    terms = held((count, wide), jnp.bfloat16)
+    half = held((count, wide + cols), jnp.bfloat16)
+    whole = held((count, 2 * (wide + cols)), jnp.bfloat16)
+    x, w, coef, rim, weight, far_rows, far_terms, mate = call(
         prepare,
         [field, held((3, wide, wide), jnp.bfloat16), held((2, 5, rows, cols), jnp.float32),
-         held((2, 2, cols), jnp.float32), held((degree + 1, cols), jnp.float32), payload, payload],
+         held((2, 2, cols), jnp.float32), held((degree + 1, cols), jnp.float32), half, half, whole],
         [outside(v) for v in (partner, states, onsite, hop_row, hop_up, coefs, coupling)],
         scratch=[
             pltpu.SMEM((rows, slots), jnp.int32),
@@ -281,6 +325,8 @@
             pltpu.SMEM((degree + 1,), jnp.float32),
             pltpu.VMEM((rows, slots, cols, cols), jnp.bfloat16),
             pltpu.VMEM((rows * (2 * REACH + 2), cols, cols), jnp.float32),
+            pltpu.VMEM((count, wide), jnp.bfloat16),
+            pltpu.VMEM((count, wide), jnp.bfloat16),
             pltpu.SemaphoreType.DMA((6,)),
             pltpu.SemaphoreType.DMA((rows,)),
         ],
@@ -291,7 +337,8 @@
     prev = filt = None
     for order in range(degree):
         scale = 1.0 / 12.0 if order == 0 else 2.0 / 12.0
-        got_far = lax.ppermute(far, "tile", far_pairs)
+        got_rows = lax.ppermute(far_rows, "tile", far_pairs)
+        got_terms = lax.ppermute(far_terms, "tile", far_pairs)
         got_mate = lax.ppermute(mate, "tile", mate_pairs)
         past = [] if order == 0 else [near(prev), near(filt)]
         part, filt = call(
@@ -300,20 +347,27 @@
         (part,) = call(
             functools.partial(from_mate, scale), [field], [near(part), w, rim, near(got_mate)]
         )
+        part = near(part)
         prev = x
-        if order < degree - 1:
-            x, far, mate = call(
-                functools.partial(outer, scale),
-                [field, payload, payload],
-                [near(part), w, rim, near(got_far)],
+        last = order == degree - 1
+        first, *made = call(
+            functools.partial(outer_first, scale, last),
+            [layer] if last else [layer, terms, terms],
+            [part, w, rim, near(got_rows)],
+        )
+        if not last:
+            x, far_rows, far_terms, mate = call(
+                functools.partial(outer_second, scale),
+                [field, half, half, whole],
+                [part, near(first), near(made[0]), near(made[1]), rim, near(got_terms)],
             )
             x = near(x)
         else:
             (out,) = call(
                 functools.partial(finish, scale, degree),
                 [jax.ShapeDtypeStruct(states.shape, jnp.float32)],
-                [near(part), near(filt), w, rim, weight, near(got_far)],
-                scratch=[pltpu.VMEM((2, count, wide), jnp.float32)],
+                [part, near(first), near(filt), rim, weight, near(got_terms)],
+                scratch=[pltpu.VMEM((count, wide), jnp.float32)],
             )
     return out
 

time: 50.5 us -> 50.4 us (level)
  waiting for transfers between devices: 19 us -> 3.95 us
  starting transfers between devices: 10.5 us -> 24.5 us
  Pallas kernels: 20.8 us -> 21.6 us
    ppermute x6 -> x12, waiting for transfers between devices: 19 us -> 3.93 us  [the longest x6 3.8 us: body(): got_rows = lax.ppermute(far_rows, 'tile', far_pairs)]
    ppermute x6 -> x12, starting transfers between devices: 0.02 us -> 10.5 us  [the longest x6 10.5 us: body(): got_terms = lax.ppermute(far_terms, 'tile', far_pairs)]
    ppermute x6, starting transfers between devices: 10.4 us -> 14 us  [body(): got_mate = lax.ppermute(mate, 'tile', mate_pairs)]
    pallas_call x19 -> x25, Pallas kernels: 20.8 us -> 21.6 us  [call(): pl.pallas_call(kernel, out_shape=outs, in_specs=specs or [IN_VMEM] * len(...]
  transfers between devices with their start and end apart: 12 -> 18, of which waited for: 6 -> 7; matrix products, arithmetic and copies ran while one was open for 0% -> 0% of each run, Pallas kernels for 19% -> 30%
where the time goes in v3:
time: 50.4 us; the launch traced here: 50.2 us
  starting transfers between devices  24.5 us (49%)
  Pallas kernels  21.6 us (43%)
  waiting for transfers between devices  3.95 us (8%)
    pallas_call x25, Pallas kernels, call(): pl.pallas_call(kernel, out_shape=outs, in_specs=specs or [IN_VMEM] * len(...  21.6 us
    ppermute x6, starting transfers between devices, body(): got_mate = lax.ppermute(mate, 'tile', mate_pairs)  14 us
    ppermute x6, starting transfers between devices, body(): got_terms = lax.ppermute(far_terms, 'tile', far_pairs)  10.5 us
    ppermute x6, waiting for transfers between devices, body(): got_rows = lax.ppermute(far_rows, 'tile', far_pairs)  3.8 us
  transfers between devices with their start and end apart: 18, of which 7 were waited for; matrix products, arithmetic and copies ran while one was open for 0% of the time, Pallas kernels for 30%

profile of v3, /device:TPU:1, one launch (start us, length us, event | category | flops | bytes accessed | tf_op | source)
XLA Modules:
  0.0 50.2 jit_solution(14240279454942208197)
XLA Ops:
  0.0 4.9 %shard_map.73 = (f32[2,32,1024]{2,1,0:T(8,128)S(1)}, bf16[3,1024,1024]{2,1,0:T(8,128)(2,1)S(1)}, f32[2,5,8,128]{3,2,1,0:T(8,128)S(1)}, f32[2,2,128]{2,1,0:T(2,12...) custom-call(s32[8,16]{1,0:T(8,128)} %partner_hbm.1, ...), custom_call_target="tpu_custom_call" | custom-call | flops 1048576 | bytes 4096 | tf_op jit(solution)/shard_map/pallas_call | solution.py:291
  4.9 3.3 %collective-permute-start = (bf16[32,2304]{1,0:T(8,128)(2,1)S(1)}, bf16[32,2304]{1,0:T(8,128)(2,1)S(1)}, u32[]{:S(2)}, u32[]{:S(2)}) collective-permute-start(bf16[32,2304]{1,0:T(8,128)(2,1)S(1)} %get-tuple-element.66), channel_id=1, source_target_pairs={{0,16},{16,0},{32,48},{48,32},{64,80},{80,64},{96,112},{112,96},{1... | collective-permute-start | bytes 442376 | tf_op jit(solution)/shard_map/ppermute | solution.py:342
  8.3 1.7 %collective-permute-start.2 = (bf16[32,1152]{1,0:T(8,128)(2,1)S(1)}, bf16[32,1152]{1,0:T(8,128)(2,1)S(1)}, u32[]{:S(2)}, u32[]{:S(2)}) collective-permute-start(bf16[32,1152]{1,0:T(8,128)(2,1)S(1)} %get-tuple-element.71), channel_id=1, source_target_pairs={{0,240},{16,32},{32,16},{48,64},{64,48},{80,96},{96,80},{112,128},... | collective-permute-start | bytes 221192 | tf_op jit(solution)/shard_map/ppermute | solution.py:341
  10.0 1.1 %shard_map.74 = (f32[2,32,1024]{2,1,0:T(8,128)S(1)}, f32[2,32,1024]{2,1,0:T(8,128)S(1)}) custom-call(f32[2,32,1024]{2,1,0:T(8,128)S(1)} %get-tuple-element.60.refs_0_.refs_1_, bf16[3,1024,1024]{2,1,0:T(8,128)(2,1)S(1)} %get-tuple-element.61.refs_1_.w_ref.refs_3_, f32[2,5,8,128]{3,2,1,0:T(8,128)S(1)} %get-tuple-element.62.refs_2_.refs_4_, ...), custom_call_target="tpu_custom_call" | custom-call | flops 1048576 | bytes 4096 | tf_op jit(solution)/shard_map/pallas_call | solution.py:291
  11.1 0.0 collective-permute-done.got_ref
  11.1 0.5 shard_map.75.sum_ref
  11.6 0.4 collective-permute-done.1.rows_ref
  12.1 1.0 %shard_map.76 = (f32[32,1024]{1,0:T(8,128)S(1)}, bf16[32,1024]{1,0:T(8,128)(2,1)S(1)}, bf16[32,1024]{1,0:T(8,128)(2,1)S(1)}) custom-call(f32[2,32,1024]{2,1,0:T(8,128)S(1)} %shard_map.75.sum_ref, bf16[3,1024,1024]{2,1,0:T(8,128)(2,1)S(1)} %get-tuple-element.61.refs_1_.w_ref.refs_3_, f32[2,2,128]{2,1,0:T(2,128)S(1)} %get-tuple-element.65.rim_ref, ...), custom_call_target="tpu_custom_call" | custom-call | flops 1048576 | bytes 4096 | tf_op jit(solution)/shard_map/pallas_call | solution.py:291
  13.0 0.2 shard_map.77
  13.2 4.5 %collective-permute-start.3 = (bf16[32,2304]{1,0:T(8,128)(2,1)S(1)}, bf16[32,2304]{1,0:T(8,128)(2,1)S(1)}, u32[]{:S(2)}, u32[]{:S(2)}) collective-permute-start(bf16[32,2304]{1,0:T(8,128)(2,1)S(1)} %get-tuple-element.75), channel_id=1, source_target_pairs={{0,16},{16,0},{32,48},{48,32},{64,80},{80,64},{96,112},{112,96},{1... | collective-permute-start | bytes 442376 | tf_op jit(solution)/shard_map/ppermute | solution.py:342
  17.7 0.0 collective-permute-start.4
  17.7 1.7 %collective-permute-start.5 = (bf16[32,1152]{1,0:T(8,128)(2,1)S(1)}, bf16[32,1152]{1,0:T(8,128)(2,1)S(1)}, u32[]{:S(2)}, u32[]{:S(2)}) collective-permute-start(bf16[32,1152]{1,0:T(8,128)(2,1)S(1)} %get-tuple-element.80), channel_id=1, source_target_pairs={{0,240},{16,32},{32,16},{48,64},{64,48},{80,96},{96,80},{112,128},... | collective-permute-start | bytes 221192 | tf_op jit(solution)/shard_map/ppermute | solution.py:341
  19.4 1.1 %shard_map.78 = (f32[2,32,1024]{2,1,0:T(8,128)S(1)}, f32[2,32,1024]{2,1,0:T(8,128)S(1)}) custom-call(f32[2,32,1024]{2,1,0:T(8,128)S(1)} %get-tuple-element.72.refs_0_.refs_1_, f32[2,32,1024]{2,1,0:T(8,128)S(1)} %get-tuple-element.60.refs_0_.refs_1_, f32[2,32,1024]{2,1,0:T(8,128)S(1)} %get-tuple-element.73.refs_2_, ...), custom_call_target="tpu_custom_call" | custom-call | flops 1048576 | bytes 4096 | tf_op jit(solution)/shard_map/pallas_call | solution.py:291
  20.6 0.5 shard_map.79.sum_ref
  21.1 0.7 %collective-permute-done.4.rows_ref = bf16[32,1152]{1,0:T(8,128)(2,1)S(1)} collective-permute-done((bf16[32,1152]{1,0:T(8,128)(2,1)S(1)}, bf16[32,1152]{1,0:T(8,128)(2,1)S(1)}, u32[]{:S(2)}, u32[]{:S(2)}) %collective-permute-start.4) | collective-permute-done | bytes 73760 | tf_op jit(solution)/shard_map/ppermute | solution.py:340
  21.8 1.0 %shard_map.80 = (f32[32,1024]{1,0:T(8,128)S(1)}, bf16[32,1024]{1,0:T(8,128)(2,1)S(1)}, bf16[32,1024]{1,0:T(8,128)(2,1)S(1)}) custom-call(f32[2,32,1024]{2,1,0:T(8,128)S(1)} %shard_map.79.sum_ref, bf16[3,1024,1024]{2,1,0:T(8,128)(2,1)S(1)} %get-tuple-element.61.refs_1_.w_ref.refs_3_, f32[2,2,128]{2,1,0:T(2,128)S(1)} %get-tuple-element.65.rim_ref, ...), custom_call_target="tpu_custom_call" | custom-call | flops 1048576 | bytes 4096 | tf_op jit(solution)/shard_map/pallas_call | solution.py:291
  22.7 0.0 collective-permute-done.5.got_ref
  22.7 0.2 shard_map.81
  22.9 1.1 %collective-permute-start.6 = (bf16[32,2304]{1,0:T(8,128)(2,1)S(1)}, bf16[32,2304]{1,0:T(8,128)(2,1)S(1)}, u32[]{:S(2)}, u32[]{:S(2)}) collective-permute-start(bf16[32,2304]{1,0:T(8,128)(2,1)S(1)} %get-tuple-element.84), channel_id=1, source_target_pairs={{0,16},{16,0},{32,48},{48,32},{64,80},{80,64},{96,112},{112,96},{1... | collective-permute-start | bytes 442376 | tf_op jit(solution)/shard_map/ppermute | solution.py:342
  24.0 1.7 %collective-permute-start.8 = (bf16[32,1152]{1,0:T(8,128)(2,1)S(1)}, bf16[32,1152]{1,0:T(8,128)(2,1)S(1)}, u32[]{:S(2)}, u32[]{:S(2)}) collective-permute-start(bf16[32,1152]{1,0:T(8,128)(2,1)S(1)} %get-tuple-element.89), channel_id=1, source_target_pairs={{0,240},{16,32},{32,16},{48,64},{64,48},{80,96},{96,80},{112,128},... | collective-permute-start | bytes 221192 | tf_op jit(solution)/shard_map/ppermute | solution.py:341
  25.7 1.1 %shard_map.82 = (f32[2,32,1024]{2,1,0:T(8,128)S(1)}, f32[2,32,1024]{2,1,0:T(8,128)S(1)}) custom-call(f32[2,32,1024]{2,1,0:T(8,128)S(1)} %get-tuple-element.81.refs_0_.refs_1_, f32[2,32,1024]{2,1,0:T(8,128)S(1)} %get-tuple-element.72.refs_0_.refs_1_, f32[2,32,1024]{2,1,0:T(8,128)S(1)} %get-tuple-element.82.refs_2_, ...), custom_call_target="tpu_custom_call" | custom-call | flops 1048576 | bytes 4096 | tf_op jit(solution)/shard_map/pallas_call | solution.py:291
  26.9 0.5 shard_map.83.sum_ref
  27.4 0.7 %collective-permute-done.7.rows_ref = bf16[32,1152]{1,0:T(8,128)(2,1)S(1)} collective-permute-done((bf16[32,1152]{1,0:T(8,128)(2,1)S(1)}, bf16[32,1152]{1,0:T(8,128)(2,1)S(1)}, u32[]{:S(2)}, u32[]{:S(2)}) %collective-permute-start.7) | collective-permute-done | bytes 73760 | tf_op jit(solution)/shard_map/ppermute | solution.py:340
  28.0 1.0 %shard_map.84 = (f32[32,1024]{1,0:T(8,128)S(1)}, bf16[32,1024]{1,0:T(8,128)(2,1)S(1)}, bf16[32,1024]{1,0:T(8,128)(2,1)S(1)}) custom-call(f32[2,32,1024]{2,1,0:T(8,128)S(1)} %shard_map.83.sum_ref, bf16[3,1024,1024]{2,1,0:T(8,128)(2,1)S(1)} %get-tuple-element.61.refs_1_.w_ref.refs_3_, f32[2,2,128]{2,1,0:T(2,128)S(1)} %get-tuple-element.65.rim_ref, ...), custom_call_target="tpu_custom_call" | custom-call | flops 1048576 | bytes 4096 | tf_op jit(solution)/shard_map/pallas_call | solution.py:291
  29.0 0.2 shard_map.85
  29.2 2.0 %collective-permute-start.9 = (bf16[32,2304]{1,0:T(8,128)(2,1)S(1)}, bf16[32,2304]{1,0:T(8,128)(2,1)S(1)}, u32[]{:S(2)}, u32[]{:S(2)}) collective-permute-start(bf16[32,2304]{1,0:T(8,128)(2,1)S(1)} %get-tuple-element.93), channel_id=1, source_target_pairs={{0,16},{16,0},{32,48},{48,32},{64,80},{80,64},{96,112},{112,96},{1... | collective-permute-start | bytes 442376 | tf_op jit(solution)/shard_map/ppermute | solution.py:342
  31.2 1.7 %collective-permute-start.11 = (bf16[32,1152]{1,0:T(8,128)(2,1)S(1)}, bf16[32,1152]{1,0:T(8,128)(2,1)S(1)}, u32[]{:S(2)}, u32[]{:S(2)}) collective-permute-start(bf16[32,1152]{1,0:T(8,128)(2,1)S(1)} %get-tuple-element.98), channel_id=1, source_target_pairs={{0,240},{16,32},{32,16},{48,64},{64,48},{80,96},{96,80},{112,128},... | collective-permute-start | bytes 221192 | tf_op jit(solution)/shard_map/ppermute | solution.py:341
  33.0 1.1 %shard_map.86 = (f32[2,32,1024]{2,1,0:T(8,128)S(1)}, f32[2,32,1024]{2,1,0:T(8,128)S(1)}) custom-call(f32[2,32,1024]{2,1,0:T(8,128)S(1)} %get-tuple-element.90.refs_0_.refs_1_, f32[2,32,1024]{2,1,0:T(8,128)S(1)} %get-tuple-element.81.refs_0_.refs_1_, f32[2,32,1024]{2,1,0:T(8,128)S(1)} %get-tuple-element.91.refs_2_, ...), custom_call_target="tpu_custom_call" | custom-call | flops 1048576 | bytes 4096 | tf_op jit(solution)/shard_map/pallas_call | solution.py:291
  34.1 0.0 collective-permute-done.9.got_ref
  34.1 0.5 shard_map.87.sum_ref
  34.6 0.7 %collective-permute-done.10.rows_ref = bf16[32,1152]{1,0:T(8,128)(2,1)S(1)} collective-permute-done((bf16[32,1152]{1,0:T(8,128)(2,1)S(1)}, bf16[32,1152]{1,0:T(8,128)(2,1)S(1)}, u32[]{:S(2)}, u32[]{:S(2)}) %collective-permute-start.10) | collective-permute-done | bytes 73760 | tf_op jit(solution)/shard_map/ppermute | solution.py:340
  35.3 1.0 %shard_map.88 = (f32[32,1024]{1,0:T(8,128)S(1)}, bf16[32,1024]{1,0:T(8,128)(2,1)S(1)}, bf16[32,1024]{1,0:T(8,128)(2,1)S(1)}) custom-call(f32[2,32,1024]{2,1,0:T(8,128)S(1)} %shard_map.87.sum_ref, bf16[3,1024,1024]{2,1,0:T(8,128)(2,1)S(1)} %get-tuple-element.61.refs_1_.w_ref.refs_3_, f32[2,2,128]{2,1,0:T(2,128)S(1)} %get-tuple-element.65.rim_ref, ...), custom_call_target="tpu_custom_call" | custom-call | flops 1048576 | bytes 4096 | tf_op jit(solution)/shard_map/pallas_call | solution.py:291
  36.3 0.2 shard_map.89
  36.5 1.1 %collective-permute-start.12 = (bf16[32,2304]{1,0:T(8,128)(2,1)S(1)}, bf16[32,2304]{1,0:T(8,128)(2,1)S(1)}, u32[]{:S(2)}, u32[]{:S(2)}) collective-permute-start(bf16[32,2304]{1,0:T(8,128)(2,1)S(1)} %get-tuple-element.102), channel_id=1, source_target_pairs={{0,16},{16,0},{32,48},{48,32},{64,80},{80,64},{96,112},{112,96},{1... | collective-permute-start | bytes 442376 | tf_op jit(solution)/shard_map/ppermute | solution.py:342
  37.5 1.7 %collective-permute-start.14 = (bf16[32,1152]{1,0:T(8,128)(2,1)S(1)}, bf16[32,1152]{1,0:T(8,128)(2,1)S(1)}, u32[]{:S(2)}, u32[]{:S(2)}) collective-permute-start(bf16[32,1152]{1,0:T(8,128)(2,1)S(1)} %get-tuple-element.107), channel_id=1, source_target_pairs={{0,240},{16,32},{32,16},{48,64},{64,48},{80,96},{96,80},{112,128},... | collective-permute-start | bytes 221192 | tf_op jit(solution)/shard_map/ppermute | solution.py:341
  39.3 1.1 %shard_map.90 = (f32[2,32,1024]{2,1,0:T(8,128)S(1)}, f32[2,32,1024]{2,1,0:T(8,128)S(1)}) custom-call(f32[2,32,1024]{2,1,0:T(8,128)S(1)} %get-tuple-element.99.refs_0_.refs_1_, f32[2,32,1024]{2,1,0:T(8,128)S(1)} %get-tuple-element.90.refs_0_.refs_1_, f32[2,32,1024]{2,1,0:T(8,128)S(1)} %get-tuple-element.100.refs_2_, ...), custom_call_target="tpu_custom_call" | custom-call | flops 1048576 | bytes 4096 | tf_op jit(solution)/shard_map/pallas_call | solution.py:291
  40.4 0.5 shard_map.91.sum_ref
  40.9 0.7 %collective-permute-done.13.rows_ref = bf16[32,1152]{1,0:T(8,128)(2,1)S(1)} collective-permute-done((bf16[32,1152]{1,0:T(8,128)(2,1)S(1)}, bf16[32,1152]{1,0:T(8,128)(2,1)S(1)}, u32[]{:S(2)}, u32[]{:S(2)}) %collective-permute-start.13) | collective-permute-done | bytes 73760 | tf_op jit(solution)/shard_map/ppermute | solution.py:340
  41.6 1.0 %shard_map.92 = (f32[32,1024]{1,0:T(8,128)S(1)}, bf16[32,1024]{1,0:T(8,128)(2,1)S(1)}, bf16[32,1024]{1,0:T(8,128)(2,1)S(1)}) custom-call(f32[2,32,1024]{2,1,0:T(8,128)S(1)} %shard_map.91.sum_ref, bf16[3,1024,1024]{2,1,0:T(8,128)(2,1)S(1)} %get-tuple-element.61.refs_1_.w_ref.refs_3_, f32[2,2,128]{2,1,0:T(2,128)S(1)} %get-tuple-element.65.rim_ref, ...), custom_call_target="tpu_custom_call" | custom-call | flops 1048576 | bytes 4096 | tf_op jit(solution)/shard_map/pallas_call | solution.py:291
  42.6 0.2 shard_map.93
  42.7 2.0 %collective-permute-start.15 = (bf16[32,2304]{1,0:T(8,128)(2,1)S(1)}, bf16[32,2304]{1,0:T(8,128)(2,1)S(1)}, u32[]{:S(2)}, u32[]{:S(2)}) collective-permute-start(bf16[32,2304]{1,0:T(8,128)(2,1)S(1)} %get-tuple-element.111), channel_id=1, source_target_pairs={{0,16},{16,0},{32,48},{48,32},{64,80},{80,64},{96,112},{112,96},{1... | collective-permute-start | bytes 442376 | tf_op jit(solution)/shard_map/ppermute | solution.py:342
  44.8 1.7 %collective-permute-start.17 = (bf16[32,1152]{1,0:T(8,128)(2,1)S(1)}, bf16[32,1152]{1,0:T(8,128)(2,1)S(1)}, u32[]{:S(2)}, u32[]{:S(2)}) collective-permute-start(bf16[32,1152]{1,0:T(8,128)(2,1)S(1)} %get-tuple-element.114), channel_id=1, source_target_pairs={{0,240},{16,32},{32,16},{48,64},{64,48},{80,96},{96,80},{112,128},... | collective-permute-start | bytes 221192 | tf_op jit(solution)/shard_map/ppermute | solution.py:341
  46.5 1.1 %shard_map.94 = (f32[2,32,1024]{2,1,0:T(8,128)S(1)}, f32[2,32,1024]{2,1,0:T(8,128)S(1)}) custom-call(f32[2,32,1024]{2,1,0:T(8,128)S(1)} %get-tuple-element.108.refs_0_, f32[2,32,1024]{2,1,0:T(8,128)S(1)} %get-tuple-element.99.refs_0_.refs_1_, f32[2,32,1024]{2,1,0:T(8,128)S(1)} %get-tuple-element.109.refs_2_, ...), custom_call_target="tpu_custom_call" | custom-call | flops 1048576 | bytes 4096 | tf_op jit(solution)/shard_map/pallas_call | solution.py:291
  47.7 0.5 shard_map.95.sum_ref
  48.2 0.7 %collective-permute-done.16.rows_ref = bf16[32,1152]{1,0:T(8,128)(2,1)S(1)} collective-permute-done((bf16[32,1152]{1,0:T(8,128)(2,1)S(1)}, bf16[32,1152]{1,0:T(8,128)(2,1)S(1)}, u32[]{:S(2)}, u32[]{:S(2)}) %collective-permute-start.16) | collective-permute-done | bytes 73760 | tf_op jit(solution)/shard_map/ppermute | solution.py:340
  48.8 0.5 shard_map.96.first_ref
  49.3 0.1 collective-permute-done.17.got_ref
  49.5 0.8 %shard_map.97 = f32[2,8,32,128]{3,2,1,0:T(8,128)} custom-call(f32[2,32,1024]{2,1,0:T(8,128)S(1)} %shard_map.95.sum_ref, f32[32,1024]{1,0:T(8,128)S(1)} %shard_map.96.first_ref, f32[2,32,1024]{2,1,0:T(8,128)S(1)} %get-tuple-element.113.filt_ref, f32[2,2,128]{2,1,0:T(2,128)S(1)} %get-tuple-element.65.rim_ref, ...), custom_call_target="tpu_custom_call" | custom-call | flops 1048576 | bytes 4096 | tf_op jit(solution)/shard_map/pallas_call | solution.py:291
  (13 shorter events, 0.0 us)
Async XLA Ops:
  4.9 6.2 %collective-permute-start = (bf16[32,2304]{1,0:T(8,128)(2,1)S(1)}, bf16[32,2304]{1,0:T(8,128)(2,1)S(1)}, u32[]{:S(2)}, u32[]{:S(2)}) collective-permute-start(bf16[32,2304]{1,0:T(8,128)(2,1)S(1)} %get-tuple-element.66), channel_id=1, source_target_pairs={{0,16},{16,0},{32,48},{48,32},{64,80},{80,64},{96,112},{112,96},{1... | collective-permute-start | bytes 442376 | tf_op jit(solution)/shard_map/ppermute | solution.py:342
  8.3 3.8 %collective-permute-start.1 = (bf16[32,1152]{1,0:T(8,128)(2,1)S(1)}, bf16[32,1152]{1,0:T(8,128)(2,1)S(1)}, u32[]{:S(2)}, u32[]{:S(2)}) collective-permute-start(bf16[32,1152]{1,0:T(8,128)(2,1)S(1)} %get-tuple-element.67), channel_id=1, source_target_pairs={{0,240},{16,32},{32,16},{48,64},{64,48},{80,96},{96,80},{112,128},... | collective-permute-start | bytes 221192 | tf_op jit(solution)/shard_map/ppermute | solution.py:340
  8.3 4.7 %collective-permute-start.2 = (bf16[32,1152]{1,0:T(8,128)(2,1)S(1)}, bf16[32,1152]{1,0:T(8,128)(2,1)S(1)}, u32[]{:S(2)}, u32[]{:S(2)}) collective-permute-start(bf16[32,1152]{1,0:T(8,128)(2,1)S(1)} %get-tuple-element.71), channel_id=1, source_target_pairs={{0,240},{16,32},{32,16},{48,64},{64,48},{80,96},{96,80},{112,128},... | collective-permute-start | bytes 221192 | tf_op jit(solution)/shard_map/ppermute | solution.py:341
  13.2 7.4 %collective-permute-start.3 = (bf16[32,2304]{1,0:T(8,128)(2,1)S(1)}, bf16[32,2304]{1,0:T(8,128)(2,1)S(1)}, u32[]{:S(2)}, u32[]{:S(2)}) collective-permute-start(bf16[32,2304]{1,0:T(8,128)(2,1)S(1)} %get-tuple-element.75), channel_id=1, source_target_pairs={{0,16},{16,0},{32,48},{48,32},{64,80},{80,64},{96,112},{112,96},{1... | collective-permute-start | bytes 442376 | tf_op jit(solution)/shard_map/ppermute | solution.py:342
  17.7 4.1 %collective-permute-start.4 = (bf16[32,1152]{1,0:T(8,128)(2,1)S(1)}, bf16[32,1152]{1,0:T(8,128)(2,1)S(1)}, u32[]{:S(2)}, u32[]{:S(2)}) collective-permute-start(bf16[32,1152]{1,0:T(8,128)(2,1)S(1)} %get-tuple-element.76), channel_id=1, source_target_pairs={{0,240},{16,32},{32,16},{48,64},{64,48},{80,96},{96,80},{112,128},... | collective-permute-start | bytes 221192 | tf_op jit(solution)/shard_map/ppermute | solution.py:340
  17.7 5.0 %collective-permute-start.5 = (bf16[32,1152]{1,0:T(8,128)(2,1)S(1)}, bf16[32,1152]{1,0:T(8,128)(2,1)S(1)}, u32[]{:S(2)}, u32[]{:S(2)}) collective-permute-start(bf16[32,1152]{1,0:T(8,128)(2,1)S(1)} %get-tuple-element.80), channel_id=1, source_target_pairs={{0,240},{16,32},{32,16},{48,64},{64,48},{80,96},{96,80},{112,128},... | collective-permute-start | bytes 221192 | tf_op jit(solution)/shard_map/ppermute | solution.py:341
  22.9 3.9 %collective-permute-start.6 = (bf16[32,2304]{1,0:T(8,128)(2,1)S(1)}, bf16[32,2304]{1,0:T(8,128)(2,1)S(1)}, u32[]{:S(2)}, u32[]{:S(2)}) collective-permute-start(bf16[32,2304]{1,0:T(8,128)(2,1)S(1)} %get-tuple-element.84), channel_id=1, source_target_pairs={{0,16},{16,0},{32,48},{48,32},{64,80},{80,64},{96,112},{112,96},{1... | collective-permute-start | bytes 442376 | tf_op jit(solution)/shard_map/ppermute | solution.py:342
  24.0 4.1 %collective-permute-start.7 = (bf16[32,1152]{1,0:T(8,128)(2,1)S(1)}, bf16[32,1152]{1,0:T(8,128)(2,1)S(1)}, u32[]{:S(2)}, u32[]{:S(2)}) collective-permute-start(bf16[32,1152]{1,0:T(8,128)(2,1)S(1)} %get-tuple-element.85), channel_id=1, source_target_pairs={{0,240},{16,32},{32,16},{48,64},{64,48},{80,96},{96,80},{112,128},... | collective-permute-start | bytes 221192 | tf_op jit(solution)/shard_map/ppermute | solution.py:340
  24.0 5.0 %collective-permute-start.8 = (bf16[32,1152]{1,0:T(8,128)(2,1)S(1)}, bf16[32,1152]{1,0:T(8,128)(2,1)S(1)}, u32[]{:S(2)}, u32[]{:S(2)}) collective-permute-start(bf16[32,1152]{1,0:T(8,128)(2,1)S(1)} %get-tuple-element.89), channel_id=1, source_target_pairs={{0,240},{16,32},{32,16},{48,64},{64,48},{80,96},{96,80},{112,128},... | collective-permute-start | bytes 221192 | tf_op jit(solution)/shard_map/ppermute | solution.py:341
  29.2 4.9 %collective-permute-start.9 = (bf16[32,2304]{1,0:T(8,128)(2,1)S(1)}, bf16[32,2304]{1,0:T(8,128)(2,1)S(1)}, u32[]{:S(2)}, u32[]{:S(2)}) collective-permute-start(bf16[32,2304]{1,0:T(8,128)(2,1)S(1)} %get-tuple-element.93), channel_id=1, source_target_pairs={{0,16},{16,0},{32,48},{48,32},{64,80},{80,64},{96,112},{112,96},{1... | collective-permute-start | bytes 442376 | tf_op jit(solution)/shard_map/ppermute | solution.py:342
  31.2 4.1 %collective-permute-start.10 = (bf16[32,1152]{1,0:T(8,128)(2,1)S(1)}, bf16[32,1152]{1,0:T(8,128)(2,1)S(1)}, u32[]{:S(2)}, u32[]{:S(2)}) collective-permute-start(bf16[32,1152]{1,0:T(8,128)(2,1)S(1)} %get-tuple-element.94), channel_id=1, source_target_pairs={{0,240},{16,32},{32,16},{48,64},{64,48},{80,96},{96,80},{112,128},... | collective-permute-start | bytes 221192 | tf_op jit(solution)/shard_map/ppermute | solution.py:340
  31.2 5.0 %collective-permute-start.11 = (bf16[32,1152]{1,0:T(8,128)(2,1)S(1)}, bf16[32,1152]{1,0:T(8,128)(2,1)S(1)}, u32[]{:S(2)}, u32[]{:S(2)}) collective-permute-start(bf16[32,1152]{1,0:T(8,128)(2,1)S(1)} %get-tuple-element.98), channel_id=1, source_target_pairs={{0,240},{16,32},{32,16},{48,64},{64,48},{80,96},{96,80},{112,128},... | collective-permute-start | bytes 221192 | tf_op jit(solution)/shard_map/ppermute | solution.py:341
  36.5 3.9 %collective-permute-start.12 = (bf16[32,2304]{1,0:T(8,128)(2,1)S(1)}, bf16[32,2304]{1,0:T(8,128)(2,1)S(1)}, u32[]{:S(2)}, u32[]{:S(2)}) collective-permute-start(bf16[32,2304]{1,0:T(8,128)(2,1)S(1)} %get-tuple-element.102), channel_id=1, source_target_pairs={{0,16},{16,0},{32,48},{48,32},{64,80},{80,64},{96,112},{112,96},{1... | collective-permute-start | bytes 442376 | tf_op jit(solution)/shard_map/ppermute | solution.py:342
  37.5 4.1 %collective-permute-start.13 = (bf16[32,1152]{1,0:T(8,128)(2,1)S(1)}, bf16[32,1152]{1,0:T(8,128)(2,1)S(1)}, u32[]{:S(2)}, u32[]{:S(2)}) collective-permute-start(bf16[32,1152]{1,0:T(8,128)(2,1)S(1)} %get-tuple-element.103), channel_id=1, source_target_pairs={{0,240},{16,32},{32,16},{48,64},{64,48},{80,96},{96,80},{112,128},... | collective-permute-start | bytes 221192 | tf_op jit(solution)/shard_map/ppermute | solution.py:340
  37.5 5.0 %collective-permute-start.14 = (bf16[32,1152]{1,0:T(8,128)(2,1)S(1)}, bf16[32,1152]{1,0:T(8,128)(2,1)S(1)}, u32[]{:S(2)}, u32[]{:S(2)}) collective-permute-start(bf16[32,1152]{1,0:T(8,128)(2,1)S(1)} %get-tuple-element.107), channel_id=1, source_target_pairs={{0,240},{16,32},{32,16},{48,64},{64,48},{80,96},{96,80},{112,128},... | collective-permute-start | bytes 221192 | tf_op jit(solution)/shard_map/ppermute | solution.py:341
  42.7 4.9 %collective-permute-start.15 = (bf16[32,2304]{1,0:T(8,128)(2,1)S(1)}, bf16[32,2304]{1,0:T(8,128)(2,1)S(1)}, u32[]{:S(2)}, u32[]{:S(2)}) collective-permute-start(bf16[32,2304]{1,0:T(8,128)(2,1)S(1)} %get-tuple-element.111), channel_id=1, source_target_pairs={{0,16},{16,0},{32,48},{48,32},{64,80},{80,64},{96,112},{112,96},{1... | collective-permute-start | bytes 442376 | tf_op jit(solution)/shard_map/ppermute | solution.py:342
  44.8 4.1 %collective-permute-start.16 = (bf16[32,1152]{1,0:T(8,128)(2,1)S(1)}, bf16[32,1152]{1,0:T(8,128)(2,1)S(1)}, u32[]{:S(2)}, u32[]{:S(2)}) collective-permute-start(bf16[32,1152]{1,0:T(8,128)(2,1)S(1)} %get-tuple-element.112), channel_id=1, source_target_pairs={{0,240},{16,32},{32,16},{48,64},{64,48},{80,96},{96,80},{112,128},... | collective-permute-start | bytes 221192 | tf_op jit(solution)/shard_map/ppermute | solution.py:340
  44.8 4.7 %collective-permute-start.17 = (bf16[32,1152]{1,0:T(8,128)(2,1)S(1)}, bf16[32,1152]{1,0:T(8,128)(2,1)S(1)}, u32[]{:S(2)}, u32[]{:S(2)}) collective-permute-start(bf16[32,1152]{1,0:T(8,128)(2,1)S(1)} %get-tuple-element.114), channel_id=1, source_target_pairs={{0,240},{16,32},{32,16},{48,64},{64,48},{80,96},{96,80},{112,128},... | collective-permute-start | bytes 221192 | tf_op jit(solution)/shard_map/ppermute | solution.py:341

commit v4 on v2

--- a/solution.py
+++ b/solution.py
@@ -58,7 +58,12 @@
     rim += pltpu.roll(x_ref[1, :, edge] * rim_ref[which, 1:2, :], cols - 1, axis=1)
     high = rim.astype(jnp.bfloat16)
     out_ref[:, 2 * wide : 2 * wide + cols] = high
-    out_ref[:, 2 * wide + cols :] = (rim - high.astype(jnp.float32)).astype(jnp.bfloat16)
+    out_ref[:, 2 * wide + cols : 2 * wide + 2 * cols] = (rim - high.astype(jnp.float32)).astype(
+        jnp.bfloat16
+    )
+    spare = out_ref.shape[1] - 2 * wide - 2 * cols
+    if spare:
+        out_ref[:, 2 * wide + 2 * cols :] = jnp.zeros((out_ref.shape[0], spare), jnp.bfloat16)
     first = x_ref[0].astype(jnp.bfloat16)
     for outs, term in products(first, w_ref, side, 0, cols):
         out_ref[:, wide + outs.start : wide + outs.stop] = term.astype(jnp.bfloat16)
@@ -73,15 +78,15 @@
     for outs, term in products(got_ref[:, 0:wide], w_ref, side, 1, cols):
         to_ref[0, :, outs] = from_ref[0, :, outs] + scale * term
     rim = got_ref[:, 2 * wide : 2 * wide + cols].astype(jnp.float32)
-    rim += got_ref[:, 2 * wide + cols :].astype(jnp.float32)
+    rim += got_ref[:, 2 * wide + cols : 2 * wide + 2 * cols].astype(jnp.float32)
     to_ref[0, :, edge] += scale * (rim * rim_ref[which, 0:1, :])
     to_ref[1, :, edge] += scale * (pltpu.roll(rim, 1, axis=1) * rim_ref[which, 1:2, :])
 
 
 def prepare(
     partner_hbm, states_hbm, onsite_hbm, hop_row_hbm, hop_up_hbm, coefs_hbm, coupling_hbm,
-    x_ref, w_ref, coef_ref, rim_ref, weight_ref, far_ref, mate_ref,
-    partner_ref, states_ref, small_ref, coefs_ref, blocks, total, sems, row_sems,
+    x_ref, w_ref, coef_ref, rim_ref, weight_ref, far_ref,
+    partner_ref, states_ref, small_ref, coefs_ref, blocks, sems, row_sems, *totals,
 ):
     rows, slots = partner_hbm.shape
     cols = onsite_hbm.shape[2]
@@ -89,7 +94,6 @@
     all_rows = rows * lax.axis_size("tile")
     here = lax.rem(tile, 2)
     offsets = 2 * REACH + 1
-    spare = offsets + 1
 
     def kept(place):
         return place + here * (rows - 1 - 2 * place)
@@ -117,7 +121,8 @@
     for copy in copies[1:]:
         copy.start()
 
-    total[...] = jnp.zeros_like(total)
+    for total in totals:
+        total[...] = jnp.zeros_like(total)
     for side, place, sigma in (
         [(FAR, p, rows - p) for p in range(1, rows, PAIR)]
         + [(MATE, p, rows - PAIR - p) for p in range(0, rows, PAIR)]
@@ -158,28 +163,35 @@
         for place in range(rows):
             x_ref[layer, :, place * cols : (place + 1) * cols] = states_ref[layer, kept(place)]
 
-    for place in range(rows):
-        row = kept(place)
-        fetch(row).wait()
+    for pair in range(0, rows, PAIR):
+        places = range(pair, pair + PAIR)
+        for place in places:
+            fetch(kept(place)).wait()
         for k in range(slots):
-            slot = partner_ref[row, k]
-            away = slot - tile * rows - row
-            away = jnp.where(away > all_rows // 2, away - all_rows, away)
-            away = jnp.where(away < -(all_rows // 2), away + all_rows, away)
-            at = jnp.where(slot >= 0, REACH + (1 - 2 * here) * away, offsets) + place * spare
-            total[at] += blocks[row, k].astype(jnp.float32)
-        for offset in range(offsets):
-            reached = place + offset - REACH
-            if reached < 0:
-                side, sigma = FAR, -1 - reached
-            elif reached < rows:
-                side, sigma = LOCAL, reached
-            else:
-                side, sigma = MATE, 2 * rows - 1 - reached
-            w_ref[side, place * cols : (place + 1) * cols, sigma * cols : (sigma + 1) * cols] = total[
-                place * spare + offset
-            ].astype(jnp.bfloat16)
+            for place in places:
+                row = kept(place)
+                slot = partner_ref[row, k]
+                away = slot - tile * rows - row
+                away = jnp.where(away > all_rows // 2, away - all_rows, away)
+                away = jnp.where(away < -(all_rows // 2), away + all_rows, away)
+                at = jnp.where(slot >= 0, REACH + (1 - 2 * here) * away, offsets)
+                totals[place][at] += blocks[row, k].astype(jnp.float32)
+        for place in places:
+            for offset in range(offsets):
+                reached = place + offset - REACH
+                if reached < 0:
+                    side, sigma = FAR, -1 - reached
+                elif reached < rows:
+                    side, sigma = LOCAL, reached
+                else:
+                    side, sigma = MATE, 2 * rows - 1 - reached
+                w_ref[
+                    side, place * cols : (place + 1) * cols, sigma * cols : (sigma + 1) * cols
+                ] = totals[place][offset].astype(jnp.bfloat16)
     write_payload(x_ref, w_ref, rim_ref, FAR, far_ref)
+
+
+def to_mate(x_ref, w_ref, rim_ref, mate_ref):
     write_payload(x_ref, w_ref, rim_ref, MATE, mate_ref)
 
 
@@ -227,10 +239,9 @@
     add_received(scale, got_ref, w_ref, rim_ref, MATE, part_ref, sum_ref)
 
 
-def outer(scale, sum_ref, w_ref, rim_ref, got_ref, x_ref, far_ref, mate_ref):
+def outer(scale, sum_ref, w_ref, rim_ref, got_ref, x_ref, far_ref):
     add_received(scale, got_ref, w_ref, rim_ref, FAR, sum_ref, x_ref)
     write_payload(x_ref, w_ref, rim_ref, FAR, far_ref)
-    write_payload(x_ref, w_ref, rim_ref, MATE, mate_ref)
 
 
 def finish(scale, degree, sum_ref, filt_ref, w_ref, rim_ref, weight_ref, got_ref, out_ref, x_ref):
@@ -246,14 +257,14 @@
             )
 
 
-def call(kernel, outs, args, scratch=(), specs=None, limit=12):
+def call(kernel, outs, args, scratch=(), specs=None, limit=12, flops=1 << 20):
     return pl.pallas_call(
         kernel,
         out_shape=outs,
         in_specs=specs or [IN_VMEM] * len(args),
         out_specs=[IN_VMEM] * len(outs),
         scratch_shapes=list(scratch),
-        cost_estimate=pl.CostEstimate(flops=1 << 20, bytes_accessed=1 << 12, transcendentals=0),
+        cost_estimate=pl.CostEstimate(flops=flops, bytes_accessed=0, transcendentals=0),
         compiler_params=pltpu.CompilerParams(vmem_limit_bytes=limit << 20),
     )(*args)
 
@@ -269,10 +280,11 @@
 
     field = held((2, count, wide), jnp.float32)
     payload = held((count, 2 * wide + 2 * cols), jnp.bfloat16)
-    x, w, coef, rim, weight, far, mate = call(
+    longer = held((count, 2 * wide + 3 * cols), jnp.bfloat16)
+    x, w, coef, rim, weight, far = call(
         prepare,
         [field, held((3, wide, wide), jnp.bfloat16), held((2, 5, rows, cols), jnp.float32),
-         held((2, 2, cols), jnp.float32), held((degree + 1, cols), jnp.float32), payload, payload],
+         held((2, 2, cols), jnp.float32), held((degree + 1, cols), jnp.float32), longer],
         [outside(v) for v in (partner, states, onsite, hop_row, hop_up, coefs, coupling)],
         scratch=[
             pltpu.SMEM((rows, slots), jnp.int32),
@@ -280,9 +292,9 @@
             pltpu.VMEM((3, 2, rows, cols), jnp.float32),
             pltpu.SMEM((degree + 1,), jnp.float32),
             pltpu.VMEM((rows, slots, cols, cols), jnp.bfloat16),
-            pltpu.VMEM((rows * (2 * REACH + 2), cols, cols), jnp.float32),
             pltpu.SemaphoreType.DMA((6,)),
             pltpu.SemaphoreType.DMA((rows,)),
+            *[pltpu.VMEM((2 * REACH + 2, cols, cols), jnp.float32)] * rows,
         ],
         specs=[ANYWHERE] * 7,
         limit=24,
@@ -292,19 +304,20 @@
     for order in range(degree):
         scale = 1.0 / 12.0 if order == 0 else 2.0 / 12.0
         got_far = lax.ppermute(far, "tile", far_pairs)
+        past = [] if order == 0 else [near(prev), near(filt)]
+        (mate,) = call(to_mate, [payload], [x, w, rim])
         got_mate = lax.ppermute(mate, "tile", mate_pairs)
-        past = [] if order == 0 else [near(prev), near(filt)]
         part, filt = call(
             functools.partial(inner, order), [field, field], [x, *past, w, coef, weight]
         )
         (part,) = call(
-            functools.partial(from_mate, scale), [field], [near(part), w, rim, near(got_mate)]
+            functools.partial(from_mate, scale), [field], [near(part), w, rim, near(got_mate)], flops=0
         )
         prev = x
         if order < degree - 1:
-            x, far, mate = call(
+            x, far = call(
                 functools.partial(outer, scale),
-                [field, payload, payload],
+                [field, longer],
                 [near(part), w, rim, near(got_far)],
             )
             x = near(x)

time: 50.5 us -> 48.3 us (0.956)
  waiting for transfers between devices: 19 us -> 0.03 us
  starting transfers between devices: 10.5 us -> 26.7 us
    ppermute x6, waiting for transfers between devices: 19 us -> 0.02 us  [body(): got_far = lax.ppermute(far, 'tile', far_pairs)]
    ppermute x6, starting transfers between devices: 10.4 us -> 23.1 us  [body(): got_mate = lax.ppermute(mate, 'tile', mate_pairs)]
    ppermute x6, starting transfers between devices: 0.02 us -> 3.53 us  [body(): got_far = lax.ppermute(far, 'tile', far_pairs)]
    pallas_call x19 -> x25, Pallas kernels: 20.8 us -> 21.3 us  [call(): pl.pallas_call(kernel, out_shape=outs, in_specs=specs or [IN_VMEM] * len(...]
  transfers between devices with their start and end apart: 12 -> 12, of which waited for: 6 -> 0; matrix products, arithmetic and copies ran while one was open for 0% -> 0% of each run, Pallas kernels for 19% -> 24%
where the time goes in v4:
time: 48.3 us; the launch traced here: 48.2 us
  starting transfers between devices  26.7 us (55%)
  Pallas kernels  21.3 us (44%)
    ppermute x6, starting transfers between devices, body(): got_mate = lax.ppermute(mate, 'tile', mate_pairs)  23.1 us
    pallas_call x25, Pallas kernels, call(): pl.pallas_call(kernel, out_shape=outs, in_specs=specs or [IN_VMEM] * len(...  21.3 us
    ppermute x6, starting transfers between devices, body(): got_far = lax.ppermute(far, 'tile', far_pairs)  3.53 us
  transfers between devices with their start and end apart: 12, of which 0 were waited for; matrix products, arithmetic and copies ran while one was open for 0% of the time, Pallas kernels for 24%

profile of v4, /device:TPU:1, one launch (start us, length us, event | category | flops | bytes accessed | tf_op | source)
XLA Modules:
  0.0 48.2 jit_solution(12078124129256747643)
XLA Ops:
  0.0 4.7 %shard_map.73 = (f32[2,32,1024]{2,1,0:T(8,128)S(1)}, bf16[3,1024,1024]{2,1,0:T(8,128)(2,1)S(1)}, f32[2,5,8,128]{3,2,1,0:T(8,128)S(1)}, f32[2,2,128]{2,1,0:T(2,12...) custom-call(s32[8,16]{1,0:T(8,128)} %partner_hbm.1, f32[2,8,32,128]{3,2,1,0:T(8,128)} %states_hbm.1, ...), custom_call_target="tpu_custom_call" | custom-call | flops 1048576 | tf_op jit(solution)/shard_map/pallas_call | solution.py:261
  4.7 3.1 %collective-permute-start.1 = (bf16[32,2432]{1,0:T(8,128)(2,1)S(1)}, bf16[32,2432]{1,0:T(8,128)(2,1)S(1)}, u32[]{:S(2)}, u32[]{:S(2)}) collective-permute-start(bf16[32,2432]{1,0:T(8,128)(2,1)S(1)} %get-tuple-element.39), channel_id=1, source_target_pairs={{0,240},{16,32},{32,16},{48,64},{64,48},{80,96},{96,80},{112,128},... | collective-permute-start | bytes 466952 | tf_op jit(solution)/shard_map/ppermute | solution.py:306
  7.8 0.3 shard_map.75
  8.2 3.8 %collective-permute-start = (bf16[32,2304]{1,0:T(8,128)(2,1)S(1)}, bf16[32,2304]{1,0:T(8,128)(2,1)S(1)}, u32[]{:S(2)}, u32[]{:S(2)}) collective-permute-start(bf16[32,2304]{1,0:T(8,128)(2,1)S(1)} %shard_map.75), channel_id=1, source_target_pairs={{0,16},{16,0},{32,48},{48,32},{64,80},{80,64},{96,112},{112,96},{1... | collective-permute-start | bytes 442376 | tf_op jit(solution)/shard_map/ppermute | solution.py:309
  12.0 1.1 %shard_map.74 = (f32[2,32,1024]{2,1,0:T(8,128)S(1)}, f32[2,32,1024]{2,1,0:T(8,128)S(1)}) custom-call(f32[2,32,1024]{2,1,0:T(8,128)S(1)} %get-tuple-element.33.refs_0_.x_ref.refs_1_, bf16[3,1024,1024]{2,1,0:T(8,128)(2,1)S(1)} %get-tuple-element.34.refs_1_.w_ref.refs_3_, f32[2,5,8,128]{3,2,1,0:T(8,128)S(1)} %get-tuple-element.35.refs_2_.refs_4_, ...), custom_call_target="tpu_custom_call" | custom-call | flops 1048576 | tf_op jit(solution)/shard_map/pallas_call | solution.py:261
  13.0 0.0 collective-permute-done.got_ref
  13.1 0.5 %shard_map.76.sum_ref = f32[2,32,1024]{2,1,0:T(8,128)S(1)} custom-call(f32[2,32,1024]{2,1,0:T(8,128)S(1)} %get-tuple-element.37.part_ref, bf16[3,1024,1024]{2,1,0:T(8,128)(2,1)S(1)} %get-tuple-element.34.refs_1_.w_ref.refs_3_, f32[2,2,128]{2,1,0:T(2,128)S(1)} %get-tuple-element.38.rim_ref, bf16[32,2304]{1,0:T(8,128)(2,1)S(1)} %collective-permute-done.got_ref), custom_call_target="tpu_custom_call" | custom-call | tf_op jit(solution)/shard_map/pallas_call | solution.py:261
  13.6 0.0 collective-permute-done.1.got_ref
  13.6 0.7 %shard_map.77 = (f32[2,32,1024]{2,1,0:T(8,128)S(1)}, bf16[32,2432]{1,0:T(8,128)(2,1)S(1)}) custom-call(f32[2,32,1024]{2,1,0:T(8,128)S(1)} %shard_map.76.sum_ref, bf16[3,1024,1024]{2,1,0:T(8,128)(2,1)S(1)} %get-tuple-element.34.refs_1_.w_ref.refs_3_, f32[2,2,128]{2,1,0:T(2,128)S(1)} %get-tuple-element.38.rim_ref, ...), custom_call_target="tpu_custom_call" | custom-call | flops 1048576 | tf_op jit(solution)/shard_map/pallas_call | solution.py:261
  14.3 0.1 collective-permute-start.3
  14.4 0.3 shard_map.79
  14.7 3.9 %collective-permute-start.2 = (bf16[32,2304]{1,0:T(8,128)(2,1)S(1)}, bf16[32,2304]{1,0:T(8,128)(2,1)S(1)}, u32[]{:S(2)}, u32[]{:S(2)}) collective-permute-start(bf16[32,2304]{1,0:T(8,128)(2,1)S(1)} %shard_map.79), channel_id=1, source_target_pairs={{0,16},{16,0},{32,48},{48,32},{64,80},{80,64},{96,112},{112,96},{1... | collective-permute-start | bytes 442376 | tf_op jit(solution)/shard_map/ppermute | solution.py:309
  18.6 1.1 %shard_map.78 = (f32[2,32,1024]{2,1,0:T(8,128)S(1)}, f32[2,32,1024]{2,1,0:T(8,128)S(1)}) custom-call(f32[2,32,1024]{2,1,0:T(8,128)S(1)} %get-tuple-element.40.refs_0_.x_ref.refs_1_, f32[2,32,1024]{2,1,0:T(8,128)S(1)} %get-tuple-element.33.refs_0_.x_ref.refs_1_, f32[2,32,1024]{2,1,0:T(8,128)S(1)} %get-tuple-element.41.refs_2_, ...), custom_call_target="tpu_custom_call" | custom-call | flops 1048576 | tf_op jit(solution)/shard_map/pallas_call | solution.py:261
  19.8 0.0 collective-permute-done.2.got_ref
  19.8 0.5 %shard_map.80.sum_ref = f32[2,32,1024]{2,1,0:T(8,128)S(1)} custom-call(f32[2,32,1024]{2,1,0:T(8,128)S(1)} %get-tuple-element.42.part_ref, bf16[3,1024,1024]{2,1,0:T(8,128)(2,1)S(1)} %get-tuple-element.34.refs_1_.w_ref.refs_3_, f32[2,2,128]{2,1,0:T(2,128)S(1)} %get-tuple-element.38.rim_ref, bf16[32,2304]{1,0:T(8,128)(2,1)S(1)} %collective-permute-done.2.got_ref), custom_call_target="tpu_custom_call" | custom-call | tf_op jit(solution)/shard_map/pallas_call | solution.py:261
  20.3 0.0 collective-permute-done.3.got_ref
  20.3 0.7 %shard_map.81 = (f32[2,32,1024]{2,1,0:T(8,128)S(1)}, bf16[32,2432]{1,0:T(8,128)(2,1)S(1)}) custom-call(f32[2,32,1024]{2,1,0:T(8,128)S(1)} %shard_map.80.sum_ref, bf16[3,1024,1024]{2,1,0:T(8,128)(2,1)S(1)} %get-tuple-element.34.refs_1_.w_ref.refs_3_, f32[2,2,128]{2,1,0:T(2,128)S(1)} %get-tuple-element.38.rim_ref, ...), custom_call_target="tpu_custom_call" | custom-call | flops 1048576 | tf_op jit(solution)/shard_map/pallas_call | solution.py:261
  21.0 0.1 collective-permute-start.5
  21.1 0.3 shard_map.83
  21.4 3.9 %collective-permute-start.4 = (bf16[32,2304]{1,0:T(8,128)(2,1)S(1)}, bf16[32,2304]{1,0:T(8,128)(2,1)S(1)}, u32[]{:S(2)}, u32[]{:S(2)}) collective-permute-start(bf16[32,2304]{1,0:T(8,128)(2,1)S(1)} %shard_map.83), channel_id=1, source_target_pairs={{0,16},{16,0},{32,48},{48,32},{64,80},{80,64},{96,112},{112,96},{1... | collective-permute-start | bytes 442376 | tf_op jit(solution)/shard_map/ppermute | solution.py:309
  25.3 1.1 %shard_map.82 = (f32[2,32,1024]{2,1,0:T(8,128)S(1)}, f32[2,32,1024]{2,1,0:T(8,128)S(1)}) custom-call(f32[2,32,1024]{2,1,0:T(8,128)S(1)} %get-tuple-element.44.refs_0_.x_ref.refs_1_, f32[2,32,1024]{2,1,0:T(8,128)S(1)} %get-tuple-element.40.refs_0_.x_ref.refs_1_, f32[2,32,1024]{2,1,0:T(8,128)S(1)} %get-tuple-element.45.refs_2_, ...), custom_call_target="tpu_custom_call" | custom-call | flops 1048576 | tf_op jit(solution)/shard_map/pallas_call | solution.py:261
  26.4 0.0 collective-permute-done.4.got_ref
  26.4 0.5 %shard_map.84.sum_ref = f32[2,32,1024]{2,1,0:T(8,128)S(1)} custom-call(f32[2,32,1024]{2,1,0:T(8,128)S(1)} %get-tuple-element.46.part_ref, bf16[3,1024,1024]{2,1,0:T(8,128)(2,1)S(1)} %get-tuple-element.34.refs_1_.w_ref.refs_3_, f32[2,2,128]{2,1,0:T(2,128)S(1)} %get-tuple-element.38.rim_ref, bf16[32,2304]{1,0:T(8,128)(2,1)S(1)} %collective-permute-done.4.got_ref), custom_call_target="tpu_custom_call" | custom-call | tf_op jit(solution)/shard_map/pallas_call | solution.py:261
  27.0 0.0 collective-permute-done.5.got_ref
  27.0 0.7 %shard_map.85 = (f32[2,32,1024]{2,1,0:T(8,128)S(1)}, bf16[32,2432]{1,0:T(8,128)(2,1)S(1)}) custom-call(f32[2,32,1024]{2,1,0:T(8,128)S(1)} %shard_map.84.sum_ref, bf16[3,1024,1024]{2,1,0:T(8,128)(2,1)S(1)} %get-tuple-element.34.refs_1_.w_ref.refs_3_, f32[2,2,128]{2,1,0:T(2,128)S(1)} %get-tuple-element.38.rim_ref, ...), custom_call_target="tpu_custom_call" | custom-call | flops 1048576 | tf_op jit(solution)/shard_map/pallas_call | solution.py:261
  27.7 0.1 collective-permute-start.7
  27.8 0.3 shard_map.87
  28.1 4.0 %collective-permute-start.6 = (bf16[32,2304]{1,0:T(8,128)(2,1)S(1)}, bf16[32,2304]{1,0:T(8,128)(2,1)S(1)}, u32[]{:S(2)}, u32[]{:S(2)}) collective-permute-start(bf16[32,2304]{1,0:T(8,128)(2,1)S(1)} %shard_map.87), channel_id=1, source_target_pairs={{0,16},{16,0},{32,48},{48,32},{64,80},{80,64},{96,112},{112,96},{1... | collective-permute-start | bytes 442376 | tf_op jit(solution)/shard_map/ppermute | solution.py:309
  32.2 1.1 %shard_map.86 = (f32[2,32,1024]{2,1,0:T(8,128)S(1)}, f32[2,32,1024]{2,1,0:T(8,128)S(1)}) custom-call(f32[2,32,1024]{2,1,0:T(8,128)S(1)} %get-tuple-element.48.refs_0_.x_ref.refs_1_, f32[2,32,1024]{2,1,0:T(8,128)S(1)} %get-tuple-element.44.refs_0_.x_ref.refs_1_, f32[2,32,1024]{2,1,0:T(8,128)S(1)} %get-tuple-element.49.refs_2_, ...), custom_call_target="tpu_custom_call" | custom-call | flops 1048576 | tf_op jit(solution)/shard_map/pallas_call | solution.py:261
  33.3 0.0 collective-permute-done.6.got_ref
  33.3 0.5 %shard_map.88.sum_ref = f32[2,32,1024]{2,1,0:T(8,128)S(1)} custom-call(f32[2,32,1024]{2,1,0:T(8,128)S(1)} %get-tuple-element.50.part_ref, bf16[3,1024,1024]{2,1,0:T(8,128)(2,1)S(1)} %get-tuple-element.34.refs_1_.w_ref.refs_3_, f32[2,2,128]{2,1,0:T(2,128)S(1)} %get-tuple-element.38.rim_ref, bf16[32,2304]{1,0:T(8,128)(2,1)S(1)} %collective-permute-done.6.got_ref), custom_call_target="tpu_custom_call" | custom-call | tf_op jit(solution)/shard_map/pallas_call | solution.py:261
  33.8 0.0 collective-permute-done.7.got_ref
  33.8 0.7 %shard_map.89 = (f32[2,32,1024]{2,1,0:T(8,128)S(1)}, bf16[32,2432]{1,0:T(8,128)(2,1)S(1)}) custom-call(f32[2,32,1024]{2,1,0:T(8,128)S(1)} %shard_map.88.sum_ref, bf16[3,1024,1024]{2,1,0:T(8,128)(2,1)S(1)} %get-tuple-element.34.refs_1_.w_ref.refs_3_, f32[2,2,128]{2,1,0:T(2,128)S(1)} %get-tuple-element.38.rim_ref, ...), custom_call_target="tpu_custom_call" | custom-call | flops 1048576 | tf_op jit(solution)/shard_map/pallas_call | solution.py:261
  34.5 0.1 collective-permute-start.9
  34.6 0.3 shard_map.91
  35.0 3.7 %collective-permute-start.8 = (bf16[32,2304]{1,0:T(8,128)(2,1)S(1)}, bf16[32,2304]{1,0:T(8,128)(2,1)S(1)}, u32[]{:S(2)}, u32[]{:S(2)}) collective-permute-start(bf16[32,2304]{1,0:T(8,128)(2,1)S(1)} %shard_map.91), channel_id=1, source_target_pairs={{0,16},{16,0},{32,48},{48,32},{64,80},{80,64},{96,112},{112,96},{1... | collective-permute-start | bytes 442376 | tf_op jit(solution)/shard_map/ppermute | solution.py:309
  38.6 1.1 %shard_map.90 = (f32[2,32,1024]{2,1,0:T(8,128)S(1)}, f32[2,32,1024]{2,1,0:T(8,128)S(1)}) custom-call(f32[2,32,1024]{2,1,0:T(8,128)S(1)} %get-tuple-element.52.refs_0_.x_ref.refs_1_, f32[2,32,1024]{2,1,0:T(8,128)S(1)} %get-tuple-element.48.refs_0_.x_ref.refs_1_, f32[2,32,1024]{2,1,0:T(8,128)S(1)} %get-tuple-element.53.refs_2_, ...), custom_call_target="tpu_custom_call" | custom-call | flops 1048576 | tf_op jit(solution)/shard_map/pallas_call | solution.py:261
  39.8 0.0 collective-permute-done.8.got_ref
  39.8 0.5 %shard_map.92.sum_ref = f32[2,32,1024]{2,1,0:T(8,128)S(1)} custom-call(f32[2,32,1024]{2,1,0:T(8,128)S(1)} %get-tuple-element.54.part_ref, bf16[3,1024,1024]{2,1,0:T(8,128)(2,1)S(1)} %get-tuple-element.34.refs_1_.w_ref.refs_3_, f32[2,2,128]{2,1,0:T(2,128)S(1)} %get-tuple-element.38.rim_ref, bf16[32,2304]{1,0:T(8,128)(2,1)S(1)} %collective-permute-done.8.got_ref), custom_call_target="tpu_custom_call" | custom-call | tf_op jit(solution)/shard_map/pallas_call | solution.py:261
  40.3 0.0 collective-permute-done.9.got_ref
  40.3 0.7 %shard_map.93 = (f32[2,32,1024]{2,1,0:T(8,128)S(1)}, bf16[32,2432]{1,0:T(8,128)(2,1)S(1)}) custom-call(f32[2,32,1024]{2,1,0:T(8,128)S(1)} %shard_map.92.sum_ref, bf16[3,1024,1024]{2,1,0:T(8,128)(2,1)S(1)} %get-tuple-element.34.refs_1_.w_ref.refs_3_, f32[2,2,128]{2,1,0:T(2,128)S(1)} %get-tuple-element.38.rim_ref, ...), custom_call_target="tpu_custom_call" | custom-call | flops 1048576 | tf_op jit(solution)/shard_map/pallas_call | solution.py:261
  41.0 0.1 collective-permute-start.11
  41.1 0.3 shard_map.95
  41.5 3.9 %collective-permute-start.10 = (bf16[32,2304]{1,0:T(8,128)(2,1)S(1)}, bf16[32,2304]{1,0:T(8,128)(2,1)S(1)}, u32[]{:S(2)}, u32[]{:S(2)}) collective-permute-start(bf16[32,2304]{1,0:T(8,128)(2,1)S(1)} %shard_map.95), channel_id=1, source_target_pairs={{0,16},{16,0},{32,48},{48,32},{64,80},{80,64},{96,112},{112,96},{1... | collective-permute-start | bytes 442376 | tf_op jit(solution)/shard_map/ppermute | solution.py:309
  45.3 1.1 %shard_map.94 = (f32[2,32,1024]{2,1,0:T(8,128)S(1)}, f32[2,32,1024]{2,1,0:T(8,128)S(1)}) custom-call(f32[2,32,1024]{2,1,0:T(8,128)S(1)} %get-tuple-element.56.refs_0_.x_ref, f32[2,32,1024]{2,1,0:T(8,128)S(1)} %get-tuple-element.52.refs_0_.x_ref.refs_1_, f32[2,32,1024]{2,1,0:T(8,128)S(1)} %get-tuple-element.57.refs_2_, ...), custom_call_target="tpu_custom_call" | custom-call | flops 1048576 | tf_op jit(solution)/shard_map/pallas_call | solution.py:261
  46.5 0.5 %shard_map.96.sum_ref = f32[2,32,1024]{2,1,0:T(8,128)S(1)} custom-call(f32[2,32,1024]{2,1,0:T(8,128)S(1)} %get-tuple-element.58.part_ref, bf16[3,1024,1024]{2,1,0:T(8,128)(2,1)S(1)} %get-tuple-element.34.refs_1_.w_ref.refs_3_, f32[2,2,128]{2,1,0:T(2,128)S(1)} %get-tuple-element.38.rim_ref, bf16[32,2304]{1,0:T(8,128)(2,1)S(1)} %collective-permute-done.10.got_ref), custom_call_target="tpu_custom_call" | custom-call | tf_op jit(solution)/shard_map/pallas_call | solution.py:261
  47.0 0.0 collective-permute-done.11.got_ref
  47.0 1.2 %shard_map.97 = f32[2,8,32,128]{3,2,1,0:T(8,128)} custom-call(f32[2,32,1024]{2,1,0:T(8,128)S(1)} %shard_map.96.sum_ref, f32[2,32,1024]{2,1,0:T(8,128)S(1)} %get-tuple-element.59.filt_ref, bf16[3,1024,1024]{2,1,0:T(8,128)(2,1)S(1)} %get-tuple-element.34.refs_1_.w_ref.refs_3_, f32[2,2,128]{2,1,0:T(2,128)S(1)} %get-tuple-element.38.rim_ref, ...), custom_call_target="tpu_custom_call" | custom-call | flops 1048576 | tf_op jit(solution)/shard_map/pallas_call | solution.py:261
  (1 shorter events, 0.0 us)
Async XLA Ops:
  4.7 8.8 %collective-permute-start.1 = (bf16[32,2432]{1,0:T(8,128)(2,1)S(1)}, bf16[32,2432]{1,0:T(8,128)(2,1)S(1)}, u32[]{:S(2)}, u32[]{:S(2)}) collective-permute-start(bf16[32,2432]{1,0:T(8,128)(2,1)S(1)} %get-tuple-element.39), channel_id=1, source_target_pairs={{0,240},{16,32},{32,16},{48,64},{64,48},{80,96},{96,80},{112,128},... | collective-permute-start | bytes 466952 | tf_op jit(solution)/shard_map/ppermute | solution.py:306
  8.2 4.9 %collective-permute-start = (bf16[32,2304]{1,0:T(8,128)(2,1)S(1)}, bf16[32,2304]{1,0:T(8,128)(2,1)S(1)}, u32[]{:S(2)}, u32[]{:S(2)}) collective-permute-start(bf16[32,2304]{1,0:T(8,128)(2,1)S(1)} %shard_map.75), channel_id=1, source_target_pairs={{0,16},{16,0},{32,48},{48,32},{64,80},{80,64},{96,112},{112,96},{1... | collective-permute-start | bytes 442376 | tf_op jit(solution)/shard_map/ppermute | solution.py:309
  14.3 6.0 %collective-permute-start.3 = (bf16[32,2432]{1,0:T(8,128)(2,1)S(1)}, bf16[32,2432]{1,0:T(8,128)(2,1)S(1)}, u32[]{:S(2)}, u32[]{:S(2)}) collective-permute-start(bf16[32,2432]{1,0:T(8,128)(2,1)S(1)} %get-tuple-element.43), channel_id=1, source_target_pairs={{0,240},{16,32},{32,16},{48,64},{64,48},{80,96},{96,80},{112,128},... | collective-permute-start | bytes 466952 | tf_op jit(solution)/shard_map/ppermute | solution.py:306
  14.7 5.0 %collective-permute-start.2 = (bf16[32,2304]{1,0:T(8,128)(2,1)S(1)}, bf16[32,2304]{1,0:T(8,128)(2,1)S(1)}, u32[]{:S(2)}, u32[]{:S(2)}) collective-permute-start(bf16[32,2304]{1,0:T(8,128)(2,1)S(1)} %shard_map.79), channel_id=1, source_target_pairs={{0,16},{16,0},{32,48},{48,32},{64,80},{80,64},{96,112},{112,96},{1... | collective-permute-start | bytes 442376 | tf_op jit(solution)/shard_map/ppermute | solution.py:309
  21.0 5.9 %collective-permute-start.5 = (bf16[32,2432]{1,0:T(8,128)(2,1)S(1)}, bf16[32,2432]{1,0:T(8,128)(2,1)S(1)}, u32[]{:S(2)}, u32[]{:S(2)}) collective-permute-start(bf16[32,2432]{1,0:T(8,128)(2,1)S(1)} %get-tuple-element.47), channel_id=1, source_target_pairs={{0,240},{16,32},{32,16},{48,64},{64,48},{80,96},{96,80},{112,128},... | collective-permute-start | bytes 466952 | tf_op jit(solution)/shard_map/ppermute | solution.py:306
  21.4 5.0 %collective-permute-start.4 = (bf16[32,2304]{1,0:T(8,128)(2,1)S(1)}, bf16[32,2304]{1,0:T(8,128)(2,1)S(1)}, u32[]{:S(2)}, u32[]{:S(2)}) collective-permute-start(bf16[32,2304]{1,0:T(8,128)(2,1)S(1)} %shard_map.83), channel_id=1, source_target_pairs={{0,16},{16,0},{32,48},{48,32},{64,80},{80,64},{96,112},{112,96},{1... | collective-permute-start | bytes 442376 | tf_op jit(solution)/shard_map/ppermute | solution.py:309
  27.7 6.1 %collective-permute-start.7 = (bf16[32,2432]{1,0:T(8,128)(2,1)S(1)}, bf16[32,2432]{1,0:T(8,128)(2,1)S(1)}, u32[]{:S(2)}, u32[]{:S(2)}) collective-permute-start(bf16[32,2432]{1,0:T(8,128)(2,1)S(1)} %get-tuple-element.51), channel_id=1, source_target_pairs={{0,240},{16,32},{32,16},{48,64},{64,48},{80,96},{96,80},{112,128},... | collective-permute-start | bytes 466952 | tf_op jit(solution)/shard_map/ppermute | solution.py:306
  28.1 5.2 %collective-permute-start.6 = (bf16[32,2304]{1,0:T(8,128)(2,1)S(1)}, bf16[32,2304]{1,0:T(8,128)(2,1)S(1)}, u32[]{:S(2)}, u32[]{:S(2)}) collective-permute-start(bf16[32,2304]{1,0:T(8,128)(2,1)S(1)} %shard_map.87), channel_id=1, source_target_pairs={{0,16},{16,0},{32,48},{48,32},{64,80},{80,64},{96,112},{112,96},{1... | collective-permute-start | bytes 442376 | tf_op jit(solution)/shard_map/ppermute | solution.py:309
  34.5 5.8 %collective-permute-start.9 = (bf16[32,2432]{1,0:T(8,128)(2,1)S(1)}, bf16[32,2432]{1,0:T(8,128)(2,1)S(1)}, u32[]{:S(2)}, u32[]{:S(2)}) collective-permute-start(bf16[32,2432]{1,0:T(8,128)(2,1)S(1)} %get-tuple-element.55), channel_id=1, source_target_pairs={{0,240},{16,32},{32,16},{48,64},{64,48},{80,96},{96,80},{112,128},... | collective-permute-start | bytes 466952 | tf_op jit(solution)/shard_map/ppermute | solution.py:306
  35.0 4.8 %collective-permute-start.8 = (bf16[32,2304]{1,0:T(8,128)(2,1)S(1)}, bf16[32,2304]{1,0:T(8,128)(2,1)S(1)}, u32[]{:S(2)}, u32[]{:S(2)}) collective-permute-start(bf16[32,2304]{1,0:T(8,128)(2,1)S(1)} %shard_map.91), channel_id=1, source_target_pairs={{0,16},{16,0},{32,48},{48,32},{64,80},{80,64},{96,112},{112,96},{1... | collective-permute-start | bytes 442376 | tf_op jit(solution)/shard_map/ppermute | solution.py:309
  41.0 5.9 %collective-permute-start.11 = (bf16[32,2432]{1,0:T(8,128)(2,1)S(1)}, bf16[32,2432]{1,0:T(8,128)(2,1)S(1)}, u32[]{:S(2)}, u32[]{:S(2)}) collective-permute-start(bf16[32,2432]{1,0:T(8,128)(2,1)S(1)} %get-tuple-element.60), channel_id=1, source_target_pairs={{0,240},{16,32},{32,16},{48,64},{64,48},{80,96},{96,80},{112,128},... | collective-permute-start | bytes 466952 | tf_op jit(solution)/shard_map/ppermute | solution.py:306
  41.5 5.0 %collective-permute-start.10 = (bf16[32,2304]{1,0:T(8,128)(2,1)S(1)}, bf16[32,2304]{1,0:T(8,128)(2,1)S(1)}, u32[]{:S(2)}, u32[]{:S(2)}) collective-permute-start(bf16[32,2304]{1,0:T(8,128)(2,1)S(1)} %shard_map.95), channel_id=1, source_target_pairs={{0,16},{16,0},{32,48},{48,32},{64,80},{80,64},{96,112},{112,96},{1... | collective-permute-start | bytes 442376 | tf_op jit(solution)/shard_map/ppermute | solution.py:309

commit v5 on v4

--- a/solution.py
+++ b/solution.py
@@ -44,7 +44,7 @@
     for group in range(groups):
         outs = slice(group * step, (group + 1) * step)
         ins = span(side, group, groups, step)
-        block = w_ref[side, ins, outs] if contract == 0 else w_ref[side, outs, ins]
+        block = w_ref[ins, outs] if contract == 0 else w_ref[outs, ins]
         yield outs, dot(x[:, ins], block, contract)
 
 
@@ -69,13 +69,13 @@
         out_ref[:, wide + outs.start : wide + outs.stop] = term.astype(jnp.bfloat16)
 
 
-def add_received(scale, got_ref, w_ref, rim_ref, side, from_ref, to_ref):
+def add_received(scale, got_ref, w_ref, contract, rim_ref, side, from_ref, to_ref):
     wide = to_ref.shape[2]
     cols = rim_ref.shape[2]
     edge = slice(0, cols) if side == FAR else slice(wide - cols, wide)
     which = side - 1
     to_ref[1] = from_ref[1] + scale * got_ref[:, wide : 2 * wide].astype(jnp.float32)
-    for outs, term in products(got_ref[:, 0:wide], w_ref, side, 1, cols):
+    for outs, term in products(got_ref[:, 0:wide], w_ref, side, contract, cols):
         to_ref[0, :, outs] = from_ref[0, :, outs] + scale * term
     rim = got_ref[:, 2 * wide : 2 * wide + cols].astype(jnp.float32)
     rim += got_ref[:, 2 * wide + cols : 2 * wide + 2 * cols].astype(jnp.float32)
@@ -83,11 +83,39 @@
     to_ref[1, :, edge] += scale * (pltpu.roll(rim, 1, axis=1) * rim_ref[which, 1:2, :])
 
 
+def settle(totals, side, w_ref, cols):
+    rows = len(totals)
+
+    def block(place, sigma):
+        return (slice(place * cols, (place + 1) * cols), slice(sigma * cols, (sigma + 1) * cols))
+
+    if side == FAR:
+        empty = [(place, rows - place) for place in range(1, rows, PAIR)]
+    elif side == MATE:
+        empty = [(place, rows - PAIR - place) for place in range(0, rows, PAIR)]
+    else:
+        empty = []
+    for place, sigma in empty:
+        w_ref[block(place, sigma)] = jnp.zeros((cols, cols), jnp.bfloat16)
+    for place in range(rows):
+        for offset in range(2 * REACH + 1):
+            reached = place + offset - REACH
+            if side == FAR and reached < 0:
+                sigma = -1 - reached
+            elif side == LOCAL and 0 <= reached < rows:
+                sigma = reached
+            elif side == MATE and reached >= rows:
+                sigma = 2 * rows - 1 - reached
+            else:
+                continue
+            w_ref[block(place, sigma)] = totals[place][offset].astype(jnp.bfloat16)
+
+
 def prepare(
     partner_hbm, states_hbm, onsite_hbm, hop_row_hbm, hop_up_hbm, coefs_hbm, coupling_hbm,
-    x_ref, w_ref, coef_ref, rim_ref, weight_ref, far_ref,
-    partner_ref, states_ref, small_ref, coefs_ref, blocks, sems, row_sems, *totals,
+    x_ref, w_ref, coef_ref, rim_ref, weight_ref, far_ref, *rest,
 ):
+    *totals, partner_ref, states_ref, small_ref, coefs_ref, blocks, sems, row_sems = rest
     rows, slots = partner_hbm.shape
     cols = onsite_hbm.shape[2]
     tile = lax.axis_index("tile")
@@ -123,14 +151,6 @@
 
     for total in totals:
         total[...] = jnp.zeros_like(total)
-    for side, place, sigma in (
-        [(FAR, p, rows - p) for p in range(1, rows, PAIR)]
-        + [(MATE, p, rows - PAIR - p) for p in range(0, rows, PAIR)]
-    ):
-        w_ref[side, place * cols : (place + 1) * cols, sigma * cols : (sigma + 1) * cols] = jnp.zeros(
-            (cols, cols), jnp.bfloat16
-        )
-
     for copy in copies:
         copy.wait()
     for n in range(coefs_ref.shape[0]):
@@ -176,18 +196,7 @@
                 away = jnp.where(away < -(all_rows // 2), away + all_rows, away)
                 at = jnp.where(slot >= 0, REACH + (1 - 2 * here) * away, offsets)
                 totals[place][at] += blocks[row, k].astype(jnp.float32)
-        for place in places:
-            for offset in range(offsets):
-                reached = place + offset - REACH
-                if reached < 0:
-                    side, sigma = FAR, -1 - reached
-                elif reached < rows:
-                    side, sigma = LOCAL, reached
-                else:
-                    side, sigma = MATE, 2 * rows - 1 - reached
-                w_ref[
-                    side, place * cols : (place + 1) * cols, sigma * cols : (sigma + 1) * cols
-                ] = totals[place][offset].astype(jnp.bfloat16)
+    settle(totals, FAR, w_ref, cols)
     write_payload(x_ref, w_ref, rim_ref, FAR, far_ref)
 
 
@@ -195,9 +204,16 @@
     write_payload(x_ref, w_ref, rim_ref, MATE, mate_ref)
 
 
+def to_mate_first(x_ref, rim_ref, *refs):
+    *totals, mate_ref, w_ref = refs
+    settle(totals, MATE, w_ref, rim_ref.shape[2])
+    write_payload(x_ref, w_ref, rim_ref, MATE, mate_ref)
+
+
 def inner(order, *refs):
     if order == 0:
-        x_ref, w_ref, coef_ref, weight_ref, sum_ref, filt_out = refs
+        x_ref, coef_ref, weight_ref, *totals, sum_ref, filt_out, w_ref = refs
+        settle(totals, LOCAL, w_ref, weight_ref.shape[1])
         scale = 1.0 / 12.0
     else:
         x_ref, prev_ref, filt_ref, w_ref, coef_ref, weight_ref, sum_ref, filt_out = refs
@@ -235,19 +251,31 @@
             sum_ref[layer, :, here] = term
 
 
-def from_mate(scale, part_ref, w_ref, rim_ref, got_ref, sum_ref):
-    add_received(scale, got_ref, w_ref, rim_ref, MATE, part_ref, sum_ref)
-
-
-def outer(scale, sum_ref, w_ref, rim_ref, got_ref, x_ref, far_ref):
-    add_received(scale, got_ref, w_ref, rim_ref, FAR, sum_ref, x_ref)
+def from_mate(scale, part_ref, w_ref, rim_ref, got_ref, *refs):
+    if len(refs) > 1:
+        far_ref, sum_ref, *turned = refs
+    else:
+        (sum_ref,), turned = refs, []
+    add_received(scale, got_ref, w_ref, 1, rim_ref, MATE, part_ref, sum_ref)
+    if turned:
+        step = PAIR * rim_ref.shape[2]
+        groups = sum_ref.shape[2] // step
+        for group in range(groups):
+            outs = slice(group * step, (group + 1) * step)
+            for other in range(groups - group):
+                ins = slice(other * step, (other + 1) * step)
+                turned[0][ins, outs] = far_ref[outs, ins].T
+
+
+def outer(scale, sum_ref, w_ref, turned_ref, rim_ref, got_ref, x_ref, far_ref):
+    add_received(scale, got_ref, turned_ref, 0, rim_ref, FAR, sum_ref, x_ref)
     write_payload(x_ref, w_ref, rim_ref, FAR, far_ref)
 
 
-def finish(scale, degree, sum_ref, filt_ref, w_ref, rim_ref, weight_ref, got_ref, out_ref, x_ref):
+def finish(scale, degree, sum_ref, filt_ref, turned_ref, rim_ref, weight_ref, got_ref, out_ref, x_ref):
     cols = rim_ref.shape[2]
     rows = out_ref.shape[1]
-    add_received(scale, got_ref, w_ref, rim_ref, FAR, sum_ref, x_ref)
+    add_received(scale, got_ref, turned_ref, 0, rim_ref, FAR, sum_ref, x_ref)
     flip = lax.rem(lax.axis_index("tile"), 2)
     for layer in range(2):
         for place in range(rows):
@@ -281,10 +309,12 @@
     field = held((2, count, wide), jnp.float32)
     payload = held((count, 2 * wide + 2 * cols), jnp.bfloat16)
     longer = held((count, 2 * wide + 3 * cols), jnp.bfloat16)
-    x, w, coef, rim, weight, far = call(
+    matrix = held((wide, wide), jnp.bfloat16)
+    x, w_far, coef, rim, weight, far, *totals = call(
         prepare,
-        [field, held((3, wide, wide), jnp.bfloat16), held((2, 5, rows, cols), jnp.float32),
-         held((2, 2, cols), jnp.float32), held((degree + 1, cols), jnp.float32), longer],
+        [field, matrix, held((2, 5, rows, cols), jnp.float32),
+         held((2, 2, cols), jnp.float32), held((degree + 1, cols), jnp.float32), longer,
+         *[held((2 * REACH + 2, cols, cols), jnp.float32)] * rows],
         [outside(v) for v in (partner, states, onsite, hop_row, hop_up, coefs, coupling)],
         scratch=[
             pltpu.SMEM((rows, slots), jnp.int32),
@@ -294,38 +324,54 @@
             pltpu.VMEM((rows, slots, cols, cols), jnp.bfloat16),
             pltpu.SemaphoreType.DMA((6,)),
             pltpu.SemaphoreType.DMA((rows,)),
-            *[pltpu.VMEM((2 * REACH + 2, cols, cols), jnp.float32)] * rows,
         ],
         specs=[ANYWHERE] * 7,
         limit=24,
     )
-    w, coef, rim, weight, x = near(w), near(coef), near(rim), near(weight), near(x)
+    w_far, coef, rim, weight, x = near(w_far), near(coef), near(rim), near(weight), near(x)
+    totals = [near(total) for total in totals]
     prev = filt = None
     for order in range(degree):
         scale = 1.0 / 12.0 if order == 0 else 2.0 / 12.0
         got_far = lax.ppermute(far, "tile", far_pairs)
-        past = [] if order == 0 else [near(prev), near(filt)]
-        (mate,) = call(to_mate, [payload], [x, w, rim])
+        if order == 0:
+            mate, w_mate = call(to_mate_first, [payload, matrix], [x, rim, *totals])
+            w_mate = near(w_mate)
+        else:
+            (mate,) = call(to_mate, [payload], [x, w_mate, rim])
         got_mate = lax.ppermute(mate, "tile", mate_pairs)
-        part, filt = call(
-            functools.partial(inner, order), [field, field], [x, *past, w, coef, weight]
+        if order == 0:
+            part, filt, w_local = call(
+                functools.partial(inner, order), [field, field, matrix], [x, coef, weight, *totals]
+            )
+            w_local = near(w_local)
+        else:
+            part, filt = call(
+                functools.partial(inner, order),
+                [field, field],
+                [x, near(prev), near(filt), w_local, coef, weight],
+            )
+        part, *turned_now = call(
+            functools.partial(from_mate, scale),
+            [field, matrix] if order == 0 else [field],
+            [near(part), w_mate, rim, near(got_mate)] + ([w_far] if order == 0 else []),
+            flops=0,
         )
-        (part,) = call(
-            functools.partial(from_mate, scale), [field], [near(part), w, rim, near(got_mate)], flops=0
-        )
+        if order == 0:
+            turned = near(turned_now[0])
         prev = x
         if order < degree - 1:
             x, far = call(
                 functools.partial(outer, scale),
                 [field, longer],
-                [near(part), w, rim, near(got_far)],
+                [near(part), w_far, turned, rim, near(got_far)],
             )
             x = near(x)
         else:
             (out,) = call(
                 functools.partial(finish, scale, degree),
                 [jax.ShapeDtypeStruct(states.shape, jnp.float32)],
-                [near(part), near(filt), w, rim, weight, near(got_far)],
+                [near(part), near(filt), turned, rim, weight, near(got_far)],
                 scratch=[pltpu.VMEM((2, count, wide), jnp.float32)],
             )
     return out

time: 48.3 us -> 47 us (0.973)
  Pallas kernels: 21.3 us -> 20.1 us
    pallas_call x25, Pallas kernels: 21.3 us -> 20.1 us  [call(): pl.pallas_call(kernel, out_shape=outs, in_specs=specs or [IN_VMEM] * len(...]
  transfers between devices with their start and end apart: 12 -> 12, of which waited for: 0 -> 0; matrix products, arithmetic and copies ran while one was open for 0% -> 0% of each run, Pallas kernels for 24% -> 25%
where the time goes in v5:
time: 47 us; the launch traced here: 46.9 us
  starting transfers between devices  26.5 us (56%)
  Pallas kernels  20.1 us (43%)
    ppermute x6, starting transfers between devices, body(): got_mate = lax.ppermute(mate, 'tile', mate_pairs)  23 us
    pallas_call x25, Pallas kernels, call(): pl.pallas_call(kernel, out_shape=outs, in_specs=specs or [IN_VMEM] * len(...  20.1 us
    ppermute x6, starting transfers between devices, body(): got_far = lax.ppermute(far, 'tile', far_pairs)  3.54 us
  transfers between devices with their start and end apart: 12, of which 0 were waited for; matrix products, arithmetic and copies ran while one was open for 0% of the time, Pallas kernels for 25%

profile of v5, /device:TPU:1, one launch (start us, length us, event | category | flops | bytes accessed | tf_op | source)
XLA Modules:
  0.0 46.9 jit_solution(6102847782591479987)
XLA Ops:
  0.0 4.2 %shard_map.73 = (f32[2,32,1024]{2,1,0:T(8,128)S(1)}, bf16[1024,1024]{1,0:T(8,128)(2,1)S(1)}, f32[2,5,8,128]{3,2,1,0:T(8,128)S(1)}, f32[2,2,128]{2,1,0:T(2,128)S(...) custom-call(s32[8,16]{1,0:T(8,128)} %partner_hbm.1, ...), custom_call_target="tpu_custom_call" | custom-call | flops 1048576 | tf_op jit(solution)/shard_map/pallas_call | solution.py:289
  4.3 3.1 %collective-permute-start.1 = (bf16[32,2432]{1,0:T(8,128)(2,1)S(1)}, bf16[32,2432]{1,0:T(8,128)(2,1)S(1)}, u32[]{:S(2)}, u32[]{:S(2)}) collective-permute-start(bf16[32,2432]{1,0:T(8,128)(2,1)S(1)} %get-tuple-element.64), channel_id=1, source_target_pairs={{0,240},{16,32},{32,16},{48,64},{64,48},{80,96},{96,80},{112,128},... | collective-permute-start | bytes 466952 | tf_op jit(solution)/shard_map/ppermute | solution.py:336
  7.4 0.4 shard_map.75
  7.8 3.9 %collective-permute-start = (bf16[32,2304]{1,0:T(8,128)(2,1)S(1)}, bf16[32,2304]{1,0:T(8,128)(2,1)S(1)}, u32[]{:S(2)}, u32[]{:S(2)}) collective-permute-start(bf16[32,2304]{1,0:T(8,128)(2,1)S(1)} %get-tuple-element.60), channel_id=1, source_target_pairs={{0,16},{16,0},{32,48},{48,32},{64,80},{80,64},{96,112},{112,96},{1... | collective-permute-start | bytes 442376 | tf_op jit(solution)/shard_map/ppermute | solution.py:342
  11.6 1.2 %shard_map.74 = (f32[2,32,1024]{2,1,0:T(8,128)S(1)}, f32[2,32,1024]{2,1,0:T(8,128)S(1)}, bf16[1024,1024]{1,0:T(8,128)(2,1)S(1)}) custom-call(f32[2,32,1024]{2,1,0:T(8,128)S(1)} %get-tuple-element.46.refs_0_.x_ref.refs_1_, f32[2,5,8,128]{3,2,1,0:T(8,128)S(1)} %get-tuple-element.47.refs_1_.refs_4_, f32[7,128]{1,0:T(8,128)S(1)} %get-tuple-element.48.refs_2_.refs_5_.weight_ref, ...), custom_call_target="tpu_custom_call" | custom-call | flops 1048576 | tf_op jit(solution)/shard_map/pallas_call | solution.py:289
  12.8 0.0 collective-permute-done.got_ref
  12.9 0.5 %shard_map.76 = (f32[2,32,1024]{2,1,0:T(8,128)S(1)}, bf16[1024,1024]{1,0:T(8,128)(2,1)S(1)}) custom-call(f32[2,32,1024]{2,1,0:T(8,128)S(1)} %get-tuple-element.57.part_ref, bf16[1024,1024]{1,0:T(8,128)(2,1)S(1)} %get-tuple-element.59.w_ref, f32[2,2,128]{2,1,0:T(2,128)S(1)} %get-tuple-element.58.rim_ref, bf16[32,2304]{1,0:T(8,128)(2,1)S(1)} %collective-permute-done.got_ref, ...), custom_call_target="tpu_custom_call" | custom-call | tf_op jit(solution)/shard_map/pallas_call | solution.py:289
  13.4 0.0 collective-permute-done.1.got_ref
  13.4 0.6 %shard_map.77 = (f32[2,32,1024]{2,1,0:T(8,128)S(1)}, bf16[32,2432]{1,0:T(8,128)(2,1)S(1)}) custom-call(f32[2,32,1024]{2,1,0:T(8,128)S(1)} %get-tuple-element.62.sum_ref, bf16[1024,1024]{1,0:T(8,128)(2,1)S(1)} %get-tuple-element.61.refs_0_.w_ref, bf16[1024,1024]{1,0:T(8,128)(2,1)S(1)} %get-tuple-element.63.turned_ref, ...), custom_call_target="tpu_custom_call" | custom-call | flops 1048576 | tf_op jit(solution)/shard_map/pallas_call | solution.py:289
  14.0 0.1 collective-permute-start.3
  14.1 0.3 shard_map.79
  14.4 3.6 %collective-permute-start.2 = (bf16[32,2304]{1,0:T(8,128)(2,1)S(1)}, bf16[32,2304]{1,0:T(8,128)(2,1)S(1)}, u32[]{:S(2)}, u32[]{:S(2)}) collective-permute-start(bf16[32,2304]{1,0:T(8,128)(2,1)S(1)} %shard_map.79), channel_id=1, source_target_pairs={{0,16},{16,0},{32,48},{48,32},{64,80},{80,64},{96,112},{112,96},{1... | collective-permute-start | bytes 442376 | tf_op jit(solution)/shard_map/ppermute | solution.py:342
  18.0 1.1 %shard_map.78 = (f32[2,32,1024]{2,1,0:T(8,128)S(1)}, f32[2,32,1024]{2,1,0:T(8,128)S(1)}) custom-call(f32[2,32,1024]{2,1,0:T(8,128)S(1)} %get-tuple-element.65.refs_0_.x_ref.refs_1_, f32[2,32,1024]{2,1,0:T(8,128)S(1)} %get-tuple-element.46.refs_0_.x_ref.refs_1_, f32[2,32,1024]{2,1,0:T(8,128)S(1)} %get-tuple-element.66.refs_2_, ...), custom_call_target="tpu_custom_call" | custom-call | flops 1048576 | tf_op jit(solution)/shard_map/pallas_call | solution.py:289
  19.1 0.0 collective-permute-done.2.got_ref
  19.1 0.5 %shard_map.80.sum_ref = f32[2,32,1024]{2,1,0:T(8,128)S(1)} custom-call(f32[2,32,1024]{2,1,0:T(8,128)S(1)} %get-tuple-element.68.part_ref, bf16[1024,1024]{1,0:T(8,128)(2,1)S(1)} %get-tuple-element.59.w_ref, f32[2,2,128]{2,1,0:T(2,128)S(1)} %get-tuple-element.58.rim_ref, bf16[32,2304]{1,0:T(8,128)(2,1)S(1)} %collective-permute-done.2.got_ref), custom_call_target="tpu_custom_call" | custom-call | tf_op jit(solution)/shard_map/pallas_call | solution.py:289
  19.7 0.0 collective-permute-done.3.got_ref
  19.7 0.6 %shard_map.81 = (f32[2,32,1024]{2,1,0:T(8,128)S(1)}, bf16[32,2432]{1,0:T(8,128)(2,1)S(1)}) custom-call(f32[2,32,1024]{2,1,0:T(8,128)S(1)} %shard_map.80.sum_ref, bf16[1024,1024]{1,0:T(8,128)(2,1)S(1)} %get-tuple-element.61.refs_0_.w_ref, bf16[1024,1024]{1,0:T(8,128)(2,1)S(1)} %get-tuple-element.63.turned_ref, f32[2,2,128]{2,1,0:T(2,128)S(1)} %get-tuple-element.58.rim_ref, ...), custom_call_target="tpu_custom_call" | custom-call | flops 1048576 | tf_op jit(solution)/shard_map/pallas_call | solution.py:289
  20.3 0.1 collective-permute-start.5
  20.3 0.3 shard_map.83
  20.7 3.9 %collective-permute-start.4 = (bf16[32,2304]{1,0:T(8,128)(2,1)S(1)}, bf16[32,2304]{1,0:T(8,128)(2,1)S(1)}, u32[]{:S(2)}, u32[]{:S(2)}) collective-permute-start(bf16[32,2304]{1,0:T(8,128)(2,1)S(1)} %shard_map.83), channel_id=1, source_target_pairs={{0,16},{16,0},{32,48},{48,32},{64,80},{80,64},{96,112},{112,96},{1... | collective-permute-start | bytes 442376 | tf_op jit(solution)/shard_map/ppermute | solution.py:342
  24.6 1.1 %shard_map.82 = (f32[2,32,1024]{2,1,0:T(8,128)S(1)}, f32[2,32,1024]{2,1,0:T(8,128)S(1)}) custom-call(f32[2,32,1024]{2,1,0:T(8,128)S(1)} %get-tuple-element.70.refs_0_.x_ref.refs_1_, f32[2,32,1024]{2,1,0:T(8,128)S(1)} %get-tuple-element.65.refs_0_.x_ref.refs_1_, f32[2,32,1024]{2,1,0:T(8,128)S(1)} %get-tuple-element.71.refs_2_, ...), custom_call_target="tpu_custom_call" | custom-call | flops 1048576 | tf_op jit(solution)/shard_map/pallas_call | solution.py:289
  25.7 0.0 collective-permute-done.4.got_ref
  25.7 0.5 %shard_map.84.sum_ref = f32[2,32,1024]{2,1,0:T(8,128)S(1)} custom-call(f32[2,32,1024]{2,1,0:T(8,128)S(1)} %get-tuple-element.72.part_ref, bf16[1024,1024]{1,0:T(8,128)(2,1)S(1)} %get-tuple-element.59.w_ref, f32[2,2,128]{2,1,0:T(2,128)S(1)} %get-tuple-element.58.rim_ref, bf16[32,2304]{1,0:T(8,128)(2,1)S(1)} %collective-permute-done.4.got_ref), custom_call_target="tpu_custom_call" | custom-call | tf_op jit(solution)/shard_map/pallas_call | solution.py:289
  26.2 0.0 collective-permute-done.5.got_ref
  26.2 0.6 %shard_map.85 = (f32[2,32,1024]{2,1,0:T(8,128)S(1)}, bf16[32,2432]{1,0:T(8,128)(2,1)S(1)}) custom-call(f32[2,32,1024]{2,1,0:T(8,128)S(1)} %shard_map.84.sum_ref, bf16[1024,1024]{1,0:T(8,128)(2,1)S(1)} %get-tuple-element.61.refs_0_.w_ref, bf16[1024,1024]{1,0:T(8,128)(2,1)S(1)} %get-tuple-element.63.turned_ref, f32[2,2,128]{2,1,0:T(2,128)S(1)} %get-tuple-element.58.rim_ref, ...), custom_call_target="tpu_custom_call" | custom-call | flops 1048576 | tf_op jit(solution)/shard_map/pallas_call | solution.py:289
  26.8 0.1 collective-permute-start.7
  26.9 0.3 shard_map.87
  27.2 4.1 %collective-permute-start.6 = (bf16[32,2304]{1,0:T(8,128)(2,1)S(1)}, bf16[32,2304]{1,0:T(8,128)(2,1)S(1)}, u32[]{:S(2)}, u32[]{:S(2)}) collective-permute-start(bf16[32,2304]{1,0:T(8,128)(2,1)S(1)} %shard_map.87), channel_id=1, source_target_pairs={{0,16},{16,0},{32,48},{48,32},{64,80},{80,64},{96,112},{112,96},{1... | collective-permute-start | bytes 442376 | tf_op jit(solution)/shard_map/ppermute | solution.py:342
  31.3 1.1 %shard_map.86 = (f32[2,32,1024]{2,1,0:T(8,128)S(1)}, f32[2,32,1024]{2,1,0:T(8,128)S(1)}) custom-call(f32[2,32,1024]{2,1,0:T(8,128)S(1)} %get-tuple-element.74.refs_0_.x_ref.refs_1_, f32[2,32,1024]{2,1,0:T(8,128)S(1)} %get-tuple-element.70.refs_0_.x_ref.refs_1_, f32[2,32,1024]{2,1,0:T(8,128)S(1)} %get-tuple-element.75.refs_2_, ...), custom_call_target="tpu_custom_call" | custom-call | flops 1048576 | tf_op jit(solution)/shard_map/pallas_call | solution.py:289
  32.4 0.0 collective-permute-done.6.got_ref
  32.4 0.5 %shard_map.88.sum_ref = f32[2,32,1024]{2,1,0:T(8,128)S(1)} custom-call(f32[2,32,1024]{2,1,0:T(8,128)S(1)} %get-tuple-element.76.part_ref, bf16[1024,1024]{1,0:T(8,128)(2,1)S(1)} %get-tuple-element.59.w_ref, f32[2,2,128]{2,1,0:T(2,128)S(1)} %get-tuple-element.58.rim_ref, bf16[32,2304]{1,0:T(8,128)(2,1)S(1)} %collective-permute-done.6.got_ref), custom_call_target="tpu_custom_call" | custom-call | tf_op jit(solution)/shard_map/pallas_call | solution.py:289
  32.9 0.0 collective-permute-done.7.got_ref
  32.9 0.6 %shard_map.89 = (f32[2,32,1024]{2,1,0:T(8,128)S(1)}, bf16[32,2432]{1,0:T(8,128)(2,1)S(1)}) custom-call(f32[2,32,1024]{2,1,0:T(8,128)S(1)} %shard_map.88.sum_ref, bf16[1024,1024]{1,0:T(8,128)(2,1)S(1)} %get-tuple-element.61.refs_0_.w_ref, bf16[1024,1024]{1,0:T(8,128)(2,1)S(1)} %get-tuple-element.63.turned_ref, f32[2,2,128]{2,1,0:T(2,128)S(1)} %get-tuple-element.58.rim_ref, ...), custom_call_target="tpu_custom_call" | custom-call | flops 1048576 | tf_op jit(solution)/shard_map/pallas_call | solution.py:289
  33.5 0.1 collective-permute-start.9
  33.6 0.3 shard_map.91
  33.9 3.7 %collective-permute-start.8 = (bf16[32,2304]{1,0:T(8,128)(2,1)S(1)}, bf16[32,2304]{1,0:T(8,128)(2,1)S(1)}, u32[]{:S(2)}, u32[]{:S(2)}) collective-permute-start(bf16[32,2304]{1,0:T(8,128)(2,1)S(1)} %shard_map.91), channel_id=1, source_target_pairs={{0,16},{16,0},{32,48},{48,32},{64,80},{80,64},{96,112},{112,96},{1... | collective-permute-start | bytes 442376 | tf_op jit(solution)/shard_map/ppermute | solution.py:342
  37.6 1.1 %shard_map.90 = (f32[2,32,1024]{2,1,0:T(8,128)S(1)}, f32[2,32,1024]{2,1,0:T(8,128)S(1)}) custom-call(f32[2,32,1024]{2,1,0:T(8,128)S(1)} %get-tuple-element.78.refs_0_.x_ref.refs_1_, f32[2,32,1024]{2,1,0:T(8,128)S(1)} %get-tuple-element.74.refs_0_.x_ref.refs_1_, f32[2,32,1024]{2,1,0:T(8,128)S(1)} %get-tuple-element.79.refs_2_, ...), custom_call_target="tpu_custom_call" | custom-call | flops 1048576 | tf_op jit(solution)/shard_map/pallas_call | solution.py:289
  38.7 0.0 collective-permute-done.8.got_ref
  38.8 0.5 %shard_map.92.sum_ref = f32[2,32,1024]{2,1,0:T(8,128)S(1)} custom-call(f32[2,32,1024]{2,1,0:T(8,128)S(1)} %get-tuple-element.80.part_ref, bf16[1024,1024]{1,0:T(8,128)(2,1)S(1)} %get-tuple-element.59.w_ref, f32[2,2,128]{2,1,0:T(2,128)S(1)} %get-tuple-element.58.rim_ref, bf16[32,2304]{1,0:T(8,128)(2,1)S(1)} %collective-permute-done.8.got_ref), custom_call_target="tpu_custom_call" | custom-call | tf_op jit(solution)/shard_map/pallas_call | solution.py:289
  39.3 0.0 collective-permute-done.9.got_ref
  39.3 0.6 %shard_map.93 = (f32[2,32,1024]{2,1,0:T(8,128)S(1)}, bf16[32,2432]{1,0:T(8,128)(2,1)S(1)}) custom-call(f32[2,32,1024]{2,1,0:T(8,128)S(1)} %shard_map.92.sum_ref, bf16[1024,1024]{1,0:T(8,128)(2,1)S(1)} %get-tuple-element.61.refs_0_.w_ref, bf16[1024,1024]{1,0:T(8,128)(2,1)S(1)} %get-tuple-element.63.turned_ref, f32[2,2,128]{2,1,0:T(2,128)S(1)} %get-tuple-element.58.rim_ref, ...), custom_call_target="tpu_custom_call" | custom-call | flops 1048576 | tf_op jit(solution)/shard_map/pallas_call | solution.py:289
  39.9 0.1 collective-permute-start.11
  40.0 0.3 shard_map.95
  40.3 3.9 %collective-permute-start.10 = (bf16[32,2304]{1,0:T(8,128)(2,1)S(1)}, bf16[32,2304]{1,0:T(8,128)(2,1)S(1)}, u32[]{:S(2)}, u32[]{:S(2)}) collective-permute-start(bf16[32,2304]{1,0:T(8,128)(2,1)S(1)} %shard_map.95), channel_id=1, source_target_pairs={{0,16},{16,0},{32,48},{48,32},{64,80},{80,64},{96,112},{112,96},{1... | collective-permute-start | bytes 442376 | tf_op jit(solution)/shard_map/ppermute | solution.py:342
  44.2 1.1 %shard_map.94 = (f32[2,32,1024]{2,1,0:T(8,128)S(1)}, f32[2,32,1024]{2,1,0:T(8,128)S(1)}) custom-call(f32[2,32,1024]{2,1,0:T(8,128)S(1)} %get-tuple-element.82.refs_0_.x_ref, f32[2,32,1024]{2,1,0:T(8,128)S(1)} %get-tuple-element.78.refs_0_.x_ref.refs_1_, f32[2,32,1024]{2,1,0:T(8,128)S(1)} %get-tuple-element.83.refs_2_, ...), custom_call_target="tpu_custom_call" | custom-call | flops 1048576 | tf_op jit(solution)/shard_map/pallas_call | solution.py:289
  45.3 0.5 %shard_map.96.sum_ref = f32[2,32,1024]{2,1,0:T(8,128)S(1)} custom-call(f32[2,32,1024]{2,1,0:T(8,128)S(1)} %get-tuple-element.84.part_ref, bf16[1024,1024]{1,0:T(8,128)(2,1)S(1)} %get-tuple-element.59.w_ref, f32[2,2,128]{2,1,0:T(2,128)S(1)} %get-tuple-element.58.rim_ref, bf16[32,2304]{1,0:T(8,128)(2,1)S(1)} %collective-permute-done.10.got_ref), custom_call_target="tpu_custom_call" | custom-call | tf_op jit(solution)/shard_map/pallas_call | solution.py:289
  45.8 0.0 collective-permute-done.11.got_ref
  45.8 1.1 %shard_map.97 = f32[2,8,32,128]{3,2,1,0:T(8,128)} custom-call(f32[2,32,1024]{2,1,0:T(8,128)S(1)} %shard_map.96.sum_ref, f32[2,32,1024]{2,1,0:T(8,128)S(1)} %get-tuple-element.85.filt_ref, bf16[1024,1024]{1,0:T(8,128)(2,1)S(1)} %get-tuple-element.63.turned_ref, f32[2,2,128]{2,1,0:T(2,128)S(1)} %get-tuple-element.58.rim_ref, ...), custom_call_target="tpu_custom_call" | custom-call | flops 1048576 | tf_op jit(solution)/shard_map/pallas_call | solution.py:289
  (1 shorter events, 0.0 us)
Async XLA Ops:
  4.3 9.2 %collective-permute-start.1 = (bf16[32,2432]{1,0:T(8,128)(2,1)S(1)}, bf16[32,2432]{1,0:T(8,128)(2,1)S(1)}, u32[]{:S(2)}, u32[]{:S(2)}) collective-permute-start(bf16[32,2432]{1,0:T(8,128)(2,1)S(1)} %get-tuple-element.64), channel_id=1, source_target_pairs={{0,240},{16,32},{32,16},{48,64},{64,48},{80,96},{96,80},{112,128},... | collective-permute-start | bytes 466952 | tf_op jit(solution)/shard_map/ppermute | solution.py:336
  7.8 5.1 %collective-permute-start = (bf16[32,2304]{1,0:T(8,128)(2,1)S(1)}, bf16[32,2304]{1,0:T(8,128)(2,1)S(1)}, u32[]{:S(2)}, u32[]{:S(2)}) collective-permute-start(bf16[32,2304]{1,0:T(8,128)(2,1)S(1)} %get-tuple-element.60), channel_id=1, source_target_pairs={{0,16},{16,0},{32,48},{48,32},{64,80},{80,64},{96,112},{112,96},{1... | collective-permute-start | bytes 442376 | tf_op jit(solution)/shard_map/ppermute | solution.py:342
  14.0 5.7 %collective-permute-start.3 = (bf16[32,2432]{1,0:T(8,128)(2,1)S(1)}, bf16[32,2432]{1,0:T(8,128)(2,1)S(1)}, u32[]{:S(2)}, u32[]{:S(2)}) collective-permute-start(bf16[32,2432]{1,0:T(8,128)(2,1)S(1)} %get-tuple-element.69), channel_id=1, source_target_pairs={{0,240},{16,32},{32,16},{48,64},{64,48},{80,96},{96,80},{112,128},... | collective-permute-start | bytes 466952 | tf_op jit(solution)/shard_map/ppermute | solution.py:336
  14.4 4.7 %collective-permute-start.2 = (bf16[32,2304]{1,0:T(8,128)(2,1)S(1)}, bf16[32,2304]{1,0:T(8,128)(2,1)S(1)}, u32[]{:S(2)}, u32[]{:S(2)}) collective-permute-start(bf16[32,2304]{1,0:T(8,128)(2,1)S(1)} %shard_map.79), channel_id=1, source_target_pairs={{0,16},{16,0},{32,48},{48,32},{64,80},{80,64},{96,112},{112,96},{1... | collective-permute-start | bytes 442376 | tf_op jit(solution)/shard_map/ppermute | solution.py:342
  20.3 5.9 %collective-permute-start.5 = (bf16[32,2432]{1,0:T(8,128)(2,1)S(1)}, bf16[32,2432]{1,0:T(8,128)(2,1)S(1)}, u32[]{:S(2)}, u32[]{:S(2)}) collective-permute-start(bf16[32,2432]{1,0:T(8,128)(2,1)S(1)} %get-tuple-element.73), channel_id=1, source_target_pairs={{0,240},{16,32},{32,16},{48,64},{64,48},{80,96},{96,80},{112,128},... | collective-permute-start | bytes 466952 | tf_op jit(solution)/shard_map/ppermute | solution.py:336
  20.7 5.0 %collective-permute-start.4 = (bf16[32,2304]{1,0:T(8,128)(2,1)S(1)}, bf16[32,2304]{1,0:T(8,128)(2,1)S(1)}, u32[]{:S(2)}, u32[]{:S(2)}) collective-permute-start(bf16[32,2304]{1,0:T(8,128)(2,1)S(1)} %shard_map.83), channel_id=1, source_target_pairs={{0,16},{16,0},{32,48},{48,32},{64,80},{80,64},{96,112},{112,96},{1... | collective-permute-start | bytes 442376 | tf_op jit(solution)/shard_map/ppermute | solution.py:342
  26.8 6.1 %collective-permute-start.7 = (bf16[32,2432]{1,0:T(8,128)(2,1)S(1)}, bf16[32,2432]{1,0:T(8,128)(2,1)S(1)}, u32[]{:S(2)}, u32[]{:S(2)}) collective-permute-start(bf16[32,2432]{1,0:T(8,128)(2,1)S(1)} %get-tuple-element.77), channel_id=1, source_target_pairs={{0,240},{16,32},{32,16},{48,64},{64,48},{80,96},{96,80},{112,128},... | collective-permute-start | bytes 466952 | tf_op jit(solution)/shard_map/ppermute | solution.py:336
  27.2 5.2 %collective-permute-start.6 = (bf16[32,2304]{1,0:T(8,128)(2,1)S(1)}, bf16[32,2304]{1,0:T(8,128)(2,1)S(1)}, u32[]{:S(2)}, u32[]{:S(2)}) collective-permute-start(bf16[32,2304]{1,0:T(8,128)(2,1)S(1)} %shard_map.87), channel_id=1, source_target_pairs={{0,16},{16,0},{32,48},{48,32},{64,80},{80,64},{96,112},{112,96},{1... | collective-permute-start | bytes 442376 | tf_op jit(solution)/shard_map/ppermute | solution.py:342
  33.5 5.8 %collective-permute-start.9 = (bf16[32,2432]{1,0:T(8,128)(2,1)S(1)}, bf16[32,2432]{1,0:T(8,128)(2,1)S(1)}, u32[]{:S(2)}, u32[]{:S(2)}) collective-permute-start(bf16[32,2432]{1,0:T(8,128)(2,1)S(1)} %get-tuple-element.81), channel_id=1, source_target_pairs={{0,240},{16,32},{32,16},{48,64},{64,48},{80,96},{96,80},{112,128},... | collective-permute-start | bytes 466952 | tf_op jit(solution)/shard_map/ppermute | solution.py:336
  33.9 4.8 %collective-permute-start.8 = (bf16[32,2304]{1,0:T(8,128)(2,1)S(1)}, bf16[32,2304]{1,0:T(8,128)(2,1)S(1)}, u32[]{:S(2)}, u32[]{:S(2)}) collective-permute-start(bf16[32,2304]{1,0:T(8,128)(2,1)S(1)} %shard_map.91), channel_id=1, source_target_pairs={{0,16},{16,0},{32,48},{48,32},{64,80},{80,64},{96,112},{112,96},{1... | collective-permute-start | bytes 442376 | tf_op jit(solution)/shard_map/ppermute | solution.py:342
  39.9 6.0 %collective-permute-start.11 = (bf16[32,2432]{1,0:T(8,128)(2,1)S(1)}, bf16[32,2432]{1,0:T(8,128)(2,1)S(1)}, u32[]{:S(2)}, u32[]{:S(2)}) collective-permute-start(bf16[32,2432]{1,0:T(8,128)(2,1)S(1)} %get-tuple-element.86), channel_id=1, source_target_pairs={{0,240},{16,32},{32,16},{48,64},{64,48},{80,96},{96,80},{112,128},... | collective-permute-start | bytes 466952 | tf_op jit(solution)/shard_map/ppermute | solution.py:336
  40.3 5.0 %collective-permute-start.10 = (bf16[32,2304]{1,0:T(8,128)(2,1)S(1)}, bf16[32,2304]{1,0:T(8,128)(2,1)S(1)}, u32[]{:S(2)}, u32[]{:S(2)}) collective-permute-start(bf16[32,2304]{1,0:T(8,128)(2,1)S(1)} %shard_map.95), channel_id=1, source_target_pairs={{0,16},{16,0},{32,48},{48,32},{64,80},{80,64},{96,112},{112,96},{1... | collective-permute-start | bytes 442376 | tf_op jit(solution)/shard_map/ppermute | solution.py:342

commit v6 on v5

--- a/solution.py
+++ b/solution.py
@@ -48,39 +48,46 @@
         yield outs, dot(x[:, ins], block, contract)
 
 
-def write_payload(x_ref, w_ref, rim_ref, side, out_ref):
+def write_payload(x_ref, w_ref, rim_ref, side, rows_ref, terms_ref):
     wide = x_ref.shape[2]
     cols = rim_ref.shape[2]
     edge = slice(0, cols) if side == FAR else slice(wide - cols, wide)
     which = side - 1
-    out_ref[:, 0:wide] = x_ref[1].astype(jnp.bfloat16)
+    rows_ref[:, 0:wide] = x_ref[1].astype(jnp.bfloat16)
     rim = x_ref[0, :, edge] * rim_ref[which, 0:1, :]
     rim += pltpu.roll(x_ref[1, :, edge] * rim_ref[which, 1:2, :], cols - 1, axis=1)
     high = rim.astype(jnp.bfloat16)
-    out_ref[:, 2 * wide : 2 * wide + cols] = high
-    out_ref[:, 2 * wide + cols : 2 * wide + 2 * cols] = (rim - high.astype(jnp.float32)).astype(
-        jnp.bfloat16
-    )
-    spare = out_ref.shape[1] - 2 * wide - 2 * cols
-    if spare:
-        out_ref[:, 2 * wide + 2 * cols :] = jnp.zeros((out_ref.shape[0], spare), jnp.bfloat16)
+    rows_ref[:, wide : wide + cols] = high
+    rows_ref[:, wide + cols :] = (rim - high.astype(jnp.float32)).astype(jnp.bfloat16)
     first = x_ref[0].astype(jnp.bfloat16)
     for outs, term in products(first, w_ref, side, 0, cols):
-        out_ref[:, wide + outs.start : wide + outs.stop] = term.astype(jnp.bfloat16)
-
-
-def add_received(scale, got_ref, w_ref, contract, rim_ref, side, from_ref, to_ref):
+        terms_ref[:, outs] = term.astype(jnp.bfloat16)
+
+
+def write_far(x_ref, w_ref, rim_ref, far_ref):
+    cut = far_ref.shape[1] - x_ref.shape[2]
+    write_payload(x_ref, w_ref, rim_ref, FAR, far_ref.at[:, 0:cut], far_ref.at[:, cut:])
+
+
+def add_received(scale, rows_ref, terms_ref, w_ref, contract, rim_ref, side, from_ref, to_ref):
     wide = to_ref.shape[2]
     cols = rim_ref.shape[2]
     edge = slice(0, cols) if side == FAR else slice(wide - cols, wide)
     which = side - 1
-    to_ref[1] = from_ref[1] + scale * got_ref[:, wide : 2 * wide].astype(jnp.float32)
-    for outs, term in products(got_ref[:, 0:wide], w_ref, side, contract, cols):
+    to_ref[1] = from_ref[1] + scale * terms_ref[...].astype(jnp.float32)
+    for outs, term in products(rows_ref[:, 0:wide], w_ref, side, contract, cols):
         to_ref[0, :, outs] = from_ref[0, :, outs] + scale * term
-    rim = got_ref[:, 2 * wide : 2 * wide + cols].astype(jnp.float32)
-    rim += got_ref[:, 2 * wide + cols : 2 * wide + 2 * cols].astype(jnp.float32)
+    rim = rows_ref[:, wide : wide + cols].astype(jnp.float32)
+    rim += rows_ref[:, wide + cols :].astype(jnp.float32)
     to_ref[0, :, edge] += scale * (rim * rim_ref[which, 0:1, :])
     to_ref[1, :, edge] += scale * (pltpu.roll(rim, 1, axis=1) * rim_ref[which, 1:2, :])
+
+
+def add_far(scale, got_ref, turned_ref, rim_ref, from_ref, to_ref):
+    cut = got_ref.shape[1] - to_ref.shape[2]
+    add_received(
+        scale, got_ref.at[:, 0:cut], got_ref.at[:, cut:], turned_ref, 0, rim_ref, FAR, from_ref, to_ref
+    )
 
 
 def settle(totals, side, w_ref, cols):
@@ -197,17 +204,17 @@
                 at = jnp.where(slot >= 0, REACH + (1 - 2 * here) * away, offsets)
                 totals[place][at] += blocks[row, k].astype(jnp.float32)
     settle(totals, FAR, w_ref, cols)
-    write_payload(x_ref, w_ref, rim_ref, FAR, far_ref)
-
-
-def to_mate(x_ref, w_ref, rim_ref, mate_ref):
-    write_payload(x_ref, w_ref, rim_ref, MATE, mate_ref)
+    write_far(x_ref, w_ref, rim_ref, far_ref)
+
+
+def to_mate(x_ref, w_ref, rim_ref, rows_ref, terms_ref):
+    write_payload(x_ref, w_ref, rim_ref, MATE, rows_ref, terms_ref)
 
 
 def to_mate_first(x_ref, rim_ref, *refs):
-    *totals, mate_ref, w_ref = refs
+    *totals, rows_ref, terms_ref, w_ref = refs
     settle(totals, MATE, w_ref, rim_ref.shape[2])
-    write_payload(x_ref, w_ref, rim_ref, MATE, mate_ref)
+    write_payload(x_ref, w_ref, rim_ref, MATE, rows_ref, terms_ref)
 
 
 def inner(order, *refs):
@@ -251,12 +258,12 @@
             sum_ref[layer, :, here] = term
 
 
-def from_mate(scale, part_ref, w_ref, rim_ref, got_ref, *refs):
+def from_mate(scale, part_ref, w_ref, rim_ref, rows_ref, terms_ref, *refs):
     if len(refs) > 1:
         far_ref, sum_ref, *turned = refs
     else:
         (sum_ref,), turned = refs, []
-    add_received(scale, got_ref, w_ref, 1, rim_ref, MATE, part_ref, sum_ref)
+    add_received(scale, rows_ref, terms_ref, w_ref, 1, rim_ref, MATE, part_ref, sum_ref)
     if turned:
         step = PAIR * rim_ref.shape[2]
         groups = sum_ref.shape[2] // step
@@ -268,14 +275,14 @@
 
 
 def outer(scale, sum_ref, w_ref, turned_ref, rim_ref, got_ref, x_ref, far_ref):
-    add_received(scale, got_ref, turned_ref, 0, rim_ref, FAR, sum_ref, x_ref)
-    write_payload(x_ref, w_ref, rim_ref, FAR, far_ref)
+    add_far(scale, got_ref, turned_ref, rim_ref, sum_ref, x_ref)
+    write_far(x_ref, w_ref, rim_ref, far_ref)
 
 
 def finish(scale, degree, sum_ref, filt_ref, turned_ref, rim_ref, weight_ref, got_ref, out_ref, x_ref):
     cols = rim_ref.shape[2]
     rows = out_ref.shape[1]
-    add_received(scale, got_ref, turned_ref, 0, rim_ref, FAR, sum_ref, x_ref)
+    add_far(scale, got_ref, turned_ref, rim_ref, sum_ref, x_ref)
     flip = lax.rem(lax.axis_index("tile"), 2)
     for layer in range(2):
         for place in range(rows):
@@ -308,12 +315,12 @@
 
     field = held((2, count, wide), jnp.float32)
     payload = held((count, 2 * wide + 2 * cols), jnp.bfloat16)
-    longer = held((count, 2 * wide + 3 * cols), jnp.bfloat16)
+    parts = [held((count, wide + 2 * cols), jnp.bfloat16), held((count, wide), jnp.bfloat16)]
     matrix = held((wide, wide), jnp.bfloat16)
     x, w_far, coef, rim, weight, far, *totals = call(
         prepare,
         [field, matrix, held((2, 5, rows, cols), jnp.float32),
-         held((2, 2, cols), jnp.float32), held((degree + 1, cols), jnp.float32), longer,
+         held((2, 2, cols), jnp.float32), held((degree + 1, cols), jnp.float32), payload,
          *[held((2 * REACH + 2, cols, cols), jnp.float32)] * rows],
         [outside(v) for v in (partner, states, onsite, hop_row, hop_up, coefs, coupling)],
         scratch=[
@@ -335,11 +342,11 @@
         scale = 1.0 / 12.0 if order == 0 else 2.0 / 12.0
         got_far = lax.ppermute(far, "tile", far_pairs)
         if order == 0:
-            mate, w_mate = call(to_mate_first, [payload, matrix], [x, rim, *totals])
+            *mate, w_mate = call(to_mate_first, [*parts, matrix], [x, rim, *totals])
             w_mate = near(w_mate)
         else:
-            (mate,) = call(to_mate, [payload], [x, w_mate, rim])
-        got_mate = lax.ppermute(mate, "tile", mate_pairs)
+            mate = call(to_mate, parts, [x, w_mate, rim])
+        got_mate = [near(lax.ppermute(part, "tile", mate_pairs)) for part in mate]
         if order == 0:
             part, filt, w_local = call(
                 functools.partial(inner, order), [field, field, matrix], [x, coef, weight, *totals]
@@ -354,7 +361,7 @@
         part, *turned_now = call(
             functools.partial(from_mate, scale),
             [field, matrix] if order == 0 else [field],
-            [near(part), w_mate, rim, near(got_mate)] + ([w_far] if order == 0 else []),
+            [near(part), w_mate, rim, *got_mate] + ([w_far] if order == 0 else []),
             flops=0,
         )
         if order == 0:
@@ -363,7 +370,7 @@
         if order < degree - 1:
             x, far = call(
                 functools.partial(outer, scale),
-                [field, longer],
+                [field, payload],
                 [near(part), w_far, turned, rim, near(got_far)],
             )
             x = near(x)

time: 47 us -> 46.9 us (level)
    ppermute x6 -> x12, starting transfers between devices: 23 us -> 22.5 us  [body(): got_mate = [near(lax.ppermute(part, 'tile', mate_pairs)) for part in mate]]
  transfers between devices with their start and end apart: 12 -> 18, of which waited for: 0 -> 0; matrix products, arithmetic and copies ran while one was open for 0% -> 0% of each run, Pallas kernels for 25% -> 25%
where the time goes in v6:
time: 46.9 us; the launch traced here: 46.8 us
  starting transfers between devices  26.2 us (56%)
  Pallas kernels  20.2 us (43%)
    ppermute x12, starting transfers between devices, body(): got_mate = [near(lax.ppermute(part, 'tile', mate_pairs)) for part in mate]  22.5 us
    pallas_call x25, Pallas kernels, call(): pl.pallas_call(kernel, out_shape=outs, in_specs=specs or [IN_VMEM] * len(...  20.2 us
    ppermute x6, starting transfers between devices, body(): got_far = lax.ppermute(far, 'tile', far_pairs)  3.72 us
  transfers between devices with their start and end apart: 18, of which 0 were waited for; matrix products, arithmetic and copies ran while one was open for 0% of the time, Pallas kernels for 25%

profile of v6, /device:TPU:1, one launch (start us, length us, event | category | flops | bytes accessed | tf_op | source)
XLA Modules:
  0.0 46.8 jit_solution(57907893106351233)
XLA Ops:
  0.0 4.3 %shard_map.73 = (f32[2,32,1024]{2,1,0:T(8,128)S(1)}, bf16[1024,1024]{1,0:T(8,128)(2,1)S(1)}, f32[2,5,8,128]{3,2,1,0:T(8,128)S(1)}, f32[2,2,128]{2,1,0:T(2,128)S(...) custom-call(s32[8,16]{1,0:T(8,128)} %partner_hbm.1, ...), custom_call_target="tpu_custom_call" | custom-call | flops 1048576 | tf_op jit(solution)/shard_map/pallas_call | solution.py:296
  4.3 3.1 %collective-permute-start.2 = (bf16[32,2304]{1,0:T(8,128)(2,1)S(1)}, bf16[32,2304]{1,0:T(8,128)(2,1)S(1)}, u32[]{:S(2)}, u32[]{:S(2)}) collective-permute-start(bf16[32,2304]{1,0:T(8,128)(2,1)S(1)} %get-tuple-element.76), channel_id=1, source_target_pairs={{0,240},{16,32},{32,16},{48,64},{64,48},{80,96},{96,80},{112,128},... | collective-permute-start | bytes 442376 | tf_op jit(solution)/shard_map/ppermute | solution.py:343
  7.4 0.4 shard_map.75
  7.8 3.8 %collective-permute-start = (bf16[32,1280]{1,0:T(8,128)(2,1)S(1)}, bf16[32,1280]{1,0:T(8,128)(2,1)S(1)}, u32[]{:S(2)}, u32[]{:S(2)}) collective-permute-start(bf16[32,1280]{1,0:T(8,128)(2,1)S(1)} %get-tuple-element.71), channel_id=1, source_target_pairs={{0,16},{16,0},{32,48},{48,32},{64,80},{80,64},{96,112},{112,96},{1... | collective-permute-start | bytes 245768 | tf_op jit(solution)/shard_map/ppermute | solution.py:349
  11.7 0.1 collective-permute-start.1
  11.8 1.2 %shard_map.74 = (f32[2,32,1024]{2,1,0:T(8,128)S(1)}, f32[2,32,1024]{2,1,0:T(8,128)S(1)}, bf16[1024,1024]{1,0:T(8,128)(2,1)S(1)}) custom-call(f32[2,32,1024]{2,1,0:T(8,128)S(1)} %get-tuple-element.57.refs_0_.x_ref.refs_1_, f32[2,5,8,128]{3,2,1,0:T(8,128)S(1)} %get-tuple-element.58.refs_1_.refs_4_, f32[7,128]{1,0:T(8,128)S(1)} %get-tuple-element.59.refs_2_.refs_5_.weight_ref, ...), custom_call_target="tpu_custom_call" | custom-call | flops 1048576 | tf_op jit(solution)/shard_map/pallas_call | solution.py:296
  13.0 0.5 %shard_map.76 = (f32[2,32,1024]{2,1,0:T(8,128)S(1)}, bf16[1024,1024]{1,0:T(8,128)(2,1)S(1)}) custom-call(f32[2,32,1024]{2,1,0:T(8,128)S(1)} %get-tuple-element.68.part_ref, bf16[1024,1024]{1,0:T(8,128)(2,1)S(1)} %get-tuple-element.70.w_ref, f32[2,2,128]{2,1,0:T(2,128)S(1)} %get-tuple-element.69.rim_ref, bf16[32,1280]{1,0:T(8,128)(2,1)S(1)} %collective-permute-done.rows_ref, ...), custom_call_target="tpu_custom_call" | custom-call | tf_op jit(solution)/shard_map/pallas_call | solution.py:296
  13.5 0.6 %shard_map.77 = (f32[2,32,1024]{2,1,0:T(8,128)S(1)}, bf16[32,2304]{1,0:T(8,128)(2,1)S(1)}) custom-call(f32[2,32,1024]{2,1,0:T(8,128)S(1)} %get-tuple-element.74.sum_ref, bf16[1024,1024]{1,0:T(8,128)(2,1)S(1)} %get-tuple-element.73.refs_0_.w_ref, bf16[1024,1024]{1,0:T(8,128)(2,1)S(1)} %get-tuple-element.75.turned_ref, ...), custom_call_target="tpu_custom_call" | custom-call | flops 1048576 | tf_op jit(solution)/shard_map/pallas_call | solution.py:296
  14.1 0.1 collective-permute-start.5
  14.2 0.3 shard_map.79
  14.5 3.4 %collective-permute-start.3 = (bf16[32,1280]{1,0:T(8,128)(2,1)S(1)}, bf16[32,1280]{1,0:T(8,128)(2,1)S(1)}, u32[]{:S(2)}, u32[]{:S(2)}) collective-permute-start(bf16[32,1280]{1,0:T(8,128)(2,1)S(1)} %get-tuple-element.81), channel_id=1, source_target_pairs={{0,16},{16,0},{32,48},{48,32},{64,80},{80,64},{96,112},{112,96},{1... | collective-permute-start | bytes 245768 | tf_op jit(solution)/shard_map/ppermute | solution.py:349
  18.0 0.1 collective-permute-start.4
  18.1 1.1 %shard_map.78 = (f32[2,32,1024]{2,1,0:T(8,128)S(1)}, f32[2,32,1024]{2,1,0:T(8,128)S(1)}) custom-call(f32[2,32,1024]{2,1,0:T(8,128)S(1)} %get-tuple-element.77.refs_0_.x_ref.refs_1_, f32[2,32,1024]{2,1,0:T(8,128)S(1)} %get-tuple-element.57.refs_0_.x_ref.refs_1_, f32[2,32,1024]{2,1,0:T(8,128)S(1)} %get-tuple-element.78.refs_2_, ...), custom_call_target="tpu_custom_call" | custom-call | flops 1048576 | tf_op jit(solution)/shard_map/pallas_call | solution.py:296
  19.2 0.0 collective-permute-done.4.terms_ref
  19.2 0.5 %shard_map.80.sum_ref = f32[2,32,1024]{2,1,0:T(8,128)S(1)} custom-call(f32[2,32,1024]{2,1,0:T(8,128)S(1)} %get-tuple-element.80.part_ref, bf16[1024,1024]{1,0:T(8,128)(2,1)S(1)} %get-tuple-element.70.w_ref, f32[2,2,128]{2,1,0:T(2,128)S(1)} %get-tuple-element.69.rim_ref, bf16[32,1280]{1,0:T(8,128)(2,1)S(1)} %collective-permute-done.3.rows_ref, ...), custom_call_target="tpu_custom_call" | custom-call | tf_op jit(solution)/shard_map/pallas_call | solution.py:296
  19.8 0.6 %shard_map.81 = (f32[2,32,1024]{2,1,0:T(8,128)S(1)}, bf16[32,2304]{1,0:T(8,128)(2,1)S(1)}) custom-call(f32[2,32,1024]{2,1,0:T(8,128)S(1)} %shard_map.80.sum_ref, bf16[1024,1024]{1,0:T(8,128)(2,1)S(1)} %get-tuple-element.73.refs_0_.w_ref, bf16[1024,1024]{1,0:T(8,128)(2,1)S(1)} %get-tuple-element.75.turned_ref, f32[2,2,128]{2,1,0:T(2,128)S(1)} %get-tuple-element.69.rim_ref, ...), custom_call_target="tpu_custom_call" | custom-call | flops 1048576 | tf_op jit(solution)/shard_map/pallas_call | solution.py:296
  20.4 0.1 collective-permute-start.8
  20.4 0.3 shard_map.83
  20.8 3.7 %collective-permute-start.6 = (bf16[32,1280]{1,0:T(8,128)(2,1)S(1)}, bf16[32,1280]{1,0:T(8,128)(2,1)S(1)}, u32[]{:S(2)}, u32[]{:S(2)}) collective-permute-start(bf16[32,1280]{1,0:T(8,128)(2,1)S(1)} %get-tuple-element.87), channel_id=1, source_target_pairs={{0,16},{16,0},{32,48},{48,32},{64,80},{80,64},{96,112},{112,96},{1... | collective-permute-start | bytes 245768 | tf_op jit(solution)/shard_map/ppermute | solution.py:349
  24.4 0.1 collective-permute-start.7
  24.5 1.1 %shard_map.82 = (f32[2,32,1024]{2,1,0:T(8,128)S(1)}, f32[2,32,1024]{2,1,0:T(8,128)S(1)}) custom-call(f32[2,32,1024]{2,1,0:T(8,128)S(1)} %get-tuple-element.84.refs_0_.x_ref.refs_1_, f32[2,32,1024]{2,1,0:T(8,128)S(1)} %get-tuple-element.77.refs_0_.x_ref.refs_1_, f32[2,32,1024]{2,1,0:T(8,128)S(1)} %get-tuple-element.85.refs_2_, ...), custom_call_target="tpu_custom_call" | custom-call | flops 1048576 | tf_op jit(solution)/shard_map/pallas_call | solution.py:296
  25.6 0.0 collective-permute-done.7.terms_ref
  25.7 0.5 %shard_map.84.sum_ref = f32[2,32,1024]{2,1,0:T(8,128)S(1)} custom-call(f32[2,32,1024]{2,1,0:T(8,128)S(1)} %get-tuple-element.86.part_ref, bf16[1024,1024]{1,0:T(8,128)(2,1)S(1)} %get-tuple-element.70.w_ref, f32[2,2,128]{2,1,0:T(2,128)S(1)} %get-tuple-element.69.rim_ref, bf16[32,1280]{1,0:T(8,128)(2,1)S(1)} %collective-permute-done.6.rows_ref, ...), custom_call_target="tpu_custom_call" | custom-call | tf_op jit(solution)/shard_map/pallas_call | solution.py:296
  26.2 0.6 %shard_map.85 = (f32[2,32,1024]{2,1,0:T(8,128)S(1)}, bf16[32,2304]{1,0:T(8,128)(2,1)S(1)}) custom-call(f32[2,32,1024]{2,1,0:T(8,128)S(1)} %shard_map.84.sum_ref, bf16[1024,1024]{1,0:T(8,128)(2,1)S(1)} %get-tuple-element.73.refs_0_.w_ref, bf16[1024,1024]{1,0:T(8,128)(2,1)S(1)} %get-tuple-element.75.turned_ref, f32[2,2,128]{2,1,0:T(2,128)S(1)} %get-tuple-element.69.rim_ref, ...), custom_call_target="tpu_custom_call" | custom-call | flops 1048576 | tf_op jit(solution)/shard_map/pallas_call | solution.py:296
  26.8 0.3 collective-permute-start.11
  27.1 0.3 shard_map.87
  27.4 3.7 %collective-permute-start.9 = (bf16[32,1280]{1,0:T(8,128)(2,1)S(1)}, bf16[32,1280]{1,0:T(8,128)(2,1)S(1)}, u32[]{:S(2)}, u32[]{:S(2)}) collective-permute-start(bf16[32,1280]{1,0:T(8,128)(2,1)S(1)} %get-tuple-element.93), channel_id=1, source_target_pairs={{0,16},{16,0},{32,48},{48,32},{64,80},{80,64},{96,112},{112,96},{1... | collective-permute-start | bytes 245768 | tf_op jit(solution)/shard_map/ppermute | solution.py:349
  31.1 0.1 collective-permute-start.10
  31.2 1.1 %shard_map.86 = (f32[2,32,1024]{2,1,0:T(8,128)S(1)}, f32[2,32,1024]{2,1,0:T(8,128)S(1)}) custom-call(f32[2,32,1024]{2,1,0:T(8,128)S(1)} %get-tuple-element.90.refs_0_.x_ref.refs_1_, f32[2,32,1024]{2,1,0:T(8,128)S(1)} %get-tuple-element.84.refs_0_.x_ref.refs_1_, f32[2,32,1024]{2,1,0:T(8,128)S(1)} %get-tuple-element.91.refs_2_, ...), custom_call_target="tpu_custom_call" | custom-call | flops 1048576 | tf_op jit(solution)/shard_map/pallas_call | solution.py:296
  32.3 0.0 collective-permute-done.10.terms_ref
  32.3 0.5 %shard_map.88.sum_ref = f32[2,32,1024]{2,1,0:T(8,128)S(1)} custom-call(f32[2,32,1024]{2,1,0:T(8,128)S(1)} %get-tuple-element.92.part_ref, bf16[1024,1024]{1,0:T(8,128)(2,1)S(1)} %get-tuple-element.70.w_ref, f32[2,2,128]{2,1,0:T(2,128)S(1)} %get-tuple-element.69.rim_ref, bf16[32,1280]{1,0:T(8,128)(2,1)S(1)} %collective-permute-done.9.rows_ref, ...), custom_call_target="tpu_custom_call" | custom-call | tf_op jit(solution)/shard_map/pallas_call | solution.py:296
  32.8 0.6 %shard_map.89 = (f32[2,32,1024]{2,1,0:T(8,128)S(1)}, bf16[32,2304]{1,0:T(8,128)(2,1)S(1)}) custom-call(f32[2,32,1024]{2,1,0:T(8,128)S(1)} %shard_map.88.sum_ref, bf16[1024,1024]{1,0:T(8,128)(2,1)S(1)} %get-tuple-element.73.refs_0_.w_ref, bf16[1024,1024]{1,0:T(8,128)(2,1)S(1)} %get-tuple-element.75.turned_ref, f32[2,2,128]{2,1,0:T(2,128)S(1)} %get-tuple-element.69.rim_ref, ...), custom_call_target="tpu_custom_call" | custom-call | flops 1048576 | tf_op jit(solution)/shard_map/pallas_call | solution.py:296
  33.4 0.1 collective-permute-start.14
  33.5 0.3 shard_map.91
  33.9 3.7 %collective-permute-start.12 = (bf16[32,1280]{1,0:T(8,128)(2,1)S(1)}, bf16[32,1280]{1,0:T(8,128)(2,1)S(1)}, u32[]{:S(2)}, u32[]{:S(2)}) collective-permute-start(bf16[32,1280]{1,0:T(8,128)(2,1)S(1)} %get-tuple-element.99), channel_id=1, source_target_pairs={{0,16},{16,0},{32,48},{48,32},{64,80},{80,64},{96,112},{112,96},{1... | collective-permute-start | bytes 245768 | tf_op jit(solution)/shard_map/ppermute | solution.py:349
  37.5 0.1 collective-permute-start.13
  37.6 1.1 %shard_map.90 = (f32[2,32,1024]{2,1,0:T(8,128)S(1)}, f32[2,32,1024]{2,1,0:T(8,128)S(1)}) custom-call(f32[2,32,1024]{2,1,0:T(8,128)S(1)} %get-tuple-element.96.refs_0_.x_ref.refs_1_, f32[2,32,1024]{2,1,0:T(8,128)S(1)} %get-tuple-element.90.refs_0_.x_ref.refs_1_, f32[2,32,1024]{2,1,0:T(8,128)S(1)} %get-tuple-element.97.refs_2_, ...), custom_call_target="tpu_custom_call" | custom-call | flops 1048576 | tf_op jit(solution)/shard_map/pallas_call | solution.py:296
  38.7 0.0 collective-permute-done.13.terms_ref
  38.8 0.5 %shard_map.92.sum_ref = f32[2,32,1024]{2,1,0:T(8,128)S(1)} custom-call(f32[2,32,1024]{2,1,0:T(8,128)S(1)} %get-tuple-element.98.part_ref, bf16[1024,1024]{1,0:T(8,128)(2,1)S(1)} %get-tuple-element.70.w_ref, f32[2,2,128]{2,1,0:T(2,128)S(1)} %get-tuple-element.69.rim_ref, bf16[32,1280]{1,0:T(8,128)(2,1)S(1)} %collective-permute-done.12.rows_ref, ...), custom_call_target="tpu_custom_call" | custom-call | tf_op jit(solution)/shard_map/pallas_call | solution.py:296
  39.3 0.6 %shard_map.93 = (f32[2,32,1024]{2,1,0:T(8,128)S(1)}, bf16[32,2304]{1,0:T(8,128)(2,1)S(1)}) custom-call(f32[2,32,1024]{2,1,0:T(8,128)S(1)} %shard_map.92.sum_ref, bf16[1024,1024]{1,0:T(8,128)(2,1)S(1)} %get-tuple-element.73.refs_0_.w_ref, bf16[1024,1024]{1,0:T(8,128)(2,1)S(1)} %get-tuple-element.75.turned_ref, f32[2,2,128]{2,1,0:T(2,128)S(1)} %get-tuple-element.69.rim_ref, ...), custom_call_target="tpu_custom_call" | custom-call | flops 1048576 | tf_op jit(solution)/shard_map/pallas_call | solution.py:296
  39.9 0.1 collective-permute-start.17
  40.0 0.3 shard_map.95
  40.3 3.7 %collective-permute-start.15 = (bf16[32,1280]{1,0:T(8,128)(2,1)S(1)}, bf16[32,1280]{1,0:T(8,128)(2,1)S(1)}, u32[]{:S(2)}, u32[]{:S(2)}) collective-permute-start(bf16[32,1280]{1,0:T(8,128)(2,1)S(1)} %get-tuple-element.105), channel_id=1, source_target_pairs={{0,16},{16,0},{32,48},{48,32},{64,80},{80,64},{96,112},{112,96},{1... | collective-permute-start | bytes 245768 | tf_op jit(solution)/shard_map/ppermute | solution.py:349
  44.0 0.1 collective-permute-start.16
  44.1 1.1 %shard_map.94 = (f32[2,32,1024]{2,1,0:T(8,128)S(1)}, f32[2,32,1024]{2,1,0:T(8,128)S(1)}) custom-call(f32[2,32,1024]{2,1,0:T(8,128)S(1)} %get-tuple-element.102.refs_0_.x_ref, f32[2,32,1024]{2,1,0:T(8,128)S(1)} %get-tuple-element.96.refs_0_.x_ref.refs_1_, f32[2,32,1024]{2,1,0:T(8,128)S(1)} %get-tuple-element.103.refs_2_, ...), custom_call_target="tpu_custom_call" | custom-call | flops 1048576 | tf_op jit(solution)/shard_map/pallas_call | solution.py:296
  45.2 0.0 collective-permute-done.16.terms_ref
  45.2 0.5 %shard_map.96.sum_ref = f32[2,32,1024]{2,1,0:T(8,128)S(1)} custom-call(f32[2,32,1024]{2,1,0:T(8,128)S(1)} %get-tuple-element.104.part_ref, bf16[1024,1024]{1,0:T(8,128)(2,1)S(1)} %get-tuple-element.70.w_ref, f32[2,2,128]{2,1,0:T(2,128)S(1)} %get-tuple-element.69.rim_ref, bf16[32,1280]{1,0:T(8,128)(2,1)S(1)} %collective-permute-done.15.rows_ref, ...), custom_call_target="tpu_custom_call" | custom-call | tf_op jit(solution)/shard_map/pallas_call | solution.py:296
  45.7 1.1 %shard_map.97 = f32[2,8,32,128]{3,2,1,0:T(8,128)} custom-call(f32[2,32,1024]{2,1,0:T(8,128)S(1)} %shard_map.96.sum_ref, f32[2,32,1024]{2,1,0:T(8,128)S(1)} %get-tuple-element.107.filt_ref, bf16[1024,1024]{1,0:T(8,128)(2,1)S(1)} %get-tuple-element.75.turned_ref, f32[2,2,128]{2,1,0:T(2,128)S(1)} %get-tuple-element.69.rim_ref, ...), custom_call_target="tpu_custom_call" | custom-call | flops 1048576 | tf_op jit(solution)/shard_map/pallas_call | solution.py:296
  (13 shorter events, 0.0 us)
Async XLA Ops:
  4.3 9.2 %collective-permute-start.2 = (bf16[32,2304]{1,0:T(8,128)(2,1)S(1)}, bf16[32,2304]{1,0:T(8,128)(2,1)S(1)}, u32[]{:S(2)}, u32[]{:S(2)}) collective-permute-start(bf16[32,2304]{1,0:T(8,128)(2,1)S(1)} %get-tuple-element.76), channel_id=1, source_target_pairs={{0,240},{16,32},{32,16},{48,64},{64,48},{80,96},{96,80},{112,128},... | collective-permute-start | bytes 442376 | tf_op jit(solution)/shard_map/ppermute | solution.py:343
  7.8 5.1 %collective-permute-start = (bf16[32,1280]{1,0:T(8,128)(2,1)S(1)}, bf16[32,1280]{1,0:T(8,128)(2,1)S(1)}, u32[]{:S(2)}, u32[]{:S(2)}) collective-permute-start(bf16[32,1280]{1,0:T(8,128)(2,1)S(1)} %get-tuple-element.71), channel_id=1, source_target_pairs={{0,16},{16,0},{32,48},{48,32},{64,80},{80,64},{96,112},{112,96},{1... | collective-permute-start | bytes 245768 | tf_op jit(solution)/shard_map/ppermute | solution.py:349
  11.7 1.3 %collective-permute-start.1 = (bf16[32,1024]{1,0:T(8,128)(2,1)S(1)}, bf16[32,1024]{1,0:T(8,128)(2,1)S(1)}, u32[]{:S(2)}, u32[]{:S(2)}) collective-permute-start(bf16[32,1024]{1,0:T(8,128)(2,1)S(1)} %get-tuple-element.72), channel_id=1, source_target_pairs={{0,16},{16,0},{32,48},{48,32},{64,80},{80,64},{96,112},{112,96},{1... | collective-permute-start | bytes 196616 | tf_op jit(solution)/shard_map/ppermute | solution.py:349
  14.1 5.6 %collective-permute-start.5 = (bf16[32,2304]{1,0:T(8,128)(2,1)S(1)}, bf16[32,2304]{1,0:T(8,128)(2,1)S(1)}, u32[]{:S(2)}, u32[]{:S(2)}) collective-permute-start(bf16[32,2304]{1,0:T(8,128)(2,1)S(1)} %get-tuple-element.83), channel_id=1, source_target_pairs={{0,240},{16,32},{32,16},{48,64},{64,48},{80,96},{96,80},{112,128},... | collective-permute-start | bytes 442376 | tf_op jit(solution)/shard_map/ppermute | solution.py:343
  14.5 4.7 %collective-permute-start.3 = (bf16[32,1280]{1,0:T(8,128)(2,1)S(1)}, bf16[32,1280]{1,0:T(8,128)(2,1)S(1)}, u32[]{:S(2)}, u32[]{:S(2)}) collective-permute-start(bf16[32,1280]{1,0:T(8,128)(2,1)S(1)} %get-tuple-element.81), channel_id=1, source_target_pairs={{0,16},{16,0},{32,48},{48,32},{64,80},{80,64},{96,112},{112,96},{1... | collective-permute-start | bytes 245768 | tf_op jit(solution)/shard_map/ppermute | solution.py:349
  18.0 1.3 %collective-permute-start.4 = (bf16[32,1024]{1,0:T(8,128)(2,1)S(1)}, bf16[32,1024]{1,0:T(8,128)(2,1)S(1)}, u32[]{:S(2)}, u32[]{:S(2)}) collective-permute-start(bf16[32,1024]{1,0:T(8,128)(2,1)S(1)} %get-tuple-element.82), channel_id=1, source_target_pairs={{0,16},{16,0},{32,48},{48,32},{64,80},{80,64},{96,112},{112,96},{1... | collective-permute-start | bytes 196616 | tf_op jit(solution)/shard_map/ppermute | solution.py:349
  20.4 5.8 %collective-permute-start.8 = (bf16[32,2304]{1,0:T(8,128)(2,1)S(1)}, bf16[32,2304]{1,0:T(8,128)(2,1)S(1)}, u32[]{:S(2)}, u32[]{:S(2)}) collective-permute-start(bf16[32,2304]{1,0:T(8,128)(2,1)S(1)} %get-tuple-element.89), channel_id=1, source_target_pairs={{0,240},{16,32},{32,16},{48,64},{64,48},{80,96},{96,80},{112,128},... | collective-permute-start | bytes 442376 | tf_op jit(solution)/shard_map/ppermute | solution.py:343
  20.8 4.9 %collective-permute-start.6 = (bf16[32,1280]{1,0:T(8,128)(2,1)S(1)}, bf16[32,1280]{1,0:T(8,128)(2,1)S(1)}, u32[]{:S(2)}, u32[]{:S(2)}) collective-permute-start(bf16[32,1280]{1,0:T(8,128)(2,1)S(1)} %get-tuple-element.87), channel_id=1, source_target_pairs={{0,16},{16,0},{32,48},{48,32},{64,80},{80,64},{96,112},{112,96},{1... | collective-permute-start | bytes 245768 | tf_op jit(solution)/shard_map/ppermute | solution.py:349
  24.4 1.3 %collective-permute-start.7 = (bf16[32,1024]{1,0:T(8,128)(2,1)S(1)}, bf16[32,1024]{1,0:T(8,128)(2,1)S(1)}, u32[]{:S(2)}, u32[]{:S(2)}) collective-permute-start(bf16[32,1024]{1,0:T(8,128)(2,1)S(1)} %get-tuple-element.88), channel_id=1, source_target_pairs={{0,16},{16,0},{32,48},{48,32},{64,80},{80,64},{96,112},{112,96},{1... | collective-permute-start | bytes 196616 | tf_op jit(solution)/shard_map/ppermute | solution.py:349
  26.8 6.0 %collective-permute-start.11 = (bf16[32,2304]{1,0:T(8,128)(2,1)S(1)}, bf16[32,2304]{1,0:T(8,128)(2,1)S(1)}, u32[]{:S(2)}, u32[]{:S(2)}) collective-permute-start(bf16[32,2304]{1,0:T(8,128)(2,1)S(1)} %get-tuple-element.95), channel_id=1, source_target_pairs={{0,240},{16,32},{32,16},{48,64},{64,48},{80,96},{96,80},{112,128},... | collective-permute-start | bytes 442376 | tf_op jit(solution)/shard_map/ppermute | solution.py:343
  27.4 4.9 %collective-permute-start.9 = (bf16[32,1280]{1,0:T(8,128)(2,1)S(1)}, bf16[32,1280]{1,0:T(8,128)(2,1)S(1)}, u32[]{:S(2)}, u32[]{:S(2)}) collective-permute-start(bf16[32,1280]{1,0:T(8,128)(2,1)S(1)} %get-tuple-element.93), channel_id=1, source_target_pairs={{0,16},{16,0},{32,48},{48,32},{64,80},{80,64},{96,112},{112,96},{1... | collective-permute-start | bytes 245768 | tf_op jit(solution)/shard_map/ppermute | solution.py:349
  31.1 1.3 %collective-permute-start.10 = (bf16[32,1024]{1,0:T(8,128)(2,1)S(1)}, bf16[32,1024]{1,0:T(8,128)(2,1)S(1)}, u32[]{:S(2)}, u32[]{:S(2)}) collective-permute-start(bf16[32,1024]{1,0:T(8,128)(2,1)S(1)} %get-tuple-element.94), channel_id=1, source_target_pairs={{0,16},{16,0},{32,48},{48,32},{64,80},{80,64},{96,112},{112,96},{1... | collective-permute-start | bytes 196616 | tf_op jit(solution)/shard_map/ppermute | solution.py:349
  33.4 5.8 %collective-permute-start.14 = (bf16[32,2304]{1,0:T(8,128)(2,1)S(1)}, bf16[32,2304]{1,0:T(8,128)(2,1)S(1)}, u32[]{:S(2)}, u32[]{:S(2)}) collective-permute-start(bf16[32,2304]{1,0:T(8,128)(2,1)S(1)} %get-tuple-element.101), channel_id=1, source_target_pairs={{0,240},{16,32},{32,16},{48,64},{64,48},{80,96},{96,80},{112,128},... | collective-permute-start | bytes 442376 | tf_op jit(solution)/shard_map/ppermute | solution.py:343
  33.9 4.9 %collective-permute-start.12 = (bf16[32,1280]{1,0:T(8,128)(2,1)S(1)}, bf16[32,1280]{1,0:T(8,128)(2,1)S(1)}, u32[]{:S(2)}, u32[]{:S(2)}) collective-permute-start(bf16[32,1280]{1,0:T(8,128)(2,1)S(1)} %get-tuple-element.99), channel_id=1, source_target_pairs={{0,16},{16,0},{32,48},{48,32},{64,80},{80,64},{96,112},{112,96},{1... | collective-permute-start | bytes 245768 | tf_op jit(solution)/shard_map/ppermute | solution.py:349
  37.5 1.3 %collective-permute-start.13 = (bf16[32,1024]{1,0:T(8,128)(2,1)S(1)}, bf16[32,1024]{1,0:T(8,128)(2,1)S(1)}, u32[]{:S(2)}, u32[]{:S(2)}) collective-permute-start(bf16[32,1024]{1,0:T(8,128)(2,1)S(1)} %get-tuple-element.100), channel_id=1, source_target_pairs={{0,16},{16,0},{32,48},{48,32},{64,80},{80,64},{96,112},{112,96},{1... | collective-permute-start | bytes 196616 | tf_op jit(solution)/shard_map/ppermute | solution.py:349
  39.9 5.9 %collective-permute-start.17 = (bf16[32,2304]{1,0:T(8,128)(2,1)S(1)}, bf16[32,2304]{1,0:T(8,128)(2,1)S(1)}, u32[]{:S(2)}, u32[]{:S(2)}) collective-permute-start(bf16[32,2304]{1,0:T(8,128)(2,1)S(1)} %get-tuple-element.108), channel_id=1, source_target_pairs={{0,240},{16,32},{32,16},{48,64},{64,48},{80,96},{96,80},{112,128},... | collective-permute-start | bytes 442376 | tf_op jit(solution)/shard_map/ppermute | solution.py:343
  40.3 4.9 %collective-permute-start.15 = (bf16[32,1280]{1,0:T(8,128)(2,1)S(1)}, bf16[32,1280]{1,0:T(8,128)(2,1)S(1)}, u32[]{:S(2)}, u32[]{:S(2)}) collective-permute-start(bf16[32,1280]{1,0:T(8,128)(2,1)S(1)} %get-tuple-element.105), channel_id=1, source_target_pairs={{0,16},{16,0},{32,48},{48,32},{64,80},{80,64},{96,112},{112,96},{1... | collective-permute-start | bytes 245768 | tf_op jit(solution)/shard_map/ppermute | solution.py:349
  44.0 1.3 %collective-permute-start.16 = (bf16[32,1024]{1,0:T(8,128)(2,1)S(1)}, bf16[32,1024]{1,0:T(8,128)(2,1)S(1)}, u32[]{:S(2)}, u32[]{:S(2)}) collective-permute-start(bf16[32,1024]{1,0:T(8,128)(2,1)S(1)} %get-tuple-element.106), channel_id=1, source_target_pairs={{0,16},{16,0},{32,48},{48,32},{64,80},{80,64},{96,112},{112,96},{1... | collective-permute-start | bytes 196616 | tf_op jit(solution)/shard_map/ppermute | solution.py:349

commit v7 on v6

--- a/solution.py
+++ b/solution.py
@@ -24,6 +24,10 @@
 
 def held(shape, dtype):
     return pltpu.VMEM(shape, dtype)
+
+
+def core():
+    return lax.rem(lax.axis_index("tile"), 2)
 
 
 def dot(x, w, contract):
@@ -274,16 +278,25 @@
                 turned[0][ins, outs] = far_ref[outs, ins].T
 
 
-def outer(scale, sum_ref, w_ref, turned_ref, rim_ref, got_ref, x_ref, far_ref):
-    add_far(scale, got_ref, turned_ref, rim_ref, sum_ref, x_ref)
-    write_far(x_ref, w_ref, rim_ref, far_ref)
-
-
-def finish(scale, degree, sum_ref, filt_ref, turned_ref, rim_ref, weight_ref, got_ref, out_ref, x_ref):
+def outer(scale, mine, sum_ref, w_ref, turned_ref, rim_ref, got_ref, *refs):
+    x_ref, far_ref = refs[-2:]
+
+    @pl.when(core() == mine)
+    def _():
+        add_far(scale, got_ref, turned_ref, rim_ref, sum_ref, x_ref)
+        write_far(x_ref, w_ref, rim_ref, far_ref)
+
+
+def finish(scale, degree, sum_ref, filt_ref, turned_ref, rim_ref, weight_ref, up_ref, down_ref, out_ref, x_ref):
     cols = rim_ref.shape[2]
     rows = out_ref.shape[1]
-    add_far(scale, got_ref, turned_ref, rim_ref, sum_ref, x_ref)
-    flip = lax.rem(lax.axis_index("tile"), 2)
+    flip = core()
+    for mine, got_ref in enumerate((up_ref, down_ref)):
+
+        @pl.when(flip == mine)
+        def _():
+            add_far(scale, got_ref, turned_ref, rim_ref, sum_ref, x_ref)
+
     for layer in range(2):
         for place in range(rows):
             here = slice(place * cols, (place + 1) * cols)
@@ -292,13 +305,14 @@
             )
 
 
-def call(kernel, outs, args, scratch=(), specs=None, limit=12, flops=1 << 20):
+def call(kernel, outs, args, scratch=(), specs=None, limit=12, flops=1 << 20, aliases=None):
     return pl.pallas_call(
         kernel,
         out_shape=outs,
         in_specs=specs or [IN_VMEM] * len(args),
         out_specs=[IN_VMEM] * len(outs),
         scratch_shapes=list(scratch),
+        input_output_aliases=aliases or {},
         cost_estimate=pl.CostEstimate(flops=flops, bytes_accessed=0, transcendentals=0),
         compiler_params=pltpu.CompilerParams(vmem_limit_bytes=limit << 20),
     )(*args)
@@ -310,7 +324,8 @@
     wide = rows * cols
     degree = coefs.shape[0] - 1
     size = lax.axis_size("tile")
-    far_pairs = [(i, (i + 1) % size if i % 2 else (i - 1) % size) for i in range(size)]
+    up_pairs = [(i, (i + 1) % size) for i in range(size)]
+    down_pairs = [((i + 1) % size, i) for i in range(size)]
     mate_pairs = [(i, i ^ 1) for i in range(size)]
 
     field = held((2, count, wide), jnp.float32)
@@ -338,9 +353,10 @@
     w_far, coef, rim, weight, x = near(w_far), near(coef), near(rim), near(weight), near(x)
     totals = [near(total) for total in totals]
     prev = filt = None
+    far = {0: far, 1: far}
     for order in range(degree):
         scale = 1.0 / 12.0 if order == 0 else 2.0 / 12.0
-        got_far = lax.ppermute(far, "tile", far_pairs)
+        got = {1: lax.ppermute(far[0], "tile", down_pairs), 0: lax.ppermute(far[1], "tile", up_pairs)}
         if order == 0:
             *mate, w_mate = call(to_mate_first, [*parts, matrix], [x, rim, *totals])
             w_mate = near(w_mate)
@@ -368,17 +384,24 @@
             turned = near(turned_now[0])
         prev = x
         if order < degree - 1:
-            x, far = call(
-                functools.partial(outer, scale),
+            now, later = (1, 0) if order % 2 == 0 else (0, 1)
+            x, far[now] = call(
+                functools.partial(outer, scale, now),
                 [field, payload],
-                [near(part), w_far, turned, rim, near(got_far)],
+                [near(part), w_far, turned, rim, near(got[now])],
+            )
+            x, far[later] = call(
+                functools.partial(outer, scale, later),
+                [field, payload],
+                [near(part), w_far, turned, rim, near(got[later]), near(x)],
+                aliases={5: 0},
             )
             x = near(x)
         else:
             (out,) = call(
                 functools.partial(finish, scale, degree),
                 [jax.ShapeDtypeStruct(states.shape, jnp.float32)],
-                [near(part), near(filt), turned, rim, weight, near(got_far)],
+                [near(part), near(filt), turned, rim, weight, near(got[0]), near(got[1])],
                 scratch=[pltpu.VMEM((2, count, wide), jnp.float32)],
             )
     return out

time: 46.9 us -> 43.3 us (0.923)
  the two profiles are of different devices: /device:TPU:1 before, /device:TPU:14 now
where the time goes in v7:
time: 43.3 us; the launch traced here: 43.2 us
  Pallas kernels  20.3 us (47%)
  starting transfers between devices  13.4 us (31%)
  waiting for transfers between devices  9.22 us (21%)
    pallas_call x30, Pallas kernels, call(): pl.pallas_call(kernel, out_shape=outs, in_specs=specs or [IN_VMEM] * len(...  20.3 us
    ppermute x6, waiting for transfers between devices, body(): lax.ppermute(far[1], 'tile', up_pairs)  9.05 us
    ppermute x6, starting transfers between devices, body(): lax.ppermute(far[0], 'tile', down_pairs)  6.18 us
    ppermute x6, starting transfers between devices, body(): lax.ppermute(far[1], 'tile', up_pairs)  3.91 us
    ppermute x12, starting transfers between devices, body(): got_mate = [near(lax.ppermute(part, 'tile', mate_pairs)) for part in mate]  3.29 us
  transfers between devices with their start and end apart: 24, of which 6 were waited for; matrix products, arithmetic and copies ran while one was open for 0% of the time, Pallas kernels for 33%

profile of v7, /device:TPU:14, one launch (start us, length us, event | category | flops | bytes accessed | tf_op | source)
XLA Modules:
  0.0 43.2 jit_solution(14881263921673322343)
XLA Ops:
  0.0 4.3 %shard_map.73 = (f32[2,32,1024]{2,1,0:T(8,128)S(1)}, bf16[1024,1024]{1,0:T(8,128)(2,1)S(1)}, f32[2,5,8,128]{3,2,1,0:T(8,128)S(1)}, f32[2,2,128]{2,1,0:T(2,128)S(...) custom-call(s32[8,16]{1,0:T(8,128)} %partner_hbm.1, ...), custom_call_target="tpu_custom_call" | custom-call | flops 1048576 | tf_op jit(solution)/shard_map/pallas_call | solution.py:309
  4.3 5.3 %collective-permute-start.3 = (bf16[32,2304]{1,0:T(8,128)(2,1)S(1)}, bf16[32,2304]{1,0:T(8,128)(2,1)S(1)}, u32[]{:S(2)}, u32[]{:S(2)}) collective-permute-start(bf16[32,2304]{1,0:T(8,128)(2,1)S(1)} %get-tuple-element.86), channel_id=1, source_target_pairs={{16,0},{32,16},{48,32},{64,48},{80,64},{96,80},{112,96},{128,112},... | collective-permute-start | bytes 442376 | tf_op jit(solution)/shard_map/ppermute | solution.py:359
  9.6 0.4 shard_map.75
  10.1 0.5 %collective-permute-start.1 = (bf16[32,1024]{1,0:T(8,128)(2,1)S(1)}, bf16[32,1024]{1,0:T(8,128)(2,1)S(1)}, u32[]{:S(2)}, u32[]{:S(2)}) collective-permute-start(bf16[32,1024]{1,0:T(8,128)(2,1)S(1)} %get-tuple-element.82), channel_id=1, source_target_pairs={{0,16},{16,0},{32,48},{48,32},{64,80},{80,64},{96,112},{112,96},{1... | collective-permute-start | bytes 196616 | tf_op jit(solution)/shard_map/ppermute | solution.py:365
  10.6 1.2 %shard_map.74 = (f32[2,32,1024]{2,1,0:T(8,128)S(1)}, f32[2,32,1024]{2,1,0:T(8,128)S(1)}, bf16[1024,1024]{1,0:T(8,128)(2,1)S(1)}) custom-call(f32[2,32,1024]{2,1,0:T(8,128)S(1)} %get-tuple-element.67.refs_0_.x_ref.refs_1_, f32[2,5,8,128]{3,2,1,0:T(8,128)S(1)} %get-tuple-element.68.refs_1_.refs_4_, f32[7,128]{1,0:T(8,128)S(1)} %get-tuple-element.69.refs_2_.refs_5_.weight_ref, ...), custom_call_target="tpu_custom_call" | custom-call | flops 1048576 | tf_op jit(solution)/shard_map/pallas_call | solution.py:309
  11.8 0.5 %shard_map.76 = (f32[2,32,1024]{2,1,0:T(8,128)S(1)}, bf16[1024,1024]{1,0:T(8,128)(2,1)S(1)}) custom-call(f32[2,32,1024]{2,1,0:T(8,128)S(1)} %get-tuple-element.78.part_ref, bf16[1024,1024]{1,0:T(8,128)(2,1)S(1)} %get-tuple-element.80.w_ref, f32[2,2,128]{2,1,0:T(2,128)S(1)} %get-tuple-element.79.rim_ref, bf16[32,1280]{1,0:T(8,128)(2,1)S(1)} %collective-permute-done.rows_ref, ...), custom_call_target="tpu_custom_call" | custom-call | tf_op jit(solution)/shard_map/pallas_call | solution.py:309
  12.4 0.7 %collective-permute-start.7 = (bf16[32,2304]{1,0:T(8,128)(2,1)S(1)}, bf16[32,2304]{1,0:T(8,128)(2,1)S(1)}, u32[]{:S(2)}, u32[]{:S(2)}) collective-permute-start(bf16[32,2304]{1,0:T(8,128)(2,1)S(1)} %get-tuple-element.95), channel_id=1, source_target_pairs={{0,16},{16,32},{32,48},{48,64},{64,80},{80,96},{96,112},{112,128},... | collective-permute-start | bytes 442376 | tf_op jit(solution)/shard_map/ppermute | solution.py:359
  13.1 2.3 %collective-permute-done.2.got_ref = bf16[32,2304]{1,0:T(8,128)(2,1)S(1)} collective-permute-done((bf16[32,2304]{1,0:T(8,128)(2,1)S(1)}, bf16[32,2304]{1,0:T(8,128)(2,1)S(1)}, u32[]{:S(2)}, u32[]{:S(2)}) %collective-permute-start.2) | collective-permute-done | bytes 147488 | tf_op jit(solution)/shard_map/ppermute | solution.py:359
  15.4 0.6 %shard_map.78 = (f32[2,32,1024]{2,1,0:T(8,128)S(1)}, bf16[32,2304]{1,0:T(8,128)(2,1)S(1)}) custom-call(f32[2,32,1024]{2,1,0:T(8,128)S(1)} %get-tuple-element.84.sum_ref, bf16[1024,1024]{1,0:T(8,128)(2,1)S(1)} %get-tuple-element.83.refs_0_.w_ref, bf16[1024,1024]{1,0:T(8,128)(2,1)S(1)} %get-tuple-element.85.turned_ref, ...), custom_call_target="tpu_custom_call", output_to_operand_aliasing={{0}: (5, {})} | custom-call | flops 1048576 | tf_op jit(solution)/shard_map/pallas_call | solution.py:309
  16.1 0.3 shard_map.80
  16.4 0.5 %collective-permute-start.4 = (bf16[32,1280]{1,0:T(8,128)(2,1)S(1)}, bf16[32,1280]{1,0:T(8,128)(2,1)S(1)}, u32[]{:S(2)}, u32[]{:S(2)}) collective-permute-start(bf16[32,1280]{1,0:T(8,128)(2,1)S(1)} %get-tuple-element.92), channel_id=1, source_target_pairs={{0,16},{16,0},{32,48},{48,32},{64,80},{80,64},{96,112},{112,96},{1... | collective-permute-start | bytes 245768 | tf_op jit(solution)/shard_map/ppermute | solution.py:365
  16.9 0.1 collective-permute-start.5
  17.0 1.1 %shard_map.79 = (f32[2,32,1024]{2,1,0:T(8,128)S(1)}, f32[2,32,1024]{2,1,0:T(8,128)S(1)}) custom-call(f32[2,32,1024]{2,1,0:T(8,128)S(1)} %get-tuple-element.88.refs_0_.x_ref.refs_1_, f32[2,32,1024]{2,1,0:T(8,128)S(1)} %get-tuple-element.67.refs_0_.x_ref.refs_1_, f32[2,32,1024]{2,1,0:T(8,128)S(1)} %get-tuple-element.89.refs_2_, ...), custom_call_target="tpu_custom_call" | custom-call | flops 1048576 | tf_op jit(solution)/shard_map/pallas_call | solution.py:309
  18.1 0.5 %shard_map.81.sum_ref = f32[2,32,1024]{2,1,0:T(8,128)S(1)} custom-call(f32[2,32,1024]{2,1,0:T(8,128)S(1)} %get-tuple-element.91.part_ref, bf16[1024,1024]{1,0:T(8,128)(2,1)S(1)} %get-tuple-element.80.w_ref, f32[2,2,128]{2,1,0:T(2,128)S(1)} %get-tuple-element.79.rim_ref, bf16[32,1280]{1,0:T(8,128)(2,1)S(1)} %collective-permute-done.4.rows_ref, ...), custom_call_target="tpu_custom_call" | custom-call | tf_op jit(solution)/shard_map/pallas_call | solution.py:309
  18.6 0.2 collective-permute-done.7.got_ref
  18.8 0.6 %shard_map.82 = (f32[2,32,1024]{2,1,0:T(8,128)S(1)}, bf16[32,2304]{1,0:T(8,128)(2,1)S(1)}) custom-call(f32[2,32,1024]{2,1,0:T(8,128)S(1)} %shard_map.81.sum_ref, bf16[1024,1024]{1,0:T(8,128)(2,1)S(1)} %get-tuple-element.83.refs_0_.w_ref, bf16[1024,1024]{1,0:T(8,128)(2,1)S(1)} %get-tuple-element.85.turned_ref, f32[2,2,128]{2,1,0:T(2,128)S(1)} %get-tuple-element.79.rim_ref, ...), custom_call_target="tpu_custom_call" | custom-call | flops 1048576 | tf_op jit(solution)/shard_map/pallas_call | solution.py:309
  19.4 0.2 collective-permute-start.11
  19.7 0.9 %collective-permute-start.10 = (bf16[32,2304]{1,0:T(8,128)(2,1)S(1)}, bf16[32,2304]{1,0:T(8,128)(2,1)S(1)}, u32[]{:S(2)}, u32[]{:S(2)}) collective-permute-start(bf16[32,2304]{1,0:T(8,128)(2,1)S(1)} %get-tuple-element.102), channel_id=1, source_target_pairs={{0,16},{16,32},{32,48},{48,64},{64,80},{80,96},{96,112},{112,128},... | collective-permute-start | bytes 442376 | tf_op jit(solution)/shard_map/ppermute | solution.py:359
  20.6 0.3 shard_map.85
  20.9 0.3 collective-permute-start.8
  21.2 0.3 collective-permute-start.9
  21.4 1.1 %shard_map.84 = (f32[2,32,1024]{2,1,0:T(8,128)S(1)}, f32[2,32,1024]{2,1,0:T(8,128)S(1)}) custom-call(f32[2,32,1024]{2,1,0:T(8,128)S(1)} %get-tuple-element.97.refs_0_.x_ref.refs_1_, f32[2,32,1024]{2,1,0:T(8,128)S(1)} %get-tuple-element.88.refs_0_.x_ref.refs_1_, f32[2,32,1024]{2,1,0:T(8,128)S(1)} %get-tuple-element.98.refs_2_, ...), custom_call_target="tpu_custom_call" | custom-call | flops 1048576 | tf_op jit(solution)/shard_map/pallas_call | solution.py:309
  22.5 0.5 %shard_map.86.sum_ref = f32[2,32,1024]{2,1,0:T(8,128)S(1)} custom-call(f32[2,32,1024]{2,1,0:T(8,128)S(1)} %get-tuple-element.99.part_ref, bf16[1024,1024]{1,0:T(8,128)(2,1)S(1)} %get-tuple-element.80.w_ref, f32[2,2,128]{2,1,0:T(2,128)S(1)} %get-tuple-element.79.rim_ref, bf16[32,1280]{1,0:T(8,128)(2,1)S(1)} %collective-permute-done.8.rows_ref, ...), custom_call_target="tpu_custom_call" | custom-call | tf_op jit(solution)/shard_map/pallas_call | solution.py:309
  23.1 1.1 %collective-permute-start.15 = (bf16[32,2304]{1,0:T(8,128)(2,1)S(1)}, bf16[32,2304]{1,0:T(8,128)(2,1)S(1)}, u32[]{:S(2)}, u32[]{:S(2)}) collective-permute-start(bf16[32,2304]{1,0:T(8,128)(2,1)S(1)} %get-tuple-element.111), channel_id=1, source_target_pairs={{0,16},{16,32},{32,48},{48,64},{64,80},{80,96},{96,112},{112,128},... | collective-permute-start | bytes 442376 | tf_op jit(solution)/shard_map/ppermute | solution.py:359
  24.2 1.2 %collective-permute-done.10.got_ref = bf16[32,2304]{1,0:T(8,128)(2,1)S(1)} collective-permute-done((bf16[32,2304]{1,0:T(8,128)(2,1)S(1)}, bf16[32,2304]{1,0:T(8,128)(2,1)S(1)}, u32[]{:S(2)}, u32[]{:S(2)}) %collective-permute-start.10) | collective-permute-done | bytes 147488 | tf_op jit(solution)/shard_map/ppermute | solution.py:359
  25.4 0.7 %shard_map.88 = (f32[2,32,1024]{2,1,0:T(8,128)S(1)}, bf16[32,2304]{1,0:T(8,128)(2,1)S(1)}) custom-call(f32[2,32,1024]{2,1,0:T(8,128)S(1)} %shard_map.86.sum_ref, bf16[1024,1024]{1,0:T(8,128)(2,1)S(1)} %get-tuple-element.83.refs_0_.w_ref, bf16[1024,1024]{1,0:T(8,128)(2,1)S(1)} %get-tuple-element.85.turned_ref, ...), custom_call_target="tpu_custom_call", output_to_operand_aliasing={{0}: (5, {})} | custom-call | flops 1048576 | tf_op jit(solution)/shard_map/pallas_call | solution.py:309
  26.3 0.3 shard_map.90
  26.6 0.5 %collective-permute-start.12 = (bf16[32,1280]{1,0:T(8,128)(2,1)S(1)}, bf16[32,1280]{1,0:T(8,128)(2,1)S(1)}, u32[]{:S(2)}, u32[]{:S(2)}) collective-permute-start(bf16[32,1280]{1,0:T(8,128)(2,1)S(1)} %get-tuple-element.108), channel_id=1, source_target_pairs={{0,16},{16,0},{32,48},{48,32},{64,80},{80,64},{96,112},{112,96},{1... | collective-permute-start | bytes 245768 | tf_op jit(solution)/shard_map/ppermute | solution.py:365
  27.1 0.1 collective-permute-start.13
  27.2 1.1 %shard_map.89 = (f32[2,32,1024]{2,1,0:T(8,128)S(1)}, f32[2,32,1024]{2,1,0:T(8,128)S(1)}) custom-call(f32[2,32,1024]{2,1,0:T(8,128)S(1)} %get-tuple-element.105.refs_0_.x_ref.refs_1_, f32[2,32,1024]{2,1,0:T(8,128)S(1)} %get-tuple-element.97.refs_0_.x_ref.refs_1_, f32[2,32,1024]{2,1,0:T(8,128)S(1)} %get-tuple-element.106.refs_2_, ...), custom_call_target="tpu_custom_call" | custom-call | flops 1048576 | tf_op jit(solution)/shard_map/pallas_call | solution.py:309
  28.3 0.5 %shard_map.91.sum_ref = f32[2,32,1024]{2,1,0:T(8,128)S(1)} custom-call(f32[2,32,1024]{2,1,0:T(8,128)S(1)} %get-tuple-element.107.part_ref, bf16[1024,1024]{1,0:T(8,128)(2,1)S(1)} %get-tuple-element.80.w_ref, f32[2,2,128]{2,1,0:T(2,128)S(1)} %get-tuple-element.79.rim_ref, bf16[32,1280]{1,0:T(8,128)(2,1)S(1)} %collective-permute-done.12.rows_ref, ...), custom_call_target="tpu_custom_call" | custom-call | tf_op jit(solution)/shard_map/pallas_call | solution.py:309
  28.9 0.6 %shard_map.92 = (f32[2,32,1024]{2,1,0:T(8,128)S(1)}, bf16[32,2304]{1,0:T(8,128)(2,1)S(1)}) custom-call(f32[2,32,1024]{2,1,0:T(8,128)S(1)} %shard_map.91.sum_ref, bf16[1024,1024]{1,0:T(8,128)(2,1)S(1)} %get-tuple-element.83.refs_0_.w_ref, bf16[1024,1024]{1,0:T(8,128)(2,1)S(1)} %get-tuple-element.85.turned_ref, f32[2,2,128]{2,1,0:T(2,128)S(1)} %get-tuple-element.79.rim_ref, ...), custom_call_target="tpu_custom_call" | custom-call | flops 1048576 | tf_op jit(solution)/shard_map/pallas_call | solution.py:309
  29.5 0.4 collective-permute-start.19
  29.9 0.7 %collective-permute-start.18 = (bf16[32,2304]{1,0:T(8,128)(2,1)S(1)}, bf16[32,2304]{1,0:T(8,128)(2,1)S(1)}, u32[]{:S(2)}, u32[]{:S(2)}) collective-permute-start(bf16[32,2304]{1,0:T(8,128)(2,1)S(1)} %get-tuple-element.118), channel_id=1, source_target_pairs={{0,16},{16,32},{32,48},{48,64},{64,80},{80,96},{96,112},{112,128},... | collective-permute-start | bytes 442376 | tf_op jit(solution)/shard_map/ppermute | solution.py:359
  30.6 0.3 shard_map.95
  30.9 0.4 %collective-permute-start.16 = (bf16[32,1280]{1,0:T(8,128)(2,1)S(1)}, bf16[32,1280]{1,0:T(8,128)(2,1)S(1)}, u32[]{:S(2)}, u32[]{:S(2)}) collective-permute-start(bf16[32,1280]{1,0:T(8,128)(2,1)S(1)} %get-tuple-element.116), channel_id=1, source_target_pairs={{0,16},{16,0},{32,48},{48,32},{64,80},{80,64},{96,112},{112,96},{1... | collective-permute-start | bytes 245768 | tf_op jit(solution)/shard_map/ppermute | solution.py:365
  31.4 0.1 collective-permute-start.17
  31.5 1.1 %shard_map.94 = (f32[2,32,1024]{2,1,0:T(8,128)S(1)}, f32[2,32,1024]{2,1,0:T(8,128)S(1)}) custom-call(f32[2,32,1024]{2,1,0:T(8,128)S(1)} %get-tuple-element.113.refs_0_.x_ref.refs_1_, f32[2,32,1024]{2,1,0:T(8,128)S(1)} %get-tuple-element.105.refs_0_.x_ref.refs_1_, f32[2,32,1024]{2,1,0:T(8,128)S(1)} %get-tuple-element.114.refs_2_, ...), custom_call_target="tpu_custom_call" | custom-call | flops 1048576 | tf_op jit(solution)/shard_map/pallas_call | solution.py:309
  32.6 0.5 %shard_map.96.sum_ref = f32[2,32,1024]{2,1,0:T(8,128)S(1)} custom-call(f32[2,32,1024]{2,1,0:T(8,128)S(1)} %get-tuple-element.115.part_ref, bf16[1024,1024]{1,0:T(8,128)(2,1)S(1)} %get-tuple-element.80.w_ref, f32[2,2,128]{2,1,0:T(2,128)S(1)} %get-tuple-element.79.rim_ref, bf16[32,1280]{1,0:T(8,128)(2,1)S(1)} %collective-permute-done.16.rows_ref, ...), custom_call_target="tpu_custom_call" | custom-call | tf_op jit(solution)/shard_map/pallas_call | solution.py:309
  33.2 2.5 %collective-permute-done.18.got_ref = bf16[32,2304]{1,0:T(8,128)(2,1)S(1)} collective-permute-done((bf16[32,2304]{1,0:T(8,128)(2,1)S(1)}, bf16[32,2304]{1,0:T(8,128)(2,1)S(1)}, u32[]{:S(2)}, u32[]{:S(2)}) %collective-permute-start.18) | collective-permute-done | bytes 147488 | tf_op jit(solution)/shard_map/ppermute | solution.py:359
  35.7 0.6 %shard_map.98 = (f32[2,32,1024]{2,1,0:T(8,128)S(1)}, bf16[32,2304]{1,0:T(8,128)(2,1)S(1)}) custom-call(f32[2,32,1024]{2,1,0:T(8,128)S(1)} %shard_map.96.sum_ref, bf16[1024,1024]{1,0:T(8,128)(2,1)S(1)} %get-tuple-element.83.refs_0_.w_ref, bf16[1024,1024]{1,0:T(8,128)(2,1)S(1)} %get-tuple-element.85.turned_ref, ...), custom_call_target="tpu_custom_call", output_to_operand_aliasing={{0}: (5, {})} | custom-call | flops 1048576 | tf_op jit(solution)/shard_map/pallas_call | solution.py:309
  36.3 0.5 %collective-permute-start.22 = (bf16[32,2304]{1,0:T(8,128)(2,1)S(1)}, bf16[32,2304]{1,0:T(8,128)(2,1)S(1)}, u32[]{:S(2)}, u32[]{:S(2)}) collective-permute-start(bf16[32,2304]{1,0:T(8,128)(2,1)S(1)} %get-tuple-element.127), channel_id=1, source_target_pairs={{0,16},{16,32},{32,48},{48,64},{64,80},{80,96},{96,112},{112,128},... | collective-permute-start | bytes 442376 | tf_op jit(solution)/shard_map/ppermute | solution.py:359
  36.8 0.3 shard_map.100
  37.1 0.5 %collective-permute-start.21 = (bf16[32,1024]{1,0:T(8,128)(2,1)S(1)}, bf16[32,1024]{1,0:T(8,128)(2,1)S(1)}, u32[]{:S(2)}, u32[]{:S(2)}) collective-permute-start(bf16[32,1024]{1,0:T(8,128)(2,1)S(1)} %get-tuple-element.125), channel_id=1, source_target_pairs={{0,16},{16,0},{32,48},{48,32},{64,80},{80,64},{96,112},{112,96},{1... | collective-permute-start | bytes 196616 | tf_op jit(solution)/shard_map/ppermute | solution.py:365
  37.6 1.1 %shard_map.99 = (f32[2,32,1024]{2,1,0:T(8,128)S(1)}, f32[2,32,1024]{2,1,0:T(8,128)S(1)}) custom-call(f32[2,32,1024]{2,1,0:T(8,128)S(1)} %get-tuple-element.121.refs_0_.x_ref, f32[2,32,1024]{2,1,0:T(8,128)S(1)} %get-tuple-element.113.refs_0_.x_ref.refs_1_, f32[2,32,1024]{2,1,0:T(8,128)S(1)} %get-tuple-element.122.refs_2_, ...), custom_call_target="tpu_custom_call" | custom-call | flops 1048576 | tf_op jit(solution)/shard_map/pallas_call | solution.py:309
  38.8 0.5 %shard_map.101.sum_ref = f32[2,32,1024]{2,1,0:T(8,128)S(1)} custom-call(f32[2,32,1024]{2,1,0:T(8,128)S(1)} %get-tuple-element.123.part_ref, bf16[1024,1024]{1,0:T(8,128)(2,1)S(1)} %get-tuple-element.80.w_ref, f32[2,2,128]{2,1,0:T(2,128)S(1)} %get-tuple-element.79.rim_ref, bf16[32,1280]{1,0:T(8,128)(2,1)S(1)} %collective-permute-done.20.rows_ref, ...), custom_call_target="tpu_custom_call" | custom-call | tf_op jit(solution)/shard_map/pallas_call | solution.py:309
  39.3 2.8 %collective-permute-done.22.up_ref = bf16[32,2304]{1,0:T(8,128)(2,1)S(1)} collective-permute-done((bf16[32,2304]{1,0:T(8,128)(2,1)S(1)}, bf16[32,2304]{1,0:T(8,128)(2,1)S(1)}, u32[]{:S(2)}, u32[]{:S(2)}) %collective-permute-start.22) | collective-permute-done | bytes 147488 | tf_op jit(solution)/shard_map/ppermute | solution.py:359
  42.1 1.1 %shard_map.102 = f32[2,8,32,128]{3,2,1,0:T(8,128)} custom-call(f32[2,32,1024]{2,1,0:T(8,128)S(1)} %shard_map.101.sum_ref, f32[2,32,1024]{2,1,0:T(8,128)S(1)} %get-tuple-element.126.filt_ref, bf16[1024,1024]{1,0:T(8,128)(2,1)S(1)} %get-tuple-element.85.turned_ref, f32[2,2,128]{2,1,0:T(2,128)S(1)} %get-tuple-element.79.rim_ref, ...), custom_call_target="tpu_custom_call" | custom-call | flops 1048576 | tf_op jit(solution)/shard_map/pallas_call | solution.py:309
  (30 shorter events, 0.6 us)
Async XLA Ops:
  4.3 8.1 %collective-permute-start.3 = (bf16[32,2304]{1,0:T(8,128)(2,1)S(1)}, bf16[32,2304]{1,0:T(8,128)(2,1)S(1)}, u32[]{:S(2)}, u32[]{:S(2)}) collective-permute-start(bf16[32,2304]{1,0:T(8,128)(2,1)S(1)} %get-tuple-element.86), channel_id=1, source_target_pairs={{16,0},{32,16},{48,32},{64,48},{80,64},{96,80},{112,96},{128,112},... | collective-permute-start | bytes 442376 | tf_op jit(solution)/shard_map/ppermute | solution.py:359
  9.6 5.8 %collective-permute-start.2 = (bf16[32,2304]{1,0:T(8,128)(2,1)S(1)}, bf16[32,2304]{1,0:T(8,128)(2,1)S(1)}, u32[]{:S(2)}, u32[]{:S(2)}) collective-permute-start(bf16[32,2304]{1,0:T(8,128)(2,1)S(1)} %get-tuple-element.86), channel_id=1, source_target_pairs={{0,16},{16,32},{32,48},{48,64},{64,80},{80,96},{96,112},{112,128},... | collective-permute-start | bytes 442376 | tf_op jit(solution)/shard_map/ppermute | solution.py:359
  10.0 1.8 %collective-permute-start = (bf16[32,1280]{1,0:T(8,128)(2,1)S(1)}, bf16[32,1280]{1,0:T(8,128)(2,1)S(1)}, u32[]{:S(2)}, u32[]{:S(2)}) collective-permute-start(bf16[32,1280]{1,0:T(8,128)(2,1)S(1)} %get-tuple-element.81), channel_id=1, source_target_pairs={{0,16},{16,0},{32,48},{48,32},{64,80},{80,64},{96,112},{112,96},{1... | collective-permute-start | bytes 245768 | tf_op jit(solution)/shard_map/ppermute | solution.py:365
  10.1 1.7 %collective-permute-start.1 = (bf16[32,1024]{1,0:T(8,128)(2,1)S(1)}, bf16[32,1024]{1,0:T(8,128)(2,1)S(1)}, u32[]{:S(2)}, u32[]{:S(2)}) collective-permute-start(bf16[32,1024]{1,0:T(8,128)(2,1)S(1)} %get-tuple-element.82), channel_id=1, source_target_pairs={{0,16},{16,0},{32,48},{48,32},{64,80},{80,64},{96,112},{112,96},{1... | collective-permute-start | bytes 196616 | tf_op jit(solution)/shard_map/ppermute | solution.py:365
  12.4 6.4 %collective-permute-start.7 = (bf16[32,2304]{1,0:T(8,128)(2,1)S(1)}, bf16[32,2304]{1,0:T(8,128)(2,1)S(1)}, u32[]{:S(2)}, u32[]{:S(2)}) collective-permute-start(bf16[32,2304]{1,0:T(8,128)(2,1)S(1)} %get-tuple-element.95), channel_id=1, source_target_pairs={{0,16},{16,32},{32,48},{48,64},{64,80},{80,96},{96,112},{112,128},... | collective-permute-start | bytes 442376 | tf_op jit(solution)/shard_map/ppermute | solution.py:359
  16.0 3.7 %collective-permute-start.6 = (bf16[32,2304]{1,0:T(8,128)(2,1)S(1)}, bf16[32,2304]{1,0:T(8,128)(2,1)S(1)}, u32[]{:S(2)}, u32[]{:S(2)}) collective-permute-start(bf16[32,2304]{1,0:T(8,128)(2,1)S(1)} %get-tuple-element.94), channel_id=1, source_target_pairs={{16,0},{32,16},{48,32},{64,48},{80,64},{96,80},{112,96},{128,112},... | collective-permute-start | bytes 442376 | tf_op jit(solution)/shard_map/ppermute | solution.py:359
  16.4 1.7 %collective-permute-start.4 = (bf16[32,1280]{1,0:T(8,128)(2,1)S(1)}, bf16[32,1280]{1,0:T(8,128)(2,1)S(1)}, u32[]{:S(2)}, u32[]{:S(2)}) collective-permute-start(bf16[32,1280]{1,0:T(8,128)(2,1)S(1)} %get-tuple-element.92), channel_id=1, source_target_pairs={{0,16},{16,0},{32,48},{48,32},{64,80},{80,64},{96,112},{112,96},{1... | collective-permute-start | bytes 245768 | tf_op jit(solution)/shard_map/ppermute | solution.py:365
  16.9 1.3 %collective-permute-start.5 = (bf16[32,1024]{1,0:T(8,128)(2,1)S(1)}, bf16[32,1024]{1,0:T(8,128)(2,1)S(1)}, u32[]{:S(2)}, u32[]{:S(2)}) collective-permute-start(bf16[32,1024]{1,0:T(8,128)(2,1)S(1)} %get-tuple-element.93), channel_id=1, source_target_pairs={{0,16},{16,0},{32,48},{48,32},{64,80},{80,64},{96,112},{112,96},{1... | collective-permute-start | bytes 196616 | tf_op jit(solution)/shard_map/ppermute | solution.py:365
  19.4 3.6 %collective-permute-start.11 = (bf16[32,2304]{1,0:T(8,128)(2,1)S(1)}, bf16[32,2304]{1,0:T(8,128)(2,1)S(1)}, u32[]{:S(2)}, u32[]{:S(2)}) collective-permute-start(bf16[32,2304]{1,0:T(8,128)(2,1)S(1)} %get-tuple-element.103), channel_id=1, source_target_pairs={{16,0},{32,16},{48,32},{64,48},{80,64},{96,80},{112,96},{128,112},... | collective-permute-start | bytes 442376 | tf_op jit(solution)/shard_map/ppermute | solution.py:359
  19.7 5.8 %collective-permute-start.10 = (bf16[32,2304]{1,0:T(8,128)(2,1)S(1)}, bf16[32,2304]{1,0:T(8,128)(2,1)S(1)}, u32[]{:S(2)}, u32[]{:S(2)}) collective-permute-start(bf16[32,2304]{1,0:T(8,128)(2,1)S(1)} %get-tuple-element.102), channel_id=1, source_target_pairs={{0,16},{16,32},{32,48},{48,64},{64,80},{80,96},{96,112},{112,128},... | collective-permute-start | bytes 442376 | tf_op jit(solution)/shard_map/ppermute | solution.py:359
  20.9 1.7 %collective-permute-start.8 = (bf16[32,1280]{1,0:T(8,128)(2,1)S(1)}, bf16[32,1280]{1,0:T(8,128)(2,1)S(1)}, u32[]{:S(2)}, u32[]{:S(2)}) collective-permute-start(bf16[32,1280]{1,0:T(8,128)(2,1)S(1)} %get-tuple-element.100), channel_id=1, source_target_pairs={{0,16},{16,0},{32,48},{48,32},{64,80},{80,64},{96,112},{112,96},{1... | collective-permute-start | bytes 245768 | tf_op jit(solution)/shard_map/ppermute | solution.py:365
  21.2 1.4 %collective-permute-start.9 = (bf16[32,1024]{1,0:T(8,128)(2,1)S(1)}, bf16[32,1024]{1,0:T(8,128)(2,1)S(1)}, u32[]{:S(2)}, u32[]{:S(2)}) collective-permute-start(bf16[32,1024]{1,0:T(8,128)(2,1)S(1)} %get-tuple-element.101), channel_id=1, source_target_pairs={{0,16},{16,0},{32,48},{48,32},{64,80},{80,64},{96,112},{112,96},{1... | collective-permute-start | bytes 196616 | tf_op jit(solution)/shard_map/ppermute | solution.py:365
  23.1 5.8 %collective-permute-start.15 = (bf16[32,2304]{1,0:T(8,128)(2,1)S(1)}, bf16[32,2304]{1,0:T(8,128)(2,1)S(1)}, u32[]{:S(2)}, u32[]{:S(2)}) collective-permute-start(bf16[32,2304]{1,0:T(8,128)(2,1)S(1)} %get-tuple-element.111), channel_id=1, source_target_pairs={{0,16},{16,32},{32,48},{48,64},{64,80},{80,96},{96,112},{112,128},... | collective-permute-start | bytes 442376 | tf_op jit(solution)/shard_map/ppermute | solution.py:359
  26.2 3.7 %collective-permute-start.14 = (bf16[32,2304]{1,0:T(8,128)(2,1)S(1)}, bf16[32,2304]{1,0:T(8,128)(2,1)S(1)}, u32[]{:S(2)}, u32[]{:S(2)}) collective-permute-start(bf16[32,2304]{1,0:T(8,128)(2,1)S(1)} %get-tuple-element.110), channel_id=1, source_target_pairs={{16,0},{32,16},{48,32},{64,48},{80,64},{96,80},{112,96},{128,112},... | collective-permute-start | bytes 442376 | tf_op jit(solution)/shard_map/ppermute | solution.py:359
  26.6 1.7 %collective-permute-start.12 = (bf16[32,1280]{1,0:T(8,128)(2,1)S(1)}, bf16[32,1280]{1,0:T(8,128)(2,1)S(1)}, u32[]{:S(2)}, u32[]{:S(2)}) collective-permute-start(bf16[32,1280]{1,0:T(8,128)(2,1)S(1)} %get-tuple-element.108), channel_id=1, source_target_pairs={{0,16},{16,0},{32,48},{48,32},{64,80},{80,64},{96,112},{112,96},{1... | collective-permute-start | bytes 245768 | tf_op jit(solution)/shard_map/ppermute | solution.py:365
  27.1 1.3 %collective-permute-start.13 = (bf16[32,1024]{1,0:T(8,128)(2,1)S(1)}, bf16[32,1024]{1,0:T(8,128)(2,1)S(1)}, u32[]{:S(2)}, u32[]{:S(2)}) collective-permute-start(bf16[32,1024]{1,0:T(8,128)(2,1)S(1)} %get-tuple-element.109), channel_id=1, source_target_pairs={{0,16},{16,0},{32,48},{48,32},{64,80},{80,64},{96,112},{112,96},{1... | collective-permute-start | bytes 196616 | tf_op jit(solution)/shard_map/ppermute | solution.py:365
  29.5 3.7 %collective-permute-start.19 = (bf16[32,2304]{1,0:T(8,128)(2,1)S(1)}, bf16[32,2304]{1,0:T(8,128)(2,1)S(1)}, u32[]{:S(2)}, u32[]{:S(2)}) collective-permute-start(bf16[32,2304]{1,0:T(8,128)(2,1)S(1)} %get-tuple-element.119), channel_id=1, source_target_pairs={{16,0},{32,16},{48,32},{64,48},{80,64},{96,80},{112,96},{128,112},... | collective-permute-start | bytes 442376 | tf_op jit(solution)/shard_map/ppermute | solution.py:359
  29.9 5.8 %collective-permute-start.18 = (bf16[32,2304]{1,0:T(8,128)(2,1)S(1)}, bf16[32,2304]{1,0:T(8,128)(2,1)S(1)}, u32[]{:S(2)}, u32[]{:S(2)}) collective-permute-start(bf16[32,2304]{1,0:T(8,128)(2,1)S(1)} %get-tuple-element.118), channel_id=1, source_target_pairs={{0,16},{16,32},{32,48},{48,64},{64,80},{80,96},{96,112},{112,128},... | collective-permute-start | bytes 442376 | tf_op jit(solution)/shard_map/ppermute | solution.py:359
  30.9 1.7 %collective-permute-start.16 = (bf16[32,1280]{1,0:T(8,128)(2,1)S(1)}, bf16[32,1280]{1,0:T(8,128)(2,1)S(1)}, u32[]{:S(2)}, u32[]{:S(2)}) collective-permute-start(bf16[32,1280]{1,0:T(8,128)(2,1)S(1)} %get-tuple-element.116), channel_id=1, source_target_pairs={{0,16},{16,0},{32,48},{48,32},{64,80},{80,64},{96,112},{112,96},{1... | collective-permute-start | bytes 245768 | tf_op jit(solution)/shard_map/ppermute | solution.py:365
  31.4 1.3 %collective-permute-start.17 = (bf16[32,1024]{1,0:T(8,128)(2,1)S(1)}, bf16[32,1024]{1,0:T(8,128)(2,1)S(1)}, u32[]{:S(2)}, u32[]{:S(2)}) collective-permute-start(bf16[32,1024]{1,0:T(8,128)(2,1)S(1)} %get-tuple-element.117), channel_id=1, source_target_pairs={{0,16},{16,0},{32,48},{48,32},{64,80},{80,64},{96,112},{112,96},{1... | collective-permute-start | bytes 196616 | tf_op jit(solution)/shard_map/ppermute | solution.py:365
  36.3 3.0 %collective-permute-start.23 = (bf16[32,2304]{1,0:T(8,128)(2,1)S(1)}, bf16[32,2304]{1,0:T(8,128)(2,1)S(1)}, u32[]{:S(2)}, u32[]{:S(2)}) collective-permute-start(bf16[32,2304]{1,0:T(8,128)(2,1)S(1)} %get-tuple-element.128), channel_id=1, source_target_pairs={{16,0},{32,16},{48,32},{64,48},{80,64},{96,80},{112,96},{128,112},... | collective-permute-start | bytes 442376 | tf_op jit(solution)/shard_map/ppermute | solution.py:359
  36.3 5.8 %collective-permute-start.22 = (bf16[32,2304]{1,0:T(8,128)(2,1)S(1)}, bf16[32,2304]{1,0:T(8,128)(2,1)S(1)}, u32[]{:S(2)}, u32[]{:S(2)}) collective-permute-start(bf16[32,2304]{1,0:T(8,128)(2,1)S(1)} %get-tuple-element.127), channel_id=1, source_target_pairs={{0,16},{16,32},{32,48},{48,64},{64,80},{80,96},{96,112},{112,128},... | collective-permute-start | bytes 442376 | tf_op jit(solution)/shard_map/ppermute | solution.py:359
  37.1 1.7 %collective-permute-start.20 = (bf16[32,1280]{1,0:T(8,128)(2,1)S(1)}, bf16[32,1280]{1,0:T(8,128)(2,1)S(1)}, u32[]{:S(2)}, u32[]{:S(2)}) collective-permute-start(bf16[32,1280]{1,0:T(8,128)(2,1)S(1)} %get-tuple-element.124), channel_id=1, source_target_pairs={{0,16},{16,0},{32,48},{48,32},{64,80},{80,64},{96,112},{112,96},{1... | collective-permute-start | bytes 245768 | tf_op jit(solution)/shard_map/ppermute | solution.py:365
  37.1 1.6 %collective-permute-start.21 = (bf16[32,1024]{1,0:T(8,128)(2,1)S(1)}, bf16[32,1024]{1,0:T(8,128)(2,1)S(1)}, u32[]{:S(2)}, u32[]{:S(2)}) collective-permute-start(bf16[32,1024]{1,0:T(8,128)(2,1)S(1)} %get-tuple-element.125), channel_id=1, source_target_pairs={{0,16},{16,0},{32,48},{48,32},{64,80},{80,64},{96,112},{112,96},{1... | collective-permute-start | bytes 196616 | tf_op jit(solution)/shard_map/ppermute | solution.py:365

commit v8 on v7

--- a/solution.py
+++ b/solution.py
@@ -326,6 +326,7 @@
     size = lax.axis_size("tile")
     up_pairs = [(i, (i + 1) % size) for i in range(size)]
     down_pairs = [((i + 1) % size, i) for i in range(size)]
+    far_pairs = [up_pairs[i] if i % 2 else down_pairs[i - 1] for i in range(size)]
     mate_pairs = [(i, i ^ 1) for i in range(size)]
 
     field = held((2, count, wide), jnp.float32)
@@ -353,10 +354,12 @@
     w_far, coef, rim, weight, x = near(w_far), near(coef), near(rim), near(weight), near(x)
     totals = [near(total) for total in totals]
     prev = filt = None
-    far = {0: far, 1: far}
     for order in range(degree):
         scale = 1.0 / 12.0 if order == 0 else 2.0 / 12.0
-        got = {1: lax.ppermute(far[0], "tile", down_pairs), 0: lax.ppermute(far[1], "tile", up_pairs)}
+        if order == 0:
+            got = [lax.ppermute(far, "tile", far_pairs)] * 2
+        else:
+            got = [lax.ppermute(far[1], "tile", up_pairs), lax.ppermute(far[0], "tile", down_pairs)]
         if order == 0:
             *mate, w_mate = call(to_mate_first, [*parts, matrix], [x, rim, *totals])
             w_mate = near(w_mate)
@@ -385,6 +388,7 @@
         prev = x
         if order < degree - 1:
             now, later = (1, 0) if order % 2 == 0 else (0, 1)
+            far = [None, None]
             x, far[now] = call(
                 functools.partial(outer, scale, now),
                 [field, payload],

time: 43.3 us -> 43.2 us (level)
  the two profiles are of different devices: /device:TPU:14 before, /device:TPU:6 now
where the time goes in v8:
time: 43.2 us; the launch traced here: 43.1 us
  Pallas kernels  20.2 us (47%)
  starting transfers between devices  15.5 us (36%)
  waiting for transfers between devices  7.21 us (17%)
    pallas_call x30, Pallas kernels, call(): pl.pallas_call(kernel, out_shape=outs, in_specs=specs or [IN_VMEM] * len(...  20.2 us
    ppermute x5, waiting for transfers between devices, body(): lax.ppermute(far[1], 'tile', up_pairs)  7.08 us
    ppermute x1, starting transfers between devices, body(): got = [lax.ppermute(far, 'tile', far_pairs)] * 2  5.38 us
    ppermute x5, starting transfers between devices, body(): lax.ppermute(far[1], 'tile', up_pairs)  3.68 us
    ppermute x12, starting transfers between devices, body(): got_mate = [near(lax.ppermute(part, 'tile', mate_pairs)) for part in mate]  3.22 us
    ppermute x5, starting transfers between devices, body(): lax.ppermute(far[0], 'tile', down_pairs)  3.17 us
  transfers between devices with their start and end apart: 23, of which 6 were waited for; matrix products, arithmetic and copies ran while one was open for 0% of the time, Pallas kernels for 33%

profile of v8, /device:TPU:6, one launch (start us, length us, event | category | flops | bytes accessed | tf_op | source)
XLA Modules:
  0.0 43.1 jit_solution(1319068402612296538)
XLA Ops:
  0.0 4.3 %shard_map.73 = (f32[2,32,1024]{2,1,0:T(8,128)S(1)}, bf16[1024,1024]{1,0:T(8,128)(2,1)S(1)}, f32[2,5,8,128]{3,2,1,0:T(8,128)S(1)}, f32[2,2,128]{2,1,0:T(2,128)S(...) custom-call(s32[8,16]{1,0:T(8,128)} %partner_hbm.1, ...), custom_call_target="tpu_custom_call" | custom-call | flops 1048576 | tf_op jit(solution)/shard_map/pallas_call | solution.py:309
  4.3 5.4 %collective-permute-start.2 = (bf16[32,2304]{1,0:T(8,128)(2,1)S(1)}, bf16[32,2304]{1,0:T(8,128)(2,1)S(1)}, u32[]{:S(2)}, u32[]{:S(2)}) collective-permute-start(bf16[32,2304]{1,0:T(8,128)(2,1)S(1)} %get-tuple-element.86), channel_id=1, source_target_pairs={{0,240},{16,32},{32,16},{48,64},{64,48},{80,96},{96,80},{112,128},... | collective-permute-start | bytes 442376 | tf_op jit(solution)/shard_map/ppermute | solution.py:360
  9.7 0.4 shard_map.75
  10.2 0.5 %collective-permute-start.1 = (bf16[32,1024]{1,0:T(8,128)(2,1)S(1)}, bf16[32,1024]{1,0:T(8,128)(2,1)S(1)}, u32[]{:S(2)}, u32[]{:S(2)}) collective-permute-start(bf16[32,1024]{1,0:T(8,128)(2,1)S(1)} %get-tuple-element.82), channel_id=1, source_target_pairs={{0,16},{16,0},{32,48},{48,32},{64,80},{80,64},{96,112},{112,96},{1... | collective-permute-start | bytes 196616 | tf_op jit(solution)/shard_map/ppermute | solution.py:368
  10.7 1.2 %shard_map.74 = (f32[2,32,1024]{2,1,0:T(8,128)S(1)}, f32[2,32,1024]{2,1,0:T(8,128)S(1)}, bf16[1024,1024]{1,0:T(8,128)(2,1)S(1)}) custom-call(f32[2,32,1024]{2,1,0:T(8,128)S(1)} %get-tuple-element.67.refs_0_.x_ref.refs_1_, f32[2,5,8,128]{3,2,1,0:T(8,128)S(1)} %get-tuple-element.68.refs_1_.refs_4_, f32[7,128]{1,0:T(8,128)S(1)} %get-tuple-element.69.refs_2_.refs_5_.weight_ref, ...), custom_call_target="tpu_custom_call" | custom-call | flops 1048576 | tf_op jit(solution)/shard_map/pallas_call | solution.py:309
  11.9 0.5 %shard_map.76 = (f32[2,32,1024]{2,1,0:T(8,128)S(1)}, bf16[1024,1024]{1,0:T(8,128)(2,1)S(1)}) custom-call(f32[2,32,1024]{2,1,0:T(8,128)S(1)} %get-tuple-element.78.part_ref, bf16[1024,1024]{1,0:T(8,128)(2,1)S(1)} %get-tuple-element.80.w_ref, f32[2,2,128]{2,1,0:T(2,128)S(1)} %get-tuple-element.79.rim_ref, bf16[32,1280]{1,0:T(8,128)(2,1)S(1)} %collective-permute-done.rows_ref, ...), custom_call_target="tpu_custom_call" | custom-call | tf_op jit(solution)/shard_map/pallas_call | solution.py:309
  12.5 0.7 %collective-permute-start.6 = (bf16[32,2304]{1,0:T(8,128)(2,1)S(1)}, bf16[32,2304]{1,0:T(8,128)(2,1)S(1)}, u32[]{:S(2)}, u32[]{:S(2)}) collective-permute-start(bf16[32,2304]{1,0:T(8,128)(2,1)S(1)} %get-tuple-element.95), channel_id=1, source_target_pairs={{0,16},{16,32},{32,48},{48,64},{64,80},{80,96},{96,112},{112,128},... | collective-permute-start | bytes 442376 | tf_op jit(solution)/shard_map/ppermute | solution.py:362
  13.2 0.6 %shard_map.78 = (f32[2,32,1024]{2,1,0:T(8,128)S(1)}, bf16[32,2304]{1,0:T(8,128)(2,1)S(1)}) custom-call(f32[2,32,1024]{2,1,0:T(8,128)S(1)} %get-tuple-element.84.sum_ref, bf16[1024,1024]{1,0:T(8,128)(2,1)S(1)} %get-tuple-element.83.refs_0_.w_ref, bf16[1024,1024]{1,0:T(8,128)(2,1)S(1)} %get-tuple-element.85.turned_ref, ...), custom_call_target="tpu_custom_call", output_to_operand_aliasing={{0}: (5, {})} | custom-call | flops 1048576 | tf_op jit(solution)/shard_map/pallas_call | solution.py:309
  13.8 2.4 %collective-permute-start.5 = (bf16[32,2304]{1,0:T(8,128)(2,1)S(1)}, bf16[32,2304]{1,0:T(8,128)(2,1)S(1)}, u32[]{:S(2)}, u32[]{:S(2)}) collective-permute-start(bf16[32,2304]{1,0:T(8,128)(2,1)S(1)} %get-tuple-element.94), channel_id=1, source_target_pairs={{16,0},{32,16},{48,32},{64,48},{80,64},{96,80},{112,96},{128,112},... | collective-permute-start | bytes 442376 | tf_op jit(solution)/shard_map/ppermute | solution.py:362
  16.1 0.3 shard_map.80
  16.5 0.5 %collective-permute-start.4 = (bf16[32,1024]{1,0:T(8,128)(2,1)S(1)}, bf16[32,1024]{1,0:T(8,128)(2,1)S(1)}, u32[]{:S(2)}, u32[]{:S(2)}) collective-permute-start(bf16[32,1024]{1,0:T(8,128)(2,1)S(1)} %get-tuple-element.93), channel_id=1, source_target_pairs={{0,16},{16,0},{32,48},{48,32},{64,80},{80,64},{96,112},{112,96},{1... | collective-permute-start | bytes 196616 | tf_op jit(solution)/shard_map/ppermute | solution.py:368
  17.0 1.1 %shard_map.79 = (f32[2,32,1024]{2,1,0:T(8,128)S(1)}, f32[2,32,1024]{2,1,0:T(8,128)S(1)}) custom-call(f32[2,32,1024]{2,1,0:T(8,128)S(1)} %get-tuple-element.88.refs_0_.x_ref.refs_1_, f32[2,32,1024]{2,1,0:T(8,128)S(1)} %get-tuple-element.67.refs_0_.x_ref.refs_1_, f32[2,32,1024]{2,1,0:T(8,128)S(1)} %get-tuple-element.89.refs_2_, ...), custom_call_target="tpu_custom_call" | custom-call | flops 1048576 | tf_op jit(solution)/shard_map/pallas_call | solution.py:309
  18.1 0.5 %shard_map.81.sum_ref = f32[2,32,1024]{2,1,0:T(8,128)S(1)} custom-call(f32[2,32,1024]{2,1,0:T(8,128)S(1)} %get-tuple-element.91.part_ref, bf16[1024,1024]{1,0:T(8,128)(2,1)S(1)} %get-tuple-element.80.w_ref, f32[2,2,128]{2,1,0:T(2,128)S(1)} %get-tuple-element.79.rim_ref, bf16[32,1280]{1,0:T(8,128)(2,1)S(1)} %collective-permute-done.3.rows_ref, ...), custom_call_target="tpu_custom_call" | custom-call | tf_op jit(solution)/shard_map/pallas_call | solution.py:309
  18.6 0.3 collective-permute-done.6.got_ref
  18.9 0.6 %shard_map.82 = (f32[2,32,1024]{2,1,0:T(8,128)S(1)}, bf16[32,2304]{1,0:T(8,128)(2,1)S(1)}) custom-call(f32[2,32,1024]{2,1,0:T(8,128)S(1)} %shard_map.81.sum_ref, bf16[1024,1024]{1,0:T(8,128)(2,1)S(1)} %get-tuple-element.83.refs_0_.w_ref, bf16[1024,1024]{1,0:T(8,128)(2,1)S(1)} %get-tuple-element.85.turned_ref, f32[2,2,128]{2,1,0:T(2,128)S(1)} %get-tuple-element.79.rim_ref, ...), custom_call_target="tpu_custom_call" | custom-call | flops 1048576 | tf_op jit(solution)/shard_map/pallas_call | solution.py:309
  19.5 0.2 collective-permute-start.10
  19.7 0.9 %collective-permute-start.9 = (bf16[32,2304]{1,0:T(8,128)(2,1)S(1)}, bf16[32,2304]{1,0:T(8,128)(2,1)S(1)}, u32[]{:S(2)}, u32[]{:S(2)}) collective-permute-start(bf16[32,2304]{1,0:T(8,128)(2,1)S(1)} %get-tuple-element.102), channel_id=1, source_target_pairs={{0,16},{16,32},{32,48},{48,64},{64,80},{80,96},{96,112},{112,128},... | collective-permute-start | bytes 442376 | tf_op jit(solution)/shard_map/ppermute | solution.py:362
  20.6 0.3 shard_map.85
  21.0 0.5 %collective-permute-start.8 = (bf16[32,1024]{1,0:T(8,128)(2,1)S(1)}, bf16[32,1024]{1,0:T(8,128)(2,1)S(1)}, u32[]{:S(2)}, u32[]{:S(2)}) collective-permute-start(bf16[32,1024]{1,0:T(8,128)(2,1)S(1)} %get-tuple-element.101), channel_id=1, source_target_pairs={{0,16},{16,0},{32,48},{48,32},{64,80},{80,64},{96,112},{112,96},{1... | collective-permute-start | bytes 196616 | tf_op jit(solution)/shard_map/ppermute | solution.py:368
  21.5 1.1 %shard_map.84 = (f32[2,32,1024]{2,1,0:T(8,128)S(1)}, f32[2,32,1024]{2,1,0:T(8,128)S(1)}) custom-call(f32[2,32,1024]{2,1,0:T(8,128)S(1)} %get-tuple-element.97.refs_0_.x_ref.refs_1_, f32[2,32,1024]{2,1,0:T(8,128)S(1)} %get-tuple-element.88.refs_0_.x_ref.refs_1_, f32[2,32,1024]{2,1,0:T(8,128)S(1)} %get-tuple-element.98.refs_2_, ...), custom_call_target="tpu_custom_call" | custom-call | flops 1048576 | tf_op jit(solution)/shard_map/pallas_call | solution.py:309
  22.6 0.5 %shard_map.86.sum_ref = f32[2,32,1024]{2,1,0:T(8,128)S(1)} custom-call(f32[2,32,1024]{2,1,0:T(8,128)S(1)} %get-tuple-element.99.part_ref, bf16[1024,1024]{1,0:T(8,128)(2,1)S(1)} %get-tuple-element.80.w_ref, f32[2,2,128]{2,1,0:T(2,128)S(1)} %get-tuple-element.79.rim_ref, bf16[32,1280]{1,0:T(8,128)(2,1)S(1)} %collective-permute-done.7.rows_ref, ...), custom_call_target="tpu_custom_call" | custom-call | tf_op jit(solution)/shard_map/pallas_call | solution.py:309
  23.2 0.8 %collective-permute-start.14 = (bf16[32,2304]{1,0:T(8,128)(2,1)S(1)}, bf16[32,2304]{1,0:T(8,128)(2,1)S(1)}, u32[]{:S(2)}, u32[]{:S(2)}) collective-permute-start(bf16[32,2304]{1,0:T(8,128)(2,1)S(1)} %get-tuple-element.111), channel_id=1, source_target_pairs={{0,16},{16,32},{32,48},{48,64},{64,80},{80,96},{96,112},{112,128},... | collective-permute-start | bytes 442376 | tf_op jit(solution)/shard_map/ppermute | solution.py:362
  24.0 1.6 %collective-permute-done.9.got_ref = bf16[32,2304]{1,0:T(8,128)(2,1)S(1)} collective-permute-done((bf16[32,2304]{1,0:T(8,128)(2,1)S(1)}, bf16[32,2304]{1,0:T(8,128)(2,1)S(1)}, u32[]{:S(2)}, u32[]{:S(2)}) %collective-permute-start.9) | collective-permute-done | bytes 147488 | tf_op jit(solution)/shard_map/ppermute | solution.py:362
  25.5 0.6 %shard_map.88 = (f32[2,32,1024]{2,1,0:T(8,128)S(1)}, bf16[32,2304]{1,0:T(8,128)(2,1)S(1)}) custom-call(f32[2,32,1024]{2,1,0:T(8,128)S(1)} %shard_map.86.sum_ref, bf16[1024,1024]{1,0:T(8,128)(2,1)S(1)} %get-tuple-element.83.refs_0_.w_ref, bf16[1024,1024]{1,0:T(8,128)(2,1)S(1)} %get-tuple-element.85.turned_ref, ...), custom_call_target="tpu_custom_call", output_to_operand_aliasing={{0}: (5, {})} | custom-call | flops 1048576 | tf_op jit(solution)/shard_map/pallas_call | solution.py:309
  26.1 0.3 collective-permute-start.13
  26.4 0.3 shard_map.90
  26.7 0.3 collective-permute-start.11
  27.0 0.2 collective-permute-start.12
  27.2 1.1 %shard_map.89 = (f32[2,32,1024]{2,1,0:T(8,128)S(1)}, f32[2,32,1024]{2,1,0:T(8,128)S(1)}) custom-call(f32[2,32,1024]{2,1,0:T(8,128)S(1)} %get-tuple-element.105.refs_0_.x_ref.refs_1_, f32[2,32,1024]{2,1,0:T(8,128)S(1)} %get-tuple-element.97.refs_0_.x_ref.refs_1_, f32[2,32,1024]{2,1,0:T(8,128)S(1)} %get-tuple-element.106.refs_2_, ...), custom_call_target="tpu_custom_call" | custom-call | flops 1048576 | tf_op jit(solution)/shard_map/pallas_call | solution.py:309
  28.4 0.5 %shard_map.91.sum_ref = f32[2,32,1024]{2,1,0:T(8,128)S(1)} custom-call(f32[2,32,1024]{2,1,0:T(8,128)S(1)} %get-tuple-element.107.part_ref, bf16[1024,1024]{1,0:T(8,128)(2,1)S(1)} %get-tuple-element.80.w_ref, f32[2,2,128]{2,1,0:T(2,128)S(1)} %get-tuple-element.79.rim_ref, bf16[32,1280]{1,0:T(8,128)(2,1)S(1)} %collective-permute-done.11.rows_ref, ...), custom_call_target="tpu_custom_call" | custom-call | tf_op jit(solution)/shard_map/pallas_call | solution.py:309
  28.9 0.1 collective-permute-done.14.got_ref
  29.0 0.6 %shard_map.92 = (f32[2,32,1024]{2,1,0:T(8,128)S(1)}, bf16[32,2304]{1,0:T(8,128)(2,1)S(1)}) custom-call(f32[2,32,1024]{2,1,0:T(8,128)S(1)} %shard_map.91.sum_ref, bf16[1024,1024]{1,0:T(8,128)(2,1)S(1)} %get-tuple-element.83.refs_0_.w_ref, bf16[1024,1024]{1,0:T(8,128)(2,1)S(1)} %get-tuple-element.85.turned_ref, f32[2,2,128]{2,1,0:T(2,128)S(1)} %get-tuple-element.79.rim_ref, ...), custom_call_target="tpu_custom_call" | custom-call | flops 1048576 | tf_op jit(solution)/shard_map/pallas_call | solution.py:309
  29.5 0.3 collective-permute-start.18
  29.8 0.9 %collective-permute-start.17 = (bf16[32,2304]{1,0:T(8,128)(2,1)S(1)}, bf16[32,2304]{1,0:T(8,128)(2,1)S(1)}, u32[]{:S(2)}, u32[]{:S(2)}) collective-permute-start(bf16[32,2304]{1,0:T(8,128)(2,1)S(1)} %get-tuple-element.118), channel_id=1, source_target_pairs={{0,16},{16,32},{32,48},{48,64},{64,80},{80,96},{96,112},{112,128},... | collective-permute-start | bytes 442376 | tf_op jit(solution)/shard_map/ppermute | solution.py:362
  30.7 0.3 shard_map.95
  31.0 0.3 collective-permute-start.15
  31.3 0.2 collective-permute-start.16
  31.5 1.1 %shard_map.94 = (f32[2,32,1024]{2,1,0:T(8,128)S(1)}, f32[2,32,1024]{2,1,0:T(8,128)S(1)}) custom-call(f32[2,32,1024]{2,1,0:T(8,128)S(1)} %get-tuple-element.113.refs_0_.x_ref.refs_1_, f32[2,32,1024]{2,1,0:T(8,128)S(1)} %get-tuple-element.105.refs_0_.x_ref.refs_1_, f32[2,32,1024]{2,1,0:T(8,128)S(1)} %get-tuple-element.114.refs_2_, ...), custom_call_target="tpu_custom_call" | custom-call | flops 1048576 | tf_op jit(solution)/shard_map/pallas_call | solution.py:309
  32.7 0.5 %shard_map.96.sum_ref = f32[2,32,1024]{2,1,0:T(8,128)S(1)} custom-call(f32[2,32,1024]{2,1,0:T(8,128)S(1)} %get-tuple-element.115.part_ref, bf16[1024,1024]{1,0:T(8,128)(2,1)S(1)} %get-tuple-element.80.w_ref, f32[2,2,128]{2,1,0:T(2,128)S(1)} %get-tuple-element.79.rim_ref, bf16[32,1280]{1,0:T(8,128)(2,1)S(1)} %collective-permute-done.15.rows_ref, ...), custom_call_target="tpu_custom_call" | custom-call | tf_op jit(solution)/shard_map/pallas_call | solution.py:309
  33.2 2.4 %collective-permute-done.17.got_ref = bf16[32,2304]{1,0:T(8,128)(2,1)S(1)} collective-permute-done((bf16[32,2304]{1,0:T(8,128)(2,1)S(1)}, bf16[32,2304]{1,0:T(8,128)(2,1)S(1)}, u32[]{:S(2)}, u32[]{:S(2)}) %collective-permute-start.17) | collective-permute-done | bytes 147488 | tf_op jit(solution)/shard_map/ppermute | solution.py:362
  35.6 0.6 %shard_map.98 = (f32[2,32,1024]{2,1,0:T(8,128)S(1)}, bf16[32,2304]{1,0:T(8,128)(2,1)S(1)}) custom-call(f32[2,32,1024]{2,1,0:T(8,128)S(1)} %shard_map.96.sum_ref, bf16[1024,1024]{1,0:T(8,128)(2,1)S(1)} %get-tuple-element.83.refs_0_.w_ref, bf16[1024,1024]{1,0:T(8,128)(2,1)S(1)} %get-tuple-element.85.turned_ref, ...), custom_call_target="tpu_custom_call", output_to_operand_aliasing={{0}: (5, {})} | custom-call | flops 1048576 | tf_op jit(solution)/shard_map/pallas_call | solution.py:309
  36.2 0.5 %collective-permute-start.21 = (bf16[32,2304]{1,0:T(8,128)(2,1)S(1)}, bf16[32,2304]{1,0:T(8,128)(2,1)S(1)}, u32[]{:S(2)}, u32[]{:S(2)}) collective-permute-start(bf16[32,2304]{1,0:T(8,128)(2,1)S(1)} %get-tuple-element.127), channel_id=1, source_target_pairs={{0,16},{16,32},{32,48},{48,64},{64,80},{80,96},{96,112},{112,128},... | collective-permute-start | bytes 442376 | tf_op jit(solution)/shard_map/ppermute | solution.py:362
  36.7 0.3 shard_map.100
  37.1 0.5 %collective-permute-start.20 = (bf16[32,1024]{1,0:T(8,128)(2,1)S(1)}, bf16[32,1024]{1,0:T(8,128)(2,1)S(1)}, u32[]{:S(2)}, u32[]{:S(2)}) collective-permute-start(bf16[32,1024]{1,0:T(8,128)(2,1)S(1)} %get-tuple-element.125), channel_id=1, source_target_pairs={{0,16},{16,0},{32,48},{48,32},{64,80},{80,64},{96,112},{112,96},{1... | collective-permute-start | bytes 196616 | tf_op jit(solution)/shard_map/ppermute | solution.py:368
  37.6 1.1 %shard_map.99 = (f32[2,32,1024]{2,1,0:T(8,128)S(1)}, f32[2,32,1024]{2,1,0:T(8,128)S(1)}) custom-call(f32[2,32,1024]{2,1,0:T(8,128)S(1)} %get-tuple-element.121.refs_0_.x_ref, f32[2,32,1024]{2,1,0:T(8,128)S(1)} %get-tuple-element.113.refs_0_.x_ref.refs_1_, f32[2,32,1024]{2,1,0:T(8,128)S(1)} %get-tuple-element.122.refs_2_, ...), custom_call_target="tpu_custom_call" | custom-call | flops 1048576 | tf_op jit(solution)/shard_map/pallas_call | solution.py:309
  38.7 0.5 %shard_map.101.sum_ref = f32[2,32,1024]{2,1,0:T(8,128)S(1)} custom-call(f32[2,32,1024]{2,1,0:T(8,128)S(1)} %get-tuple-element.123.part_ref, bf16[1024,1024]{1,0:T(8,128)(2,1)S(1)} %get-tuple-element.80.w_ref, f32[2,2,128]{2,1,0:T(2,128)S(1)} %get-tuple-element.79.rim_ref, bf16[32,1280]{1,0:T(8,128)(2,1)S(1)} %collective-permute-done.19.rows_ref, ...), custom_call_target="tpu_custom_call" | custom-call | tf_op jit(solution)/shard_map/pallas_call | solution.py:309
  39.2 2.8 %collective-permute-done.21.up_ref = bf16[32,2304]{1,0:T(8,128)(2,1)S(1)} collective-permute-done((bf16[32,2304]{1,0:T(8,128)(2,1)S(1)}, bf16[32,2304]{1,0:T(8,128)(2,1)S(1)}, u32[]{:S(2)}, u32[]{:S(2)}) %collective-permute-start.21) | collective-permute-done | bytes 147488 | tf_op jit(solution)/shard_map/ppermute | solution.py:362
  42.0 1.1 %shard_map.102 = f32[2,8,32,128]{3,2,1,0:T(8,128)} custom-call(f32[2,32,1024]{2,1,0:T(8,128)S(1)} %shard_map.101.sum_ref, f32[2,32,1024]{2,1,0:T(8,128)S(1)} %get-tuple-element.126.filt_ref, bf16[1024,1024]{1,0:T(8,128)(2,1)S(1)} %get-tuple-element.85.turned_ref, f32[2,2,128]{2,1,0:T(2,128)S(1)} %get-tuple-element.79.rim_ref, ...), custom_call_target="tpu_custom_call" | custom-call | flops 1048576 | tf_op jit(solution)/shard_map/pallas_call | solution.py:309
  (28 shorter events, 0.4 us)
Async XLA Ops:
  4.3 8.2 %collective-permute-start.2 = (bf16[32,2304]{1,0:T(8,128)(2,1)S(1)}, bf16[32,2304]{1,0:T(8,128)(2,1)S(1)}, u32[]{:S(2)}, u32[]{:S(2)}) collective-permute-start(bf16[32,2304]{1,0:T(8,128)(2,1)S(1)} %get-tuple-element.86), channel_id=1, source_target_pairs={{0,240},{16,32},{32,16},{48,64},{64,48},{80,96},{96,80},{112,128},... | collective-permute-start | bytes 442376 | tf_op jit(solution)/shard_map/ppermute | solution.py:360
  10.1 1.8 %collective-permute-start = (bf16[32,1280]{1,0:T(8,128)(2,1)S(1)}, bf16[32,1280]{1,0:T(8,128)(2,1)S(1)}, u32[]{:S(2)}, u32[]{:S(2)}) collective-permute-start(bf16[32,1280]{1,0:T(8,128)(2,1)S(1)} %get-tuple-element.81), channel_id=1, source_target_pairs={{0,16},{16,0},{32,48},{48,32},{64,80},{80,64},{96,112},{112,96},{1... | collective-permute-start | bytes 245768 | tf_op jit(solution)/shard_map/ppermute | solution.py:368
  10.2 1.7 %collective-permute-start.1 = (bf16[32,1024]{1,0:T(8,128)(2,1)S(1)}, bf16[32,1024]{1,0:T(8,128)(2,1)S(1)}, u32[]{:S(2)}, u32[]{:S(2)}) collective-permute-start(bf16[32,1024]{1,0:T(8,128)(2,1)S(1)} %get-tuple-element.82), channel_id=1, source_target_pairs={{0,16},{16,0},{32,48},{48,32},{64,80},{80,64},{96,112},{112,96},{1... | collective-permute-start | bytes 196616 | tf_op jit(solution)/shard_map/ppermute | solution.py:368
  12.5 6.4 %collective-permute-start.6 = (bf16[32,2304]{1,0:T(8,128)(2,1)S(1)}, bf16[32,2304]{1,0:T(8,128)(2,1)S(1)}, u32[]{:S(2)}, u32[]{:S(2)}) collective-permute-start(bf16[32,2304]{1,0:T(8,128)(2,1)S(1)} %get-tuple-element.95), channel_id=1, source_target_pairs={{0,16},{16,32},{32,48},{48,64},{64,80},{80,96},{96,112},{112,128},... | collective-permute-start | bytes 442376 | tf_op jit(solution)/shard_map/ppermute | solution.py:362
  13.8 6.0 %collective-permute-start.5 = (bf16[32,2304]{1,0:T(8,128)(2,1)S(1)}, bf16[32,2304]{1,0:T(8,128)(2,1)S(1)}, u32[]{:S(2)}, u32[]{:S(2)}) collective-permute-start(bf16[32,2304]{1,0:T(8,128)(2,1)S(1)} %get-tuple-element.94), channel_id=1, source_target_pairs={{16,0},{32,16},{48,32},{64,48},{80,64},{96,80},{112,96},{128,112},... | collective-permute-start | bytes 442376 | tf_op jit(solution)/shard_map/ppermute | solution.py:362
  16.4 1.7 %collective-permute-start.3 = (bf16[32,1280]{1,0:T(8,128)(2,1)S(1)}, bf16[32,1280]{1,0:T(8,128)(2,1)S(1)}, u32[]{:S(2)}, u32[]{:S(2)}) collective-permute-start(bf16[32,1280]{1,0:T(8,128)(2,1)S(1)} %get-tuple-element.92), channel_id=1, source_target_pairs={{0,16},{16,0},{32,48},{48,32},{64,80},{80,64},{96,112},{112,96},{1... | collective-permute-start | bytes 245768 | tf_op jit(solution)/shard_map/ppermute | solution.py:368
  16.5 1.6 %collective-permute-start.4 = (bf16[32,1024]{1,0:T(8,128)(2,1)S(1)}, bf16[32,1024]{1,0:T(8,128)(2,1)S(1)}, u32[]{:S(2)}, u32[]{:S(2)}) collective-permute-start(bf16[32,1024]{1,0:T(8,128)(2,1)S(1)} %get-tuple-element.93), channel_id=1, source_target_pairs={{0,16},{16,0},{32,48},{48,32},{64,80},{80,64},{96,112},{112,96},{1... | collective-permute-start | bytes 196616 | tf_op jit(solution)/shard_map/ppermute | solution.py:368
  19.5 3.6 %collective-permute-start.10 = (bf16[32,2304]{1,0:T(8,128)(2,1)S(1)}, bf16[32,2304]{1,0:T(8,128)(2,1)S(1)}, u32[]{:S(2)}, u32[]{:S(2)}) collective-permute-start(bf16[32,2304]{1,0:T(8,128)(2,1)S(1)} %get-tuple-element.103), channel_id=1, source_target_pairs={{16,0},{32,16},{48,32},{64,48},{80,64},{96,80},{112,96},{128,112},... | collective-permute-start | bytes 442376 | tf_op jit(solution)/shard_map/ppermute | solution.py:362
  19.7 5.8 %collective-permute-start.9 = (bf16[32,2304]{1,0:T(8,128)(2,1)S(1)}, bf16[32,2304]{1,0:T(8,128)(2,1)S(1)}, u32[]{:S(2)}, u32[]{:S(2)}) collective-permute-start(bf16[32,2304]{1,0:T(8,128)(2,1)S(1)} %get-tuple-element.102), channel_id=1, source_target_pairs={{0,16},{16,32},{32,48},{48,64},{64,80},{80,96},{96,112},{112,128},... | collective-permute-start | bytes 442376 | tf_op jit(solution)/shard_map/ppermute | solution.py:362
  20.9 1.7 %collective-permute-start.7 = (bf16[32,1280]{1,0:T(8,128)(2,1)S(1)}, bf16[32,1280]{1,0:T(8,128)(2,1)S(1)}, u32[]{:S(2)}, u32[]{:S(2)}) collective-permute-start(bf16[32,1280]{1,0:T(8,128)(2,1)S(1)} %get-tuple-element.100), channel_id=1, source_target_pairs={{0,16},{16,0},{32,48},{48,32},{64,80},{80,64},{96,112},{112,96},{1... | collective-permute-start | bytes 245768 | tf_op jit(solution)/shard_map/ppermute | solution.py:368
  21.0 1.6 %collective-permute-start.8 = (bf16[32,1024]{1,0:T(8,128)(2,1)S(1)}, bf16[32,1024]{1,0:T(8,128)(2,1)S(1)}, u32[]{:S(2)}, u32[]{:S(2)}) collective-permute-start(bf16[32,1024]{1,0:T(8,128)(2,1)S(1)} %get-tuple-element.101), channel_id=1, source_target_pairs={{0,16},{16,0},{32,48},{48,32},{64,80},{80,64},{96,112},{112,96},{1... | collective-permute-start | bytes 196616 | tf_op jit(solution)/shard_map/ppermute | solution.py:368
  23.2 5.8 %collective-permute-start.14 = (bf16[32,2304]{1,0:T(8,128)(2,1)S(1)}, bf16[32,2304]{1,0:T(8,128)(2,1)S(1)}, u32[]{:S(2)}, u32[]{:S(2)}) collective-permute-start(bf16[32,2304]{1,0:T(8,128)(2,1)S(1)} %get-tuple-element.111), channel_id=1, source_target_pairs={{0,16},{16,32},{32,48},{48,64},{64,80},{80,96},{96,112},{112,128},... | collective-permute-start | bytes 442376 | tf_op jit(solution)/shard_map/ppermute | solution.py:362
  26.1 3.7 %collective-permute-start.13 = (bf16[32,2304]{1,0:T(8,128)(2,1)S(1)}, bf16[32,2304]{1,0:T(8,128)(2,1)S(1)}, u32[]{:S(2)}, u32[]{:S(2)}) collective-permute-start(bf16[32,2304]{1,0:T(8,128)(2,1)S(1)} %get-tuple-element.110), channel_id=1, source_target_pairs={{16,0},{32,16},{48,32},{64,48},{80,64},{96,80},{112,96},{128,112},... | collective-permute-start | bytes 442376 | tf_op jit(solution)/shard_map/ppermute | solution.py:362
  26.7 1.7 %collective-permute-start.11 = (bf16[32,1280]{1,0:T(8,128)(2,1)S(1)}, bf16[32,1280]{1,0:T(8,128)(2,1)S(1)}, u32[]{:S(2)}, u32[]{:S(2)}) collective-permute-start(bf16[32,1280]{1,0:T(8,128)(2,1)S(1)} %get-tuple-element.108), channel_id=1, source_target_pairs={{0,16},{16,0},{32,48},{48,32},{64,80},{80,64},{96,112},{112,96},{1... | collective-permute-start | bytes 245768 | tf_op jit(solution)/shard_map/ppermute | solution.py:368
  27.0 1.4 %collective-permute-start.12 = (bf16[32,1024]{1,0:T(8,128)(2,1)S(1)}, bf16[32,1024]{1,0:T(8,128)(2,1)S(1)}, u32[]{:S(2)}, u32[]{:S(2)}) collective-permute-start(bf16[32,1024]{1,0:T(8,128)(2,1)S(1)} %get-tuple-element.109), channel_id=1, source_target_pairs={{0,16},{16,0},{32,48},{48,32},{64,80},{80,64},{96,112},{112,96},{1... | collective-permute-start | bytes 196616 | tf_op jit(solution)/shard_map/ppermute | solution.py:368
  29.5 3.6 %collective-permute-start.18 = (bf16[32,2304]{1,0:T(8,128)(2,1)S(1)}, bf16[32,2304]{1,0:T(8,128)(2,1)S(1)}, u32[]{:S(2)}, u32[]{:S(2)}) collective-permute-start(bf16[32,2304]{1,0:T(8,128)(2,1)S(1)} %get-tuple-element.119), channel_id=1, source_target_pairs={{16,0},{32,16},{48,32},{64,48},{80,64},{96,80},{112,96},{128,112},... | collective-permute-start | bytes 442376 | tf_op jit(solution)/shard_map/ppermute | solution.py:362
  29.8 5.8 %collective-permute-start.17 = (bf16[32,2304]{1,0:T(8,128)(2,1)S(1)}, bf16[32,2304]{1,0:T(8,128)(2,1)S(1)}, u32[]{:S(2)}, u32[]{:S(2)}) collective-permute-start(bf16[32,2304]{1,0:T(8,128)(2,1)S(1)} %get-tuple-element.118), channel_id=1, source_target_pairs={{0,16},{16,32},{32,48},{48,64},{64,80},{80,96},{96,112},{112,128},... | collective-permute-start | bytes 442376 | tf_op jit(solution)/shard_map/ppermute | solution.py:362
  31.0 1.7 %collective-permute-start.15 = (bf16[32,1280]{1,0:T(8,128)(2,1)S(1)}, bf16[32,1280]{1,0:T(8,128)(2,1)S(1)}, u32[]{:S(2)}, u32[]{:S(2)}) collective-permute-start(bf16[32,1280]{1,0:T(8,128)(2,1)S(1)} %get-tuple-element.116), channel_id=1, source_target_pairs={{0,16},{16,0},{32,48},{48,32},{64,80},{80,64},{96,112},{112,96},{1... | collective-permute-start | bytes 245768 | tf_op jit(solution)/shard_map/ppermute | solution.py:368
  31.3 1.4 %collective-permute-start.16 = (bf16[32,1024]{1,0:T(8,128)(2,1)S(1)}, bf16[32,1024]{1,0:T(8,128)(2,1)S(1)}, u32[]{:S(2)}, u32[]{:S(2)}) collective-permute-start(bf16[32,1024]{1,0:T(8,128)(2,1)S(1)} %get-tuple-element.117), channel_id=1, source_target_pairs={{0,16},{16,0},{32,48},{48,32},{64,80},{80,64},{96,112},{112,96},{1... | collective-permute-start | bytes 196616 | tf_op jit(solution)/shard_map/ppermute | solution.py:368
  36.2 3.0 %collective-permute-start.22 = (bf16[32,2304]{1,0:T(8,128)(2,1)S(1)}, bf16[32,2304]{1,0:T(8,128)(2,1)S(1)}, u32[]{:S(2)}, u32[]{:S(2)}) collective-permute-start(bf16[32,2304]{1,0:T(8,128)(2,1)S(1)} %get-tuple-element.128), channel_id=1, source_target_pairs={{16,0},{32,16},{48,32},{64,48},{80,64},{96,80},{112,96},{128,112},... | collective-permute-start | bytes 442376 | tf_op jit(solution)/shard_map/ppermute | solution.py:362
  36.2 5.8 %collective-permute-start.21 = (bf16[32,2304]{1,0:T(8,128)(2,1)S(1)}, bf16[32,2304]{1,0:T(8,128)(2,1)S(1)}, u32[]{:S(2)}, u32[]{:S(2)}) collective-permute-start(bf16[32,2304]{1,0:T(8,128)(2,1)S(1)} %get-tuple-element.127), channel_id=1, source_target_pairs={{0,16},{16,32},{32,48},{48,64},{64,80},{80,96},{96,112},{112,128},... | collective-permute-start | bytes 442376 | tf_op jit(solution)/shard_map/ppermute | solution.py:362
  37.0 1.7 %collective-permute-start.19 = (bf16[32,1280]{1,0:T(8,128)(2,1)S(1)}, bf16[32,1280]{1,0:T(8,128)(2,1)S(1)}, u32[]{:S(2)}, u32[]{:S(2)}) collective-permute-start(bf16[32,1280]{1,0:T(8,128)(2,1)S(1)} %get-tuple-element.124), channel_id=1, source_target_pairs={{0,16},{16,0},{32,48},{48,32},{64,80},{80,64},{96,112},{112,96},{1... | collective-permute-start | bytes 245768 | tf_op jit(solution)/shard_map/ppermute | solution.py:368
  37.1 1.6 %collective-permute-start.20 = (bf16[32,1024]{1,0:T(8,128)(2,1)S(1)}, bf16[32,1024]{1,0:T(8,128)(2,1)S(1)}, u32[]{:S(2)}, u32[]{:S(2)}) collective-permute-start(bf16[32,1024]{1,0:T(8,128)(2,1)S(1)} %get-tuple-element.125), channel_id=1, source_target_pairs={{0,16},{16,0},{32,48},{48,32},{64,80},{80,64},{96,112},{112,96},{1... | collective-permute-start | bytes 196616 | tf_op jit(solution)/shard_map/ppermute | solution.py:368

commit v9 on v7

--- a/solution.py
+++ b/solution.py
@@ -384,7 +384,7 @@
             turned = near(turned_now[0])
         prev = x
         if order < degree - 1:
-            now, later = (1, 0) if order % 2 == 0 else (0, 1)
+            now, later = (0, 1) if order % 2 == 0 else (1, 0)
             x, far[now] = call(
                 functools.partial(outer, scale, now),
                 [field, payload],

time: 43.3 us -> 42.3 us (0.977)
  the two profiles are of different devices: /device:TPU:14 before, /device:TPU:1 now
where the time goes in v9:
time: 42.3 us; the launch traced here: 42.2 us
  starting transfers between devices  21 us (50%)
  Pallas kernels  20.4 us (48%)
  waiting for transfers between devices  0.56 us (1%)
    pallas_call x30, Pallas kernels, call(): pl.pallas_call(kernel, out_shape=outs, in_specs=specs or [IN_VMEM] * len(...  20.4 us
    ppermute x12, starting transfers between devices, body(): got_mate = [near(lax.ppermute(part, 'tile', mate_pairs)) for part in mate]  9.11 us
    ppermute x6, starting transfers between devices, body(): lax.ppermute(far[0], 'tile', down_pairs)  8.51 us
    ppermute x6, starting transfers between devices, body(): lax.ppermute(far[1], 'tile', up_pairs)  3.34 us
  transfers between devices with their start and end apart: 24, of which 2 were waited for; matrix products, arithmetic and copies ran while one was open for 0% of the time, Pallas kernels for 34%

profile of v9, /device:TPU:1, one launch (start us, length us, event | category | flops | bytes accessed | tf_op | source)
XLA Modules:
  0.0 42.2 jit_solution(12411524336237455197)
XLA Ops:
  0.0 4.3 %shard_map.73 = (f32[2,32,1024]{2,1,0:T(8,128)S(1)}, bf16[1024,1024]{1,0:T(8,128)(2,1)S(1)}, f32[2,5,8,128]{3,2,1,0:T(8,128)S(1)}, f32[2,2,128]{2,1,0:T(2,128)S(...) custom-call(s32[8,16]{1,0:T(8,128)} %partner_hbm.1, ...), custom_call_target="tpu_custom_call" | custom-call | flops 1048576 | tf_op jit(solution)/shard_map/pallas_call | solution.py:309
  4.3 3.0 %collective-permute-start.3 = (bf16[32,2304]{1,0:T(8,128)(2,1)S(1)}, bf16[32,2304]{1,0:T(8,128)(2,1)S(1)}, u32[]{:S(2)}, u32[]{:S(2)}) collective-permute-start(bf16[32,2304]{1,0:T(8,128)(2,1)S(1)} %get-tuple-element.86), channel_id=1, source_target_pairs={{0,16},{16,32},{32,48},{48,64},{64,80},{80,96},{96,112},{112,128},... | collective-permute-start | bytes 442376 | tf_op jit(solution)/shard_map/ppermute | solution.py:359
  7.3 0.2 collective-permute-start.2
  7.6 0.4 shard_map.75
  8.0 3.6 %collective-permute-start = (bf16[32,1280]{1,0:T(8,128)(2,1)S(1)}, bf16[32,1280]{1,0:T(8,128)(2,1)S(1)}, u32[]{:S(2)}, u32[]{:S(2)}) collective-permute-start(bf16[32,1280]{1,0:T(8,128)(2,1)S(1)} %get-tuple-element.81), channel_id=1, source_target_pairs={{0,16},{16,0},{32,48},{48,32},{64,80},{80,64},{96,112},{112,96},{1... | collective-permute-start | bytes 245768 | tf_op jit(solution)/shard_map/ppermute | solution.py:365
  11.6 0.1 collective-permute-start.1
  11.7 1.2 %shard_map.74 = (f32[2,32,1024]{2,1,0:T(8,128)S(1)}, f32[2,32,1024]{2,1,0:T(8,128)S(1)}, bf16[1024,1024]{1,0:T(8,128)(2,1)S(1)}) custom-call(f32[2,32,1024]{2,1,0:T(8,128)S(1)} %get-tuple-element.67.refs_0_.x_ref.refs_1_, f32[2,5,8,128]{3,2,1,0:T(8,128)S(1)} %get-tuple-element.68.refs_1_.refs_4_, f32[7,128]{1,0:T(8,128)S(1)} %get-tuple-element.69.refs_2_.refs_5_.weight_ref, ...), custom_call_target="tpu_custom_call" | custom-call | flops 1048576 | tf_op jit(solution)/shard_map/pallas_call | solution.py:309
  12.9 0.5 %shard_map.76 = (f32[2,32,1024]{2,1,0:T(8,128)S(1)}, bf16[1024,1024]{1,0:T(8,128)(2,1)S(1)}) custom-call(f32[2,32,1024]{2,1,0:T(8,128)S(1)} %get-tuple-element.78.part_ref, bf16[1024,1024]{1,0:T(8,128)(2,1)S(1)} %get-tuple-element.80.w_ref, f32[2,2,128]{2,1,0:T(2,128)S(1)} %get-tuple-element.79.rim_ref, bf16[32,1280]{1,0:T(8,128)(2,1)S(1)} %collective-permute-done.rows_ref, ...), custom_call_target="tpu_custom_call" | custom-call | tf_op jit(solution)/shard_map/pallas_call | solution.py:309
  13.5 1.0 %collective-permute-start.7 = (bf16[32,2304]{1,0:T(8,128)(2,1)S(1)}, bf16[32,2304]{1,0:T(8,128)(2,1)S(1)}, u32[]{:S(2)}, u32[]{:S(2)}) collective-permute-start(bf16[32,2304]{1,0:T(8,128)(2,1)S(1)} %get-tuple-element.95), channel_id=1, source_target_pairs={{16,0},{32,16},{48,32},{64,48},{80,64},{96,80},{112,96},{128,112},... | collective-permute-start | bytes 442376 | tf_op jit(solution)/shard_map/ppermute | solution.py:359
  14.6 0.6 %shard_map.78 = (f32[2,32,1024]{2,1,0:T(8,128)S(1)}, bf16[32,2304]{1,0:T(8,128)(2,1)S(1)}) custom-call(f32[2,32,1024]{2,1,0:T(8,128)S(1)} %get-tuple-element.84.sum_ref, bf16[1024,1024]{1,0:T(8,128)(2,1)S(1)} %get-tuple-element.83.refs_0_.w_ref, bf16[1024,1024]{1,0:T(8,128)(2,1)S(1)} %get-tuple-element.85.turned_ref, ...), custom_call_target="tpu_custom_call", output_to_operand_aliasing={{0}: (5, {})} | custom-call | flops 1048576 | tf_op jit(solution)/shard_map/pallas_call | solution.py:309
  15.1 0.1 collective-permute-start.6
  15.3 0.3 shard_map.80
  15.6 0.7 %collective-permute-start.4 = (bf16[32,1280]{1,0:T(8,128)(2,1)S(1)}, bf16[32,1280]{1,0:T(8,128)(2,1)S(1)}, u32[]{:S(2)}, u32[]{:S(2)}) collective-permute-start(bf16[32,1280]{1,0:T(8,128)(2,1)S(1)} %get-tuple-element.92), channel_id=1, source_target_pairs={{0,16},{16,0},{32,48},{48,32},{64,80},{80,64},{96,112},{112,96},{1... | collective-permute-start | bytes 245768 | tf_op jit(solution)/shard_map/ppermute | solution.py:365
  16.3 0.1 collective-permute-start.5
  16.4 1.1 %shard_map.79 = (f32[2,32,1024]{2,1,0:T(8,128)S(1)}, f32[2,32,1024]{2,1,0:T(8,128)S(1)}) custom-call(f32[2,32,1024]{2,1,0:T(8,128)S(1)} %get-tuple-element.88.refs_0_.x_ref.refs_1_, f32[2,32,1024]{2,1,0:T(8,128)S(1)} %get-tuple-element.67.refs_0_.x_ref.refs_1_, f32[2,32,1024]{2,1,0:T(8,128)S(1)} %get-tuple-element.89.refs_2_, ...), custom_call_target="tpu_custom_call" | custom-call | flops 1048576 | tf_op jit(solution)/shard_map/pallas_call | solution.py:309
  17.5 0.5 %shard_map.81.sum_ref = f32[2,32,1024]{2,1,0:T(8,128)S(1)} custom-call(f32[2,32,1024]{2,1,0:T(8,128)S(1)} %get-tuple-element.91.part_ref, bf16[1024,1024]{1,0:T(8,128)(2,1)S(1)} %get-tuple-element.80.w_ref, f32[2,2,128]{2,1,0:T(2,128)S(1)} %get-tuple-element.79.rim_ref, bf16[32,1280]{1,0:T(8,128)(2,1)S(1)} %collective-permute-done.4.rows_ref, ...), custom_call_target="tpu_custom_call" | custom-call | tf_op jit(solution)/shard_map/pallas_call | solution.py:309
  18.0 0.1 collective-permute-done.7.got_ref
  18.1 0.6 %shard_map.82 = (f32[2,32,1024]{2,1,0:T(8,128)S(1)}, bf16[32,2304]{1,0:T(8,128)(2,1)S(1)}) custom-call(f32[2,32,1024]{2,1,0:T(8,128)S(1)} %shard_map.81.sum_ref, bf16[1024,1024]{1,0:T(8,128)(2,1)S(1)} %get-tuple-element.83.refs_0_.w_ref, bf16[1024,1024]{1,0:T(8,128)(2,1)S(1)} %get-tuple-element.85.turned_ref, f32[2,2,128]{2,1,0:T(2,128)S(1)} %get-tuple-element.79.rim_ref, ...), custom_call_target="tpu_custom_call" | custom-call | flops 1048576 | tf_op jit(solution)/shard_map/pallas_call | solution.py:309
  18.8 3.6 %collective-permute-start.10 = (bf16[32,2304]{1,0:T(8,128)(2,1)S(1)}, bf16[32,2304]{1,0:T(8,128)(2,1)S(1)}, u32[]{:S(2)}, u32[]{:S(2)}) collective-permute-start(bf16[32,2304]{1,0:T(8,128)(2,1)S(1)} %get-tuple-element.102), channel_id=1, source_target_pairs={{16,0},{32,16},{48,32},{64,48},{80,64},{96,80},{112,96},{128,112},... | collective-permute-start | bytes 442376 | tf_op jit(solution)/shard_map/ppermute | solution.py:359
  22.3 0.3 shard_map.85
  22.6 0.1 collective-permute-start.8
  22.7 0.5 %collective-permute-start.9 = (bf16[32,1024]{1,0:T(8,128)(2,1)S(1)}, bf16[32,1024]{1,0:T(8,128)(2,1)S(1)}, u32[]{:S(2)}, u32[]{:S(2)}) collective-permute-start(bf16[32,1024]{1,0:T(8,128)(2,1)S(1)} %get-tuple-element.101), channel_id=1, source_target_pairs={{0,16},{16,0},{32,48},{48,32},{64,80},{80,64},{96,112},{112,96},{1... | collective-permute-start | bytes 196616 | tf_op jit(solution)/shard_map/ppermute | solution.py:365
  23.2 1.1 %shard_map.84 = (f32[2,32,1024]{2,1,0:T(8,128)S(1)}, f32[2,32,1024]{2,1,0:T(8,128)S(1)}) custom-call(f32[2,32,1024]{2,1,0:T(8,128)S(1)} %get-tuple-element.97.refs_0_.x_ref.refs_1_, f32[2,32,1024]{2,1,0:T(8,128)S(1)} %get-tuple-element.88.refs_0_.x_ref.refs_1_, f32[2,32,1024]{2,1,0:T(8,128)S(1)} %get-tuple-element.98.refs_2_, ...), custom_call_target="tpu_custom_call" | custom-call | flops 1048576 | tf_op jit(solution)/shard_map/pallas_call | solution.py:309
  24.3 0.5 %shard_map.86.sum_ref = f32[2,32,1024]{2,1,0:T(8,128)S(1)} custom-call(f32[2,32,1024]{2,1,0:T(8,128)S(1)} %get-tuple-element.99.part_ref, bf16[1024,1024]{1,0:T(8,128)(2,1)S(1)} %get-tuple-element.80.w_ref, f32[2,2,128]{2,1,0:T(2,128)S(1)} %get-tuple-element.79.rim_ref, bf16[32,1280]{1,0:T(8,128)(2,1)S(1)} %collective-permute-done.8.rows_ref, ...), custom_call_target="tpu_custom_call" | custom-call | tf_op jit(solution)/shard_map/pallas_call | solution.py:309
  24.9 0.9 %collective-permute-start.15 = (bf16[32,2304]{1,0:T(8,128)(2,1)S(1)}, bf16[32,2304]{1,0:T(8,128)(2,1)S(1)}, u32[]{:S(2)}, u32[]{:S(2)}) collective-permute-start(bf16[32,2304]{1,0:T(8,128)(2,1)S(1)} %get-tuple-element.111), channel_id=1, source_target_pairs={{16,0},{32,16},{48,32},{64,48},{80,64},{96,80},{112,96},{128,112},... | collective-permute-start | bytes 442376 | tf_op jit(solution)/shard_map/ppermute | solution.py:359
  25.8 0.7 %shard_map.88 = (f32[2,32,1024]{2,1,0:T(8,128)S(1)}, bf16[32,2304]{1,0:T(8,128)(2,1)S(1)}) custom-call(f32[2,32,1024]{2,1,0:T(8,128)S(1)} %shard_map.86.sum_ref, bf16[1024,1024]{1,0:T(8,128)(2,1)S(1)} %get-tuple-element.83.refs_0_.w_ref, bf16[1024,1024]{1,0:T(8,128)(2,1)S(1)} %get-tuple-element.85.turned_ref, ...), custom_call_target="tpu_custom_call", output_to_operand_aliasing={{0}: (5, {})} | custom-call | flops 1048576 | tf_op jit(solution)/shard_map/pallas_call | solution.py:309
  26.5 0.1 collective-permute-start.14
  26.6 0.3 shard_map.90
  26.9 0.4 %collective-permute-start.12 = (bf16[32,1280]{1,0:T(8,128)(2,1)S(1)}, bf16[32,1280]{1,0:T(8,128)(2,1)S(1)}, u32[]{:S(2)}, u32[]{:S(2)}) collective-permute-start(bf16[32,1280]{1,0:T(8,128)(2,1)S(1)} %get-tuple-element.108), channel_id=1, source_target_pairs={{0,16},{16,0},{32,48},{48,32},{64,80},{80,64},{96,112},{112,96},{1... | collective-permute-start | bytes 245768 | tf_op jit(solution)/shard_map/ppermute | solution.py:365
  27.4 0.1 collective-permute-start.13
  27.5 1.1 %shard_map.89 = (f32[2,32,1024]{2,1,0:T(8,128)S(1)}, f32[2,32,1024]{2,1,0:T(8,128)S(1)}) custom-call(f32[2,32,1024]{2,1,0:T(8,128)S(1)} %get-tuple-element.105.refs_0_.x_ref.refs_1_, f32[2,32,1024]{2,1,0:T(8,128)S(1)} %get-tuple-element.97.refs_0_.x_ref.refs_1_, f32[2,32,1024]{2,1,0:T(8,128)S(1)} %get-tuple-element.106.refs_2_, ...), custom_call_target="tpu_custom_call" | custom-call | flops 1048576 | tf_op jit(solution)/shard_map/pallas_call | solution.py:309
  28.6 0.5 %shard_map.91.sum_ref = f32[2,32,1024]{2,1,0:T(8,128)S(1)} custom-call(f32[2,32,1024]{2,1,0:T(8,128)S(1)} %get-tuple-element.107.part_ref, bf16[1024,1024]{1,0:T(8,128)(2,1)S(1)} %get-tuple-element.80.w_ref, f32[2,2,128]{2,1,0:T(2,128)S(1)} %get-tuple-element.79.rim_ref, bf16[32,1280]{1,0:T(8,128)(2,1)S(1)} %collective-permute-done.12.rows_ref, ...), custom_call_target="tpu_custom_call" | custom-call | tf_op jit(solution)/shard_map/pallas_call | solution.py:309
  29.1 0.3 collective-permute-done.15.got_ref
  29.4 0.6 %shard_map.92 = (f32[2,32,1024]{2,1,0:T(8,128)S(1)}, bf16[32,2304]{1,0:T(8,128)(2,1)S(1)}) custom-call(f32[2,32,1024]{2,1,0:T(8,128)S(1)} %shard_map.91.sum_ref, bf16[1024,1024]{1,0:T(8,128)(2,1)S(1)} %get-tuple-element.83.refs_0_.w_ref, bf16[1024,1024]{1,0:T(8,128)(2,1)S(1)} %get-tuple-element.85.turned_ref, f32[2,2,128]{2,1,0:T(2,128)S(1)} %get-tuple-element.79.rim_ref, ...), custom_call_target="tpu_custom_call" | custom-call | flops 1048576 | tf_op jit(solution)/shard_map/pallas_call | solution.py:309
  30.1 2.3 %collective-permute-start.18 = (bf16[32,2304]{1,0:T(8,128)(2,1)S(1)}, bf16[32,2304]{1,0:T(8,128)(2,1)S(1)}, u32[]{:S(2)}, u32[]{:S(2)}) collective-permute-start(bf16[32,2304]{1,0:T(8,128)(2,1)S(1)} %get-tuple-element.118), channel_id=1, source_target_pairs={{16,0},{32,16},{48,32},{64,48},{80,64},{96,80},{112,96},{128,112},... | collective-permute-start | bytes 442376 | tf_op jit(solution)/shard_map/ppermute | solution.py:359
  32.4 0.3 shard_map.95
  32.7 0.2 collective-permute-start.16
  32.9 0.4 collective-permute-start.17
  33.2 1.1 %shard_map.94 = (f32[2,32,1024]{2,1,0:T(8,128)S(1)}, f32[2,32,1024]{2,1,0:T(8,128)S(1)}) custom-call(f32[2,32,1024]{2,1,0:T(8,128)S(1)} %get-tuple-element.113.refs_0_.x_ref.refs_1_, f32[2,32,1024]{2,1,0:T(8,128)S(1)} %get-tuple-element.105.refs_0_.x_ref.refs_1_, f32[2,32,1024]{2,1,0:T(8,128)S(1)} %get-tuple-element.114.refs_2_, ...), custom_call_target="tpu_custom_call" | custom-call | flops 1048576 | tf_op jit(solution)/shard_map/pallas_call | solution.py:309
  34.4 0.5 %shard_map.96.sum_ref = f32[2,32,1024]{2,1,0:T(8,128)S(1)} custom-call(f32[2,32,1024]{2,1,0:T(8,128)S(1)} %get-tuple-element.115.part_ref, bf16[1024,1024]{1,0:T(8,128)(2,1)S(1)} %get-tuple-element.80.w_ref, f32[2,2,128]{2,1,0:T(2,128)S(1)} %get-tuple-element.79.rim_ref, bf16[32,1280]{1,0:T(8,128)(2,1)S(1)} %collective-permute-done.16.rows_ref, ...), custom_call_target="tpu_custom_call" | custom-call | tf_op jit(solution)/shard_map/pallas_call | solution.py:309
  35.0 0.6 %shard_map.98 = (f32[2,32,1024]{2,1,0:T(8,128)S(1)}, bf16[32,2304]{1,0:T(8,128)(2,1)S(1)}) custom-call(f32[2,32,1024]{2,1,0:T(8,128)S(1)} %shard_map.96.sum_ref, bf16[1024,1024]{1,0:T(8,128)(2,1)S(1)} %get-tuple-element.83.refs_0_.w_ref, bf16[1024,1024]{1,0:T(8,128)(2,1)S(1)} %get-tuple-element.85.turned_ref, ...), custom_call_target="tpu_custom_call", output_to_operand_aliasing={{0}: (5, {})} | custom-call | flops 1048576 | tf_op jit(solution)/shard_map/pallas_call | solution.py:309
  35.6 0.5 %collective-permute-start.23 = (bf16[32,2304]{1,0:T(8,128)(2,1)S(1)}, bf16[32,2304]{1,0:T(8,128)(2,1)S(1)}, u32[]{:S(2)}, u32[]{:S(2)}) collective-permute-start(bf16[32,2304]{1,0:T(8,128)(2,1)S(1)} %get-tuple-element.128), channel_id=1, source_target_pairs={{16,0},{32,16},{48,32},{64,48},{80,64},{96,80},{112,96},{128,112},... | collective-permute-start | bytes 442376 | tf_op jit(solution)/shard_map/ppermute | solution.py:359
  36.1 0.3 shard_map.100
  36.4 2.9 %collective-permute-start.20 = (bf16[32,1280]{1,0:T(8,128)(2,1)S(1)}, bf16[32,1280]{1,0:T(8,128)(2,1)S(1)}, u32[]{:S(2)}, u32[]{:S(2)}) collective-permute-start(bf16[32,1280]{1,0:T(8,128)(2,1)S(1)} %get-tuple-element.124), channel_id=1, source_target_pairs={{0,16},{16,0},{32,48},{48,32},{64,80},{80,64},{96,112},{112,96},{1... | collective-permute-start | bytes 245768 | tf_op jit(solution)/shard_map/ppermute | solution.py:365
  39.3 0.1 collective-permute-start.21
  39.4 1.1 %shard_map.99 = (f32[2,32,1024]{2,1,0:T(8,128)S(1)}, f32[2,32,1024]{2,1,0:T(8,128)S(1)}) custom-call(f32[2,32,1024]{2,1,0:T(8,128)S(1)} %get-tuple-element.121.refs_0_.x_ref, f32[2,32,1024]{2,1,0:T(8,128)S(1)} %get-tuple-element.113.refs_0_.x_ref.refs_1_, f32[2,32,1024]{2,1,0:T(8,128)S(1)} %get-tuple-element.122.refs_2_, ...), custom_call_target="tpu_custom_call" | custom-call | flops 1048576 | tf_op jit(solution)/shard_map/pallas_call | solution.py:309
  40.6 0.5 %shard_map.101.sum_ref = f32[2,32,1024]{2,1,0:T(8,128)S(1)} custom-call(f32[2,32,1024]{2,1,0:T(8,128)S(1)} %get-tuple-element.123.part_ref, bf16[1024,1024]{1,0:T(8,128)(2,1)S(1)} %get-tuple-element.80.w_ref, f32[2,2,128]{2,1,0:T(2,128)S(1)} %get-tuple-element.79.rim_ref, bf16[32,1280]{1,0:T(8,128)(2,1)S(1)} %collective-permute-done.20.rows_ref, ...), custom_call_target="tpu_custom_call" | custom-call | tf_op jit(solution)/shard_map/pallas_call | solution.py:309
  41.1 1.1 %shard_map.102 = f32[2,8,32,128]{3,2,1,0:T(8,128)} custom-call(f32[2,32,1024]{2,1,0:T(8,128)S(1)} %shard_map.101.sum_ref, f32[2,32,1024]{2,1,0:T(8,128)S(1)} %get-tuple-element.126.filt_ref, bf16[1024,1024]{1,0:T(8,128)(2,1)S(1)} %get-tuple-element.85.turned_ref, f32[2,2,128]{2,1,0:T(2,128)S(1)} %get-tuple-element.79.rim_ref, ...), custom_call_target="tpu_custom_call" | custom-call | flops 1048576 | tf_op jit(solution)/shard_map/pallas_call | solution.py:309
  (30 shorter events, 0.3 us)
Async XLA Ops:
  4.3 9.2 %collective-permute-start.3 = (bf16[32,2304]{1,0:T(8,128)(2,1)S(1)}, bf16[32,2304]{1,0:T(8,128)(2,1)S(1)}, u32[]{:S(2)}, u32[]{:S(2)}) collective-permute-start(bf16[32,2304]{1,0:T(8,128)(2,1)S(1)} %get-tuple-element.86), channel_id=1, source_target_pairs={{0,16},{16,32},{32,48},{48,64},{64,80},{80,96},{96,112},{112,128},... | collective-permute-start | bytes 442376 | tf_op jit(solution)/shard_map/ppermute | solution.py:359
  7.3 7.2 %collective-permute-start.2 = (bf16[32,2304]{1,0:T(8,128)(2,1)S(1)}, bf16[32,2304]{1,0:T(8,128)(2,1)S(1)}, u32[]{:S(2)}, u32[]{:S(2)}) collective-permute-start(bf16[32,2304]{1,0:T(8,128)(2,1)S(1)} %get-tuple-element.86), channel_id=1, source_target_pairs={{16,0},{32,16},{48,32},{64,48},{80,64},{96,80},{112,96},{128,112},... | collective-permute-start | bytes 442376 | tf_op jit(solution)/shard_map/ppermute | solution.py:359
  8.0 4.9 %collective-permute-start = (bf16[32,1280]{1,0:T(8,128)(2,1)S(1)}, bf16[32,1280]{1,0:T(8,128)(2,1)S(1)}, u32[]{:S(2)}, u32[]{:S(2)}) collective-permute-start(bf16[32,1280]{1,0:T(8,128)(2,1)S(1)} %get-tuple-element.81), channel_id=1, source_target_pairs={{0,16},{16,0},{32,48},{48,32},{64,80},{80,64},{96,112},{112,96},{1... | collective-permute-start | bytes 245768 | tf_op jit(solution)/shard_map/ppermute | solution.py:365
  11.6 1.3 %collective-permute-start.1 = (bf16[32,1024]{1,0:T(8,128)(2,1)S(1)}, bf16[32,1024]{1,0:T(8,128)(2,1)S(1)}, u32[]{:S(2)}, u32[]{:S(2)}) collective-permute-start(bf16[32,1024]{1,0:T(8,128)(2,1)S(1)} %get-tuple-element.82), channel_id=1, source_target_pairs={{0,16},{16,0},{32,48},{48,32},{64,80},{80,64},{96,112},{112,96},{1... | collective-permute-start | bytes 196616 | tf_op jit(solution)/shard_map/ppermute | solution.py:365
  13.5 4.6 %collective-permute-start.7 = (bf16[32,2304]{1,0:T(8,128)(2,1)S(1)}, bf16[32,2304]{1,0:T(8,128)(2,1)S(1)}, u32[]{:S(2)}, u32[]{:S(2)}) collective-permute-start(bf16[32,2304]{1,0:T(8,128)(2,1)S(1)} %get-tuple-element.95), channel_id=1, source_target_pairs={{16,0},{32,16},{48,32},{64,48},{80,64},{96,80},{112,96},{128,112},... | collective-permute-start | bytes 442376 | tf_op jit(solution)/shard_map/ppermute | solution.py:359
  15.1 3.6 %collective-permute-start.6 = (bf16[32,2304]{1,0:T(8,128)(2,1)S(1)}, bf16[32,2304]{1,0:T(8,128)(2,1)S(1)}, u32[]{:S(2)}, u32[]{:S(2)}) collective-permute-start(bf16[32,2304]{1,0:T(8,128)(2,1)S(1)} %get-tuple-element.94), channel_id=1, source_target_pairs={{0,16},{16,32},{32,48},{48,64},{64,80},{80,96},{96,112},{112,128},... | collective-permute-start | bytes 442376 | tf_op jit(solution)/shard_map/ppermute | solution.py:359
  15.6 1.9 %collective-permute-start.4 = (bf16[32,1280]{1,0:T(8,128)(2,1)S(1)}, bf16[32,1280]{1,0:T(8,128)(2,1)S(1)}, u32[]{:S(2)}, u32[]{:S(2)}) collective-permute-start(bf16[32,1280]{1,0:T(8,128)(2,1)S(1)} %get-tuple-element.92), channel_id=1, source_target_pairs={{0,16},{16,0},{32,48},{48,32},{64,80},{80,64},{96,112},{112,96},{1... | collective-permute-start | bytes 245768 | tf_op jit(solution)/shard_map/ppermute | solution.py:365
  16.3 1.3 %collective-permute-start.5 = (bf16[32,1024]{1,0:T(8,128)(2,1)S(1)}, bf16[32,1024]{1,0:T(8,128)(2,1)S(1)}, u32[]{:S(2)}, u32[]{:S(2)}) collective-permute-start(bf16[32,1024]{1,0:T(8,128)(2,1)S(1)} %get-tuple-element.93), channel_id=1, source_target_pairs={{0,16},{16,0},{32,48},{48,32},{64,80},{80,64},{96,112},{112,96},{1... | collective-permute-start | bytes 196616 | tf_op jit(solution)/shard_map/ppermute | solution.py:365
  18.7 6.1 %collective-permute-start.11 = (bf16[32,2304]{1,0:T(8,128)(2,1)S(1)}, bf16[32,2304]{1,0:T(8,128)(2,1)S(1)}, u32[]{:S(2)}, u32[]{:S(2)}) collective-permute-start(bf16[32,2304]{1,0:T(8,128)(2,1)S(1)} %get-tuple-element.103), channel_id=1, source_target_pairs={{0,16},{16,32},{32,48},{48,64},{64,80},{80,96},{96,112},{112,128},... | collective-permute-start | bytes 442376 | tf_op jit(solution)/shard_map/ppermute | solution.py:359
  18.8 7.0 %collective-permute-start.10 = (bf16[32,2304]{1,0:T(8,128)(2,1)S(1)}, bf16[32,2304]{1,0:T(8,128)(2,1)S(1)}, u32[]{:S(2)}, u32[]{:S(2)}) collective-permute-start(bf16[32,2304]{1,0:T(8,128)(2,1)S(1)} %get-tuple-element.102), channel_id=1, source_target_pairs={{16,0},{32,16},{48,32},{64,48},{80,64},{96,80},{112,96},{128,112},... | collective-permute-start | bytes 442376 | tf_op jit(solution)/shard_map/ppermute | solution.py:359
  22.6 1.7 %collective-permute-start.8 = (bf16[32,1280]{1,0:T(8,128)(2,1)S(1)}, bf16[32,1280]{1,0:T(8,128)(2,1)S(1)}, u32[]{:S(2)}, u32[]{:S(2)}) collective-permute-start(bf16[32,1280]{1,0:T(8,128)(2,1)S(1)} %get-tuple-element.100), channel_id=1, source_target_pairs={{0,16},{16,0},{32,48},{48,32},{64,80},{80,64},{96,112},{112,96},{1... | collective-permute-start | bytes 245768 | tf_op jit(solution)/shard_map/ppermute | solution.py:365
  22.7 1.6 %collective-permute-start.9 = (bf16[32,1024]{1,0:T(8,128)(2,1)S(1)}, bf16[32,1024]{1,0:T(8,128)(2,1)S(1)}, u32[]{:S(2)}, u32[]{:S(2)}) collective-permute-start(bf16[32,1024]{1,0:T(8,128)(2,1)S(1)} %get-tuple-element.101), channel_id=1, source_target_pairs={{0,16},{16,0},{32,48},{48,32},{64,80},{80,64},{96,112},{112,96},{1... | collective-permute-start | bytes 196616 | tf_op jit(solution)/shard_map/ppermute | solution.py:365
  24.9 4.6 %collective-permute-start.15 = (bf16[32,2304]{1,0:T(8,128)(2,1)S(1)}, bf16[32,2304]{1,0:T(8,128)(2,1)S(1)}, u32[]{:S(2)}, u32[]{:S(2)}) collective-permute-start(bf16[32,2304]{1,0:T(8,128)(2,1)S(1)} %get-tuple-element.111), channel_id=1, source_target_pairs={{16,0},{32,16},{48,32},{64,48},{80,64},{96,80},{112,96},{128,112},... | collective-permute-start | bytes 442376 | tf_op jit(solution)/shard_map/ppermute | solution.py:359
  26.5 3.6 %collective-permute-start.14 = (bf16[32,2304]{1,0:T(8,128)(2,1)S(1)}, bf16[32,2304]{1,0:T(8,128)(2,1)S(1)}, u32[]{:S(2)}, u32[]{:S(2)}) collective-permute-start(bf16[32,2304]{1,0:T(8,128)(2,1)S(1)} %get-tuple-element.110), channel_id=1, source_target_pairs={{0,16},{16,32},{32,48},{48,64},{64,80},{80,96},{96,112},{112,128},... | collective-permute-start | bytes 442376 | tf_op jit(solution)/shard_map/ppermute | solution.py:359
  26.9 1.7 %collective-permute-start.12 = (bf16[32,1280]{1,0:T(8,128)(2,1)S(1)}, bf16[32,1280]{1,0:T(8,128)(2,1)S(1)}, u32[]{:S(2)}, u32[]{:S(2)}) collective-permute-start(bf16[32,1280]{1,0:T(8,128)(2,1)S(1)} %get-tuple-element.108), channel_id=1, source_target_pairs={{0,16},{16,0},{32,48},{48,32},{64,80},{80,64},{96,112},{112,96},{1... | collective-permute-start | bytes 245768 | tf_op jit(solution)/shard_map/ppermute | solution.py:365
  27.4 1.3 %collective-permute-start.13 = (bf16[32,1024]{1,0:T(8,128)(2,1)S(1)}, bf16[32,1024]{1,0:T(8,128)(2,1)S(1)}, u32[]{:S(2)}, u32[]{:S(2)}) collective-permute-start(bf16[32,1024]{1,0:T(8,128)(2,1)S(1)} %get-tuple-element.109), channel_id=1, source_target_pairs={{0,16},{16,0},{32,48},{48,32},{64,80},{80,64},{96,112},{112,96},{1... | collective-permute-start | bytes 196616 | tf_op jit(solution)/shard_map/ppermute | solution.py:365
  30.0 4.9 %collective-permute-start.19 = (bf16[32,2304]{1,0:T(8,128)(2,1)S(1)}, bf16[32,2304]{1,0:T(8,128)(2,1)S(1)}, u32[]{:S(2)}, u32[]{:S(2)}) collective-permute-start(bf16[32,2304]{1,0:T(8,128)(2,1)S(1)} %get-tuple-element.119), channel_id=1, source_target_pairs={{0,16},{16,32},{32,48},{48,64},{64,80},{80,96},{96,112},{112,128},... | collective-permute-start | bytes 442376 | tf_op jit(solution)/shard_map/ppermute | solution.py:359
  30.1 4.9 %collective-permute-start.18 = (bf16[32,2304]{1,0:T(8,128)(2,1)S(1)}, bf16[32,2304]{1,0:T(8,128)(2,1)S(1)}, u32[]{:S(2)}, u32[]{:S(2)}) collective-permute-start(bf16[32,2304]{1,0:T(8,128)(2,1)S(1)} %get-tuple-element.118), channel_id=1, source_target_pairs={{16,0},{32,16},{48,32},{64,48},{80,64},{96,80},{112,96},{128,112},... | collective-permute-start | bytes 442376 | tf_op jit(solution)/shard_map/ppermute | solution.py:359
  32.7 1.7 %collective-permute-start.16 = (bf16[32,1280]{1,0:T(8,128)(2,1)S(1)}, bf16[32,1280]{1,0:T(8,128)(2,1)S(1)}, u32[]{:S(2)}, u32[]{:S(2)}) collective-permute-start(bf16[32,1280]{1,0:T(8,128)(2,1)S(1)} %get-tuple-element.116), channel_id=1, source_target_pairs={{0,16},{16,0},{32,48},{48,32},{64,80},{80,64},{96,112},{112,96},{1... | collective-permute-start | bytes 245768 | tf_op jit(solution)/shard_map/ppermute | solution.py:365
  32.9 1.5 %collective-permute-start.17 = (bf16[32,1024]{1,0:T(8,128)(2,1)S(1)}, bf16[32,1024]{1,0:T(8,128)(2,1)S(1)}, u32[]{:S(2)}, u32[]{:S(2)}) collective-permute-start(bf16[32,1024]{1,0:T(8,128)(2,1)S(1)} %get-tuple-element.117), channel_id=1, source_target_pairs={{0,16},{16,0},{32,48},{48,32},{64,80},{80,64},{96,112},{112,96},{1... | collective-permute-start | bytes 196616 | tf_op jit(solution)/shard_map/ppermute | solution.py:365
  35.6 5.5 %collective-permute-start.22 = (bf16[32,2304]{1,0:T(8,128)(2,1)S(1)}, bf16[32,2304]{1,0:T(8,128)(2,1)S(1)}, u32[]{:S(2)}, u32[]{:S(2)}) collective-permute-start(bf16[32,2304]{1,0:T(8,128)(2,1)S(1)} %get-tuple-element.127), channel_id=1, source_target_pairs={{0,16},{16,32},{32,48},{48,64},{64,80},{80,96},{96,112},{112,128},... | collective-permute-start | bytes 442376 | tf_op jit(solution)/shard_map/ppermute | solution.py:359
  35.6 5.5 %collective-permute-start.23 = (bf16[32,2304]{1,0:T(8,128)(2,1)S(1)}, bf16[32,2304]{1,0:T(8,128)(2,1)S(1)}, u32[]{:S(2)}, u32[]{:S(2)}) collective-permute-start(bf16[32,2304]{1,0:T(8,128)(2,1)S(1)} %get-tuple-element.128), channel_id=1, source_target_pairs={{16,0},{32,16},{48,32},{64,48},{80,64},{96,80},{112,96},{128,112},... | collective-permute-start | bytes 442376 | tf_op jit(solution)/shard_map/ppermute | solution.py:359
  36.4 4.2 %collective-permute-start.20 = (bf16[32,1280]{1,0:T(8,128)(2,1)S(1)}, bf16[32,1280]{1,0:T(8,128)(2,1)S(1)}, u32[]{:S(2)}, u32[]{:S(2)}) collective-permute-start(bf16[32,1280]{1,0:T(8,128)(2,1)S(1)} %get-tuple-element.124), channel_id=1, source_target_pairs={{0,16},{16,0},{32,48},{48,32},{64,80},{80,64},{96,112},{112,96},{1... | collective-permute-start | bytes 245768 | tf_op jit(solution)/shard_map/ppermute | solution.py:365
  39.3 1.3 %collective-permute-start.21 = (bf16[32,1024]{1,0:T(8,128)(2,1)S(1)}, bf16[32,1024]{1,0:T(8,128)(2,1)S(1)}, u32[]{:S(2)}, u32[]{:S(2)}) collective-permute-start(bf16[32,1024]{1,0:T(8,128)(2,1)S(1)} %get-tuple-element.125), channel_id=1, source_target_pairs={{0,16},{16,0},{32,48},{48,32},{64,80},{80,64},{96,112},{112,96},{1... | collective-permute-start | bytes 196616 | tf_op jit(solution)/shard_map/ppermute | solution.py:365

commit v10 on v9

--- a/solution.py
+++ b/solution.py
@@ -162,7 +162,22 @@
 
     for total in totals:
         total[...] = jnp.zeros_like(total)
-    for copy in copies:
+    copies[0].wait()
+    for pair in range(0, rows, PAIR):
+        places = range(pair, pair + PAIR)
+        for place in places:
+            fetch(kept(place)).wait()
+        for k in range(slots):
+            for place in places:
+                row = kept(place)
+                slot = partner_ref[row, k]
+                away = slot - tile * rows - row
+                away = jnp.where(away > all_rows // 2, away - all_rows, away)
+                away = jnp.where(away < -(all_rows // 2), away + all_rows, away)
+                at = jnp.where(slot >= 0, REACH + (1 - 2 * here) * away, offsets)
+                totals[place][at] += blocks[row, k].astype(jnp.float32)
+
+    for copy in copies[1:]:
         copy.wait()
     for n in range(coefs_ref.shape[0]):
         weight_ref[n : n + 1, :] = jnp.full((1, cols), coefs_ref[n], jnp.float32)
@@ -194,19 +209,6 @@
         for place in range(rows):
             x_ref[layer, :, place * cols : (place + 1) * cols] = states_ref[layer, kept(place)]
 
-    for pair in range(0, rows, PAIR):
-        places = range(pair, pair + PAIR)
-        for place in places:
-            fetch(kept(place)).wait()
-        for k in range(slots):
-            for place in places:
-                row = kept(place)
-                slot = partner_ref[row, k]
-                away = slot - tile * rows - row
-                away = jnp.where(away > all_rows // 2, away - all_rows, away)
-                away = jnp.where(away < -(all_rows // 2), away + all_rows, away)
-                at = jnp.where(slot >= 0, REACH + (1 - 2 * here) * away, offsets)
-                totals[place][at] += blocks[row, k].astype(jnp.float32)
     settle(totals, FAR, w_ref, cols)
     write_far(x_ref, w_ref, rim_ref, far_ref)
 

time: 42.3 us -> 41.6 us (0.983)
  Pallas kernels: 20.4 us -> 19.5 us
    pallas_call x30, Pallas kernels: 20.4 us -> 19.5 us  [call(): pl.pallas_call(kernel, out_shape=outs, in_specs=specs or [IN_VMEM] * len(...]
  transfers between devices with their start and end apart: 24 -> 24, of which waited for: 2 -> 3; matrix products, arithmetic and copies ran while one was open for 0% -> 0% of each run, Pallas kernels for 34% -> 34%
where the time goes in v10:
time: 41.6 us; the launch traced here: 41.5 us
  starting transfers between devices  21.3 us (51%)
  Pallas kernels  19.5 us (47%)
    pallas_call x30, Pallas kernels, call(): pl.pallas_call(kernel, out_shape=outs, in_specs=specs or [IN_VMEM] * len(...  19.5 us
    ppermute x12, starting transfers between devices, body(): got_mate = [near(lax.ppermute(part, 'tile', mate_pairs)) for part in mate]  9.3 us
    ppermute x6, starting transfers between devices, body(): lax.ppermute(far[0], 'tile', down_pairs)  8.5 us
    ppermute x6, starting transfers between devices, body(): lax.ppermute(far[1], 'tile', up_pairs)  3.5 us
  transfers between devices with their start and end apart: 24, of which 3 were waited for; matrix products, arithmetic and copies ran while one was open for 0% of the time, Pallas kernels for 34%

profile of v10, /device:TPU:1, one launch (start us, length us, event | category | flops | bytes accessed | tf_op | source)
XLA Modules:
  0.0 41.5 jit_solution(3585153045794844566)
XLA Ops:
  0.0 3.5 %shard_map.73 = (f32[2,32,1024]{2,1,0:T(8,128)S(1)}, bf16[1024,1024]{1,0:T(8,128)(2,1)S(1)}, f32[2,5,8,128]{3,2,1,0:T(8,128)S(1)}, f32[2,2,128]{2,1,0:T(2,128)S(...) custom-call(s32[8,16]{1,0:T(8,128)} %partner_hbm.1, ...), custom_call_target="tpu_custom_call" | custom-call | flops 1048576 | tf_op jit(solution)/shard_map/pallas_call | solution.py:311
  3.5 3.0 %collective-permute-start.3 = (bf16[32,2304]{1,0:T(8,128)(2,1)S(1)}, bf16[32,2304]{1,0:T(8,128)(2,1)S(1)}, u32[]{:S(2)}, u32[]{:S(2)}) collective-permute-start(bf16[32,2304]{1,0:T(8,128)(2,1)S(1)} %get-tuple-element.86), channel_id=1, source_target_pairs={{0,16},{16,32},{32,48},{48,64},{64,80},{80,96},{96,112},{112,128},... | collective-permute-start | bytes 442376 | tf_op jit(solution)/shard_map/ppermute | solution.py:361
  6.6 0.2 collective-permute-start.2
  6.8 0.4 shard_map.75
  7.2 3.6 %collective-permute-start = (bf16[32,1280]{1,0:T(8,128)(2,1)S(1)}, bf16[32,1280]{1,0:T(8,128)(2,1)S(1)}, u32[]{:S(2)}, u32[]{:S(2)}) collective-permute-start(bf16[32,1280]{1,0:T(8,128)(2,1)S(1)} %get-tuple-element.81), channel_id=1, source_target_pairs={{0,16},{16,0},{32,48},{48,32},{64,80},{80,64},{96,112},{112,96},{1... | collective-permute-start | bytes 245768 | tf_op jit(solution)/shard_map/ppermute | solution.py:367
  10.9 0.1 collective-permute-start.1
  11.0 1.2 %shard_map.74 = (f32[2,32,1024]{2,1,0:T(8,128)S(1)}, f32[2,32,1024]{2,1,0:T(8,128)S(1)}, bf16[1024,1024]{1,0:T(8,128)(2,1)S(1)}) custom-call(f32[2,32,1024]{2,1,0:T(8,128)S(1)} %get-tuple-element.67.refs_0_.x_ref.refs_1_, f32[2,5,8,128]{3,2,1,0:T(8,128)S(1)} %get-tuple-element.68.refs_1_.refs_4_, f32[7,128]{1,0:T(8,128)S(1)} %get-tuple-element.69.refs_2_.refs_5_.weight_ref, ...), custom_call_target="tpu_custom_call" | custom-call | flops 1048576 | tf_op jit(solution)/shard_map/pallas_call | solution.py:311
  12.2 0.5 %shard_map.76 = (f32[2,32,1024]{2,1,0:T(8,128)S(1)}, bf16[1024,1024]{1,0:T(8,128)(2,1)S(1)}) custom-call(f32[2,32,1024]{2,1,0:T(8,128)S(1)} %get-tuple-element.78.part_ref, bf16[1024,1024]{1,0:T(8,128)(2,1)S(1)} %get-tuple-element.80.w_ref, f32[2,2,128]{2,1,0:T(2,128)S(1)} %get-tuple-element.79.rim_ref, bf16[32,1280]{1,0:T(8,128)(2,1)S(1)} %collective-permute-done.rows_ref, ...), custom_call_target="tpu_custom_call" | custom-call | tf_op jit(solution)/shard_map/pallas_call | solution.py:311
  12.8 1.0 %collective-permute-start.7 = (bf16[32,2304]{1,0:T(8,128)(2,1)S(1)}, bf16[32,2304]{1,0:T(8,128)(2,1)S(1)}, u32[]{:S(2)}, u32[]{:S(2)}) collective-permute-start(bf16[32,2304]{1,0:T(8,128)(2,1)S(1)} %get-tuple-element.95), channel_id=1, source_target_pairs={{16,0},{32,16},{48,32},{64,48},{80,64},{96,80},{112,96},{128,112},... | collective-permute-start | bytes 442376 | tf_op jit(solution)/shard_map/ppermute | solution.py:361
  13.8 0.6 %shard_map.78 = (f32[2,32,1024]{2,1,0:T(8,128)S(1)}, bf16[32,2304]{1,0:T(8,128)(2,1)S(1)}) custom-call(f32[2,32,1024]{2,1,0:T(8,128)S(1)} %get-tuple-element.84.sum_ref, bf16[1024,1024]{1,0:T(8,128)(2,1)S(1)} %get-tuple-element.83.refs_0_.w_ref, bf16[1024,1024]{1,0:T(8,128)(2,1)S(1)} %get-tuple-element.85.turned_ref, ...), custom_call_target="tpu_custom_call", output_to_operand_aliasing={{0}: (5, {})} | custom-call | flops 1048576 | tf_op jit(solution)/shard_map/pallas_call | solution.py:311
  14.4 0.1 collective-permute-start.6
  14.5 0.3 shard_map.80
  14.9 0.7 %collective-permute-start.4 = (bf16[32,1280]{1,0:T(8,128)(2,1)S(1)}, bf16[32,1280]{1,0:T(8,128)(2,1)S(1)}, u32[]{:S(2)}, u32[]{:S(2)}) collective-permute-start(bf16[32,1280]{1,0:T(8,128)(2,1)S(1)} %get-tuple-element.92), channel_id=1, source_target_pairs={{0,16},{16,0},{32,48},{48,32},{64,80},{80,64},{96,112},{112,96},{1... | collective-permute-start | bytes 245768 | tf_op jit(solution)/shard_map/ppermute | solution.py:367
  15.5 0.1 collective-permute-start.5
  15.6 1.1 %shard_map.79 = (f32[2,32,1024]{2,1,0:T(8,128)S(1)}, f32[2,32,1024]{2,1,0:T(8,128)S(1)}) custom-call(f32[2,32,1024]{2,1,0:T(8,128)S(1)} %get-tuple-element.88.refs_0_.x_ref.refs_1_, f32[2,32,1024]{2,1,0:T(8,128)S(1)} %get-tuple-element.67.refs_0_.x_ref.refs_1_, f32[2,32,1024]{2,1,0:T(8,128)S(1)} %get-tuple-element.89.refs_2_, ...), custom_call_target="tpu_custom_call" | custom-call | flops 1048576 | tf_op jit(solution)/shard_map/pallas_call | solution.py:311
  16.8 0.5 %shard_map.81.sum_ref = f32[2,32,1024]{2,1,0:T(8,128)S(1)} custom-call(f32[2,32,1024]{2,1,0:T(8,128)S(1)} %get-tuple-element.91.part_ref, bf16[1024,1024]{1,0:T(8,128)(2,1)S(1)} %get-tuple-element.80.w_ref, f32[2,2,128]{2,1,0:T(2,128)S(1)} %get-tuple-element.79.rim_ref, bf16[32,1280]{1,0:T(8,128)(2,1)S(1)} %collective-permute-done.4.rows_ref, ...), custom_call_target="tpu_custom_call" | custom-call | tf_op jit(solution)/shard_map/pallas_call | solution.py:311
  17.3 0.1 collective-permute-done.7.got_ref
  17.4 0.6 %shard_map.82 = (f32[2,32,1024]{2,1,0:T(8,128)S(1)}, bf16[32,2304]{1,0:T(8,128)(2,1)S(1)}) custom-call(f32[2,32,1024]{2,1,0:T(8,128)S(1)} %shard_map.81.sum_ref, bf16[1024,1024]{1,0:T(8,128)(2,1)S(1)} %get-tuple-element.83.refs_0_.w_ref, bf16[1024,1024]{1,0:T(8,128)(2,1)S(1)} %get-tuple-element.85.turned_ref, f32[2,2,128]{2,1,0:T(2,128)S(1)} %get-tuple-element.79.rim_ref, ...), custom_call_target="tpu_custom_call" | custom-call | flops 1048576 | tf_op jit(solution)/shard_map/pallas_call | solution.py:311
  18.0 3.6 %collective-permute-start.10 = (bf16[32,2304]{1,0:T(8,128)(2,1)S(1)}, bf16[32,2304]{1,0:T(8,128)(2,1)S(1)}, u32[]{:S(2)}, u32[]{:S(2)}) collective-permute-start(bf16[32,2304]{1,0:T(8,128)(2,1)S(1)} %get-tuple-element.102), channel_id=1, source_target_pairs={{16,0},{32,16},{48,32},{64,48},{80,64},{96,80},{112,96},{128,112},... | collective-permute-start | bytes 442376 | tf_op jit(solution)/shard_map/ppermute | solution.py:361
  21.6 0.3 shard_map.85
  21.9 0.1 collective-permute-start.8
  22.0 0.5 %collective-permute-start.9 = (bf16[32,1024]{1,0:T(8,128)(2,1)S(1)}, bf16[32,1024]{1,0:T(8,128)(2,1)S(1)}, u32[]{:S(2)}, u32[]{:S(2)}) collective-permute-start(bf16[32,1024]{1,0:T(8,128)(2,1)S(1)} %get-tuple-element.101), channel_id=1, source_target_pairs={{0,16},{16,0},{32,48},{48,32},{64,80},{80,64},{96,112},{112,96},{1... | collective-permute-start | bytes 196616 | tf_op jit(solution)/shard_map/ppermute | solution.py:367
  22.4 1.1 %shard_map.84 = (f32[2,32,1024]{2,1,0:T(8,128)S(1)}, f32[2,32,1024]{2,1,0:T(8,128)S(1)}) custom-call(f32[2,32,1024]{2,1,0:T(8,128)S(1)} %get-tuple-element.97.refs_0_.x_ref.refs_1_, f32[2,32,1024]{2,1,0:T(8,128)S(1)} %get-tuple-element.88.refs_0_.x_ref.refs_1_, f32[2,32,1024]{2,1,0:T(8,128)S(1)} %get-tuple-element.98.refs_2_, ...), custom_call_target="tpu_custom_call" | custom-call | flops 1048576 | tf_op jit(solution)/shard_map/pallas_call | solution.py:311
  23.6 0.5 %shard_map.86.sum_ref = f32[2,32,1024]{2,1,0:T(8,128)S(1)} custom-call(f32[2,32,1024]{2,1,0:T(8,128)S(1)} %get-tuple-element.99.part_ref, bf16[1024,1024]{1,0:T(8,128)(2,1)S(1)} %get-tuple-element.80.w_ref, f32[2,2,128]{2,1,0:T(2,128)S(1)} %get-tuple-element.79.rim_ref, bf16[32,1280]{1,0:T(8,128)(2,1)S(1)} %collective-permute-done.8.rows_ref, ...), custom_call_target="tpu_custom_call" | custom-call | tf_op jit(solution)/shard_map/pallas_call | solution.py:311
  24.1 0.9 %collective-permute-start.15 = (bf16[32,2304]{1,0:T(8,128)(2,1)S(1)}, bf16[32,2304]{1,0:T(8,128)(2,1)S(1)}, u32[]{:S(2)}, u32[]{:S(2)}) collective-permute-start(bf16[32,2304]{1,0:T(8,128)(2,1)S(1)} %get-tuple-element.111), channel_id=1, source_target_pairs={{16,0},{32,16},{48,32},{64,48},{80,64},{96,80},{112,96},{128,112},... | collective-permute-start | bytes 442376 | tf_op jit(solution)/shard_map/ppermute | solution.py:361
  25.0 0.6 %shard_map.88 = (f32[2,32,1024]{2,1,0:T(8,128)S(1)}, bf16[32,2304]{1,0:T(8,128)(2,1)S(1)}) custom-call(f32[2,32,1024]{2,1,0:T(8,128)S(1)} %shard_map.86.sum_ref, bf16[1024,1024]{1,0:T(8,128)(2,1)S(1)} %get-tuple-element.83.refs_0_.w_ref, bf16[1024,1024]{1,0:T(8,128)(2,1)S(1)} %get-tuple-element.85.turned_ref, ...), custom_call_target="tpu_custom_call", output_to_operand_aliasing={{0}: (5, {})} | custom-call | flops 1048576 | tf_op jit(solution)/shard_map/pallas_call | solution.py:311
  25.6 0.3 collective-permute-start.14
  25.9 0.3 shard_map.90
  26.2 0.4 %collective-permute-start.12 = (bf16[32,1280]{1,0:T(8,128)(2,1)S(1)}, bf16[32,1280]{1,0:T(8,128)(2,1)S(1)}, u32[]{:S(2)}, u32[]{:S(2)}) collective-permute-start(bf16[32,1280]{1,0:T(8,128)(2,1)S(1)} %get-tuple-element.108), channel_id=1, source_target_pairs={{0,16},{16,0},{32,48},{48,32},{64,80},{80,64},{96,112},{112,96},{1... | collective-permute-start | bytes 245768 | tf_op jit(solution)/shard_map/ppermute | solution.py:367
  26.6 0.3 collective-permute-start.13
  26.9 1.1 %shard_map.89 = (f32[2,32,1024]{2,1,0:T(8,128)S(1)}, f32[2,32,1024]{2,1,0:T(8,128)S(1)}) custom-call(f32[2,32,1024]{2,1,0:T(8,128)S(1)} %get-tuple-element.105.refs_0_.x_ref.refs_1_, f32[2,32,1024]{2,1,0:T(8,128)S(1)} %get-tuple-element.97.refs_0_.x_ref.refs_1_, f32[2,32,1024]{2,1,0:T(8,128)S(1)} %get-tuple-element.106.refs_2_, ...), custom_call_target="tpu_custom_call" | custom-call | flops 1048576 | tf_op jit(solution)/shard_map/pallas_call | solution.py:311
  28.0 0.5 %shard_map.91.sum_ref = f32[2,32,1024]{2,1,0:T(8,128)S(1)} custom-call(f32[2,32,1024]{2,1,0:T(8,128)S(1)} %get-tuple-element.107.part_ref, bf16[1024,1024]{1,0:T(8,128)(2,1)S(1)} %get-tuple-element.80.w_ref, f32[2,2,128]{2,1,0:T(2,128)S(1)} %get-tuple-element.79.rim_ref, bf16[32,1280]{1,0:T(8,128)(2,1)S(1)} %collective-permute-done.12.rows_ref, ...), custom_call_target="tpu_custom_call" | custom-call | tf_op jit(solution)/shard_map/pallas_call | solution.py:311
  28.5 0.1 collective-permute-done.15.got_ref
  28.7 0.6 %shard_map.92 = (f32[2,32,1024]{2,1,0:T(8,128)S(1)}, bf16[32,2304]{1,0:T(8,128)(2,1)S(1)}) custom-call(f32[2,32,1024]{2,1,0:T(8,128)S(1)} %shard_map.91.sum_ref, bf16[1024,1024]{1,0:T(8,128)(2,1)S(1)} %get-tuple-element.83.refs_0_.w_ref, bf16[1024,1024]{1,0:T(8,128)(2,1)S(1)} %get-tuple-element.85.turned_ref, f32[2,2,128]{2,1,0:T(2,128)S(1)} %get-tuple-element.79.rim_ref, ...), custom_call_target="tpu_custom_call" | custom-call | flops 1048576 | tf_op jit(solution)/shard_map/pallas_call | solution.py:311
  29.3 2.3 %collective-permute-start.18 = (bf16[32,2304]{1,0:T(8,128)(2,1)S(1)}, bf16[32,2304]{1,0:T(8,128)(2,1)S(1)}, u32[]{:S(2)}, u32[]{:S(2)}) collective-permute-start(bf16[32,2304]{1,0:T(8,128)(2,1)S(1)} %get-tuple-element.118), channel_id=1, source_target_pairs={{16,0},{32,16},{48,32},{64,48},{80,64},{96,80},{112,96},{128,112},... | collective-permute-start | bytes 442376 | tf_op jit(solution)/shard_map/ppermute | solution.py:361
  31.6 0.3 shard_map.95
  31.9 0.2 collective-permute-start.16
  32.2 0.3 collective-permute-start.17
  32.5 1.1 %shard_map.94 = (f32[2,32,1024]{2,1,0:T(8,128)S(1)}, f32[2,32,1024]{2,1,0:T(8,128)S(1)}) custom-call(f32[2,32,1024]{2,1,0:T(8,128)S(1)} %get-tuple-element.113.refs_0_.x_ref.refs_1_, f32[2,32,1024]{2,1,0:T(8,128)S(1)} %get-tuple-element.105.refs_0_.x_ref.refs_1_, f32[2,32,1024]{2,1,0:T(8,128)S(1)} %get-tuple-element.114.refs_2_, ...), custom_call_target="tpu_custom_call" | custom-call | flops 1048576 | tf_op jit(solution)/shard_map/pallas_call | solution.py:311
  33.6 0.5 %shard_map.96.sum_ref = f32[2,32,1024]{2,1,0:T(8,128)S(1)} custom-call(f32[2,32,1024]{2,1,0:T(8,128)S(1)} %get-tuple-element.115.part_ref, bf16[1024,1024]{1,0:T(8,128)(2,1)S(1)} %get-tuple-element.80.w_ref, f32[2,2,128]{2,1,0:T(2,128)S(1)} %get-tuple-element.79.rim_ref, bf16[32,1280]{1,0:T(8,128)(2,1)S(1)} %collective-permute-done.16.rows_ref, ...), custom_call_target="tpu_custom_call" | custom-call | tf_op jit(solution)/shard_map/pallas_call | solution.py:311
  34.2 0.6 %shard_map.98 = (f32[2,32,1024]{2,1,0:T(8,128)S(1)}, bf16[32,2304]{1,0:T(8,128)(2,1)S(1)}) custom-call(f32[2,32,1024]{2,1,0:T(8,128)S(1)} %shard_map.96.sum_ref, bf16[1024,1024]{1,0:T(8,128)(2,1)S(1)} %get-tuple-element.83.refs_0_.w_ref, bf16[1024,1024]{1,0:T(8,128)(2,1)S(1)} %get-tuple-element.85.turned_ref, ...), custom_call_target="tpu_custom_call", output_to_operand_aliasing={{0}: (5, {})} | custom-call | flops 1048576 | tf_op jit(solution)/shard_map/pallas_call | solution.py:311
  34.8 0.5 %collective-permute-start.23 = (bf16[32,2304]{1,0:T(8,128)(2,1)S(1)}, bf16[32,2304]{1,0:T(8,128)(2,1)S(1)}, u32[]{:S(2)}, u32[]{:S(2)}) collective-permute-start(bf16[32,2304]{1,0:T(8,128)(2,1)S(1)} %get-tuple-element.128), channel_id=1, source_target_pairs={{16,0},{32,16},{48,32},{64,48},{80,64},{96,80},{112,96},{128,112},... | collective-permute-start | bytes 442376 | tf_op jit(solution)/shard_map/ppermute | solution.py:361
  35.3 0.3 shard_map.100
  35.7 2.9 %collective-permute-start.20 = (bf16[32,1280]{1,0:T(8,128)(2,1)S(1)}, bf16[32,1280]{1,0:T(8,128)(2,1)S(1)}, u32[]{:S(2)}, u32[]{:S(2)}) collective-permute-start(bf16[32,1280]{1,0:T(8,128)(2,1)S(1)} %get-tuple-element.124), channel_id=1, source_target_pairs={{0,16},{16,0},{32,48},{48,32},{64,80},{80,64},{96,112},{112,96},{1... | collective-permute-start | bytes 245768 | tf_op jit(solution)/shard_map/ppermute | solution.py:367
  38.6 0.1 collective-permute-start.21
  38.7 1.1 %shard_map.99 = (f32[2,32,1024]{2,1,0:T(8,128)S(1)}, f32[2,32,1024]{2,1,0:T(8,128)S(1)}) custom-call(f32[2,32,1024]{2,1,0:T(8,128)S(1)} %get-tuple-element.121.refs_0_.x_ref, f32[2,32,1024]{2,1,0:T(8,128)S(1)} %get-tuple-element.113.refs_0_.x_ref.refs_1_, f32[2,32,1024]{2,1,0:T(8,128)S(1)} %get-tuple-element.122.refs_2_, ...), custom_call_target="tpu_custom_call" | custom-call | flops 1048576 | tf_op jit(solution)/shard_map/pallas_call | solution.py:311
  39.8 0.5 %shard_map.101.sum_ref = f32[2,32,1024]{2,1,0:T(8,128)S(1)} custom-call(f32[2,32,1024]{2,1,0:T(8,128)S(1)} %get-tuple-element.123.part_ref, bf16[1024,1024]{1,0:T(8,128)(2,1)S(1)} %get-tuple-element.80.w_ref, f32[2,2,128]{2,1,0:T(2,128)S(1)} %get-tuple-element.79.rim_ref, bf16[32,1280]{1,0:T(8,128)(2,1)S(1)} %collective-permute-done.20.rows_ref, ...), custom_call_target="tpu_custom_call" | custom-call | tf_op jit(solution)/shard_map/pallas_call | solution.py:311
  40.4 1.1 %shard_map.102 = f32[2,8,32,128]{3,2,1,0:T(8,128)} custom-call(f32[2,32,1024]{2,1,0:T(8,128)S(1)} %shard_map.101.sum_ref, f32[2,32,1024]{2,1,0:T(8,128)S(1)} %get-tuple-element.126.filt_ref, bf16[1024,1024]{1,0:T(8,128)(2,1)S(1)} %get-tuple-element.85.turned_ref, f32[2,2,128]{2,1,0:T(2,128)S(1)} %get-tuple-element.79.rim_ref, ...), custom_call_target="tpu_custom_call" | custom-call | flops 1048576 | tf_op jit(solution)/shard_map/pallas_call | solution.py:311
  (30 shorter events, 0.3 us)
Async XLA Ops:
  3.5 9.2 %collective-permute-start.3 = (bf16[32,2304]{1,0:T(8,128)(2,1)S(1)}, bf16[32,2304]{1,0:T(8,128)(2,1)S(1)}, u32[]{:S(2)}, u32[]{:S(2)}) collective-permute-start(bf16[32,2304]{1,0:T(8,128)(2,1)S(1)} %get-tuple-element.86), channel_id=1, source_target_pairs={{0,16},{16,32},{32,48},{48,64},{64,80},{80,96},{96,112},{112,128},... | collective-permute-start | bytes 442376 | tf_op jit(solution)/shard_map/ppermute | solution.py:361
  6.6 7.2 %collective-permute-start.2 = (bf16[32,2304]{1,0:T(8,128)(2,1)S(1)}, bf16[32,2304]{1,0:T(8,128)(2,1)S(1)}, u32[]{:S(2)}, u32[]{:S(2)}) collective-permute-start(bf16[32,2304]{1,0:T(8,128)(2,1)S(1)} %get-tuple-element.86), channel_id=1, source_target_pairs={{16,0},{32,16},{48,32},{64,48},{80,64},{96,80},{112,96},{128,112},... | collective-permute-start | bytes 442376 | tf_op jit(solution)/shard_map/ppermute | solution.py:361
  7.2 4.9 %collective-permute-start = (bf16[32,1280]{1,0:T(8,128)(2,1)S(1)}, bf16[32,1280]{1,0:T(8,128)(2,1)S(1)}, u32[]{:S(2)}, u32[]{:S(2)}) collective-permute-start(bf16[32,1280]{1,0:T(8,128)(2,1)S(1)} %get-tuple-element.81), channel_id=1, source_target_pairs={{0,16},{16,0},{32,48},{48,32},{64,80},{80,64},{96,112},{112,96},{1... | collective-permute-start | bytes 245768 | tf_op jit(solution)/shard_map/ppermute | solution.py:367
  10.9 1.3 %collective-permute-start.1 = (bf16[32,1024]{1,0:T(8,128)(2,1)S(1)}, bf16[32,1024]{1,0:T(8,128)(2,1)S(1)}, u32[]{:S(2)}, u32[]{:S(2)}) collective-permute-start(bf16[32,1024]{1,0:T(8,128)(2,1)S(1)} %get-tuple-element.82), channel_id=1, source_target_pairs={{0,16},{16,0},{32,48},{48,32},{64,80},{80,64},{96,112},{112,96},{1... | collective-permute-start | bytes 196616 | tf_op jit(solution)/shard_map/ppermute | solution.py:367
  12.8 4.6 %collective-permute-start.7 = (bf16[32,2304]{1,0:T(8,128)(2,1)S(1)}, bf16[32,2304]{1,0:T(8,128)(2,1)S(1)}, u32[]{:S(2)}, u32[]{:S(2)}) collective-permute-start(bf16[32,2304]{1,0:T(8,128)(2,1)S(1)} %get-tuple-element.95), channel_id=1, source_target_pairs={{16,0},{32,16},{48,32},{64,48},{80,64},{96,80},{112,96},{128,112},... | collective-permute-start | bytes 442376 | tf_op jit(solution)/shard_map/ppermute | solution.py:361
  14.4 3.6 %collective-permute-start.6 = (bf16[32,2304]{1,0:T(8,128)(2,1)S(1)}, bf16[32,2304]{1,0:T(8,128)(2,1)S(1)}, u32[]{:S(2)}, u32[]{:S(2)}) collective-permute-start(bf16[32,2304]{1,0:T(8,128)(2,1)S(1)} %get-tuple-element.94), channel_id=1, source_target_pairs={{0,16},{16,32},{32,48},{48,64},{64,80},{80,96},{96,112},{112,128},... | collective-permute-start | bytes 442376 | tf_op jit(solution)/shard_map/ppermute | solution.py:361
  14.9 1.9 %collective-permute-start.4 = (bf16[32,1280]{1,0:T(8,128)(2,1)S(1)}, bf16[32,1280]{1,0:T(8,128)(2,1)S(1)}, u32[]{:S(2)}, u32[]{:S(2)}) collective-permute-start(bf16[32,1280]{1,0:T(8,128)(2,1)S(1)} %get-tuple-element.92), channel_id=1, source_target_pairs={{0,16},{16,0},{32,48},{48,32},{64,80},{80,64},{96,112},{112,96},{1... | collective-permute-start | bytes 245768 | tf_op jit(solution)/shard_map/ppermute | solution.py:367
  15.5 1.3 %collective-permute-start.5 = (bf16[32,1024]{1,0:T(8,128)(2,1)S(1)}, bf16[32,1024]{1,0:T(8,128)(2,1)S(1)}, u32[]{:S(2)}, u32[]{:S(2)}) collective-permute-start(bf16[32,1024]{1,0:T(8,128)(2,1)S(1)} %get-tuple-element.93), channel_id=1, source_target_pairs={{0,16},{16,0},{32,48},{48,32},{64,80},{80,64},{96,112},{112,96},{1... | collective-permute-start | bytes 196616 | tf_op jit(solution)/shard_map/ppermute | solution.py:367
  17.9 6.1 %collective-permute-start.11 = (bf16[32,2304]{1,0:T(8,128)(2,1)S(1)}, bf16[32,2304]{1,0:T(8,128)(2,1)S(1)}, u32[]{:S(2)}, u32[]{:S(2)}) collective-permute-start(bf16[32,2304]{1,0:T(8,128)(2,1)S(1)} %get-tuple-element.103), channel_id=1, source_target_pairs={{0,16},{16,32},{32,48},{48,64},{64,80},{80,96},{96,112},{112,128},... | collective-permute-start | bytes 442376 | tf_op jit(solution)/shard_map/ppermute | solution.py:361
  18.0 7.0 %collective-permute-start.10 = (bf16[32,2304]{1,0:T(8,128)(2,1)S(1)}, bf16[32,2304]{1,0:T(8,128)(2,1)S(1)}, u32[]{:S(2)}, u32[]{:S(2)}) collective-permute-start(bf16[32,2304]{1,0:T(8,128)(2,1)S(1)} %get-tuple-element.102), channel_id=1, source_target_pairs={{16,0},{32,16},{48,32},{64,48},{80,64},{96,80},{112,96},{128,112},... | collective-permute-start | bytes 442376 | tf_op jit(solution)/shard_map/ppermute | solution.py:361
  21.9 1.7 %collective-permute-start.8 = (bf16[32,1280]{1,0:T(8,128)(2,1)S(1)}, bf16[32,1280]{1,0:T(8,128)(2,1)S(1)}, u32[]{:S(2)}, u32[]{:S(2)}) collective-permute-start(bf16[32,1280]{1,0:T(8,128)(2,1)S(1)} %get-tuple-element.100), channel_id=1, source_target_pairs={{0,16},{16,0},{32,48},{48,32},{64,80},{80,64},{96,112},{112,96},{1... | collective-permute-start | bytes 245768 | tf_op jit(solution)/shard_map/ppermute | solution.py:367
  22.0 1.6 %collective-permute-start.9 = (bf16[32,1024]{1,0:T(8,128)(2,1)S(1)}, bf16[32,1024]{1,0:T(8,128)(2,1)S(1)}, u32[]{:S(2)}, u32[]{:S(2)}) collective-permute-start(bf16[32,1024]{1,0:T(8,128)(2,1)S(1)} %get-tuple-element.101), channel_id=1, source_target_pairs={{0,16},{16,0},{32,48},{48,32},{64,80},{80,64},{96,112},{112,96},{1... | collective-permute-start | bytes 196616 | tf_op jit(solution)/shard_map/ppermute | solution.py:367
  24.1 4.6 %collective-permute-start.15 = (bf16[32,2304]{1,0:T(8,128)(2,1)S(1)}, bf16[32,2304]{1,0:T(8,128)(2,1)S(1)}, u32[]{:S(2)}, u32[]{:S(2)}) collective-permute-start(bf16[32,2304]{1,0:T(8,128)(2,1)S(1)} %get-tuple-element.111), channel_id=1, source_target_pairs={{16,0},{32,16},{48,32},{64,48},{80,64},{96,80},{112,96},{128,112},... | collective-permute-start | bytes 442376 | tf_op jit(solution)/shard_map/ppermute | solution.py:361
  25.6 3.7 %collective-permute-start.14 = (bf16[32,2304]{1,0:T(8,128)(2,1)S(1)}, bf16[32,2304]{1,0:T(8,128)(2,1)S(1)}, u32[]{:S(2)}, u32[]{:S(2)}) collective-permute-start(bf16[32,2304]{1,0:T(8,128)(2,1)S(1)} %get-tuple-element.110), channel_id=1, source_target_pairs={{0,16},{16,32},{32,48},{48,64},{64,80},{80,96},{96,112},{112,128},... | collective-permute-start | bytes 442376 | tf_op jit(solution)/shard_map/ppermute | solution.py:361
  26.2 1.8 %collective-permute-start.12 = (bf16[32,1280]{1,0:T(8,128)(2,1)S(1)}, bf16[32,1280]{1,0:T(8,128)(2,1)S(1)}, u32[]{:S(2)}, u32[]{:S(2)}) collective-permute-start(bf16[32,1280]{1,0:T(8,128)(2,1)S(1)} %get-tuple-element.108), channel_id=1, source_target_pairs={{0,16},{16,0},{32,48},{48,32},{64,80},{80,64},{96,112},{112,96},{1... | collective-permute-start | bytes 245768 | tf_op jit(solution)/shard_map/ppermute | solution.py:367
  26.6 1.4 %collective-permute-start.13 = (bf16[32,1024]{1,0:T(8,128)(2,1)S(1)}, bf16[32,1024]{1,0:T(8,128)(2,1)S(1)}, u32[]{:S(2)}, u32[]{:S(2)}) collective-permute-start(bf16[32,1024]{1,0:T(8,128)(2,1)S(1)} %get-tuple-element.109), channel_id=1, source_target_pairs={{0,16},{16,0},{32,48},{48,32},{64,80},{80,64},{96,112},{112,96},{1... | collective-permute-start | bytes 196616 | tf_op jit(solution)/shard_map/ppermute | solution.py:367
  29.3 4.8 %collective-permute-start.19 = (bf16[32,2304]{1,0:T(8,128)(2,1)S(1)}, bf16[32,2304]{1,0:T(8,128)(2,1)S(1)}, u32[]{:S(2)}, u32[]{:S(2)}) collective-permute-start(bf16[32,2304]{1,0:T(8,128)(2,1)S(1)} %get-tuple-element.119), channel_id=1, source_target_pairs={{0,16},{16,32},{32,48},{48,64},{64,80},{80,96},{96,112},{112,128},... | collective-permute-start | bytes 442376 | tf_op jit(solution)/shard_map/ppermute | solution.py:361
  29.3 4.9 %collective-permute-start.18 = (bf16[32,2304]{1,0:T(8,128)(2,1)S(1)}, bf16[32,2304]{1,0:T(8,128)(2,1)S(1)}, u32[]{:S(2)}, u32[]{:S(2)}) collective-permute-start(bf16[32,2304]{1,0:T(8,128)(2,1)S(1)} %get-tuple-element.118), channel_id=1, source_target_pairs={{16,0},{32,16},{48,32},{64,48},{80,64},{96,80},{112,96},{128,112},... | collective-permute-start | bytes 442376 | tf_op jit(solution)/shard_map/ppermute | solution.py:361
  31.9 1.7 %collective-permute-start.16 = (bf16[32,1280]{1,0:T(8,128)(2,1)S(1)}, bf16[32,1280]{1,0:T(8,128)(2,1)S(1)}, u32[]{:S(2)}, u32[]{:S(2)}) collective-permute-start(bf16[32,1280]{1,0:T(8,128)(2,1)S(1)} %get-tuple-element.116), channel_id=1, source_target_pairs={{0,16},{16,0},{32,48},{48,32},{64,80},{80,64},{96,112},{112,96},{1... | collective-permute-start | bytes 245768 | tf_op jit(solution)/shard_map/ppermute | solution.py:367
  32.2 1.4 %collective-permute-start.17 = (bf16[32,1024]{1,0:T(8,128)(2,1)S(1)}, bf16[32,1024]{1,0:T(8,128)(2,1)S(1)}, u32[]{:S(2)}, u32[]{:S(2)}) collective-permute-start(bf16[32,1024]{1,0:T(8,128)(2,1)S(1)} %get-tuple-element.117), channel_id=1, source_target_pairs={{0,16},{16,0},{32,48},{48,32},{64,80},{80,64},{96,112},{112,96},{1... | collective-permute-start | bytes 196616 | tf_op jit(solution)/shard_map/ppermute | solution.py:367
  34.8 5.5 %collective-permute-start.22 = (bf16[32,2304]{1,0:T(8,128)(2,1)S(1)}, bf16[32,2304]{1,0:T(8,128)(2,1)S(1)}, u32[]{:S(2)}, u32[]{:S(2)}) collective-permute-start(bf16[32,2304]{1,0:T(8,128)(2,1)S(1)} %get-tuple-element.127), channel_id=1, source_target_pairs={{0,16},{16,32},{32,48},{48,64},{64,80},{80,96},{96,112},{112,128},... | collective-permute-start | bytes 442376 | tf_op jit(solution)/shard_map/ppermute | solution.py:361
  34.8 5.5 %collective-permute-start.23 = (bf16[32,2304]{1,0:T(8,128)(2,1)S(1)}, bf16[32,2304]{1,0:T(8,128)(2,1)S(1)}, u32[]{:S(2)}, u32[]{:S(2)}) collective-permute-start(bf16[32,2304]{1,0:T(8,128)(2,1)S(1)} %get-tuple-element.128), channel_id=1, source_target_pairs={{16,0},{32,16},{48,32},{64,48},{80,64},{96,80},{112,96},{128,112},... | collective-permute-start | bytes 442376 | tf_op jit(solution)/shard_map/ppermute | solution.py:361
  35.7 4.2 %collective-permute-start.20 = (bf16[32,1280]{1,0:T(8,128)(2,1)S(1)}, bf16[32,1280]{1,0:T(8,128)(2,1)S(1)}, u32[]{:S(2)}, u32[]{:S(2)}) collective-permute-start(bf16[32,1280]{1,0:T(8,128)(2,1)S(1)} %get-tuple-element.124), channel_id=1, source_target_pairs={{0,16},{16,0},{32,48},{48,32},{64,80},{80,64},{96,112},{112,96},{1... | collective-permute-start | bytes 245768 | tf_op jit(solution)/shard_map/ppermute | solution.py:367
  38.6 1.3 %collective-permute-start.21 = (bf16[32,1024]{1,0:T(8,128)(2,1)S(1)}, bf16[32,1024]{1,0:T(8,128)(2,1)S(1)}, u32[]{:S(2)}, u32[]{:S(2)}) collective-permute-start(bf16[32,1024]{1,0:T(8,128)(2,1)S(1)} %get-tuple-element.125), channel_id=1, source_target_pairs={{0,16},{16,0},{32,48},{48,32},{64,80},{80,64},{96,112},{112,96},{1... | collective-permute-start | bytes 196616 | tf_op jit(solution)/shard_map/ppermute | solution.py:367

commit v11 on v9

--- a/solution.py
+++ b/solution.py
@@ -154,11 +154,10 @@
     def fetch(r):
         return pltpu.make_async_copy(coupling_hbm.at[r], blocks.at[r], row_sems.at[r])
 
-    copies[0].start()
+    for copy in copies:
+        copy.start()
     for place in range(rows):
         fetch(kept(place)).start()
-    for copy in copies[1:]:
-        copy.start()
 
     for total in totals:
         total[...] = jnp.zeros_like(total)
@@ -207,6 +206,7 @@
                 away = jnp.where(away < -(all_rows // 2), away + all_rows, away)
                 at = jnp.where(slot >= 0, REACH + (1 - 2 * here) * away, offsets)
                 totals[place][at] += blocks[row, k].astype(jnp.float32)
+
     settle(totals, FAR, w_ref, cols)
     write_far(x_ref, w_ref, rim_ref, far_ref)
 

time: 42.3 us -> 42.2 us (level)
  no operation moved by 1% of the time
where the time goes in v11:
time: 42.2 us; the launch traced here: 42 us
  starting transfers between devices  21 us (50%)
  Pallas kernels  20.2 us (48%)
  waiting for transfers between devices  0.56 us (1%)
    pallas_call x30, Pallas kernels, call(): pl.pallas_call(kernel, out_shape=outs, in_specs=specs or [IN_VMEM] * len(...  20.2 us
    ppermute x12, starting transfers between devices, body(): got_mate = [near(lax.ppermute(part, 'tile', mate_pairs)) for part in mate]  9.11 us
    ppermute x6, starting transfers between devices, body(): lax.ppermute(far[0], 'tile', down_pairs)  8.51 us
    ppermute x6, starting transfers between devices, body(): lax.ppermute(far[1], 'tile', up_pairs)  3.34 us
  transfers between devices with their start and end apart: 24, of which 2 were waited for; matrix products, arithmetic and copies ran while one was open for 0% of the time, Pallas kernels for 34%

profile of v11, /device:TPU:1, one launch (start us, length us, event | category | flops | bytes accessed | tf_op | source)
XLA Modules:
  0.0 42.0 jit_solution(11507958131010534103)
XLA Ops:
  0.0 4.1 %shard_map.73 = (f32[2,32,1024]{2,1,0:T(8,128)S(1)}, bf16[1024,1024]{1,0:T(8,128)(2,1)S(1)}, f32[2,5,8,128]{3,2,1,0:T(8,128)S(1)}, f32[2,2,128]{2,1,0:T(2,128)S(...) custom-call(s32[8,16]{1,0:T(8,128)} %partner_hbm.1, ...), custom_call_target="tpu_custom_call" | custom-call | flops 1048576 | tf_op jit(solution)/shard_map/pallas_call | solution.py:309
  4.1 3.0 %collective-permute-start.3 = (bf16[32,2304]{1,0:T(8,128)(2,1)S(1)}, bf16[32,2304]{1,0:T(8,128)(2,1)S(1)}, u32[]{:S(2)}, u32[]{:S(2)}) collective-permute-start(bf16[32,2304]{1,0:T(8,128)(2,1)S(1)} %get-tuple-element.86), channel_id=1, source_target_pairs={{0,16},{16,32},{32,48},{48,64},{64,80},{80,96},{96,112},{112,128},... | collective-permute-start | bytes 442376 | tf_op jit(solution)/shard_map/ppermute | solution.py:359
  7.2 0.2 collective-permute-start.2
  7.4 0.4 shard_map.75
  7.8 3.6 %collective-permute-start = (bf16[32,1280]{1,0:T(8,128)(2,1)S(1)}, bf16[32,1280]{1,0:T(8,128)(2,1)S(1)}, u32[]{:S(2)}, u32[]{:S(2)}) collective-permute-start(bf16[32,1280]{1,0:T(8,128)(2,1)S(1)} %get-tuple-element.81), channel_id=1, source_target_pairs={{0,16},{16,0},{32,48},{48,32},{64,80},{80,64},{96,112},{112,96},{1... | collective-permute-start | bytes 245768 | tf_op jit(solution)/shard_map/ppermute | solution.py:365
  11.5 0.1 collective-permute-start.1
  11.6 1.2 %shard_map.74 = (f32[2,32,1024]{2,1,0:T(8,128)S(1)}, f32[2,32,1024]{2,1,0:T(8,128)S(1)}, bf16[1024,1024]{1,0:T(8,128)(2,1)S(1)}) custom-call(f32[2,32,1024]{2,1,0:T(8,128)S(1)} %get-tuple-element.67.refs_0_.x_ref.refs_1_, f32[2,5,8,128]{3,2,1,0:T(8,128)S(1)} %get-tuple-element.68.refs_1_.refs_4_, f32[7,128]{1,0:T(8,128)S(1)} %get-tuple-element.69.refs_2_.refs_5_.weight_ref, ...), custom_call_target="tpu_custom_call" | custom-call | flops 1048576 | tf_op jit(solution)/shard_map/pallas_call | solution.py:309
  12.8 0.5 %shard_map.76 = (f32[2,32,1024]{2,1,0:T(8,128)S(1)}, bf16[1024,1024]{1,0:T(8,128)(2,1)S(1)}) custom-call(f32[2,32,1024]{2,1,0:T(8,128)S(1)} %get-tuple-element.78.part_ref, bf16[1024,1024]{1,0:T(8,128)(2,1)S(1)} %get-tuple-element.80.w_ref, f32[2,2,128]{2,1,0:T(2,128)S(1)} %get-tuple-element.79.rim_ref, bf16[32,1280]{1,0:T(8,128)(2,1)S(1)} %collective-permute-done.rows_ref, ...), custom_call_target="tpu_custom_call" | custom-call | tf_op jit(solution)/shard_map/pallas_call | solution.py:309
  13.4 1.0 %collective-permute-start.7 = (bf16[32,2304]{1,0:T(8,128)(2,1)S(1)}, bf16[32,2304]{1,0:T(8,128)(2,1)S(1)}, u32[]{:S(2)}, u32[]{:S(2)}) collective-permute-start(bf16[32,2304]{1,0:T(8,128)(2,1)S(1)} %get-tuple-element.95), channel_id=1, source_target_pairs={{16,0},{32,16},{48,32},{64,48},{80,64},{96,80},{112,96},{128,112},... | collective-permute-start | bytes 442376 | tf_op jit(solution)/shard_map/ppermute | solution.py:359
  14.4 0.6 %shard_map.78 = (f32[2,32,1024]{2,1,0:T(8,128)S(1)}, bf16[32,2304]{1,0:T(8,128)(2,1)S(1)}) custom-call(f32[2,32,1024]{2,1,0:T(8,128)S(1)} %get-tuple-element.84.sum_ref, bf16[1024,1024]{1,0:T(8,128)(2,1)S(1)} %get-tuple-element.83.refs_0_.w_ref, bf16[1024,1024]{1,0:T(8,128)(2,1)S(1)} %get-tuple-element.85.turned_ref, ...), custom_call_target="tpu_custom_call", output_to_operand_aliasing={{0}: (5, {})} | custom-call | flops 1048576 | tf_op jit(solution)/shard_map/pallas_call | solution.py:309
  15.0 0.1 collective-permute-start.6
  15.1 0.3 shard_map.80
  15.4 0.7 %collective-permute-start.4 = (bf16[32,1280]{1,0:T(8,128)(2,1)S(1)}, bf16[32,1280]{1,0:T(8,128)(2,1)S(1)}, u32[]{:S(2)}, u32[]{:S(2)}) collective-permute-start(bf16[32,1280]{1,0:T(8,128)(2,1)S(1)} %get-tuple-element.92), channel_id=1, source_target_pairs={{0,16},{16,0},{32,48},{48,32},{64,80},{80,64},{96,112},{112,96},{1... | collective-permute-start | bytes 245768 | tf_op jit(solution)/shard_map/ppermute | solution.py:365
  16.1 0.1 collective-permute-start.5
  16.2 1.1 %shard_map.79 = (f32[2,32,1024]{2,1,0:T(8,128)S(1)}, f32[2,32,1024]{2,1,0:T(8,128)S(1)}) custom-call(f32[2,32,1024]{2,1,0:T(8,128)S(1)} %get-tuple-element.88.refs_0_.x_ref.refs_1_, f32[2,32,1024]{2,1,0:T(8,128)S(1)} %get-tuple-element.67.refs_0_.x_ref.refs_1_, f32[2,32,1024]{2,1,0:T(8,128)S(1)} %get-tuple-element.89.refs_2_, ...), custom_call_target="tpu_custom_call" | custom-call | flops 1048576 | tf_op jit(solution)/shard_map/pallas_call | solution.py:309
  17.4 0.5 %shard_map.81.sum_ref = f32[2,32,1024]{2,1,0:T(8,128)S(1)} custom-call(f32[2,32,1024]{2,1,0:T(8,128)S(1)} %get-tuple-element.91.part_ref, bf16[1024,1024]{1,0:T(8,128)(2,1)S(1)} %get-tuple-element.80.w_ref, f32[2,2,128]{2,1,0:T(2,128)S(1)} %get-tuple-element.79.rim_ref, bf16[32,1280]{1,0:T(8,128)(2,1)S(1)} %collective-permute-done.4.rows_ref, ...), custom_call_target="tpu_custom_call" | custom-call | tf_op jit(solution)/shard_map/pallas_call | solution.py:309
  17.9 0.1 collective-permute-done.7.got_ref
  17.9 0.6 %shard_map.82 = (f32[2,32,1024]{2,1,0:T(8,128)S(1)}, bf16[32,2304]{1,0:T(8,128)(2,1)S(1)}) custom-call(f32[2,32,1024]{2,1,0:T(8,128)S(1)} %shard_map.81.sum_ref, bf16[1024,1024]{1,0:T(8,128)(2,1)S(1)} %get-tuple-element.83.refs_0_.w_ref, bf16[1024,1024]{1,0:T(8,128)(2,1)S(1)} %get-tuple-element.85.turned_ref, f32[2,2,128]{2,1,0:T(2,128)S(1)} %get-tuple-element.79.rim_ref, ...), custom_call_target="tpu_custom_call" | custom-call | flops 1048576 | tf_op jit(solution)/shard_map/pallas_call | solution.py:309
  18.6 3.6 %collective-permute-start.10 = (bf16[32,2304]{1,0:T(8,128)(2,1)S(1)}, bf16[32,2304]{1,0:T(8,128)(2,1)S(1)}, u32[]{:S(2)}, u32[]{:S(2)}) collective-permute-start(bf16[32,2304]{1,0:T(8,128)(2,1)S(1)} %get-tuple-element.102), channel_id=1, source_target_pairs={{16,0},{32,16},{48,32},{64,48},{80,64},{96,80},{112,96},{128,112},... | collective-permute-start | bytes 442376 | tf_op jit(solution)/shard_map/ppermute | solution.py:359
  22.2 0.3 shard_map.85
  22.5 0.1 collective-permute-start.8
  22.6 0.5 %collective-permute-start.9 = (bf16[32,1024]{1,0:T(8,128)(2,1)S(1)}, bf16[32,1024]{1,0:T(8,128)(2,1)S(1)}, u32[]{:S(2)}, u32[]{:S(2)}) collective-permute-start(bf16[32,1024]{1,0:T(8,128)(2,1)S(1)} %get-tuple-element.101), channel_id=1, source_target_pairs={{0,16},{16,0},{32,48},{48,32},{64,80},{80,64},{96,112},{112,96},{1... | collective-permute-start | bytes 196616 | tf_op jit(solution)/shard_map/ppermute | solution.py:365
  23.0 1.1 %shard_map.84 = (f32[2,32,1024]{2,1,0:T(8,128)S(1)}, f32[2,32,1024]{2,1,0:T(8,128)S(1)}) custom-call(f32[2,32,1024]{2,1,0:T(8,128)S(1)} %get-tuple-element.97.refs_0_.x_ref.refs_1_, f32[2,32,1024]{2,1,0:T(8,128)S(1)} %get-tuple-element.88.refs_0_.x_ref.refs_1_, f32[2,32,1024]{2,1,0:T(8,128)S(1)} %get-tuple-element.98.refs_2_, ...), custom_call_target="tpu_custom_call" | custom-call | flops 1048576 | tf_op jit(solution)/shard_map/pallas_call | solution.py:309
  24.2 0.5 %shard_map.86.sum_ref = f32[2,32,1024]{2,1,0:T(8,128)S(1)} custom-call(f32[2,32,1024]{2,1,0:T(8,128)S(1)} %get-tuple-element.99.part_ref, bf16[1024,1024]{1,0:T(8,128)(2,1)S(1)} %get-tuple-element.80.w_ref, f32[2,2,128]{2,1,0:T(2,128)S(1)} %get-tuple-element.79.rim_ref, bf16[32,1280]{1,0:T(8,128)(2,1)S(1)} %collective-permute-done.8.rows_ref, ...), custom_call_target="tpu_custom_call" | custom-call | tf_op jit(solution)/shard_map/pallas_call | solution.py:309
  24.7 0.9 %collective-permute-start.15 = (bf16[32,2304]{1,0:T(8,128)(2,1)S(1)}, bf16[32,2304]{1,0:T(8,128)(2,1)S(1)}, u32[]{:S(2)}, u32[]{:S(2)}) collective-permute-start(bf16[32,2304]{1,0:T(8,128)(2,1)S(1)} %get-tuple-element.111), channel_id=1, source_target_pairs={{16,0},{32,16},{48,32},{64,48},{80,64},{96,80},{112,96},{128,112},... | collective-permute-start | bytes 442376 | tf_op jit(solution)/shard_map/ppermute | solution.py:359
  25.6 0.7 %shard_map.88 = (f32[2,32,1024]{2,1,0:T(8,128)S(1)}, bf16[32,2304]{1,0:T(8,128)(2,1)S(1)}) custom-call(f32[2,32,1024]{2,1,0:T(8,128)S(1)} %shard_map.86.sum_ref, bf16[1024,1024]{1,0:T(8,128)(2,1)S(1)} %get-tuple-element.83.refs_0_.w_ref, bf16[1024,1024]{1,0:T(8,128)(2,1)S(1)} %get-tuple-element.85.turned_ref, ...), custom_call_target="tpu_custom_call", output_to_operand_aliasing={{0}: (5, {})} | custom-call | flops 1048576 | tf_op jit(solution)/shard_map/pallas_call | solution.py:309
  26.3 0.1 collective-permute-start.14
  26.5 0.3 shard_map.90
  26.8 0.4 %collective-permute-start.12 = (bf16[32,1280]{1,0:T(8,128)(2,1)S(1)}, bf16[32,1280]{1,0:T(8,128)(2,1)S(1)}, u32[]{:S(2)}, u32[]{:S(2)}) collective-permute-start(bf16[32,1280]{1,0:T(8,128)(2,1)S(1)} %get-tuple-element.108), channel_id=1, source_target_pairs={{0,16},{16,0},{32,48},{48,32},{64,80},{80,64},{96,112},{112,96},{1... | collective-permute-start | bytes 245768 | tf_op jit(solution)/shard_map/ppermute | solution.py:365
  27.2 0.1 collective-permute-start.13
  27.3 1.1 %shard_map.89 = (f32[2,32,1024]{2,1,0:T(8,128)S(1)}, f32[2,32,1024]{2,1,0:T(8,128)S(1)}) custom-call(f32[2,32,1024]{2,1,0:T(8,128)S(1)} %get-tuple-element.105.refs_0_.x_ref.refs_1_, f32[2,32,1024]{2,1,0:T(8,128)S(1)} %get-tuple-element.97.refs_0_.x_ref.refs_1_, f32[2,32,1024]{2,1,0:T(8,128)S(1)} %get-tuple-element.106.refs_2_, ...), custom_call_target="tpu_custom_call" | custom-call | flops 1048576 | tf_op jit(solution)/shard_map/pallas_call | solution.py:309
  28.5 0.5 %shard_map.91.sum_ref = f32[2,32,1024]{2,1,0:T(8,128)S(1)} custom-call(f32[2,32,1024]{2,1,0:T(8,128)S(1)} %get-tuple-element.107.part_ref, bf16[1024,1024]{1,0:T(8,128)(2,1)S(1)} %get-tuple-element.80.w_ref, f32[2,2,128]{2,1,0:T(2,128)S(1)} %get-tuple-element.79.rim_ref, bf16[32,1280]{1,0:T(8,128)(2,1)S(1)} %collective-permute-done.12.rows_ref, ...), custom_call_target="tpu_custom_call" | custom-call | tf_op jit(solution)/shard_map/pallas_call | solution.py:309
  29.0 0.3 collective-permute-done.15.got_ref
  29.3 0.6 %shard_map.92 = (f32[2,32,1024]{2,1,0:T(8,128)S(1)}, bf16[32,2304]{1,0:T(8,128)(2,1)S(1)}) custom-call(f32[2,32,1024]{2,1,0:T(8,128)S(1)} %shard_map.91.sum_ref, bf16[1024,1024]{1,0:T(8,128)(2,1)S(1)} %get-tuple-element.83.refs_0_.w_ref, bf16[1024,1024]{1,0:T(8,128)(2,1)S(1)} %get-tuple-element.85.turned_ref, f32[2,2,128]{2,1,0:T(2,128)S(1)} %get-tuple-element.79.rim_ref, ...), custom_call_target="tpu_custom_call" | custom-call | flops 1048576 | tf_op jit(solution)/shard_map/pallas_call | solution.py:309
  29.9 2.3 %collective-permute-start.18 = (bf16[32,2304]{1,0:T(8,128)(2,1)S(1)}, bf16[32,2304]{1,0:T(8,128)(2,1)S(1)}, u32[]{:S(2)}, u32[]{:S(2)}) collective-permute-start(bf16[32,2304]{1,0:T(8,128)(2,1)S(1)} %get-tuple-element.118), channel_id=1, source_target_pairs={{16,0},{32,16},{48,32},{64,48},{80,64},{96,80},{112,96},{128,112},... | collective-permute-start | bytes 442376 | tf_op jit(solution)/shard_map/ppermute | solution.py:359
  32.2 0.3 shard_map.95
  32.5 0.2 collective-permute-start.16
  32.7 0.4 collective-permute-start.17
  33.1 1.1 %shard_map.94 = (f32[2,32,1024]{2,1,0:T(8,128)S(1)}, f32[2,32,1024]{2,1,0:T(8,128)S(1)}) custom-call(f32[2,32,1024]{2,1,0:T(8,128)S(1)} %get-tuple-element.113.refs_0_.x_ref.refs_1_, f32[2,32,1024]{2,1,0:T(8,128)S(1)} %get-tuple-element.105.refs_0_.x_ref.refs_1_, f32[2,32,1024]{2,1,0:T(8,128)S(1)} %get-tuple-element.114.refs_2_, ...), custom_call_target="tpu_custom_call" | custom-call | flops 1048576 | tf_op jit(solution)/shard_map/pallas_call | solution.py:309
  34.2 0.5 %shard_map.96.sum_ref = f32[2,32,1024]{2,1,0:T(8,128)S(1)} custom-call(f32[2,32,1024]{2,1,0:T(8,128)S(1)} %get-tuple-element.115.part_ref, bf16[1024,1024]{1,0:T(8,128)(2,1)S(1)} %get-tuple-element.80.w_ref, f32[2,2,128]{2,1,0:T(2,128)S(1)} %get-tuple-element.79.rim_ref, bf16[32,1280]{1,0:T(8,128)(2,1)S(1)} %collective-permute-done.16.rows_ref, ...), custom_call_target="tpu_custom_call" | custom-call | tf_op jit(solution)/shard_map/pallas_call | solution.py:309
  34.8 0.6 %shard_map.98 = (f32[2,32,1024]{2,1,0:T(8,128)S(1)}, bf16[32,2304]{1,0:T(8,128)(2,1)S(1)}) custom-call(f32[2,32,1024]{2,1,0:T(8,128)S(1)} %shard_map.96.sum_ref, bf16[1024,1024]{1,0:T(8,128)(2,1)S(1)} %get-tuple-element.83.refs_0_.w_ref, bf16[1024,1024]{1,0:T(8,128)(2,1)S(1)} %get-tuple-element.85.turned_ref, ...), custom_call_target="tpu_custom_call", output_to_operand_aliasing={{0}: (5, {})} | custom-call | flops 1048576 | tf_op jit(solution)/shard_map/pallas_call | solution.py:309
  35.4 0.5 %collective-permute-start.23 = (bf16[32,2304]{1,0:T(8,128)(2,1)S(1)}, bf16[32,2304]{1,0:T(8,128)(2,1)S(1)}, u32[]{:S(2)}, u32[]{:S(2)}) collective-permute-start(bf16[32,2304]{1,0:T(8,128)(2,1)S(1)} %get-tuple-element.128), channel_id=1, source_target_pairs={{16,0},{32,16},{48,32},{64,48},{80,64},{96,80},{112,96},{128,112},... | collective-permute-start | bytes 442376 | tf_op jit(solution)/shard_map/ppermute | solution.py:359
  35.9 0.3 shard_map.100
  36.2 2.9 %collective-permute-start.20 = (bf16[32,1280]{1,0:T(8,128)(2,1)S(1)}, bf16[32,1280]{1,0:T(8,128)(2,1)S(1)}, u32[]{:S(2)}, u32[]{:S(2)}) collective-permute-start(bf16[32,1280]{1,0:T(8,128)(2,1)S(1)} %get-tuple-element.124), channel_id=1, source_target_pairs={{0,16},{16,0},{32,48},{48,32},{64,80},{80,64},{96,112},{112,96},{1... | collective-permute-start | bytes 245768 | tf_op jit(solution)/shard_map/ppermute | solution.py:365
  39.1 0.1 collective-permute-start.21
  39.2 1.1 %shard_map.99 = (f32[2,32,1024]{2,1,0:T(8,128)S(1)}, f32[2,32,1024]{2,1,0:T(8,128)S(1)}) custom-call(f32[2,32,1024]{2,1,0:T(8,128)S(1)} %get-tuple-element.121.refs_0_.x_ref, f32[2,32,1024]{2,1,0:T(8,128)S(1)} %get-tuple-element.113.refs_0_.x_ref.refs_1_, f32[2,32,1024]{2,1,0:T(8,128)S(1)} %get-tuple-element.122.refs_2_, ...), custom_call_target="tpu_custom_call" | custom-call | flops 1048576 | tf_op jit(solution)/shard_map/pallas_call | solution.py:309
  40.4 0.5 %shard_map.101.sum_ref = f32[2,32,1024]{2,1,0:T(8,128)S(1)} custom-call(f32[2,32,1024]{2,1,0:T(8,128)S(1)} %get-tuple-element.123.part_ref, bf16[1024,1024]{1,0:T(8,128)(2,1)S(1)} %get-tuple-element.80.w_ref, f32[2,2,128]{2,1,0:T(2,128)S(1)} %get-tuple-element.79.rim_ref, bf16[32,1280]{1,0:T(8,128)(2,1)S(1)} %collective-permute-done.20.rows_ref, ...), custom_call_target="tpu_custom_call" | custom-call | tf_op jit(solution)/shard_map/pallas_call | solution.py:309
  40.9 1.1 %shard_map.102 = f32[2,8,32,128]{3,2,1,0:T(8,128)} custom-call(f32[2,32,1024]{2,1,0:T(8,128)S(1)} %shard_map.101.sum_ref, f32[2,32,1024]{2,1,0:T(8,128)S(1)} %get-tuple-element.126.filt_ref, bf16[1024,1024]{1,0:T(8,128)(2,1)S(1)} %get-tuple-element.85.turned_ref, f32[2,2,128]{2,1,0:T(2,128)S(1)} %get-tuple-element.79.rim_ref, ...), custom_call_target="tpu_custom_call" | custom-call | flops 1048576 | tf_op jit(solution)/shard_map/pallas_call | solution.py:309
  (30 shorter events, 0.3 us)
Async XLA Ops:
  4.1 9.2 %collective-permute-start.3 = (bf16[32,2304]{1,0:T(8,128)(2,1)S(1)}, bf16[32,2304]{1,0:T(8,128)(2,1)S(1)}, u32[]{:S(2)}, u32[]{:S(2)}) collective-permute-start(bf16[32,2304]{1,0:T(8,128)(2,1)S(1)} %get-tuple-element.86), channel_id=1, source_target_pairs={{0,16},{16,32},{32,48},{48,64},{64,80},{80,96},{96,112},{112,128},... | collective-permute-start | bytes 442376 | tf_op jit(solution)/shard_map/ppermute | solution.py:359
  7.2 7.2 %collective-permute-start.2 = (bf16[32,2304]{1,0:T(8,128)(2,1)S(1)}, bf16[32,2304]{1,0:T(8,128)(2,1)S(1)}, u32[]{:S(2)}, u32[]{:S(2)}) collective-permute-start(bf16[32,2304]{1,0:T(8,128)(2,1)S(1)} %get-tuple-element.86), channel_id=1, source_target_pairs={{16,0},{32,16},{48,32},{64,48},{80,64},{96,80},{112,96},{128,112},... | collective-permute-start | bytes 442376 | tf_op jit(solution)/shard_map/ppermute | solution.py:359
  7.8 4.9 %collective-permute-start = (bf16[32,1280]{1,0:T(8,128)(2,1)S(1)}, bf16[32,1280]{1,0:T(8,128)(2,1)S(1)}, u32[]{:S(2)}, u32[]{:S(2)}) collective-permute-start(bf16[32,1280]{1,0:T(8,128)(2,1)S(1)} %get-tuple-element.81), channel_id=1, source_target_pairs={{0,16},{16,0},{32,48},{48,32},{64,80},{80,64},{96,112},{112,96},{1... | collective-permute-start | bytes 245768 | tf_op jit(solution)/shard_map/ppermute | solution.py:365
  11.5 1.3 %collective-permute-start.1 = (bf16[32,1024]{1,0:T(8,128)(2,1)S(1)}, bf16[32,1024]{1,0:T(8,128)(2,1)S(1)}, u32[]{:S(2)}, u32[]{:S(2)}) collective-permute-start(bf16[32,1024]{1,0:T(8,128)(2,1)S(1)} %get-tuple-element.82), channel_id=1, source_target_pairs={{0,16},{16,0},{32,48},{48,32},{64,80},{80,64},{96,112},{112,96},{1... | collective-permute-start | bytes 196616 | tf_op jit(solution)/shard_map/ppermute | solution.py:365
  13.4 4.6 %collective-permute-start.7 = (bf16[32,2304]{1,0:T(8,128)(2,1)S(1)}, bf16[32,2304]{1,0:T(8,128)(2,1)S(1)}, u32[]{:S(2)}, u32[]{:S(2)}) collective-permute-start(bf16[32,2304]{1,0:T(8,128)(2,1)S(1)} %get-tuple-element.95), channel_id=1, source_target_pairs={{16,0},{32,16},{48,32},{64,48},{80,64},{96,80},{112,96},{128,112},... | collective-permute-start | bytes 442376 | tf_op jit(solution)/shard_map/ppermute | solution.py:359
  15.0 3.6 %collective-permute-start.6 = (bf16[32,2304]{1,0:T(8,128)(2,1)S(1)}, bf16[32,2304]{1,0:T(8,128)(2,1)S(1)}, u32[]{:S(2)}, u32[]{:S(2)}) collective-permute-start(bf16[32,2304]{1,0:T(8,128)(2,1)S(1)} %get-tuple-element.94), channel_id=1, source_target_pairs={{0,16},{16,32},{32,48},{48,64},{64,80},{80,96},{96,112},{112,128},... | collective-permute-start | bytes 442376 | tf_op jit(solution)/shard_map/ppermute | solution.py:359
  15.4 1.9 %collective-permute-start.4 = (bf16[32,1280]{1,0:T(8,128)(2,1)S(1)}, bf16[32,1280]{1,0:T(8,128)(2,1)S(1)}, u32[]{:S(2)}, u32[]{:S(2)}) collective-permute-start(bf16[32,1280]{1,0:T(8,128)(2,1)S(1)} %get-tuple-element.92), channel_id=1, source_target_pairs={{0,16},{16,0},{32,48},{48,32},{64,80},{80,64},{96,112},{112,96},{1... | collective-permute-start | bytes 245768 | tf_op jit(solution)/shard_map/ppermute | solution.py:365
  16.1 1.3 %collective-permute-start.5 = (bf16[32,1024]{1,0:T(8,128)(2,1)S(1)}, bf16[32,1024]{1,0:T(8,128)(2,1)S(1)}, u32[]{:S(2)}, u32[]{:S(2)}) collective-permute-start(bf16[32,1024]{1,0:T(8,128)(2,1)S(1)} %get-tuple-element.93), channel_id=1, source_target_pairs={{0,16},{16,0},{32,48},{48,32},{64,80},{80,64},{96,112},{112,96},{1... | collective-permute-start | bytes 196616 | tf_op jit(solution)/shard_map/ppermute | solution.py:365
  18.5 6.1 %collective-permute-start.11 = (bf16[32,2304]{1,0:T(8,128)(2,1)S(1)}, bf16[32,2304]{1,0:T(8,128)(2,1)S(1)}, u32[]{:S(2)}, u32[]{:S(2)}) collective-permute-start(bf16[32,2304]{1,0:T(8,128)(2,1)S(1)} %get-tuple-element.103), channel_id=1, source_target_pairs={{0,16},{16,32},{32,48},{48,64},{64,80},{80,96},{96,112},{112,128},... | collective-permute-start | bytes 442376 | tf_op jit(solution)/shard_map/ppermute | solution.py:359
  18.6 7.0 %collective-permute-start.10 = (bf16[32,2304]{1,0:T(8,128)(2,1)S(1)}, bf16[32,2304]{1,0:T(8,128)(2,1)S(1)}, u32[]{:S(2)}, u32[]{:S(2)}) collective-permute-start(bf16[32,2304]{1,0:T(8,128)(2,1)S(1)} %get-tuple-element.102), channel_id=1, source_target_pairs={{16,0},{32,16},{48,32},{64,48},{80,64},{96,80},{112,96},{128,112},... | collective-permute-start | bytes 442376 | tf_op jit(solution)/shard_map/ppermute | solution.py:359
  22.5 1.7 %collective-permute-start.8 = (bf16[32,1280]{1,0:T(8,128)(2,1)S(1)}, bf16[32,1280]{1,0:T(8,128)(2,1)S(1)}, u32[]{:S(2)}, u32[]{:S(2)}) collective-permute-start(bf16[32,1280]{1,0:T(8,128)(2,1)S(1)} %get-tuple-element.100), channel_id=1, source_target_pairs={{0,16},{16,0},{32,48},{48,32},{64,80},{80,64},{96,112},{112,96},{1... | collective-permute-start | bytes 245768 | tf_op jit(solution)/shard_map/ppermute | solution.py:365
  22.6 1.6 %collective-permute-start.9 = (bf16[32,1024]{1,0:T(8,128)(2,1)S(1)}, bf16[32,1024]{1,0:T(8,128)(2,1)S(1)}, u32[]{:S(2)}, u32[]{:S(2)}) collective-permute-start(bf16[32,1024]{1,0:T(8,128)(2,1)S(1)} %get-tuple-element.101), channel_id=1, source_target_pairs={{0,16},{16,0},{32,48},{48,32},{64,80},{80,64},{96,112},{112,96},{1... | collective-permute-start | bytes 196616 | tf_op jit(solution)/shard_map/ppermute | solution.py:365
  24.7 4.6 %collective-permute-start.15 = (bf16[32,2304]{1,0:T(8,128)(2,1)S(1)}, bf16[32,2304]{1,0:T(8,128)(2,1)S(1)}, u32[]{:S(2)}, u32[]{:S(2)}) collective-permute-start(bf16[32,2304]{1,0:T(8,128)(2,1)S(1)} %get-tuple-element.111), channel_id=1, source_target_pairs={{16,0},{32,16},{48,32},{64,48},{80,64},{96,80},{112,96},{128,112},... | collective-permute-start | bytes 442376 | tf_op jit(solution)/shard_map/ppermute | solution.py:359
  26.3 3.6 %collective-permute-start.14 = (bf16[32,2304]{1,0:T(8,128)(2,1)S(1)}, bf16[32,2304]{1,0:T(8,128)(2,1)S(1)}, u32[]{:S(2)}, u32[]{:S(2)}) collective-permute-start(bf16[32,2304]{1,0:T(8,128)(2,1)S(1)} %get-tuple-element.110), channel_id=1, source_target_pairs={{0,16},{16,32},{32,48},{48,64},{64,80},{80,96},{96,112},{112,128},... | collective-permute-start | bytes 442376 | tf_op jit(solution)/shard_map/ppermute | solution.py:359
  26.8 1.7 %collective-permute-start.12 = (bf16[32,1280]{1,0:T(8,128)(2,1)S(1)}, bf16[32,1280]{1,0:T(8,128)(2,1)S(1)}, u32[]{:S(2)}, u32[]{:S(2)}) collective-permute-start(bf16[32,1280]{1,0:T(8,128)(2,1)S(1)} %get-tuple-element.108), channel_id=1, source_target_pairs={{0,16},{16,0},{32,48},{48,32},{64,80},{80,64},{96,112},{112,96},{1... | collective-permute-start | bytes 245768 | tf_op jit(solution)/shard_map/ppermute | solution.py:365
  27.2 1.3 %collective-permute-start.13 = (bf16[32,1024]{1,0:T(8,128)(2,1)S(1)}, bf16[32,1024]{1,0:T(8,128)(2,1)S(1)}, u32[]{:S(2)}, u32[]{:S(2)}) collective-permute-start(bf16[32,1024]{1,0:T(8,128)(2,1)S(1)} %get-tuple-element.109), channel_id=1, source_target_pairs={{0,16},{16,0},{32,48},{48,32},{64,80},{80,64},{96,112},{112,96},{1... | collective-permute-start | bytes 196616 | tf_op jit(solution)/shard_map/ppermute | solution.py:365
  29.9 4.9 %collective-permute-start.19 = (bf16[32,2304]{1,0:T(8,128)(2,1)S(1)}, bf16[32,2304]{1,0:T(8,128)(2,1)S(1)}, u32[]{:S(2)}, u32[]{:S(2)}) collective-permute-start(bf16[32,2304]{1,0:T(8,128)(2,1)S(1)} %get-tuple-element.119), channel_id=1, source_target_pairs={{0,16},{16,32},{32,48},{48,64},{64,80},{80,96},{96,112},{112,128},... | collective-permute-start | bytes 442376 | tf_op jit(solution)/shard_map/ppermute | solution.py:359
  29.9 4.9 %collective-permute-start.18 = (bf16[32,2304]{1,0:T(8,128)(2,1)S(1)}, bf16[32,2304]{1,0:T(8,128)(2,1)S(1)}, u32[]{:S(2)}, u32[]{:S(2)}) collective-permute-start(bf16[32,2304]{1,0:T(8,128)(2,1)S(1)} %get-tuple-element.118), channel_id=1, source_target_pairs={{16,0},{32,16},{48,32},{64,48},{80,64},{96,80},{112,96},{128,112},... | collective-permute-start | bytes 442376 | tf_op jit(solution)/shard_map/ppermute | solution.py:359
  32.5 1.7 %collective-permute-start.16 = (bf16[32,1280]{1,0:T(8,128)(2,1)S(1)}, bf16[32,1280]{1,0:T(8,128)(2,1)S(1)}, u32[]{:S(2)}, u32[]{:S(2)}) collective-permute-start(bf16[32,1280]{1,0:T(8,128)(2,1)S(1)} %get-tuple-element.116), channel_id=1, source_target_pairs={{0,16},{16,0},{32,48},{48,32},{64,80},{80,64},{96,112},{112,96},{1... | collective-permute-start | bytes 245768 | tf_op jit(solution)/shard_map/ppermute | solution.py:365
  32.7 1.5 %collective-permute-start.17 = (bf16[32,1024]{1,0:T(8,128)(2,1)S(1)}, bf16[32,1024]{1,0:T(8,128)(2,1)S(1)}, u32[]{:S(2)}, u32[]{:S(2)}) collective-permute-start(bf16[32,1024]{1,0:T(8,128)(2,1)S(1)} %get-tuple-element.117), channel_id=1, source_target_pairs={{0,16},{16,0},{32,48},{48,32},{64,80},{80,64},{96,112},{112,96},{1... | collective-permute-start | bytes 196616 | tf_op jit(solution)/shard_map/ppermute | solution.py:365
  35.4 5.5 %collective-permute-start.22 = (bf16[32,2304]{1,0:T(8,128)(2,1)S(1)}, bf16[32,2304]{1,0:T(8,128)(2,1)S(1)}, u32[]{:S(2)}, u32[]{:S(2)}) collective-permute-start(bf16[32,2304]{1,0:T(8,128)(2,1)S(1)} %get-tuple-element.127), channel_id=1, source_target_pairs={{0,16},{16,32},{32,48},{48,64},{64,80},{80,96},{96,112},{112,128},... | collective-permute-start | bytes 442376 | tf_op jit(solution)/shard_map/ppermute | solution.py:359
  35.4 5.5 %collective-permute-start.23 = (bf16[32,2304]{1,0:T(8,128)(2,1)S(1)}, bf16[32,2304]{1,0:T(8,128)(2,1)S(1)}, u32[]{:S(2)}, u32[]{:S(2)}) collective-permute-start(bf16[32,2304]{1,0:T(8,128)(2,1)S(1)} %get-tuple-element.128), channel_id=1, source_target_pairs={{16,0},{32,16},{48,32},{64,48},{80,64},{96,80},{112,96},{128,112},... | collective-permute-start | bytes 442376 | tf_op jit(solution)/shard_map/ppermute | solution.py:359
  36.2 4.2 %collective-permute-start.20 = (bf16[32,1280]{1,0:T(8,128)(2,1)S(1)}, bf16[32,1280]{1,0:T(8,128)(2,1)S(1)}, u32[]{:S(2)}, u32[]{:S(2)}) collective-permute-start(bf16[32,1280]{1,0:T(8,128)(2,1)S(1)} %get-tuple-element.124), channel_id=1, source_target_pairs={{0,16},{16,0},{32,48},{48,32},{64,80},{80,64},{96,112},{112,96},{1... | collective-permute-start | bytes 245768 | tf_op jit(solution)/shard_map/ppermute | solution.py:365
  39.1 1.3 %collective-permute-start.21 = (bf16[32,1024]{1,0:T(8,128)(2,1)S(1)}, bf16[32,1024]{1,0:T(8,128)(2,1)S(1)}, u32[]{:S(2)}, u32[]{:S(2)}) collective-permute-start(bf16[32,1024]{1,0:T(8,128)(2,1)S(1)} %get-tuple-element.125), channel_id=1, source_target_pairs={{0,16},{16,0},{32,48},{48,32},{64,80},{80,64},{96,112},{112,96},{1... | collective-permute-start | bytes 196616 | tf_op jit(solution)/shard_map/ppermute | solution.py:365

commit v12 on v10

--- a/solution.py
+++ b/solution.py
@@ -122,6 +122,17 @@
             w_ref[block(place, sigma)] = totals[place][offset].astype(jnp.bfloat16)
 
 
+def turn(w_ref, side, turned_ref, cols):
+    step = PAIR * cols
+    groups = w_ref.shape[1] // step
+    for group in range(groups):
+        outs = slice(group * step, (group + 1) * step)
+        inside = span(side, group, groups, step)
+        for start in range(inside.start, inside.stop, step):
+            ins = slice(start, start + step)
+            turned_ref[ins, outs] = w_ref[outs, ins].T
+
+
 def prepare(
     partner_hbm, states_hbm, onsite_hbm, hop_row_hbm, hop_up_hbm, coefs_hbm, coupling_hbm,
     x_ref, w_ref, coef_ref, rim_ref, weight_ref, far_ref, *rest,
@@ -218,25 +229,27 @@
 
 
 def to_mate_first(x_ref, rim_ref, *refs):
-    *totals, rows_ref, terms_ref, w_ref = refs
+    *totals, rows_ref, terms_ref, w_ref, turned_ref = refs
     settle(totals, MATE, w_ref, rim_ref.shape[2])
+    turn(w_ref, MATE, turned_ref, rim_ref.shape[2])
     write_payload(x_ref, w_ref, rim_ref, MATE, rows_ref, terms_ref)
 
 
 def inner(order, *refs):
     if order == 0:
-        x_ref, coef_ref, weight_ref, *totals, sum_ref, filt_out, w_ref = refs
+        x_ref, coef_ref, weight_ref, *totals, sum_ref, filt_out, w_ref, turned_ref = refs
         settle(totals, LOCAL, w_ref, weight_ref.shape[1])
+        turn(w_ref, LOCAL, turned_ref, weight_ref.shape[1])
         scale = 1.0 / 12.0
     else:
-        x_ref, prev_ref, filt_ref, w_ref, coef_ref, weight_ref, sum_ref, filt_out = refs
+        x_ref, prev_ref, filt_ref, w_ref, turned_ref, coef_ref, weight_ref, sum_ref, filt_out = refs
         scale = 2.0 / 12.0
     wide = x_ref.shape[2]
     cols = weight_ref.shape[1]
     rows = wide // cols
     first = x_ref[0].astype(jnp.bfloat16)
     second = x_ref[1].astype(jnp.bfloat16)
-    for outs, term in products(second, w_ref, LOCAL, 1, cols):
+    for outs, term in products(second, turned_ref, LOCAL, 0, cols):
         sum_ref[0, :, outs] = scale * term
     for outs, term in products(first, w_ref, LOCAL, 0, cols):
         sum_ref[1, :, outs] = scale * term
@@ -269,15 +282,9 @@
         far_ref, sum_ref, *turned = refs
     else:
         (sum_ref,), turned = refs, []
-    add_received(scale, rows_ref, terms_ref, w_ref, 1, rim_ref, MATE, part_ref, sum_ref)
+    add_received(scale, rows_ref, terms_ref, w_ref, 0, rim_ref, MATE, part_ref, sum_ref)
     if turned:
-        step = PAIR * rim_ref.shape[2]
-        groups = sum_ref.shape[2] // step
-        for group in range(groups):
-            outs = slice(group * step, (group + 1) * step)
-            for other in range(groups - group):
-                ins = slice(other * step, (other + 1) * step)
-                turned[0][ins, outs] = far_ref[outs, ins].T
+        turn(far_ref, FAR, turned[0], rim_ref.shape[2])
 
 
 def outer(scale, mine, sum_ref, w_ref, turned_ref, rim_ref, got_ref, *refs):
@@ -360,26 +367,30 @@
         scale = 1.0 / 12.0 if order == 0 else 2.0 / 12.0
         got = {1: lax.ppermute(far[0], "tile", down_pairs), 0: lax.ppermute(far[1], "tile", up_pairs)}
         if order == 0:
-            *mate, w_mate = call(to_mate_first, [*parts, matrix], [x, rim, *totals])
-            w_mate = near(w_mate)
+            *mate, w_mate, m_turned = call(
+                to_mate_first, [*parts, matrix, matrix], [x, rim, *totals]
+            )
+            w_mate, m_turned = near(w_mate), near(m_turned)
         else:
             mate = call(to_mate, parts, [x, w_mate, rim])
         got_mate = [near(lax.ppermute(part, "tile", mate_pairs)) for part in mate]
         if order == 0:
-            part, filt, w_local = call(
-                functools.partial(inner, order), [field, field, matrix], [x, coef, weight, *totals]
-            )
-            w_local = near(w_local)
+            part, filt, w_local, w_turned = call(
+                functools.partial(inner, order),
+                [field, field, matrix, matrix],
+                [x, coef, weight, *totals],
+            )
+            w_local, w_turned = near(w_local), near(w_turned)
         else:
             part, filt = call(
                 functools.partial(inner, order),
                 [field, field],
-                [x, near(prev), near(filt), w_local, coef, weight],
+                [x, near(prev), near(filt), w_local, w_turned, coef, weight],
             )
         part, *turned_now = call(
             functools.partial(from_mate, scale),
             [field, matrix] if order == 0 else [field],
-            [near(part), w_mate, rim, *got_mate] + ([w_far] if order == 0 else []),
+            [near(part), m_turned, rim, *got_mate] + ([w_far] if order == 0 else []),
             flops=0,
         )
         if order == 0:

time: 41.6 us -> 41.2 us (level)
  Pallas kernels: 19.5 us -> 17.8 us
  waiting for transfers between devices: 0.38 us -> 1.34 us
    pallas_call x30, Pallas kernels: 19.5 us -> 17.8 us  [call(): pl.pallas_call(kernel, out_shape=outs, in_specs=specs or [IN_VMEM] * len(...]
    ppermute x12, waiting for transfers between devices: 0.11 us -> 0.79 us  [body(): got_mate = [near(lax.ppermute(part, 'tile', mate_pairs)) for part in mate]]
    ppermute x6, starting transfers between devices: 8.5 us -> 9.05 us  [body(): lax.ppermute(far[0], 'tile', down_pairs)]
  transfers between devices with their start and end apart: 24 -> 24, of which waited for: 3 -> 6; matrix products, arithmetic and copies ran while one was open for 0% -> 0% of each run, Pallas kernels for 34% -> 30%
where the time goes in v12:
time: 41.2 us; the launch traced here: 41.1 us
  starting transfers between devices  21.7 us (53%)
  Pallas kernels  17.8 us (43%)
  waiting for transfers between devices  1.34 us (3%)
    pallas_call x30, Pallas kernels, call(): pl.pallas_call(kernel, out_shape=outs, in_specs=specs or [IN_VMEM] * len(...  17.8 us
    ppermute x12, starting transfers between devices, body(): got_mate = [near(lax.ppermute(part, 'tile', mate_pairs)) for part in mate]  9.42 us
    ppermute x6, starting transfers between devices, body(): lax.ppermute(far[0], 'tile', down_pairs)  9.05 us
    ppermute x6, starting transfers between devices, body(): lax.ppermute(far[1], 'tile', up_pairs)  3.25 us
  transfers between devices with their start and end apart: 24, of which 6 were waited for; matrix products, arithmetic and copies ran while one was open for 0% of the time, Pallas kernels for 30%

profile of v12, /device:TPU:1, one launch (start us, length us, event | category | flops | bytes accessed | tf_op | source)
XLA Modules:
  0.0 41.1 jit_solution(17478430980984869567)
XLA Ops:
  0.0 3.6 %shard_map.73 = (f32[2,32,1024]{2,1,0:T(8,128)S(1)}, bf16[1024,1024]{1,0:T(8,128)(2,1)S(1)}, f32[2,5,8,128]{3,2,1,0:T(8,128)S(1)}, f32[2,2,128]{2,1,0:T(2,128)S(...) custom-call(s32[8,16]{1,0:T(8,128)} %partner_hbm.1, ...), custom_call_target="tpu_custom_call" | custom-call | flops 1048576 | tf_op jit(solution)/shard_map/pallas_call | solution.py:318
  3.6 3.0 %collective-permute-start.3 = (bf16[32,2304]{1,0:T(8,128)(2,1)S(1)}, bf16[32,2304]{1,0:T(8,128)(2,1)S(1)}, u32[]{:S(2)}, u32[]{:S(2)}) collective-permute-start(bf16[32,2304]{1,0:T(8,128)(2,1)S(1)} %get-tuple-element.88), channel_id=1, source_target_pairs={{0,16},{16,32},{32,48},{48,64},{64,80},{80,96},{96,112},{112,128},... | collective-permute-start | bytes 442376 | tf_op jit(solution)/shard_map/ppermute | solution.py:368
  6.6 0.2 collective-permute-start.2
  6.8 0.6 %shard_map.75 = (bf16[32,1280]{1,0:T(8,128)(2,1)S(1)}, bf16[32,1024]{1,0:T(8,128)(2,1)S(1)}, bf16[1024,1024]{1,0:T(8,128)(2,1)S(1)}, bf16[1024,1024]{1,0:T(8,128)(2,1)S(1)}) custom-call(f32[2,32,1024]{2,1,0:T(8,128)S(1)} %get-tuple-element.69.refs_0_.x_ref.refs_1_, f32[2,2,128]{2,1,0:T(2,128)S(1)} %get-tuple-element.81.rim_ref, ...), custom_call_target="tpu_custom_call" | custom-call | flops 1048576 | tf_op jit(solution)/shard_map/pallas_call | solution.py:318
  7.4 3.6 %collective-permute-start = (bf16[32,1280]{1,0:T(8,128)(2,1)S(1)}, bf16[32,1280]{1,0:T(8,128)(2,1)S(1)}, u32[]{:S(2)}, u32[]{:S(2)}) collective-permute-start(bf16[32,1280]{1,0:T(8,128)(2,1)S(1)} %get-tuple-element.83), channel_id=1, source_target_pairs={{0,16},{16,0},{32,48},{48,32},{64,80},{80,64},{96,112},{112,96},{1... | collective-permute-start | bytes 245768 | tf_op jit(solution)/shard_map/ppermute | solution.py:376
  11.1 0.1 collective-permute-start.1
  11.2 1.2 %shard_map.74 = (f32[2,32,1024]{2,1,0:T(8,128)S(1)}, f32[2,32,1024]{2,1,0:T(8,128)S(1)}, bf16[1024,1024]{1,0:T(8,128)(2,1)S(1)}, bf16[1024,1024]{1,0:T(8,128)(2,1)S(1)}) custom-call(f32[2,32,1024]{2,1,0:T(8,128)S(1)} %get-tuple-element.69.refs_0_.x_ref.refs_1_, f32[2,5,8,128]{3,2,1,0:T(8,128)S(1)} %get-tuple-element.70.refs_1_.refs_5_, ...), custom_call_target="tpu_custom_call" | custom-call | flops 1048576 | tf_op jit(solution)/shard_map/pallas_call | solution.py:318
  12.4 0.5 %shard_map.76 = (f32[2,32,1024]{2,1,0:T(8,128)S(1)}, bf16[1024,1024]{1,0:T(8,128)(2,1)S(1)}) custom-call(f32[2,32,1024]{2,1,0:T(8,128)S(1)} %get-tuple-element.80.part_ref, bf16[1024,1024]{1,0:T(8,128)(2,1)S(1)} %get-tuple-element.82.w_ref, f32[2,2,128]{2,1,0:T(2,128)S(1)} %get-tuple-element.81.rim_ref, bf16[32,1280]{1,0:T(8,128)(2,1)S(1)} %collective-permute-done.rows_ref, ...), custom_call_target="tpu_custom_call" | custom-call | tf_op jit(solution)/shard_map/pallas_call | solution.py:318
  12.9 1.0 %collective-permute-start.7 = (bf16[32,2304]{1,0:T(8,128)(2,1)S(1)}, bf16[32,2304]{1,0:T(8,128)(2,1)S(1)}, u32[]{:S(2)}, u32[]{:S(2)}) collective-permute-start(bf16[32,2304]{1,0:T(8,128)(2,1)S(1)} %get-tuple-element.99), channel_id=1, source_target_pairs={{16,0},{32,16},{48,32},{64,48},{80,64},{96,80},{112,96},{128,112},... | collective-permute-start | bytes 442376 | tf_op jit(solution)/shard_map/ppermute | solution.py:368
  13.9 0.6 %shard_map.78 = (f32[2,32,1024]{2,1,0:T(8,128)S(1)}, bf16[32,2304]{1,0:T(8,128)(2,1)S(1)}) custom-call(f32[2,32,1024]{2,1,0:T(8,128)S(1)} %get-tuple-element.86.sum_ref, bf16[1024,1024]{1,0:T(8,128)(2,1)S(1)} %get-tuple-element.85.refs_0_.w_ref, bf16[1024,1024]{1,0:T(8,128)(2,1)S(1)} %get-tuple-element.87.turned_ref, ...), custom_call_target="tpu_custom_call", output_to_operand_aliasing={{0}: (5, {})} | custom-call | flops 1048576 | tf_op jit(solution)/shard_map/pallas_call | solution.py:318
  14.5 0.2 collective-permute-start.6
  14.7 0.3 shard_map.80
  15.0 0.7 %collective-permute-start.4 = (bf16[32,1280]{1,0:T(8,128)(2,1)S(1)}, bf16[32,1280]{1,0:T(8,128)(2,1)S(1)}, u32[]{:S(2)}, u32[]{:S(2)}) collective-permute-start(bf16[32,1280]{1,0:T(8,128)(2,1)S(1)} %get-tuple-element.96), channel_id=1, source_target_pairs={{0,16},{16,0},{32,48},{48,32},{64,80},{80,64},{96,112},{112,96},{1... | collective-permute-start | bytes 245768 | tf_op jit(solution)/shard_map/ppermute | solution.py:376
  15.7 0.1 collective-permute-start.5
  15.8 0.9 %shard_map.79 = (f32[2,32,1024]{2,1,0:T(8,128)S(1)}, f32[2,32,1024]{2,1,0:T(8,128)S(1)}) custom-call(f32[2,32,1024]{2,1,0:T(8,128)S(1)} %get-tuple-element.90.refs_0_.x_ref.refs_1_, f32[2,32,1024]{2,1,0:T(8,128)S(1)} %get-tuple-element.69.refs_0_.x_ref.refs_1_, f32[2,32,1024]{2,1,0:T(8,128)S(1)} %get-tuple-element.91.refs_2_, ...), custom_call_target="tpu_custom_call" | custom-call | flops 1048576 | tf_op jit(solution)/shard_map/pallas_call | solution.py:318
  16.7 0.3 collective-permute-done.5.terms_ref
  16.9 0.3 shard_map.81.sum_ref
  17.3 0.2 collective-permute-done.7.got_ref
  17.5 0.6 %shard_map.82 = (f32[2,32,1024]{2,1,0:T(8,128)S(1)}, bf16[32,2304]{1,0:T(8,128)(2,1)S(1)}) custom-call(f32[2,32,1024]{2,1,0:T(8,128)S(1)} %shard_map.81.sum_ref, bf16[1024,1024]{1,0:T(8,128)(2,1)S(1)} %get-tuple-element.85.refs_0_.w_ref, bf16[1024,1024]{1,0:T(8,128)(2,1)S(1)} %get-tuple-element.87.turned_ref, f32[2,2,128]{2,1,0:T(2,128)S(1)} %get-tuple-element.81.rim_ref, ...), custom_call_target="tpu_custom_call" | custom-call | flops 1048576 | tf_op jit(solution)/shard_map/pallas_call | solution.py:318
  18.2 3.6 %collective-permute-start.10 = (bf16[32,2304]{1,0:T(8,128)(2,1)S(1)}, bf16[32,2304]{1,0:T(8,128)(2,1)S(1)}, u32[]{:S(2)}, u32[]{:S(2)}) collective-permute-start(bf16[32,2304]{1,0:T(8,128)(2,1)S(1)} %get-tuple-element.106), channel_id=1, source_target_pairs={{16,0},{32,16},{48,32},{64,48},{80,64},{96,80},{112,96},{128,112},... | collective-permute-start | bytes 442376 | tf_op jit(solution)/shard_map/ppermute | solution.py:368
  21.7 0.3 shard_map.85
  22.1 0.5 %collective-permute-start.9 = (bf16[32,1024]{1,0:T(8,128)(2,1)S(1)}, bf16[32,1024]{1,0:T(8,128)(2,1)S(1)}, u32[]{:S(2)}, u32[]{:S(2)}) collective-permute-start(bf16[32,1024]{1,0:T(8,128)(2,1)S(1)} %get-tuple-element.105), channel_id=1, source_target_pairs={{0,16},{16,0},{32,48},{48,32},{64,80},{80,64},{96,112},{112,96},{1... | collective-permute-start | bytes 196616 | tf_op jit(solution)/shard_map/ppermute | solution.py:376
  22.6 0.9 %shard_map.84 = (f32[2,32,1024]{2,1,0:T(8,128)S(1)}, f32[2,32,1024]{2,1,0:T(8,128)S(1)}) custom-call(f32[2,32,1024]{2,1,0:T(8,128)S(1)} %get-tuple-element.101.refs_0_.x_ref.refs_1_, f32[2,32,1024]{2,1,0:T(8,128)S(1)} %get-tuple-element.90.refs_0_.x_ref.refs_1_, f32[2,32,1024]{2,1,0:T(8,128)S(1)} %get-tuple-element.102.refs_2_, ...), custom_call_target="tpu_custom_call" | custom-call | flops 1048576 | tf_op jit(solution)/shard_map/pallas_call | solution.py:318
  23.5 0.3 shard_map.86.sum_ref
  23.9 1.3 %collective-permute-start.15 = (bf16[32,2304]{1,0:T(8,128)(2,1)S(1)}, bf16[32,2304]{1,0:T(8,128)(2,1)S(1)}, u32[]{:S(2)}, u32[]{:S(2)}) collective-permute-start(bf16[32,2304]{1,0:T(8,128)(2,1)S(1)} %get-tuple-element.115), channel_id=1, source_target_pairs={{16,0},{32,16},{48,32},{64,48},{80,64},{96,80},{112,96},{128,112},... | collective-permute-start | bytes 442376 | tf_op jit(solution)/shard_map/ppermute | solution.py:368
  25.2 0.6 %shard_map.88 = (f32[2,32,1024]{2,1,0:T(8,128)S(1)}, bf16[32,2304]{1,0:T(8,128)(2,1)S(1)}) custom-call(f32[2,32,1024]{2,1,0:T(8,128)S(1)} %shard_map.86.sum_ref, bf16[1024,1024]{1,0:T(8,128)(2,1)S(1)} %get-tuple-element.85.refs_0_.w_ref, bf16[1024,1024]{1,0:T(8,128)(2,1)S(1)} %get-tuple-element.87.turned_ref, ...), custom_call_target="tpu_custom_call", output_to_operand_aliasing={{0}: (5, {})} | custom-call | flops 1048576 | tf_op jit(solution)/shard_map/pallas_call | solution.py:318
  25.8 0.3 shard_map.90
  26.1 0.7 %collective-permute-start.12 = (bf16[32,1280]{1,0:T(8,128)(2,1)S(1)}, bf16[32,1280]{1,0:T(8,128)(2,1)S(1)}, u32[]{:S(2)}, u32[]{:S(2)}) collective-permute-start(bf16[32,1280]{1,0:T(8,128)(2,1)S(1)} %get-tuple-element.112), channel_id=1, source_target_pairs={{0,16},{16,0},{32,48},{48,32},{64,80},{80,64},{96,112},{112,96},{1... | collective-permute-start | bytes 245768 | tf_op jit(solution)/shard_map/ppermute | solution.py:376
  26.8 0.1 collective-permute-start.13
  26.9 0.9 %shard_map.89 = (f32[2,32,1024]{2,1,0:T(8,128)S(1)}, f32[2,32,1024]{2,1,0:T(8,128)S(1)}) custom-call(f32[2,32,1024]{2,1,0:T(8,128)S(1)} %get-tuple-element.109.refs_0_.x_ref.refs_1_, f32[2,32,1024]{2,1,0:T(8,128)S(1)} %get-tuple-element.101.refs_0_.x_ref.refs_1_, f32[2,32,1024]{2,1,0:T(8,128)S(1)} %get-tuple-element.110.refs_2_, ...), custom_call_target="tpu_custom_call" | custom-call | flops 1048576 | tf_op jit(solution)/shard_map/pallas_call | solution.py:318
  27.8 0.3 collective-permute-done.13.terms_ref
  28.1 0.3 shard_map.91.sum_ref
  28.5 0.6 %shard_map.92 = (f32[2,32,1024]{2,1,0:T(8,128)S(1)}, bf16[32,2304]{1,0:T(8,128)(2,1)S(1)}) custom-call(f32[2,32,1024]{2,1,0:T(8,128)S(1)} %shard_map.91.sum_ref, bf16[1024,1024]{1,0:T(8,128)(2,1)S(1)} %get-tuple-element.85.refs_0_.w_ref, bf16[1024,1024]{1,0:T(8,128)(2,1)S(1)} %get-tuple-element.87.turned_ref, f32[2,2,128]{2,1,0:T(2,128)S(1)} %get-tuple-element.81.rim_ref, ...), custom_call_target="tpu_custom_call" | custom-call | flops 1048576 | tf_op jit(solution)/shard_map/pallas_call | solution.py:318
  29.1 2.5 %collective-permute-start.18 = (bf16[32,2304]{1,0:T(8,128)(2,1)S(1)}, bf16[32,2304]{1,0:T(8,128)(2,1)S(1)}, u32[]{:S(2)}, u32[]{:S(2)}) collective-permute-start(bf16[32,2304]{1,0:T(8,128)(2,1)S(1)} %get-tuple-element.122), channel_id=1, source_target_pairs={{16,0},{32,16},{48,32},{64,48},{80,64},{96,80},{112,96},{128,112},... | collective-permute-start | bytes 442376 | tf_op jit(solution)/shard_map/ppermute | solution.py:368
  31.6 0.3 shard_map.95
  32.0 0.5 %collective-permute-start.17 = (bf16[32,1024]{1,0:T(8,128)(2,1)S(1)}, bf16[32,1024]{1,0:T(8,128)(2,1)S(1)}, u32[]{:S(2)}, u32[]{:S(2)}) collective-permute-start(bf16[32,1024]{1,0:T(8,128)(2,1)S(1)} %get-tuple-element.121), channel_id=1, source_target_pairs={{0,16},{16,0},{32,48},{48,32},{64,80},{80,64},{96,112},{112,96},{1... | collective-permute-start | bytes 196616 | tf_op jit(solution)/shard_map/ppermute | solution.py:376
  32.5 0.9 %shard_map.94 = (f32[2,32,1024]{2,1,0:T(8,128)S(1)}, f32[2,32,1024]{2,1,0:T(8,128)S(1)}) custom-call(f32[2,32,1024]{2,1,0:T(8,128)S(1)} %get-tuple-element.117.refs_0_.x_ref.refs_1_, f32[2,32,1024]{2,1,0:T(8,128)S(1)} %get-tuple-element.109.refs_0_.x_ref.refs_1_, f32[2,32,1024]{2,1,0:T(8,128)S(1)} %get-tuple-element.118.refs_2_, ...), custom_call_target="tpu_custom_call" | custom-call | flops 1048576 | tf_op jit(solution)/shard_map/pallas_call | solution.py:318
  33.4 0.3 shard_map.96.sum_ref
  33.8 0.3 collective-permute-done.18.got_ref
  34.0 0.6 %shard_map.98 = (f32[2,32,1024]{2,1,0:T(8,128)S(1)}, bf16[32,2304]{1,0:T(8,128)(2,1)S(1)}) custom-call(f32[2,32,1024]{2,1,0:T(8,128)S(1)} %shard_map.96.sum_ref, bf16[1024,1024]{1,0:T(8,128)(2,1)S(1)} %get-tuple-element.85.refs_0_.w_ref, bf16[1024,1024]{1,0:T(8,128)(2,1)S(1)} %get-tuple-element.87.turned_ref, ...), custom_call_target="tpu_custom_call", output_to_operand_aliasing={{0}: (5, {})} | custom-call | flops 1048576 | tf_op jit(solution)/shard_map/pallas_call | solution.py:318
  34.6 0.5 %collective-permute-start.23 = (bf16[32,2304]{1,0:T(8,128)(2,1)S(1)}, bf16[32,2304]{1,0:T(8,128)(2,1)S(1)}, u32[]{:S(2)}, u32[]{:S(2)}) collective-permute-start(bf16[32,2304]{1,0:T(8,128)(2,1)S(1)} %get-tuple-element.132), channel_id=1, source_target_pairs={{16,0},{32,16},{48,32},{64,48},{80,64},{96,80},{112,96},{128,112},... | collective-permute-start | bytes 442376 | tf_op jit(solution)/shard_map/ppermute | solution.py:368
  35.1 0.3 shard_map.100
  35.5 2.9 %collective-permute-start.20 = (bf16[32,1280]{1,0:T(8,128)(2,1)S(1)}, bf16[32,1280]{1,0:T(8,128)(2,1)S(1)}, u32[]{:S(2)}, u32[]{:S(2)}) collective-permute-start(bf16[32,1280]{1,0:T(8,128)(2,1)S(1)} %get-tuple-element.128), channel_id=1, source_target_pairs={{0,16},{16,0},{32,48},{48,32},{64,80},{80,64},{96,112},{112,96},{1... | collective-permute-start | bytes 245768 | tf_op jit(solution)/shard_map/ppermute | solution.py:376
  38.4 0.1 collective-permute-start.21
  38.5 0.9 %shard_map.99 = (f32[2,32,1024]{2,1,0:T(8,128)S(1)}, f32[2,32,1024]{2,1,0:T(8,128)S(1)}) custom-call(f32[2,32,1024]{2,1,0:T(8,128)S(1)} %get-tuple-element.125.refs_0_.x_ref, f32[2,32,1024]{2,1,0:T(8,128)S(1)} %get-tuple-element.117.refs_0_.x_ref.refs_1_, f32[2,32,1024]{2,1,0:T(8,128)S(1)} %get-tuple-element.126.refs_2_, ...), custom_call_target="tpu_custom_call" | custom-call | flops 1048576 | tf_op jit(solution)/shard_map/pallas_call | solution.py:318
  39.4 0.3 collective-permute-done.21.terms_ref
  39.6 0.3 shard_map.101.sum_ref
  40.0 1.1 %shard_map.102 = f32[2,8,32,128]{3,2,1,0:T(8,128)} custom-call(f32[2,32,1024]{2,1,0:T(8,128)S(1)} %shard_map.101.sum_ref, f32[2,32,1024]{2,1,0:T(8,128)S(1)} %get-tuple-element.130.filt_ref, bf16[1024,1024]{1,0:T(8,128)(2,1)S(1)} %get-tuple-element.87.turned_ref, f32[2,2,128]{2,1,0:T(2,128)S(1)} %get-tuple-element.81.rim_ref, ...), custom_call_target="tpu_custom_call" | custom-call | flops 1048576 | tf_op jit(solution)/shard_map/pallas_call | solution.py:318
  (30 shorter events, 0.4 us)
Async XLA Ops:
  3.6 9.3 %collective-permute-start.3 = (bf16[32,2304]{1,0:T(8,128)(2,1)S(1)}, bf16[32,2304]{1,0:T(8,128)(2,1)S(1)}, u32[]{:S(2)}, u32[]{:S(2)}) collective-permute-start(bf16[32,2304]{1,0:T(8,128)(2,1)S(1)} %get-tuple-element.88), channel_id=1, source_target_pairs={{0,16},{16,32},{32,48},{48,64},{64,80},{80,96},{96,112},{112,128},... | collective-permute-start | bytes 442376 | tf_op jit(solution)/shard_map/ppermute | solution.py:368
  6.6 7.3 %collective-permute-start.2 = (bf16[32,2304]{1,0:T(8,128)(2,1)S(1)}, bf16[32,2304]{1,0:T(8,128)(2,1)S(1)}, u32[]{:S(2)}, u32[]{:S(2)}) collective-permute-start(bf16[32,2304]{1,0:T(8,128)(2,1)S(1)} %get-tuple-element.88), channel_id=1, source_target_pairs={{16,0},{32,16},{48,32},{64,48},{80,64},{96,80},{112,96},{128,112},... | collective-permute-start | bytes 442376 | tf_op jit(solution)/shard_map/ppermute | solution.py:368
  7.4 5.0 %collective-permute-start = (bf16[32,1280]{1,0:T(8,128)(2,1)S(1)}, bf16[32,1280]{1,0:T(8,128)(2,1)S(1)}, u32[]{:S(2)}, u32[]{:S(2)}) collective-permute-start(bf16[32,1280]{1,0:T(8,128)(2,1)S(1)} %get-tuple-element.83), channel_id=1, source_target_pairs={{0,16},{16,0},{32,48},{48,32},{64,80},{80,64},{96,112},{112,96},{1... | collective-permute-start | bytes 245768 | tf_op jit(solution)/shard_map/ppermute | solution.py:376
  11.1 1.3 %collective-permute-start.1 = (bf16[32,1024]{1,0:T(8,128)(2,1)S(1)}, bf16[32,1024]{1,0:T(8,128)(2,1)S(1)}, u32[]{:S(2)}, u32[]{:S(2)}) collective-permute-start(bf16[32,1024]{1,0:T(8,128)(2,1)S(1)} %get-tuple-element.84), channel_id=1, source_target_pairs={{0,16},{16,0},{32,48},{48,32},{64,80},{80,64},{96,112},{112,96},{1... | collective-permute-start | bytes 196616 | tf_op jit(solution)/shard_map/ppermute | solution.py:376
  12.9 4.6 %collective-permute-start.7 = (bf16[32,2304]{1,0:T(8,128)(2,1)S(1)}, bf16[32,2304]{1,0:T(8,128)(2,1)S(1)}, u32[]{:S(2)}, u32[]{:S(2)}) collective-permute-start(bf16[32,2304]{1,0:T(8,128)(2,1)S(1)} %get-tuple-element.99), channel_id=1, source_target_pairs={{16,0},{32,16},{48,32},{64,48},{80,64},{96,80},{112,96},{128,112},... | collective-permute-start | bytes 442376 | tf_op jit(solution)/shard_map/ppermute | solution.py:368
  14.5 3.6 %collective-permute-start.6 = (bf16[32,2304]{1,0:T(8,128)(2,1)S(1)}, bf16[32,2304]{1,0:T(8,128)(2,1)S(1)}, u32[]{:S(2)}, u32[]{:S(2)}) collective-permute-start(bf16[32,2304]{1,0:T(8,128)(2,1)S(1)} %get-tuple-element.98), channel_id=1, source_target_pairs={{0,16},{16,32},{32,48},{48,64},{64,80},{80,96},{96,112},{112,128},... | collective-permute-start | bytes 442376 | tf_op jit(solution)/shard_map/ppermute | solution.py:368
  15.0 1.9 %collective-permute-start.4 = (bf16[32,1280]{1,0:T(8,128)(2,1)S(1)}, bf16[32,1280]{1,0:T(8,128)(2,1)S(1)}, u32[]{:S(2)}, u32[]{:S(2)}) collective-permute-start(bf16[32,1280]{1,0:T(8,128)(2,1)S(1)} %get-tuple-element.96), channel_id=1, source_target_pairs={{0,16},{16,0},{32,48},{48,32},{64,80},{80,64},{96,112},{112,96},{1... | collective-permute-start | bytes 245768 | tf_op jit(solution)/shard_map/ppermute | solution.py:376
  15.7 1.3 %collective-permute-start.5 = (bf16[32,1024]{1,0:T(8,128)(2,1)S(1)}, bf16[32,1024]{1,0:T(8,128)(2,1)S(1)}, u32[]{:S(2)}, u32[]{:S(2)}) collective-permute-start(bf16[32,1024]{1,0:T(8,128)(2,1)S(1)} %get-tuple-element.97), channel_id=1, source_target_pairs={{0,16},{16,0},{32,48},{48,32},{64,80},{80,64},{96,112},{112,96},{1... | collective-permute-start | bytes 196616 | tf_op jit(solution)/shard_map/ppermute | solution.py:376
  18.1 5.8 %collective-permute-start.11 = (bf16[32,2304]{1,0:T(8,128)(2,1)S(1)}, bf16[32,2304]{1,0:T(8,128)(2,1)S(1)}, u32[]{:S(2)}, u32[]{:S(2)}) collective-permute-start(bf16[32,2304]{1,0:T(8,128)(2,1)S(1)} %get-tuple-element.107), channel_id=1, source_target_pairs={{0,16},{16,32},{32,48},{48,64},{64,80},{80,96},{96,112},{112,128},... | collective-permute-start | bytes 442376 | tf_op jit(solution)/shard_map/ppermute | solution.py:368
  18.2 7.0 %collective-permute-start.10 = (bf16[32,2304]{1,0:T(8,128)(2,1)S(1)}, bf16[32,2304]{1,0:T(8,128)(2,1)S(1)}, u32[]{:S(2)}, u32[]{:S(2)}) collective-permute-start(bf16[32,2304]{1,0:T(8,128)(2,1)S(1)} %get-tuple-element.106), channel_id=1, source_target_pairs={{16,0},{32,16},{48,32},{64,48},{80,64},{96,80},{112,96},{128,112},... | collective-permute-start | bytes 442376 | tf_op jit(solution)/shard_map/ppermute | solution.py:368
  22.1 1.4 %collective-permute-start.8 = (bf16[32,1280]{1,0:T(8,128)(2,1)S(1)}, bf16[32,1280]{1,0:T(8,128)(2,1)S(1)}, u32[]{:S(2)}, u32[]{:S(2)}) collective-permute-start(bf16[32,1280]{1,0:T(8,128)(2,1)S(1)} %get-tuple-element.104), channel_id=1, source_target_pairs={{0,16},{16,0},{32,48},{48,32},{64,80},{80,64},{96,112},{112,96},{1... | collective-permute-start | bytes 245768 | tf_op jit(solution)/shard_map/ppermute | solution.py:376
  22.1 1.4 %collective-permute-start.9 = (bf16[32,1024]{1,0:T(8,128)(2,1)S(1)}, bf16[32,1024]{1,0:T(8,128)(2,1)S(1)}, u32[]{:S(2)}, u32[]{:S(2)}) collective-permute-start(bf16[32,1024]{1,0:T(8,128)(2,1)S(1)} %get-tuple-element.105), channel_id=1, source_target_pairs={{0,16},{16,0},{32,48},{48,32},{64,80},{80,64},{96,112},{112,96},{1... | collective-permute-start | bytes 196616 | tf_op jit(solution)/shard_map/ppermute | solution.py:376
  23.9 4.6 %collective-permute-start.15 = (bf16[32,2304]{1,0:T(8,128)(2,1)S(1)}, bf16[32,2304]{1,0:T(8,128)(2,1)S(1)}, u32[]{:S(2)}, u32[]{:S(2)}) collective-permute-start(bf16[32,2304]{1,0:T(8,128)(2,1)S(1)} %get-tuple-element.115), channel_id=1, source_target_pairs={{16,0},{32,16},{48,32},{64,48},{80,64},{96,80},{112,96},{128,112},... | collective-permute-start | bytes 442376 | tf_op jit(solution)/shard_map/ppermute | solution.py:368
  25.8 3.3 %collective-permute-start.14 = (bf16[32,2304]{1,0:T(8,128)(2,1)S(1)}, bf16[32,2304]{1,0:T(8,128)(2,1)S(1)}, u32[]{:S(2)}, u32[]{:S(2)}) collective-permute-start(bf16[32,2304]{1,0:T(8,128)(2,1)S(1)} %get-tuple-element.114), channel_id=1, source_target_pairs={{0,16},{16,32},{32,48},{48,64},{64,80},{80,96},{96,112},{112,128},... | collective-permute-start | bytes 442376 | tf_op jit(solution)/shard_map/ppermute | solution.py:368
  26.1 2.0 %collective-permute-start.12 = (bf16[32,1280]{1,0:T(8,128)(2,1)S(1)}, bf16[32,1280]{1,0:T(8,128)(2,1)S(1)}, u32[]{:S(2)}, u32[]{:S(2)}) collective-permute-start(bf16[32,1280]{1,0:T(8,128)(2,1)S(1)} %get-tuple-element.112), channel_id=1, source_target_pairs={{0,16},{16,0},{32,48},{48,32},{64,80},{80,64},{96,112},{112,96},{1... | collective-permute-start | bytes 245768 | tf_op jit(solution)/shard_map/ppermute | solution.py:376
  26.8 1.3 %collective-permute-start.13 = (bf16[32,1024]{1,0:T(8,128)(2,1)S(1)}, bf16[32,1024]{1,0:T(8,128)(2,1)S(1)}, u32[]{:S(2)}, u32[]{:S(2)}) collective-permute-start(bf16[32,1024]{1,0:T(8,128)(2,1)S(1)} %get-tuple-element.113), channel_id=1, source_target_pairs={{0,16},{16,0},{32,48},{48,32},{64,80},{80,64},{96,112},{112,96},{1... | collective-permute-start | bytes 196616 | tf_op jit(solution)/shard_map/ppermute | solution.py:376
  29.1 4.7 %collective-permute-start.19 = (bf16[32,2304]{1,0:T(8,128)(2,1)S(1)}, bf16[32,2304]{1,0:T(8,128)(2,1)S(1)}, u32[]{:S(2)}, u32[]{:S(2)}) collective-permute-start(bf16[32,2304]{1,0:T(8,128)(2,1)S(1)} %get-tuple-element.123), channel_id=1, source_target_pairs={{0,16},{16,32},{32,48},{48,64},{64,80},{80,96},{96,112},{112,128},... | collective-permute-start | bytes 442376 | tf_op jit(solution)/shard_map/ppermute | solution.py:368
  29.1 4.9 %collective-permute-start.18 = (bf16[32,2304]{1,0:T(8,128)(2,1)S(1)}, bf16[32,2304]{1,0:T(8,128)(2,1)S(1)}, u32[]{:S(2)}, u32[]{:S(2)}) collective-permute-start(bf16[32,2304]{1,0:T(8,128)(2,1)S(1)} %get-tuple-element.122), channel_id=1, source_target_pairs={{16,0},{32,16},{48,32},{64,48},{80,64},{96,80},{112,96},{128,112},... | collective-permute-start | bytes 442376 | tf_op jit(solution)/shard_map/ppermute | solution.py:368
  31.9 1.4 %collective-permute-start.16 = (bf16[32,1280]{1,0:T(8,128)(2,1)S(1)}, bf16[32,1280]{1,0:T(8,128)(2,1)S(1)}, u32[]{:S(2)}, u32[]{:S(2)}) collective-permute-start(bf16[32,1280]{1,0:T(8,128)(2,1)S(1)} %get-tuple-element.120), channel_id=1, source_target_pairs={{0,16},{16,0},{32,48},{48,32},{64,80},{80,64},{96,112},{112,96},{1... | collective-permute-start | bytes 245768 | tf_op jit(solution)/shard_map/ppermute | solution.py:376
  32.0 1.4 %collective-permute-start.17 = (bf16[32,1024]{1,0:T(8,128)(2,1)S(1)}, bf16[32,1024]{1,0:T(8,128)(2,1)S(1)}, u32[]{:S(2)}, u32[]{:S(2)}) collective-permute-start(bf16[32,1024]{1,0:T(8,128)(2,1)S(1)} %get-tuple-element.121), channel_id=1, source_target_pairs={{0,16},{16,0},{32,48},{48,32},{64,80},{80,64},{96,112},{112,96},{1... | collective-permute-start | bytes 196616 | tf_op jit(solution)/shard_map/ppermute | solution.py:376
  34.6 5.4 %collective-permute-start.22 = (bf16[32,2304]{1,0:T(8,128)(2,1)S(1)}, bf16[32,2304]{1,0:T(8,128)(2,1)S(1)}, u32[]{:S(2)}, u32[]{:S(2)}) collective-permute-start(bf16[32,2304]{1,0:T(8,128)(2,1)S(1)} %get-tuple-element.131), channel_id=1, source_target_pairs={{0,16},{16,32},{32,48},{48,64},{64,80},{80,96},{96,112},{112,128},... | collective-permute-start | bytes 442376 | tf_op jit(solution)/shard_map/ppermute | solution.py:368
  34.6 5.4 %collective-permute-start.23 = (bf16[32,2304]{1,0:T(8,128)(2,1)S(1)}, bf16[32,2304]{1,0:T(8,128)(2,1)S(1)}, u32[]{:S(2)}, u32[]{:S(2)}) collective-permute-start(bf16[32,2304]{1,0:T(8,128)(2,1)S(1)} %get-tuple-element.132), channel_id=1, source_target_pairs={{16,0},{32,16},{48,32},{64,48},{80,64},{96,80},{112,96},{128,112},... | collective-permute-start | bytes 442376 | tf_op jit(solution)/shard_map/ppermute | solution.py:368
  35.5 4.2 %collective-permute-start.20 = (bf16[32,1280]{1,0:T(8,128)(2,1)S(1)}, bf16[32,1280]{1,0:T(8,128)(2,1)S(1)}, u32[]{:S(2)}, u32[]{:S(2)}) collective-permute-start(bf16[32,1280]{1,0:T(8,128)(2,1)S(1)} %get-tuple-element.128), channel_id=1, source_target_pairs={{0,16},{16,0},{32,48},{48,32},{64,80},{80,64},{96,112},{112,96},{1... | collective-permute-start | bytes 245768 | tf_op jit(solution)/shard_map/ppermute | solution.py:376
  38.4 1.3 %collective-permute-start.21 = (bf16[32,1024]{1,0:T(8,128)(2,1)S(1)}, bf16[32,1024]{1,0:T(8,128)(2,1)S(1)}, u32[]{:S(2)}, u32[]{:S(2)}) collective-permute-start(bf16[32,1024]{1,0:T(8,128)(2,1)S(1)} %get-tuple-element.129), channel_id=1, source_target_pairs={{0,16},{16,0},{32,48},{48,32},{64,80},{80,64},{96,112},{112,96},{1... | collective-permute-start | bytes 196616 | tf_op jit(solution)/shard_map/ppermute | solution.py:376
